TPU v7x, 256 devices: a whole 4x4x8 slice. The times are simulated.
256 devices in a mesh: span: 16 (over x, y), plane: 16 (over z, core).
Axes of the slice: x: 4, y: 4, z: 8, core: 2. Of those that a mesh axis runs over, the one named last changes fastest.
Arguments:
- state: float32 [512, 80, 640], P('span', 'plane'), may hold values from -8 to 8, as said below
- wall_tag: int32 [128], replicated, may hold values 0 or 1
Outputs:
- new_state: float32 [512, 80, 640], P('span', 'plane')
Inputs may be any that keep to these rules, and one draw needn't show every extreme that they name: `state`: spectral coefficients of the conserved variable.
All inputs are finite; a program needn't handle non-finite values.
Results may differ from a plain program's by a relative error of at most 0.0001.
Values sent between devices are 32-bit elements; how exact they have to be, the bound alone decides.
No kernel may reach another device: no remote copies, remote signals or barrier semaphores. Data moves between devices by JAX's collectives and lax.ppermute only.
A program may use at most 64 MiB of HBM per device.

v0:
```python
import math

import jax
import jax.numpy as jnp
import numpy as np
from jax import lax
from jax.experimental import pallas as pl
from jax.experimental.pallas import tpu as pltpu
from jax.sharding import PartitionSpec as P

KMODES = 256
PLANES = 768
HALF = 384
ITERS = 3
GRID = 16
STEP_SIZE = 0.03
VISCOUS = 0.05
SPAN_STIFF = 4.0


def gll_tables():
    abscissae = np.array([-1.0, -math.sqrt(3.0 / 7.0), 0.0, math.sqrt(3.0 / 7.0), 1.0])
    weights = np.array([0.1, 49.0 / 90.0, 32.0 / 45.0, 49.0 / 90.0, 0.1])
    squared = abscissae * abscissae
    legendre = (35.0 * squared * squared - 30.0 * squared + 3.0) / 8.0
    identity = np.eye(5)
    spacing = abscissae[:, None] - abscissae[None, :] + identity
    differ = np.where(identity > 0, 0.0, legendre[:, None] / legendre[None, :] / spacing)
    differ[0, 0] = -5.0
    differ[4, 4] = 5.0
    stiffness = differ.T @ (weights[:, None] * differ)
    return differ, weights, stiffness


DIFFER, WEIGHTS, STIFFNESS = gll_tables()


def split_table(table):
    high = table.astype(np.float32).astype(jnp.bfloat16)
    low = (table - high.astype(np.float64)).astype(np.float32).astype(jnp.bfloat16)
    return jnp.asarray(high), jnp.asarray(low)


def transform_tables():
    plane = np.arange(HALF)
    inverse, forward = [], []
    for parity in range(2):
        k = 2 * np.arange(128) + parity
        angle = (k[:, None] * plane[None, :] % PLANES) * (2.0 * math.pi / PLANES)
        cosine, sine = np.cos(angle), np.sin(angle)
        inverse.append(np.concatenate([cosine, sine]) / math.sqrt(KMODES))
        scale = np.where(k == 0, 1.0, 2.0)[:, None] * math.sqrt(KMODES) / PLANES * STEP_SIZE
        ratio = (k / KMODES)[:, None]
        from_rhs = np.concatenate([cosine, sine]) * np.concatenate([scale, scale])
        from_flux = np.concatenate([-ratio * scale * sine, ratio * scale * cosine])
        forward.append(np.concatenate([from_rhs, from_flux], axis=1))
    return split_table(np.stack(inverse)), split_table(np.stack(forward))


def dot(left, right, contract):
    return lax.dot_general(
        left, right, (contract, ((), ())), preferred_element_type=jnp.float32
    )


def halves(value):
    high = value.astype(jnp.bfloat16)
    low = (value - high.astype(jnp.float32)).astype(jnp.bfloat16)
    return high, low


def thirds(value):
    high = value.astype(jnp.bfloat16)
    rest = value - high.astype(jnp.float32)
    middle = rest.astype(jnp.bfloat16)
    low = (rest - middle.astype(jnp.float32)).astype(jnp.bfloat16)
    return high, middle, low


def dot_split(left, right, contract):
    (left_high, left_low), (right_high, right_low) = left, right
    return (
        dot(left_high, right_low, contract)
        + dot(left_low, right_high, contract)
        + dot(left_high, right_high, contract)
    )


def column_order():
    column = lax.broadcasted_iota(jnp.int32, (640, 128), 0)
    element = lax.broadcasted_iota(jnp.int32, (640, 128), 1)
    tiles = [jnp.where(column == 5 * element + i, 1.0, 0.0).astype(jnp.bfloat16) for i in range(5)]
    return jnp.concatenate(tiles, axis=1)


def exchange_chunks(values):
    values = list(values)
    lane = lax.broadcasted_iota(jnp.int32, values[0].shape, 1)
    for bit in (1, 2, 4, 8):
        upper = (lane & (8 * bit)) != 0
        for a in range(16):
            if a & bit == 0:
                first, second = values[a], values[a | bit]
                values[a] = jnp.where(upper, pltpu.roll(second, 8 * bit, 1), first)
                values[a | bit] = jnp.where(upper, second, pltpu.roll(first, 128 - 8 * bit, 1))
    return values


def pack_kernel(state_ref, out_ref, chunk_ref):
    stacked = jnp.concatenate([state_ref[j] for j in range(5)], axis=0)
    order = column_order()
    contract = ((1,), (0,))
    high, middle, low = thirds(stacked)
    nodes = dot(low, order, contract) + dot(middle, order, contract) + dot(high, order, contract)
    for i in range(5):
        chunk_ref[160 * i : 160 * i + 160, :] = nodes[:, 128 * i : 128 * i + 128]
    chunk = [
        jnp.concatenate(
            [chunk_ref[pl.ds(160 * i + 32 * j + t, 8, stride=4), :] for t in range(4)], axis=0
        )
        for j in range(5)
        for i in range(5)
    ]
    lane = lax.broadcasted_iota(jnp.int32, (32, 128), 1) & 7
    for j in range(5):
        left = pltpu.roll(chunk[j * 5 + 4], 1, 1)
        right = pltpu.roll(chunk[j * 5], 127, 1)
        chunk.append(jnp.where(lane == 0, left, jnp.where(lane == 7, right, 0.0)))
    zero = jnp.zeros((32, 128), jnp.float32)
    chunk = chunk + [zero, zero]
    for half in range(2):
        block = exchange_chunks(chunk[16 * half : 16 * half + 16])
        for d in range(GRID):
            out_ref[d, :, 128 * half : 128 * half + 128] = block[d]


def turn_kernel(modal_ref, nodal_ref, low_ref, high_ref):
    for parity in range(2):
        rows = [
            modal_ref[s, 16 * parity + 8 * t : 16 * parity + 8 * t + 8, :]
            for t in range(2)
            for s in range(GRID)
        ]
        turned = jnp.concatenate(rows, axis=0).T
        nodal_ref[parity] = turned
        low_ref[parity] = turned[0:40]
        high_ref[parity] = turned[160:200]


def synthesize(nodal, high_ref, low_ref):
    part = [
        dot_split(
            halves(nodal[parity]), (high_ref[parity], low_ref[parity]), ((1,), (0,))
        )
        for parity in range(2)
    ]
    return part[0] + part[1], part[0] - part[1]


def two_point(left, right):
    mean = (left * left + left * right + right * right) * (1.0 / 6.0)
    speed = jnp.maximum(jnp.abs(left), jnp.abs(right))
    return mean - 0.5 * speed * (right - left)


def volume_kernel(nodal_ref, high_ref, low_ref, field_ref, rhs_ref, side_ref):
    nodal = [nodal_ref[0], nodal_ref[1]]
    pair = synthesize(nodal, high_ref, low_ref)
    for q in range(2):
        field_ref[:, HALF * q : HALF * q + HALF] = pair[q][0:200]
        side_ref[:, HALF * q : HALF * q + HALF] = pair[q][200:240]
    row = lax.broadcasted_iota(jnp.int32, (8, 128), 0)

    def column(block, carry):
        lanes = pl.ds(pl.multiple_of(block * 128, 128), 128)
        f = [field_ref[8 * n : 8 * n + 8, lanes] for n in range(25)]
        square = [v * v for v in f]
        for j in range(5):
            for i in range(5):
                n = j * 5 + i
                plain = None
                power = None
                for other in range(5):
                    terms = [(DIFFER[i][other], j * 5 + other), (DIFFER[j][other], other * 5 + i)]
                    for weight, m in terms:
                        if weight == 0.0:
                            continue
                        weight = float(weight) / -3.0
                        plain = weight * f[m] if plain is None else plain + weight * f[m]
                        power = weight * square[m] if power is None else power + weight * square[m]
                total = power + f[n] * plain
                own = (i == 4) + (j == 4) - (i == 0) - (j == 0)
                if own:
                    total = total + (5.0 * own) * square[n]
                if i == 0 or i == 4:
                    side = side_ref[8 * j : 8 * j + 8, lanes]
                    if i == 0:
                        left = jnp.where(row == 0, side, pltpu.roll(f[j * 5 + 4], 1, 0))
                        total = total + 10.0 * two_point(left, f[n])
                    else:
                        right = jnp.where(row == 7, side, pltpu.roll(f[j * 5], 7, 0))
                        total = total - 10.0 * two_point(f[n], right)
                rhs_ref[8 * n : 8 * n + 8, lanes] = total
        return carry

    lax.fori_loop(0, PLANES // 128, column, 0)


def forward_kernel(
    modal_ref, field_ref, rhs_ref, below_ref, above_ref, mirror_ref, edge_ref, inverse_high_ref,
    inverse_low_ref, forward_high_ref, forward_low_ref, out_ref, outer_ref,
):
    bottom = edge_ref[0] == 1
    top = edge_ref[1] == 1
    outer = [
        jnp.concatenate([below_ref[parity], above_ref[parity]], axis=0) for parity in range(2)
    ]
    pair = synthesize(outer, inverse_high_ref, inverse_low_ref)
    for q in range(2):
        outer_ref[:, HALF * q : HALF * q + HALF] = pair[q]
    mirror = jnp.concatenate([mirror_ref[...]] * 6, axis=1)
    bottom_rows, top_rows = [], []
    for i in range(5):
        inside = field_ref[8 * i : 8 * i + 8, :]
        below = jnp.where(bottom, mirror * inside, outer_ref[8 * i : 8 * i + 8, :])
        bottom_rows.append(
            rhs_ref[8 * i : 8 * i + 8, :] + 10.0 * two_point(below, inside)
        )
        n = 20 + i
        inside = field_ref[8 * n : 8 * n + 8, :]
        above = jnp.where(top, inside, outer_ref[40 + 8 * i : 48 + 8 * i, :])
        top_rows.append(rhs_ref[8 * n : 8 * n + 8, :] - 10.0 * two_point(inside, above))
    rhs = jnp.concatenate(bottom_rows + [rhs_ref[40:160, :]] + top_rows, axis=0)
    field = field_ref[...]
    flux = 0.5 * field * field
    for parity in range(2):
        if parity == 0:
            folded = [rhs[:, :HALF] + rhs[:, HALF:], flux[:, :HALF] + flux[:, HALF:]]
        else:
            folded = [rhs[:, :HALF] - rhs[:, HALF:], flux[:, :HALF] - flux[:, HALF:]]
        planar = jnp.concatenate(folded, axis=1)
        change = dot_split(
            (forward_high_ref[parity], forward_low_ref[parity]), halves(planar), ((1,), (1,))
        )
        for t in range(2):
            first = 16 * parity + 8 * t
            modal = jnp.concatenate(
                [modal_ref[s, first : first + 8, :] for s in range(GRID)], axis=0
            )
            rows = change[128 * t : 128 * t + 128]
            out_ref[pl.ds(4 * parity + 2 * t, 128, stride=8), :] = modal[:, :128] + rows[:, :128]
            out_ref[pl.ds(4 * parity + 2 * t + 1, 128, stride=8), 0:72] = (
                modal[:, 128:200] + rows[:, 128:200]
            )


def assemble(values):
    values = list(values)
    row = lax.broadcasted_iota(jnp.int32, (32, 128), 0) & 15
    for j in range(5):
        joint = values[j * 5 + 4] + pltpu.roll(values[j * 5], 127, 1)
        values[j * 5 + 4] = joint
        values[j * 5] = pltpu.roll(joint, 1, 1)
    for i in range(5):
        lower, upper = values[i], values[20 + i]
        values[i] = lower + jnp.where(row == 0, 0.0, pltpu.roll(upper, 1, 0))
        values[20 + i] = upper + jnp.where(row == 15, 0.0, pltpu.roll(lower, 31, 0))
    return values


def mode_sum(total):
    sums = [
        jnp.sum(total[16 * t : 16 * t + 16], axis=(0, 1), keepdims=True) for t in range(2)
    ]
    return jnp.concatenate([jnp.broadcast_to(s, (16, 128)) for s in sums], axis=0)


def weighted_square(values):
    row = lax.broadcasted_iota(jnp.int32, (32, 128), 0) & 15
    total = None
    for j in range(5):
        part = None
        for i in range(5):
            v = values[j * 5 + i]
            term = v * v if 0 < i < 4 else 0.5 * (v * v)
            part = term if part is None else part + term
        if j == 0:
            part = jnp.where(row == 0, part, 0.5 * part)
        elif j == 4:
            part = jnp.where(row == 15, part, 0.5 * part)
        total = part if total is None else total + part
    return mode_sum(total)


def solve_kernel(shift_ref, modal_ref, out_ref, residual_ref, direction_ref, applied_ref):
    shift = shift_ref[0, 0]
    predicted = []
    for half in range(2):
        block = [
            jnp.concatenate(
                [
                    modal_ref[pl.ds(64 * s + 2 * t + half, 16, stride=4), :] for t in range(2)
                ],
                axis=0,
            )
            for s in range(GRID)
        ]
        predicted += exchange_chunks(block)
    load = assemble(
        [float(WEIGHTS[n // 5] * WEIGHTS[n % 5]) * predicted[n] for n in range(25)]
    )
    for n in range(25):
        residual_ref[n] = load[n]
        direction_ref[n] = load[n]
    norm = weighted_square(load)
    for step in range(ITERS):
        direction = [direction_ref[n] for n in range(25)]
        total = None
        local = []
        for j in range(5):
            for i in range(5):
                n = j * 5 + i
                mass = float(WEIGHTS[j] * WEIGHTS[i])
                diagonal = VISCOUS * float(
                    WEIGHTS[j] * STIFFNESS[i][i] + WEIGHTS[i] * STIFFNESS[j][j]
                )
                value = (shift * mass + diagonal) * direction[n]
                for other in range(5):
                    if other != i:
                        weight = VISCOUS * float(WEIGHTS[j] * STIFFNESS[i][other])
                        value = value + weight * direction[j * 5 + other]
                    if other != j:
                        weight = VISCOUS * float(WEIGHTS[i] * STIFFNESS[j][other])
                        value = value + weight * direction[other * 5 + i]
                local.append(value)
                term = value * direction[n]
                total = term if total is None else total + term
        length = norm / mode_sum(total)
        if step < ITERS - 1:
            applied = assemble(local)
            residual = [residual_ref[n] - length * applied[n] for n in range(25)]
            fresh = weighted_square(residual)
            ratio = fresh / norm
            norm = fresh
        for n in range(25):
            gain = length * direction[n]
            applied_ref[n] = gain if step == 0 else applied_ref[n] + gain
            if step < ITERS - 1:
                residual_ref[n] = residual[n]
                direction_ref[n] = residual[n] + ratio * direction[n]
    for n in range(25):
        for t in range(2):
            out_ref[pl.ds(25 * t + n, 16, stride=56), :] = applied_ref[n, 16 * t : 16 * t + 16, :]


def unpack_kernel(modal_ref, out_ref, column_ref):
    order = column_order()
    rows = []
    for j in range(5):
        tiles = []
        for i in range(5):
            n = j * 5 + i
            tiles.append(
                jnp.concatenate(
                    [modal_ref[pl.ds(25 * t + n, 16, stride=56), :] for t in range(2)], axis=0
                )
            )
        rows.append(jnp.concatenate(tiles, axis=1))
    stacked = jnp.concatenate(rows, axis=0)
    contract = ((1,), (1,))
    high, middle, low = thirds(stacked)
    columns = dot(low, order, contract) + dot(middle, order, contract) + dot(high, order, contract)
    for i in range(5):
        for j in range(5):
            for t in range(2):
                first = 32 * j + 16 * t
                column_ref[pl.ds(160 * i + 32 * j + t, 16, stride=2), :] = columns[
                    first : first + 16, 128 * i : 128 * i + 128
                ]
    for j in range(5):
        for i in range(5):
            first = 160 * i + 32 * j
            out_ref[j, :, 128 * i : 128 * i + 128] = column_ref[first : first + 32, :]


def call(kernel, name, out_shapes, *args, smem=(), scratch=()):
    vmem = pl.BlockSpec(memory_space=pltpu.VMEM)
    scalar = pl.BlockSpec(memory_space=pltpu.SMEM)
    return pl.pallas_call(
        kernel,
        name=name,
        out_shape=[jax.ShapeDtypeStruct(s, jnp.float32) for s in out_shapes],
        in_specs=[scalar if n in smem else vmem for n in range(len(args))],
        out_specs=[vmem] * len(out_shapes),
        scratch_shapes=list(scratch),
        compiler_params=pltpu.CompilerParams(vmem_limit_bytes=48 * 1024 * 1024),
    )(*args)


def on_device(state, wall_tag):
    (inverse_high, inverse_low), (forward_high, forward_low) = transform_tables()
    span = lax.axis_index("span")
    plane = lax.axis_index("plane")
    last = lax.axis_size("plane") - 1
    wavenumber = (span * GRID + plane).astype(jnp.float32) / KMODES
    shift = (1.0 + SPAN_STIFF * wavenumber * wavenumber).reshape(1, 1)
    edge = jnp.stack([plane == 0, plane == last]).astype(jnp.int32)
    tags = lax.dynamic_slice_in_dim(wall_tag, span * 8, 8)
    mirror = jnp.broadcast_to(jnp.where(tags == 1, -1.0, 1.0).astype(jnp.float32)[:, None], (8, 128))

    (packed,) = call(
        pack_kernel, "pack", [(16, 32, 256)], jnp.transpose(state, (1, 0, 2)),
        scratch=[pltpu.VMEM((800, 128), jnp.float32)],
    )
    modal = lax.all_to_all(packed, "span", 0, 0, tiled=True)
    nodal, low, high = call(
        turn_kernel, "turn", [(2, 256, 256), (2, 40, 256), (2, 40, 256)], modal
    )
    below = lax.ppermute(high, "plane", [(p, (p + 1) % GRID) for p in range(GRID)])
    above = lax.ppermute(low, "plane", [(p, (p - 1) % GRID) for p in range(GRID)])
    field, rhs = call(
        volume_kernel, "volume", [(200, PLANES), (200, PLANES)], nodal, inverse_high, inverse_low,
        scratch=[pltpu.VMEM((40, PLANES), jnp.float32)],
    )
    (sent,) = call(
        forward_kernel, "forward", [(1024, 128)], modal, field, rhs, below, above, mirror, edge,
        inverse_high, inverse_low, forward_high, forward_low, smem=(6,),
        scratch=[pltpu.VMEM((80, PLANES), jnp.float32)],
    )
    predicted = lax.all_to_all(sent.reshape(256, 4, 128), ("span", "plane"), 0, 0, tiled=True)
    (solved,) = call(
        solve_kernel, "solve", [(896, 128)], shift, predicted.reshape(1024, 128), smem=(0,),
        scratch=[pltpu.VMEM((25, 32, 128), jnp.float32)] * 3,
    )
    returned = lax.all_to_all(solved.reshape(16, 56, 128), "plane", 0, 0, tiled=True)
    (columns,) = call(
        unpack_kernel, "unpack", [(5, 32, 640)], returned.reshape(896, 128),
        scratch=[pltpu.VMEM((800, 128), jnp.float32)],
    )
    return jnp.transpose(columns, (1, 0, 2))


def solution(mesh):
    in_specs = (P("span", "plane", None), P())
    out_specs = P("span", "plane", None)
    return jax.shard_map(
        on_device, mesh=mesh, in_specs=in_specs, out_specs=out_specs, check_vma=False
    )
```

profile of v0, /device:TPU:1, one launch (start us, length us, event | category | flops | bytes accessed | tf_op | source)
XLA Modules:
  0.0 86.3 jit_solution(10369382835136908105)
XLA Ops:
  0.0 1.0 %copy-done.4 = f32[32,5,640]{2,0,1:T(8,128)S(1)} copy-done((f32[32,5,640]{2,0,1:T(8,128)S(1)}, f32[32,5,640]{2,0,1:T(8,128)}, u32[]{:S(2)}) %copy-start.4) | copy-done | bytes 409624
  1.0 2.2 %pack.1 = f32[16,32,256]{2,1,0:T(8,128)} custom-call(f32[5,32,640]{2,1,0:T(8,128)S(1)} %bitcast.12), custom_call_target="tpu_custom_call" | custom-call | tf_op jit(solution)/shard_map/pack/pallas_call | solution.py:389
  3.2 7.7 %all-to-all-start = ((f32[16,32,256]{2,1,0:T(8,128)}), f32[16,32,256]{2,1,0:T(8,128)S(1)}, u32[]{:S(2)}, u32[]{:S(2)}) async-start(f32[16,32,256]{2,1,0:T(8,128)} %pack.1), calls=%async_computation | async-start | bytes 1048576 | tf_op jit(solution)/shard_map/all_to_all | solution.py:415
  10.9 0.0 copy-start
  10.9 0.0 copy-done.5
  10.9 0.1 compare_select_fusion
  11.0 10.3 %all-to-all-done.modal_ref = f32[16,32,256]{2,1,0:T(8,128)S(1)} async-done(((f32[16,32,256]{2,1,0:T(8,128)}), f32[16,32,256]{2,1,0:T(8,128)S(1)}, u32[]{:S(2)}, u32[]{:S(2)}) %all-to-all-start) | async-done | bytes 524320 | tf_op jit(solution)/shard_map/all_to_all | solution.py:415
  21.3 0.2 turn.1
  21.5 0.0 copy-start.2
  21.5 3.6 %collective-permute-start = (f32[2,40,256]{2,1,0:T(8,128)S(1)}, f32[2,40,256]{2,1,0:T(8,128)S(1)}, u32[]{:S(2)}, u32[]{:S(2)}) collective-permute-start(f32[2,40,256]{2,1,0:T(8,128)S(1)} %get-tuple-element.13), channel_id=1, source_target_pairs={{0,1},{1,2},{2,3},{3,4},{4,5},{5,6},{6,7},{7,8},{8,9},{9,10},{10,1... | collective-permute-start | bytes 245768 | tf_op jit(solution)/shard_map/ppermute | solution.py:419
  25.1 0.0 collective-permute-start.1
  25.1 0.1 add_convert_fusion.edge_ref
  25.2 0.0 copy-done.1
  25.2 0.0 copy-done
  25.2 1.5 %volume.1 = (f32[200,768]{1,0:T(8,128)S(1)}, f32[200,768]{1,0:T(8,128)S(1)}) custom-call(f32[2,256,256]{2,1,0:T(8,128)S(1)} %get-tuple-element.10.nodal_ref, bf16[2,256,384]{2,1,0:T(8,128)(2,1)S(1)} %copy-done, bf16[2,256,384]{2,1,0:T(8,128)(2,1)S(1)} %copy-done.1), custom_call_target="tpu_custom_call" | custom-call | tf_op jit(solution)/shard_map/volume/pallas_call | solution.py:389
  26.7 0.0 collective-permute-done.below_ref
  26.7 2.5 %collective-permute-done.1.above_ref = f32[2,40,256]{2,1,0:T(8,128)S(1)} collective-permute-done((f32[2,40,256]{2,1,0:T(8,128)S(1)}, f32[2,40,256]{2,1,0:T(8,128)S(1)}, u32[]{:S(2)}, u32[]{:S(2)}) %collective-permute-start.1) | collective-permute-done | bytes 81952 | tf_op jit(solution)/shard_map/ppermute | solution.py:420
  29.2 0.1 broadcast_in_dim.16.mirror_ref
  29.3 2.6 %forward.1 = f32[1024,128]{1,0:T(8,128)} custom-call(f32[16,32,256]{2,1,0:T(8,128)S(1)} %all-to-all-done.modal_ref, f32[200,768]{1,0:T(8,128)S(1)} %get-tuple-element.11.field_ref, f32[200,768]{1,0:T(8,128)S(1)} %get-tuple-element.12.rhs_ref, f32[2,40,256]{2,1,0:T(8,128)S(1)} %collective-permute-done.below_ref, ...), custom_call_target="tpu_custom_call" | custom-call | tf_op jit(solution)/shard_map/forward/pallas_call | solution.py:389
  31.9 10.3 %all-to-all-start.1 = ((f32[256,4,128]{2,1,0:T(4,128)}), f32[256,4,128]{2,1,0:T(4,128)S(1)}, u32[]{:S(2)}, u32[]{:S(2)}) async-start(f32[256,4,128]{2,1,0:T(4,128)} %bitcast.4), calls=%async_computation.1 | async-start | bytes 1048576 | tf_op jit(solution)/shard_map/all_to_all | solution.py:430
  42.2 21.4 %all-to-all-done.1 = f32[256,4,128]{2,1,0:T(4,128)S(1)} async-done(((f32[256,4,128]{2,1,0:T(4,128)}), f32[256,4,128]{2,1,0:T(4,128)S(1)}, u32[]{:S(2)}, u32[]{:S(2)}) %all-to-all-start.1) | async-done | bytes 524320 | tf_op jit(solution)/shard_map/all_to_all | solution.py:430
  63.6 2.2 %solve.1 = f32[896,128]{1,0:T(8,128)S(1)} custom-call(f32[1,1]{1,0:T(1,128)} %bitcast.shift_ref, f32[1024,128]{1,0:T(8,128)S(1)} %bitcast.9), custom_call_target="tpu_custom_call" | custom-call | tf_op jit(solution)/shard_map/solve/pallas_call | solution.py:389
  65.8 18.8 %all_to_all.15 = f32[16,56,128]{2,1,0:T(8,128)S(1)} all-to-all(f32[16,56,128]{2,1,0:T(8,128)S(1)} %bitcast.10), channel_id=1, replica_groups=mesh['span'=16,'plane'=16] {'plane'}, dimensions={0} | all-to-all | bytes 917504 | tf_op jit(solution)/shard_map/all_to_all | solution.py:435
  84.6 1.7 %unpack.1 = f32[5,32,640]{2,1,0:T(8,128)} custom-call(f32[896,128]{1,0:T(8,128)S(1)} %bitcast.11), custom_call_target="tpu_custom_call" | custom-call | tf_op jit(solution)/shard_map/unpack/pallas_call | solution.py:389
  (6 shorter events, 0.0 us)
Async XLA Ops:
  0.0 1.0 %copy-start.4 = (f32[32,5,640]{2,0,1:T(8,128)S(1)}, f32[32,5,640]{2,0,1:T(8,128)}, u32[]{:S(2)}) copy-start(f32[32,5,640]{2,0,1:T(8,128)} %param.6) | copy-start | bytes 1228804
  1.0 9.9 %copy-start.5 = (s32[128]{0:T(128)S(1)}, s32[128]{0:T(128)}, u32[]{:S(2)}) copy-start(s32[128]{0:T(128)} %param.7) | copy-start | bytes 1540
  3.2 22.0 %copy-start.1 = (bf16[2,256,384]{2,1,0:T(8,128)(2,1)S(1)}, bf16[2,256,384]{2,1,0:T(8,128)(2,1)}, u32[]{:S(2)}) copy-start(bf16[2,256,384]{2,1,0:T(8,128)(2,1)} %constant.38.clone.low_ref.inverse_low_ref) | copy-start | bytes 1179652
  3.2 26.1 %copy-start.3 = (bf16[2,256,768]{2,1,0:T(8,128)(2,1)S(1)}, bf16[2,256,768]{2,1,0:T(8,128)(2,1)}, u32[]{:S(2)}) copy-start(bf16[2,256,768]{2,1,0:T(8,128)(2,1)} %constant.40.clone.forward_low_ref) | copy-start | bytes 2359300
  3.2 18.1 %all-to-all-start = ((f32[16,32,256]{2,1,0:T(8,128)}), f32[16,32,256]{2,1,0:T(8,128)S(1)}, u32[]{:S(2)}, u32[]{:S(2)}) async-start(f32[16,32,256]{2,1,0:T(8,128)} %pack.1), calls=%async_computation | async-start | bytes 1048576 | tf_op jit(solution)/shard_map/all_to_all | solution.py:415
  10.9 14.3 %copy-start = (bf16[2,256,384]{2,1,0:T(8,128)(2,1)S(1)}, bf16[2,256,384]{2,1,0:T(8,128)(2,1)}, u32[]{:S(2)}) copy-start(bf16[2,256,384]{2,1,0:T(8,128)(2,1)} %constant.37.clone.high_ref.inverse_high_ref) | copy-start | bytes 1179652
  21.5 7.8 %copy-start.2 = (bf16[2,256,768]{2,1,0:T(8,128)(2,1)S(1)}, bf16[2,256,768]{2,1,0:T(8,128)(2,1)}, u32[]{:S(2)}) copy-start(bf16[2,256,768]{2,1,0:T(8,128)(2,1)} %constant.39.clone.forward_high_ref) | copy-start | bytes 2359300
  21.5 5.2 %collective-permute-start = (f32[2,40,256]{2,1,0:T(8,128)S(1)}, f32[2,40,256]{2,1,0:T(8,128)S(1)}, u32[]{:S(2)}, u32[]{:S(2)}) collective-permute-start(f32[2,40,256]{2,1,0:T(8,128)S(1)} %get-tuple-element.13), channel_id=1, source_target_pairs={{0,1},{1,2},{2,3},{3,4},{4,5},{5,6},{6,7},{7,8},{8,9},{9,10},{10,1... | collective-permute-start | bytes 245768 | tf_op jit(solution)/shard_map/ppermute | solution.py:419
  25.1 4.1 %collective-permute-start.1 = (f32[2,40,256]{2,1,0:T(8,128)S(1)}, f32[2,40,256]{2,1,0:T(8,128)S(1)}, u32[]{:S(2)}, u32[]{:S(2)}) collective-permute-start(f32[2,40,256]{2,1,0:T(8,128)S(1)} %get-tuple-element.14), channel_id=1, source_target_pairs={{0,15},{1,0},{2,1},{3,2},{4,3},{5,4},{6,5},{7,6},{8,7},{9,8},{10,9... | collective-permute-start | bytes 245768 | tf_op jit(solution)/shard_map/ppermute | solution.py:420
  31.9 31.7 %all-to-all-start.1 = ((f32[256,4,128]{2,1,0:T(4,128)}), f32[256,4,128]{2,1,0:T(4,128)S(1)}, u32[]{:S(2)}, u32[]{:S(2)}) async-start(f32[256,4,128]{2,1,0:T(4,128)} %bitcast.4), calls=%async_computation.1 | async-start | bytes 1048576 | tf_op jit(solution)/shard_map/all_to_all | solution.py:430
where the time goes:
time: 86.6 us; the launch traced here: 86.3 us
  waiting for transfers between devices  34.1 us (39%)
  starting transfers between devices  21.6 us (25%)
  blocking collectives  18.8 us (22%)
  Pallas kernels  10.4 us (12%)
  local copies, waits for them, and re-layouts  1.09 us (1%)
    all_to_all x1, waiting for transfers between devices, on_device(): lax.all_to_all(sent.reshape(256, 4, 128), ('span', 'plane'), 0, 0, tiled=...  21.4 us
    all_to_all x1, blocking collectives, on_device(): lax.all_to_all(solved.reshape(16, 56, 128), 'plane', 0, 0, tiled=True)  18.8 us
    pallas_call x6, Pallas kernels, call(): pl.pallas_call(kernel, name=name, out_shape=[jax.ShapeDtypeStruct(s, jnp....  10.4 us
    all_to_all x1, starting transfers between devices, on_device(): lax.all_to_all(sent.reshape(256, 4, 128), ('span', 'plane'), 0, 0, tiled=...  10.3 us
    all_to_all x1, waiting for transfers between devices, on_device(): modal = lax.all_to_all(packed, 'span', 0, 0, tiled=True)  10.3 us
    all_to_all x1, starting transfers between devices, on_device(): modal = lax.all_to_all(packed, 'span', 0, 0, tiled=True)  7.71 us
    ppermute x1, starting transfers between devices, on_device(): lax.ppermute(high, 'plane', [(p, (p + 1) % GRID) for p in range(GRID)])  3.61 us
    ppermute x1, waiting for transfers between devices, on_device(): lax.ppermute(low, 'plane', [(p, (p - 1) % GRID) for p in range(GRID)])  2.5 us
  transfers between devices with their start and end apart: 4, of which 3 were waited for; matrix products, arithmetic and copies ran while one was open for 0% of the time, Pallas kernels for 2%

commit v1 on v0

--- a/solution.py
+++ b/solution.py
@@ -207,11 +207,11 @@
 
 
 def forward_kernel(
-    modal_ref, field_ref, rhs_ref, below_ref, above_ref, mirror_ref, edge_ref, inverse_high_ref,
+    modal_ref, field_ref, rhs_ref, below_ref, above_ref, mirror_ref, scalar_ref, inverse_high_ref,
     inverse_low_ref, forward_high_ref, forward_low_ref, out_ref, outer_ref,
 ):
-    bottom = edge_ref[0] == 1
-    top = edge_ref[1] == 1
+    bottom = scalar_ref[0] == 1
+    top = scalar_ref[1] == 1
     outer = [
         jnp.concatenate([below_ref[parity], above_ref[parity]], axis=0) for parity in range(2)
     ]
@@ -248,139 +248,216 @@
                 [modal_ref[s, first : first + 8, :] for s in range(GRID)], axis=0
             )
             rows = change[128 * t : 128 * t + 128]
-            out_ref[pl.ds(4 * parity + 2 * t, 128, stride=8), :] = modal[:, :128] + rows[:, :128]
-            out_ref[pl.ds(4 * parity + 2 * t + 1, 128, stride=8), 0:72] = (
-                modal[:, 128:200] + rows[:, 128:200]
-            )
-
-
-def assemble(values):
+            for s in range(GRID):
+                part = slice(8 * s, 8 * s + 8)
+                out_ref[s, first : first + 8, 0:128] = modal[part, :128] + rows[part, :128]
+                out_ref[s, first : first + 8, 128:200] = modal[part, 128:200] + rows[part, 128:200]
+
+
+def local_operator(values, shift):
+    out = []
+    for j in range(5):
+        for i in range(5):
+            n = j * 5 + i
+            mass = float(WEIGHTS[j] * WEIGHTS[i])
+            diagonal = VISCOUS * float(WEIGHTS[j] * STIFFNESS[i][i] + WEIGHTS[i] * STIFFNESS[j][j])
+            value = (shift * mass + diagonal) * values[n]
+            for other in range(5):
+                if other != i:
+                    weight = VISCOUS * float(WEIGHTS[j] * STIFFNESS[i][other])
+                    value = value + weight * values[j * 5 + other]
+                if other != j:
+                    weight = VISCOUS * float(WEIGHTS[i] * STIFFNESS[j][other])
+                    value = value + weight * values[other * 5 + i]
+            out.append(value)
+    return out
+
+
+def store_joined(values, joined_ref, low_ref, high_ref):
     values = list(values)
-    row = lax.broadcasted_iota(jnp.int32, (32, 128), 0) & 15
     for j in range(5):
         joint = values[j * 5 + 4] + pltpu.roll(values[j * 5], 127, 1)
         values[j * 5 + 4] = joint
         values[j * 5] = pltpu.roll(joint, 1, 1)
+    for n in range(25):
+        joined_ref[n] = values[n]
     for i in range(5):
-        lower, upper = values[i], values[20 + i]
-        values[i] = lower + jnp.where(row == 0, 0.0, pltpu.roll(upper, 1, 0))
-        values[20 + i] = upper + jnp.where(row == 15, 0.0, pltpu.roll(lower, 31, 0))
+        low_ref[i] = values[i]
+        high_ref[i] = values[20 + i]
+
+
+def assembled(scalar_ref, joined_ref, below_ref, above_ref):
+    values = [joined_ref[n] for n in range(25)]
+    for i in range(5):
+        values[i] = values[i] + jnp.where(scalar_ref[0] == 1, 0.0, below_ref[i])
+        values[20 + i] = values[20 + i] + jnp.where(scalar_ref[1] == 1, 0.0, above_ref[i])
     return values
 
 
-def mode_sum(total):
-    sums = [
-        jnp.sum(total[16 * t : 16 * t + 16], axis=(0, 1), keepdims=True) for t in range(2)
-    ]
-    return jnp.concatenate([jnp.broadcast_to(s, (16, 128)) for s in sums], axis=0)
-
-
-def weighted_square(values):
-    row = lax.broadcasted_iota(jnp.int32, (32, 128), 0) & 15
+def mode_terms(scalar_ref):
+    row = lax.broadcasted_iota(jnp.int32, (32, 128), 0)
+    mode_pair = 16 * scalar_ref[2] + 2 * (row & 7) + (row >> 4)
+    ratio = mode_pair.astype(jnp.float32) * (1.0 / KMODES)
+    shift = 1.0 + SPAN_STIFF * ratio * ratio
+    return shift, 0.2 * shift + 0.15
+
+
+def inner(scalar_ref, left, right):
     total = None
     for j in range(5):
         part = None
         for i in range(5):
-            v = values[j * 5 + i]
-            term = v * v if 0 < i < 4 else 0.5 * (v * v)
+            term = left[j * 5 + i] * right[j * 5 + i]
+            term = term if 0 < i < 4 else 0.5 * term
             part = term if part is None else part + term
         if j == 0:
-            part = jnp.where(row == 0, part, 0.5 * part)
+            part = jnp.where(scalar_ref[0] == 1, 1.0, 0.5) * part
         elif j == 4:
-            part = jnp.where(row == 15, part, 0.5 * part)
+            part = jnp.where(scalar_ref[1] == 1, 1.0, 0.5) * part
         total = part if total is None else total + part
-    return mode_sum(total)
-
-
-def solve_kernel(shift_ref, modal_ref, out_ref, residual_ref, direction_ref, applied_ref):
-    shift = shift_ref[0, 0]
+    return total
+
+
+def load_kernel(modal_ref, joined_ref, low_ref, high_ref):
     predicted = []
     for half in range(2):
-        block = [
-            jnp.concatenate(
-                [
-                    modal_ref[pl.ds(64 * s + 2 * t + half, 16, stride=4), :] for t in range(2)
-                ],
-                axis=0,
-            )
-            for s in range(GRID)
-        ]
-        predicted += exchange_chunks(block)
-    load = assemble(
-        [float(WEIGHTS[n // 5] * WEIGHTS[n % 5]) * predicted[n] for n in range(25)]
-    )
+        predicted += exchange_chunks(
+            [modal_ref[s, :, 128 * half : 128 * half + 128] for s in range(GRID)]
+        )
+    weighted = [float(WEIGHTS[n // 5] * WEIGHTS[n % 5]) * predicted[n] for n in range(25)]
+    store_joined(weighted, joined_ref, low_ref, high_ref)
+
+
+def first_kernel(
+    scalar_ref, joined_ref, below_ref, above_ref, vector_ref, next_ref, low_ref, high_ref
+):
+    shift, _ = mode_terms(scalar_ref)
+    vector = assembled(scalar_ref, joined_ref, below_ref, above_ref)
     for n in range(25):
-        residual_ref[n] = load[n]
-        direction_ref[n] = load[n]
-    norm = weighted_square(load)
-    for step in range(ITERS):
-        direction = [direction_ref[n] for n in range(25)]
-        total = None
-        local = []
-        for j in range(5):
-            for i in range(5):
-                n = j * 5 + i
-                mass = float(WEIGHTS[j] * WEIGHTS[i])
-                diagonal = VISCOUS * float(
-                    WEIGHTS[j] * STIFFNESS[i][i] + WEIGHTS[i] * STIFFNESS[j][j]
-                )
-                value = (shift * mass + diagonal) * direction[n]
-                for other in range(5):
-                    if other != i:
-                        weight = VISCOUS * float(WEIGHTS[j] * STIFFNESS[i][other])
-                        value = value + weight * direction[j * 5 + other]
-                    if other != j:
-                        weight = VISCOUS * float(WEIGHTS[i] * STIFFNESS[j][other])
-                        value = value + weight * direction[other * 5 + i]
-                local.append(value)
-                term = value * direction[n]
-                total = term if total is None else total + term
-        length = norm / mode_sum(total)
-        if step < ITERS - 1:
-            applied = assemble(local)
-            residual = [residual_ref[n] - length * applied[n] for n in range(25)]
-            fresh = weighted_square(residual)
-            ratio = fresh / norm
-            norm = fresh
-        for n in range(25):
-            gain = length * direction[n]
-            applied_ref[n] = gain if step == 0 else applied_ref[n] + gain
-            if step < ITERS - 1:
-                residual_ref[n] = residual[n]
-                direction_ref[n] = residual[n] + ratio * direction[n]
+        vector_ref[n] = vector[n]
+    store_joined(local_operator(vector, shift), next_ref, low_ref, high_ref)
+
+
+def second_kernel(
+    scalar_ref, joined_ref, below_ref, above_ref, before_ref, vector_ref, next_ref, low_ref,
+    high_ref,
+):
+    shift, center = mode_terms(scalar_ref)
+    applied = assembled(scalar_ref, joined_ref, below_ref, above_ref)
+    vector = [applied[n] - center * before_ref[n] for n in range(25)]
     for n in range(25):
-        for t in range(2):
-            out_ref[pl.ds(25 * t + n, 16, stride=56), :] = applied_ref[n, 16 * t : 16 * t + 16, :]
-
-
-def unpack_kernel(modal_ref, out_ref, column_ref):
+        vector_ref[n] = vector[n]
+    store_joined(local_operator(vector, shift), next_ref, low_ref, high_ref)
+
+
+def third_kernel(
+    scalar_ref, joined_ref, below_ref, above_ref, first_ref, second_ref, vector_ref, sums_ref,
+    turn_ref,
+):
+    shift, center = mode_terms(scalar_ref)
+    applied = assembled(scalar_ref, joined_ref, below_ref, above_ref)
+    first = [first_ref[n] for n in range(25)]
+    second = [second_ref[n] for n in range(25)]
+    third = [applied[n] - center * second[n] for n in range(25)]
+    for n in range(25):
+        vector_ref[n] = third[n]
+    fourth = inner(scalar_ref, third, third)
+    local = local_operator(third, shift)
+    fifth = -center * fourth
+    for n in range(25):
+        fifth = fifth + local[n] * third[n]
+    moments = [
+        inner(scalar_ref, first, first),
+        inner(scalar_ref, first, second),
+        inner(scalar_ref, second, second),
+        inner(scalar_ref, second, third),
+        fourth,
+        fifth,
+    ]
+    lane = lax.broadcasted_iota(jnp.int32, (32, 128), 1)
+    packed = jnp.zeros((32, 128), jnp.float32)
+    for n, moment in enumerate(moments):
+        packed = jnp.where(lane == n, jnp.sum(moment, axis=1, keepdims=True), packed)
+    turn_ref[...] = jnp.zeros((128, 128), jnp.float32)
+    for t in range(4):
+        turn_ref[pl.ds(t, 8, stride=4), :] = packed[8 * t : 8 * t + 8]
+    turned = turn_ref[...].T[0:8]
+    for p in range(GRID):
+        sums_ref[p] = turned
+
+
+def natural_kernel(vector_ref, out_ref, column_ref):
     order = column_order()
-    rows = []
-    for j in range(5):
-        tiles = []
-        for i in range(5):
-            n = j * 5 + i
-            tiles.append(
-                jnp.concatenate(
-                    [modal_ref[pl.ds(25 * t + n, 16, stride=56), :] for t in range(2)], axis=0
-                )
-            )
-        rows.append(jnp.concatenate(tiles, axis=1))
-    stacked = jnp.concatenate(rows, axis=0)
+    stacked = jnp.concatenate(
+        [
+            jnp.concatenate([vector_ref[j * 5 + i] for i in range(5)], axis=1) for j in range(5)
+        ],
+        axis=0,
+    )
     contract = ((1,), (1,))
     high, middle, low = thirds(stacked)
     columns = dot(low, order, contract) + dot(middle, order, contract) + dot(high, order, contract)
     for i in range(5):
         for j in range(5):
-            for t in range(2):
-                first = 32 * j + 16 * t
-                column_ref[pl.ds(160 * i + 32 * j + t, 16, stride=2), :] = columns[
-                    first : first + 16, 128 * i : 128 * i + 128
+            for t in range(4):
+                first = 32 * j + 8 * t
+                column_ref[pl.ds(160 * i + 32 * j + t, 8, stride=4), :] = columns[
+                    first : first + 8, 128 * i : 128 * i + 128
                 ]
     for j in range(5):
         for i in range(5):
             first = 160 * i + 32 * j
             out_ref[j, :, 128 * i : 128 * i + 128] = column_ref[first : first + 32, :]
+
+
+def combine_kernel(scalar_ref, sums_ref, first_ref, second_ref, third_ref, out_ref, turn_ref):
+    total = sums_ref[0]
+    for p in range(1, GRID):
+        total = total + sums_ref[p]
+    moment = [total[n : n + 1] for n in range(6)]
+    lane = lax.broadcasted_iota(jnp.int32, (1, 128), 1)
+    mode_pair = 16 * scalar_ref[2] + (lane >> 1)
+    ratio = mode_pair.astype(jnp.float32) * (1.0 / KMODES)
+    center = 0.2 * (1.0 + SPAN_STIFF * ratio * ratio) + 0.15
+
+    def product(left, right):
+        terms = None
+        for a in range(len(left)):
+            for b in range(len(right)):
+                term = left[a] * right[b] * moment[a + b]
+                terms = term if terms is None else terms + term
+        return terms
+
+    def operator(c):
+        shifted = [center * v for v in c] + [0.0]
+        return [shifted[0]] + [shifted[a + 1] + c[a] for a in range(len(c))]
+
+    residual = [jnp.ones((1, 128), jnp.float32)]
+    direction = residual
+    result = [0.0, 0.0, 0.0]
+    norm = moment[0]
+    for step in range(ITERS):
+        applied = operator(direction)
+        length = norm / product(direction, applied)
+        for a in range(len(direction)):
+            result[a] = result[a] + length * direction[a]
+        if step < ITERS - 1:
+            padded = residual + [0.0]
+            residual = [padded[a] - length * applied[a] for a in range(len(applied))]
+            fresh = product(residual, residual)
+            ratio = fresh / norm
+            norm = fresh
+            padded = direction + [0.0]
+            direction = [residual[a] + ratio * padded[a] for a in range(len(residual))]
+    turn_ref[...] = jnp.zeros((128, 128), jnp.float32)
+    for a in range(3):
+        turn_ref[a : a + 1, :] = result[a]
+    turned = turn_ref[...].T[0:32]
+    weight = [turned[:, a : a + 1] for a in range(3)]
+    for j in range(5):
+        out_ref[j] = (
+            weight[0] * first_ref[j] + weight[1] * second_ref[j] + weight[2] * third_ref[j]
+        )
 
 
 def call(kernel, name, out_shapes, *args, smem=(), scratch=()):
@@ -397,14 +474,18 @@
     )(*args)
 
 
+def from_neighbours(low, high):
+    below = lax.ppermute(high, "plane", [(p, (p + 1) % GRID) for p in range(GRID)])
+    above = lax.ppermute(low, "plane", [(p, (p - 1) % GRID) for p in range(GRID)])
+    return below, above
+
+
 def on_device(state, wall_tag):
     (inverse_high, inverse_low), (forward_high, forward_low) = transform_tables()
     span = lax.axis_index("span")
     plane = lax.axis_index("plane")
     last = lax.axis_size("plane") - 1
-    wavenumber = (span * GRID + plane).astype(jnp.float32) / KMODES
-    shift = (1.0 + SPAN_STIFF * wavenumber * wavenumber).reshape(1, 1)
-    edge = jnp.stack([plane == 0, plane == last]).astype(jnp.int32)
+    scalars = jnp.stack([(plane == 0).astype(jnp.int32), (plane == last).astype(jnp.int32), span])
     tags = lax.dynamic_slice_in_dim(wall_tag, span * 8, 8)
     mirror = jnp.broadcast_to(jnp.where(tags == 1, -1.0, 1.0).astype(jnp.float32)[:, None], (8, 128))
 
@@ -416,26 +497,44 @@
     nodal, low, high = call(
         turn_kernel, "turn", [(2, 256, 256), (2, 40, 256), (2, 40, 256)], modal
     )
-    below = lax.ppermute(high, "plane", [(p, (p + 1) % GRID) for p in range(GRID)])
-    above = lax.ppermute(low, "plane", [(p, (p - 1) % GRID) for p in range(GRID)])
+    below, above = from_neighbours(low, high)
     field, rhs = call(
         volume_kernel, "volume", [(200, PLANES), (200, PLANES)], nodal, inverse_high, inverse_low,
         scratch=[pltpu.VMEM((40, PLANES), jnp.float32)],
     )
     (sent,) = call(
-        forward_kernel, "forward", [(1024, 128)], modal, field, rhs, below, above, mirror, edge,
+        forward_kernel, "forward", [(16, 32, 256)], modal, field, rhs, below, above, mirror, scalars,
         inverse_high, inverse_low, forward_high, forward_low, smem=(6,),
         scratch=[pltpu.VMEM((80, PLANES), jnp.float32)],
     )
-    predicted = lax.all_to_all(sent.reshape(256, 4, 128), ("span", "plane"), 0, 0, tiled=True)
-    (solved,) = call(
-        solve_kernel, "solve", [(896, 128)], shift, predicted.reshape(1024, 128), smem=(0,),
-        scratch=[pltpu.VMEM((25, 32, 128), jnp.float32)] * 3,
-    )
-    returned = lax.all_to_all(solved.reshape(16, 56, 128), "plane", 0, 0, tiled=True)
+    predicted = lax.all_to_all(sent, "span", 0, 0, tiled=True)
+    nodes, trace = (25, 32, 128), (5, 32, 128)
+    joined, low, high = call(load_kernel, "load", [nodes, trace, trace], predicted)
+    below, above = from_neighbours(low, high)
+    first, joined, low, high = call(
+        first_kernel, "first", [nodes, nodes, trace, trace], scalars, joined, below, above, smem=(0,)
+    )
+    below, above = from_neighbours(low, high)
+    second, joined, low, high = call(
+        second_kernel, "second", [nodes, nodes, trace, trace], scalars, joined, below, above, first,
+        smem=(0,),
+    )
+    below, above = from_neighbours(low, high)
+    third, sums = call(
+        third_kernel, "third", [nodes, (16, 8, 128)], scalars, joined, below, above, first, second,
+        smem=(0,), scratch=[pltpu.VMEM((128, 128), jnp.float32)],
+    )
+    sums = lax.all_to_all(sums, "plane", 0, 0, tiled=True)
+    columns = [
+        call(
+            natural_kernel, "natural", [(5, 32, 640)], vector,
+            scratch=[pltpu.VMEM((800, 128), jnp.float32)],
+        )[0]
+        for vector in (first, second, third)
+    ]
     (columns,) = call(
-        unpack_kernel, "unpack", [(5, 32, 640)], returned.reshape(896, 128),
-        scratch=[pltpu.VMEM((800, 128), jnp.float32)],
+        combine_kernel, "combine", [(5, 32, 640)], scalars, sums, *columns, smem=(0,),
+        scratch=[pltpu.VMEM((128, 128), jnp.float32)],
     )
     return jnp.transpose(columns, (1, 0, 2))
 

time: 86.6 us -> 83.8 us (0.968)
  waiting for transfers between devices: 34.1 us -> 23.1 us
  starting transfers between devices: 21.6 us -> 31.1 us
  blocking collectives: 18.8 us -> 13.4 us
  Pallas kernels: 10.4 us -> 14.6 us
    all_to_all x1, waiting for transfers between devices: 21.4 us -> 4.96 us  [on_device(): sums = lax.all_to_all(sums, 'plane', 0, 0, tiled=True)]
    ppermute x2 -> x8, starting transfers between devices: 3.61 us -> 11.4 us  [the longest x4 6.9 us: from_neighbours(): lax.ppermute(low, 'plane', [(p, (p - 1) % GRID) for p in range(GRID)])]
    ppermute x2 -> x8, waiting for transfers between devices: 2.5 us -> 7.86 us  [the longest x4 5.61 us: from_neighbours(): lax.ppermute(low, 'plane', [(p, (p - 1) % GRID) for p in range(GRID)])]
    all_to_all x1, blocking collectives: 18.8 us -> 13.4 us  [on_device(): predicted = lax.all_to_all(sent, 'span', 0, 0, tiled=True)]
    pallas_call x6 -> x12, Pallas kernels: 10.4 us -> 14.6 us  [call(): pl.pallas_call(kernel, name=name, out_shape=[jax.ShapeDtypeStruct(s, jnp....]
    all_to_all x1, starting transfers between devices: 10.3 us -> 11.9 us  [on_device(): sums = lax.all_to_all(sums, 'plane', 0, 0, tiled=True)]
  transfers between devices with their start and end apart: 4 -> 10, of which waited for: 3 -> 9; matrix products, arithmetic and copies ran while one was open for 0% -> 0% of each run, Pallas kernels for 2% -> 5%
where the time goes in v1:
time: 83.8 us; the launch traced here: 83.5 us
  starting transfers between devices  31.1 us (37%)
  waiting for transfers between devices  23.1 us (28%)
  Pallas kernels  14.6 us (17%)
  blocking collectives  13.4 us (16%)
  local copies, waits for them, and re-layouts  1.09 us (1%)
    pallas_call x12, Pallas kernels, call(): pl.pallas_call(kernel, name=name, out_shape=[jax.ShapeDtypeStruct(s, jnp....  14.6 us
    all_to_all x1, blocking collectives, on_device(): predicted = lax.all_to_all(sent, 'span', 0, 0, tiled=True)  13.4 us
    all_to_all x1, starting transfers between devices, on_device(): sums = lax.all_to_all(sums, 'plane', 0, 0, tiled=True)  11.9 us
    all_to_all x1, waiting for transfers between devices, on_device(): modal = lax.all_to_all(packed, 'span', 0, 0, tiled=True)  10.3 us
    all_to_all x1, starting transfers between devices, on_device(): modal = lax.all_to_all(packed, 'span', 0, 0, tiled=True)  7.71 us
    ppermute x4, starting transfers between devices, from_neighbours(): lax.ppermute(low, 'plane', [(p, (p - 1) % GRID) for p in range(GRID)])  6.9 us
    ppermute x4, waiting for transfers between devices, from_neighbours(): lax.ppermute(low, 'plane', [(p, (p - 1) % GRID) for p in range(GRID)])  5.61 us
    all_to_all x1, waiting for transfers between devices, on_device(): sums = lax.all_to_all(sums, 'plane', 0, 0, tiled=True)  4.96 us
  transfers between devices with their start and end apart: 10, of which 9 were waited for; matrix products, arithmetic and copies ran while one was open for 0% of the time, Pallas kernels for 5%

profile of v1, /device:TPU:1, one launch (start us, length us, event | category | flops | bytes accessed | tf_op | source)
XLA Modules:
  0.0 83.5 jit_solution(6936057782481513592)
XLA Ops:
  0.0 1.0 %copy-done.4 = f32[32,5,640]{2,0,1:T(8,128)S(1)} copy-done((f32[32,5,640]{2,0,1:T(8,128)S(1)}, f32[32,5,640]{2,0,1:T(8,128)}, u32[]{:S(2)}) %copy-start.4) | copy-done | bytes 409624
  1.0 2.2 %pack.1 = f32[16,32,256]{2,1,0:T(8,128)} custom-call(f32[5,32,640]{2,1,0:T(8,128)S(1)} %bitcast.5), custom_call_target="tpu_custom_call" | custom-call | tf_op jit(solution)/shard_map/pack/pallas_call | solution.py:466
  3.2 7.7 %all-to-all-start = ((f32[16,32,256]{2,1,0:T(8,128)}), f32[16,32,256]{2,1,0:T(8,128)S(1)}, u32[]{:S(2)}, u32[]{:S(2)}) async-start(f32[16,32,256]{2,1,0:T(8,128)} %pack.1), calls=%async_computation | async-start | bytes 1048576 | tf_op jit(solution)/shard_map/all_to_all | solution.py:496
  11.0 10.3 %all-to-all-done.modal_ref = f32[16,32,256]{2,1,0:T(8,128)S(1)} async-done(((f32[16,32,256]{2,1,0:T(8,128)}), f32[16,32,256]{2,1,0:T(8,128)S(1)}, u32[]{:S(2)}, u32[]{:S(2)}) %all-to-all-start) | async-done | bytes 524320 | tf_op jit(solution)/shard_map/all_to_all | solution.py:496
  21.5 3.6 %collective-permute-start = (f32[2,40,256]{2,1,0:T(8,128)S(1)}, f32[2,40,256]{2,1,0:T(8,128)S(1)}, u32[]{:S(2)}, u32[]{:S(2)}) collective-permute-start(f32[2,40,256]{2,1,0:T(8,128)S(1)} %get-tuple-element.26), channel_id=1, source_target_pairs={{0,1},{1,2},{2,3},{3,4},{4,5},{5,6},{6,7},{7,8},{8,9},{9,10},{10,1... | collective-permute-start | bytes 245768 | tf_op jit(solution)/shard_map/ppermute | solution.py:478
  25.2 1.5 %volume.1 = (f32[200,768]{1,0:T(8,128)S(1)}, f32[200,768]{1,0:T(8,128)S(1)}) custom-call(f32[2,256,256]{2,1,0:T(8,128)S(1)} %get-tuple-element.23.nodal_ref, bf16[2,256,384]{2,1,0:T(8,128)(2,1)S(1)} %copy-done, bf16[2,256,384]{2,1,0:T(8,128)(2,1)S(1)} %copy-done.1), custom_call_target="tpu_custom_call" | custom-call | tf_op jit(solution)/shard_map/volume/pallas_call | solution.py:466
  26.7 2.5 %collective-permute-done.1.above_ref = f32[2,40,256]{2,1,0:T(8,128)S(1)} collective-permute-done((f32[2,40,256]{2,1,0:T(8,128)S(1)}, f32[2,40,256]{2,1,0:T(8,128)S(1)}, u32[]{:S(2)}, u32[]{:S(2)}) %collective-permute-start.1) | collective-permute-done | bytes 81952 | tf_op jit(solution)/shard_map/ppermute | solution.py:479
  29.3 1.8 %forward.1 = f32[16,32,256]{2,1,0:T(8,128)S(1)} custom-call(f32[16,32,256]{2,1,0:T(8,128)S(1)} %all-to-all-done.modal_ref, f32[200,768]{1,0:T(8,128)S(1)} %get-tuple-element.24.field_ref, f32[200,768]{1,0:T(8,128)S(1)} %get-tuple-element.25.rhs_ref, f32[2,40,256]{2,1,0:T(8,128)S(1)} %collective-permute-done.below_ref, ...), custom_call_target="tpu_custom_call" | custom-call | tf_op jit(solution)/shard_map/forward/pallas_call | solution.py:466
  31.1 13.4 %all_to_all.15.modal_ref = f32[16,32,256]{2,1,0:T(8,128)S(1)} all-to-all(f32[16,32,256]{2,1,0:T(8,128)S(1)} %forward.1), channel_id=1, replica_groups=mesh['span'=16,'plane'=16] {'span'}, dimensions={0} | all-to-all | bytes 1048576 | tf_op jit(solution)/shard_map/all_to_all | solution.py:510
  45.3 0.9 %collective-permute-start.2 = (f32[5,32,128]{2,1,0:T(8,128)S(1)}, f32[5,32,128]{2,1,0:T(8,128)S(1)}, u32[]{:S(2)}, u32[]{:S(2)}) collective-permute-start(f32[5,32,128]{2,1,0:T(8,128)S(1)} %get-tuple-element.29), channel_id=1, source_target_pairs={{0,1},{1,2},{2,3},{3,4},{4,5},{5,6},{6,7},{7,8},{8,9},{9,10},{10,1... | collective-permute-start | bytes 245768 | tf_op jit(solution)/shard_map/ppermute | solution.py:478
  46.2 1.2 %collective-permute-start.3 = (f32[5,32,128]{2,1,0:T(8,128)S(1)}, f32[5,32,128]{2,1,0:T(8,128)S(1)}, u32[]{:S(2)}, u32[]{:S(2)}) collective-permute-start(f32[5,32,128]{2,1,0:T(8,128)S(1)} %get-tuple-element.30), channel_id=1, source_target_pairs={{0,15},{1,0},{2,1},{3,2},{4,3},{5,4},{6,5},{7,6},{8,7},{9,8},{10,9... | collective-permute-start | bytes 245768 | tf_op jit(solution)/shard_map/ppermute | solution.py:479
  48.1 1.9 %collective-permute-done.3.above_ref = f32[5,32,128]{2,1,0:T(8,128)S(1)} collective-permute-done((f32[5,32,128]{2,1,0:T(8,128)S(1)}, f32[5,32,128]{2,1,0:T(8,128)S(1)}, u32[]{:S(2)}, u32[]{:S(2)}) %collective-permute-start.3) | collective-permute-done | bytes 81952 | tf_op jit(solution)/shard_map/ppermute | solution.py:479
  50.0 0.9 %first.1 = (f32[25,32,128]{2,1,0:T(8,128)S(1)}, f32[25,32,128]{2,1,0:T(8,128)S(1)}, f32[5,32,128]{2,1,0:T(8,128)S(1)}, f32[5,32,128]{2,1,0:T(8,128)S(1)}) custom-call(s32[3]{0:T(128)S(1)} %pad_add_fusion.scalar_ref, f32[25,32,128]{2,1,0:T(8,128)S(1)} %get-tuple-element.28.joined_ref, f32[5,32,128]{2,1,0:T(8,128)S(1)} %collective-permute-done.2.below_ref, ...), custom_call_target="tpu_custom_call" | custom-call | tf_op jit(solution)/shard_map/first/pallas_call | solution.py:466
  50.9 2.4 %collective-permute-start.5 = (f32[5,32,128]{2,1,0:T(8,128)S(1)}, f32[5,32,128]{2,1,0:T(8,128)S(1)}, u32[]{:S(2)}, u32[]{:S(2)}) collective-permute-start(f32[5,32,128]{2,1,0:T(8,128)S(1)} %get-tuple-element.33), channel_id=1, source_target_pairs={{0,15},{1,0},{2,1},{3,2},{4,3},{5,4},{6,5},{7,6},{8,7},{9,8},{10,9... | collective-permute-start | bytes 245768 | tf_op jit(solution)/shard_map/ppermute | solution.py:479
  54.1 1.0 %collective-permute-done.5.above_ref = f32[5,32,128]{2,1,0:T(8,128)S(1)} collective-permute-done((f32[5,32,128]{2,1,0:T(8,128)S(1)}, f32[5,32,128]{2,1,0:T(8,128)S(1)}, u32[]{:S(2)}, u32[]{:S(2)}) %collective-permute-start.5) | collective-permute-done | bytes 81952 | tf_op jit(solution)/shard_map/ppermute | solution.py:479
  55.1 0.9 %second.1 = (f32[25,32,128]{2,1,0:T(8,128)S(1)}, f32[25,32,128]{2,1,0:T(8,128)S(1)}, f32[5,32,128]{2,1,0:T(8,128)S(1)}, f32[5,32,128]{2,1,0:T(8,128)S(1)}) custom-call(s32[3]{0:T(128)S(1)} %pad_add_fusion.scalar_ref, f32[25,32,128]{2,1,0:T(8,128)S(1)} %get-tuple-element.31.joined_ref, f32[5,32,128]{2,1,0:T(8,128)S(1)} %collective-permute-done.4.below_ref, ...), custom_call_target="tpu_custom_call" | custom-call | tf_op jit(solution)/shard_map/second/pallas_call | solution.py:466
  56.0 3.3 %collective-permute-start.7 = (f32[5,32,128]{2,1,0:T(8,128)S(1)}, f32[5,32,128]{2,1,0:T(8,128)S(1)}, u32[]{:S(2)}, u32[]{:S(2)}) collective-permute-start(f32[5,32,128]{2,1,0:T(8,128)S(1)} %get-tuple-element.37), channel_id=1, source_target_pairs={{0,15},{1,0},{2,1},{3,2},{4,3},{5,4},{6,5},{7,6},{8,7},{9,8},{10,9... | collective-permute-start | bytes 245768 | tf_op jit(solution)/shard_map/ppermute | solution.py:479
  60.3 1.9 %third.1 = (f32[25,32,128]{2,1,0:T(8,128)S(1)}, f32[16,8,128]{2,1,0:T(8,128)}) custom-call(s32[3]{0:T(128)S(1)} %pad_add_fusion.scalar_ref, f32[25,32,128]{2,1,0:T(8,128)S(1)} %get-tuple-element.35.joined_ref, f32[5,32,128]{2,1,0:T(8,128)S(1)} %collective-permute-done.6.below_ref, f32[5,32,128]{2,1,0:T(8,128)S(1)} %collective-permute-done.7.above_ref, ...), custom_call_target="tpu_custom_call" | custom-call | tf_op jit(solution)/shard_map/third/pallas_call | solution.py:466
  62.2 11.9 %all-to-all-start.2 = ((f32[16,8,128]{2,1,0:T(8,128)}), f32[16,8,128]{2,1,0:T(8,128)S(1)}, u32[]{:S(2)}, u32[]{:S(2)}) async-start(f32[16,8,128]{2,1,0:T(8,128)} %get-tuple-element.39), calls=%async_computation.2 | async-start | bytes 131072 | tf_op jit(solution)/shard_map/all_to_all | solution.py:527
  74.1 0.9 %natural.3.first_ref = f32[5,32,640]{2,1,0:T(8,128)S(1)} custom-call(f32[25,32,128]{2,1,0:T(8,128)S(1)} %get-tuple-element.34.before_ref.first_ref.vector_ref), custom_call_target="tpu_custom_call" | custom-call | tf_op jit(solution)/shard_map/natural/pallas_call | solution.py:466
  75.1 0.9 %natural.4.second_ref = f32[5,32,640]{2,1,0:T(8,128)S(1)} custom-call(f32[25,32,128]{2,1,0:T(8,128)S(1)} %get-tuple-element.38.second_ref.vector_ref), custom_call_target="tpu_custom_call" | custom-call | tf_op jit(solution)/shard_map/natural/pallas_call | solution.py:466
  76.0 0.9 %natural.5.third_ref = f32[5,32,640]{2,1,0:T(8,128)S(1)} custom-call(f32[25,32,128]{2,1,0:T(8,128)S(1)} %get-tuple-element.40.vector_ref), custom_call_target="tpu_custom_call" | custom-call | tf_op jit(solution)/shard_map/natural/pallas_call | solution.py:466
  76.9 5.0 %all-to-all-done.2.sums_ref = f32[16,8,128]{2,1,0:T(8,128)S(1)} async-done(((f32[16,8,128]{2,1,0:T(8,128)}), f32[16,8,128]{2,1,0:T(8,128)S(1)}, u32[]{:S(2)}, u32[]{:S(2)}) %all-to-all-start.2) | async-done | bytes 65568 | tf_op jit(solution)/shard_map/all_to_all | solution.py:527
  81.9 1.6 %combine.1 = f32[5,32,640]{2,1,0:T(8,128)} custom-call(s32[3]{0:T(128)S(1)} %pad_add_fusion.scalar_ref, f32[16,8,128]{2,1,0:T(8,128)S(1)} %all-to-all-done.2.sums_ref, f32[5,32,640]{2,1,0:T(8,128)S(1)} %natural.3.first_ref, f32[5,32,640]{2,1,0:T(8,128)S(1)} %natural.4.second_ref, f32[5,32,640]{2,1,0:T(8,128)S(1)} %natural.5.third_ref), custom_call_target="tpu_custom_call" | custom-call | tf_op jit(solution)/shard_map/combine/pallas_call | solution.py:466
  (24 shorter events, 3.7 us)
Async XLA Ops:
  0.0 1.0 %copy-start.4 = (f32[32,5,640]{2,0,1:T(8,128)S(1)}, f32[32,5,640]{2,0,1:T(8,128)}, u32[]{:S(2)}) copy-start(f32[32,5,640]{2,0,1:T(8,128)} %param.6) | copy-start | bytes 1228804
  1.0 9.9 %copy-start.5 = (s32[128]{0:T(128)S(1)}, s32[128]{0:T(128)}, u32[]{:S(2)}) copy-start(s32[128]{0:T(128)} %param.7) | copy-start | bytes 1540
  3.2 22.0 %copy-start.1 = (bf16[2,256,384]{2,1,0:T(8,128)(2,1)S(1)}, bf16[2,256,384]{2,1,0:T(8,128)(2,1)}, u32[]{:S(2)}) copy-start(bf16[2,256,384]{2,1,0:T(8,128)(2,1)} %constant.30.clone.low_ref.inverse_low_ref) | copy-start | bytes 1179652
  3.2 26.1 %copy-start.3 = (bf16[2,256,768]{2,1,0:T(8,128)(2,1)S(1)}, bf16[2,256,768]{2,1,0:T(8,128)(2,1)}, u32[]{:S(2)}) copy-start(bf16[2,256,768]{2,1,0:T(8,128)(2,1)} %constant.32.clone.forward_low_ref) | copy-start | bytes 2359300
  3.2 18.1 %all-to-all-start = ((f32[16,32,256]{2,1,0:T(8,128)}), f32[16,32,256]{2,1,0:T(8,128)S(1)}, u32[]{:S(2)}, u32[]{:S(2)}) async-start(f32[16,32,256]{2,1,0:T(8,128)} %pack.1), calls=%async_computation | async-start | bytes 1048576 | tf_op jit(solution)/shard_map/all_to_all | solution.py:496
  10.9 14.3 %copy-start = (bf16[2,256,384]{2,1,0:T(8,128)(2,1)S(1)}, bf16[2,256,384]{2,1,0:T(8,128)(2,1)}, u32[]{:S(2)}) copy-start(bf16[2,256,384]{2,1,0:T(8,128)(2,1)} %constant.29.clone.high_ref.inverse_high_ref) | copy-start | bytes 1179652
  21.5 7.8 %copy-start.2 = (bf16[2,256,768]{2,1,0:T(8,128)(2,1)S(1)}, bf16[2,256,768]{2,1,0:T(8,128)(2,1)}, u32[]{:S(2)}) copy-start(bf16[2,256,768]{2,1,0:T(8,128)(2,1)} %constant.31.clone.forward_high_ref) | copy-start | bytes 2359300
  21.5 5.2 %collective-permute-start = (f32[2,40,256]{2,1,0:T(8,128)S(1)}, f32[2,40,256]{2,1,0:T(8,128)S(1)}, u32[]{:S(2)}, u32[]{:S(2)}) collective-permute-start(f32[2,40,256]{2,1,0:T(8,128)S(1)} %get-tuple-element.26), channel_id=1, source_target_pairs={{0,1},{1,2},{2,3},{3,4},{4,5},{5,6},{6,7},{7,8},{8,9},{9,10},{10,1... | collective-permute-start | bytes 245768 | tf_op jit(solution)/shard_map/ppermute | solution.py:478
  25.1 4.1 %collective-permute-start.1 = (f32[2,40,256]{2,1,0:T(8,128)S(1)}, f32[2,40,256]{2,1,0:T(8,128)S(1)}, u32[]{:S(2)}, u32[]{:S(2)}) collective-permute-start(f32[2,40,256]{2,1,0:T(8,128)S(1)} %get-tuple-element.27), channel_id=1, source_target_pairs={{0,15},{1,0},{2,1},{3,2},{4,3},{5,4},{6,5},{7,6},{8,7},{9,8},{10,9... | collective-permute-start | bytes 245768 | tf_op jit(solution)/shard_map/ppermute | solution.py:479
  45.3 2.9 %collective-permute-start.2 = (f32[5,32,128]{2,1,0:T(8,128)S(1)}, f32[5,32,128]{2,1,0:T(8,128)S(1)}, u32[]{:S(2)}, u32[]{:S(2)}) collective-permute-start(f32[5,32,128]{2,1,0:T(8,128)S(1)} %get-tuple-element.29), channel_id=1, source_target_pairs={{0,1},{1,2},{2,3},{3,4},{4,5},{5,6},{6,7},{7,8},{8,9},{9,10},{10,1... | collective-permute-start | bytes 245768 | tf_op jit(solution)/shard_map/ppermute | solution.py:478
  46.2 3.9 %collective-permute-start.3 = (f32[5,32,128]{2,1,0:T(8,128)S(1)}, f32[5,32,128]{2,1,0:T(8,128)S(1)}, u32[]{:S(2)}, u32[]{:S(2)}) collective-permute-start(f32[5,32,128]{2,1,0:T(8,128)S(1)} %get-tuple-element.30), channel_id=1, source_target_pairs={{0,15},{1,0},{2,1},{3,2},{4,3},{5,4},{6,5},{7,6},{8,7},{9,8},{10,9... | collective-permute-start | bytes 245768 | tf_op jit(solution)/shard_map/ppermute | solution.py:479
  50.9 3.2 %collective-permute-start.4 = (f32[5,32,128]{2,1,0:T(8,128)S(1)}, f32[5,32,128]{2,1,0:T(8,128)S(1)}, u32[]{:S(2)}, u32[]{:S(2)}) collective-permute-start(f32[5,32,128]{2,1,0:T(8,128)S(1)} %get-tuple-element.32), channel_id=1, source_target_pairs={{0,1},{1,2},{2,3},{3,4},{4,5},{5,6},{6,7},{7,8},{8,9},{9,10},{10,1... | collective-permute-start | bytes 245768 | tf_op jit(solution)/shard_map/ppermute | solution.py:478
  50.9 4.2 %collective-permute-start.5 = (f32[5,32,128]{2,1,0:T(8,128)S(1)}, f32[5,32,128]{2,1,0:T(8,128)S(1)}, u32[]{:S(2)}, u32[]{:S(2)}) collective-permute-start(f32[5,32,128]{2,1,0:T(8,128)S(1)} %get-tuple-element.33), channel_id=1, source_target_pairs={{0,15},{1,0},{2,1},{3,2},{4,3},{5,4},{6,5},{7,6},{8,7},{9,8},{10,9... | collective-permute-start | bytes 245768 | tf_op jit(solution)/shard_map/ppermute | solution.py:479
  56.0 4.1 %collective-permute-start.6 = (f32[5,32,128]{2,1,0:T(8,128)S(1)}, f32[5,32,128]{2,1,0:T(8,128)S(1)}, u32[]{:S(2)}, u32[]{:S(2)}) collective-permute-start(f32[5,32,128]{2,1,0:T(8,128)S(1)} %get-tuple-element.36), channel_id=1, source_target_pairs={{0,1},{1,2},{2,3},{3,4},{4,5},{5,6},{6,7},{7,8},{8,9},{9,10},{10,1... | collective-permute-start | bytes 245768 | tf_op jit(solution)/shard_map/ppermute | solution.py:478
  56.0 4.2 %collective-permute-start.7 = (f32[5,32,128]{2,1,0:T(8,128)S(1)}, f32[5,32,128]{2,1,0:T(8,128)S(1)}, u32[]{:S(2)}, u32[]{:S(2)}) collective-permute-start(f32[5,32,128]{2,1,0:T(8,128)S(1)} %get-tuple-element.37), channel_id=1, source_target_pairs={{0,15},{1,0},{2,1},{3,2},{4,3},{5,4},{6,5},{7,6},{8,7},{9,8},{10,9... | collective-permute-start | bytes 245768 | tf_op jit(solution)/shard_map/ppermute | solution.py:479
  62.2 19.7 %all-to-all-start.2 = ((f32[16,8,128]{2,1,0:T(8,128)}), f32[16,8,128]{2,1,0:T(8,128)S(1)}, u32[]{:S(2)}, u32[]{:S(2)}) async-start(f32[16,8,128]{2,1,0:T(8,128)} %get-tuple-element.39), calls=%async_computation.2 | async-start | bytes 131072 | tf_op jit(solution)/shard_map/all_to_all | solution.py:527

commit v2 on v1

--- a/solution.py
+++ b/solution.py
@@ -41,20 +41,14 @@
     return jnp.asarray(high), jnp.asarray(low)
 
 
-def transform_tables():
+def wave_table():
     plane = np.arange(HALF)
-    inverse, forward = [], []
+    waves = []
     for parity in range(2):
         k = 2 * np.arange(128) + parity
         angle = (k[:, None] * plane[None, :] % PLANES) * (2.0 * math.pi / PLANES)
-        cosine, sine = np.cos(angle), np.sin(angle)
-        inverse.append(np.concatenate([cosine, sine]) / math.sqrt(KMODES))
-        scale = np.where(k == 0, 1.0, 2.0)[:, None] * math.sqrt(KMODES) / PLANES * STEP_SIZE
-        ratio = (k / KMODES)[:, None]
-        from_rhs = np.concatenate([cosine, sine]) * np.concatenate([scale, scale])
-        from_flux = np.concatenate([-ratio * scale * sine, ratio * scale * cosine])
-        forward.append(np.concatenate([from_rhs, from_flux], axis=1))
-    return split_table(np.stack(inverse)), split_table(np.stack(forward))
+        waves.append(np.concatenate([np.cos(angle), np.sin(angle)]))
+    return split_table(np.stack(waves))
 
 
 def dot(left, right, contract):
@@ -106,9 +100,13 @@
     return values
 
 
-def pack_kernel(state_ref, out_ref, chunk_ref):
+def pack_kernel(state_hbm, out_ref, chunk_ref, state_ref, order_ref, arrived):
+    copy = pltpu.make_async_copy(state_hbm, state_ref, arrived)
+    copy.start()
+    order_ref[...] = column_order()
+    copy.wait()
     stacked = jnp.concatenate([state_ref[j] for j in range(5)], axis=0)
-    order = column_order()
+    order = order_ref[...]
     contract = ((1,), (0,))
     high, middle, low = thirds(stacked)
     nodes = dot(low, order, contract) + dot(middle, order, contract) + dot(high, order, contract)
@@ -154,7 +152,8 @@
         )
         for parity in range(2)
     ]
-    return part[0] + part[1], part[0] - part[1]
+    scale = 1.0 / math.sqrt(KMODES)
+    return scale * (part[0] + part[1]), scale * (part[0] - part[1])
 
 
 def two_point(left, right):
@@ -163,7 +162,9 @@
     return mean - 0.5 * speed * (right - left)
 
 
-def volume_kernel(nodal_ref, high_ref, low_ref, field_ref, rhs_ref, side_ref):
+def volume_kernel(
+    nodal_ref, high_ref, low_ref, field_ref, rhs_ref, rhs_low_ref, rhs_high_ref, side_ref
+):
     nodal = [nodal_ref[0], nodal_ref[1]]
     pair = synthesize(nodal, high_ref, low_ref)
     for q in range(2):
@@ -201,57 +202,106 @@
                         right = jnp.where(row == 7, side, pltpu.roll(f[j * 5], 7, 0))
                         total = total - 10.0 * two_point(f[n], right)
                 rhs_ref[8 * n : 8 * n + 8, lanes] = total
+                if j == 0:
+                    rhs_low_ref[8 * i : 8 * i + 8, lanes] = total
+                elif j == 4:
+                    rhs_high_ref[8 * i : 8 * i + 8, lanes] = total
         return carry
 
     lax.fori_loop(0, PLANES // 128, column, 0)
 
 
-def forward_kernel(
-    modal_ref, field_ref, rhs_ref, below_ref, above_ref, mirror_ref, scalar_ref, inverse_high_ref,
-    inverse_low_ref, forward_high_ref, forward_low_ref, out_ref, outer_ref,
+def project(planar, parity, high_ref, low_ref):
+    folded = planar[:, :HALF] + planar[:, HALF:] if parity == 0 else planar[:, :HALF] - planar[:, HALF:]
+    return dot_split((high_ref[parity], low_ref[parity]), halves(folded), ((1,), (1,)))
+
+
+def tendency(parity, from_rhs, from_flux):
+    k = 2 * lax.broadcasted_iota(jnp.int32, (128, 128), 0) + parity
+    scale = jnp.where(k == 0, 1.0, 2.0) * (math.sqrt(KMODES) / PLANES * STEP_SIZE)
+    ratio = k.astype(jnp.float32) * (1.0 / KMODES)
+    return (
+        scale * (from_rhs[0:128] - ratio * from_flux[128:256]),
+        scale * (from_rhs[128:256] + ratio * from_flux[0:128]),
+    )
+
+
+def inside_kernel(modal_ref, field_ref, rhs_ref, high_ref, low_ref, out_ref):
+    field = field_ref[...]
+    flux = 0.5 * field * field
+    rhs = rhs_ref[...]
+    tail = jnp.zeros((56, PLANES), jnp.float32)
+    flux = jnp.concatenate([flux, tail], axis=0)
+    rhs = jnp.concatenate([rhs, tail], axis=0)
+    for parity in range(2):
+        from_rhs = project(rhs, parity, high_ref, low_ref)
+        from_flux = project(flux, parity, high_ref, low_ref)
+        for half in range(2):
+            lanes = slice(128 * half, 128 * half + 128)
+            change = tendency(parity, from_rhs[:, lanes], from_flux[:, lanes])
+            for t in range(2):
+                first = 16 * parity + 8 * t
+                modal = jnp.concatenate(
+                    [modal_ref[s, first : first + 8, lanes] for s in range(GRID)], axis=0
+                )
+                out_ref[parity, 128 * t : 128 * t + 128, lanes] = modal + change[t]
+
+
+def facing_kernel(
+    tag_ref, inside_ref, field_ref, below_ref, above_ref, rhs_below_ref, rhs_above_ref, high_ref,
+    low_ref, out_ref, outer_ref,
 ):
-    bottom = scalar_ref[0] == 1
-    top = scalar_ref[1] == 1
+    bottom, top = at_ends()
+    span = lax.axis_index("span")
+    row = lax.broadcasted_iota(jnp.int32, (8, 128), 0)
+    mirror = jnp.ones((8, 128), jnp.float32)
+    for e in range(8):
+        mirror = jnp.where((row == e) & (tag_ref[8 * span + e] == 1), -1.0, mirror)
     outer = [
         jnp.concatenate([below_ref[parity], above_ref[parity]], axis=0) for parity in range(2)
     ]
-    pair = synthesize(outer, inverse_high_ref, inverse_low_ref)
+    pair = synthesize(outer, high_ref, low_ref)
     for q in range(2):
         outer_ref[:, HALF * q : HALF * q + HALF] = pair[q]
-    mirror = jnp.concatenate([mirror_ref[...]] * 6, axis=1)
-    bottom_rows, top_rows = [], []
-    for i in range(5):
-        inside = field_ref[8 * i : 8 * i + 8, :]
-        below = jnp.where(bottom, mirror * inside, outer_ref[8 * i : 8 * i + 8, :])
-        bottom_rows.append(
-            rhs_ref[8 * i : 8 * i + 8, :] + 10.0 * two_point(below, inside)
-        )
-        n = 20 + i
-        inside = field_ref[8 * n : 8 * n + 8, :]
-        above = jnp.where(top, inside, outer_ref[40 + 8 * i : 48 + 8 * i, :])
-        top_rows.append(rhs_ref[8 * n : 8 * n + 8, :] - 10.0 * two_point(inside, above))
-    rhs = jnp.concatenate(bottom_rows + [rhs_ref[40:160, :]] + top_rows, axis=0)
-    field = field_ref[...]
-    flux = 0.5 * field * field
+    mirror = jnp.concatenate([mirror] * 6, axis=1)
+    mirror = jnp.concatenate([mirror] * 5, axis=0)
+    inside = field_ref[0:40, :]
+    below = outer_ref[0:40, :]
+    lift = 10.0 * two_point(jnp.where(bottom, mirror * inside, below), inside)
+    rhs_lower = lift + jnp.where(bottom, 0.0, rhs_below_ref[...] - lift)
+    flux_lower = jnp.where(bottom, 0.0, 0.5 * below * below)
+    inside = field_ref[160:200, :]
+    above = outer_ref[40:80, :]
+    lift = 10.0 * two_point(inside, jnp.where(top, inside, above))
+    rhs_upper = jnp.where(top, 0.0, rhs_above_ref[...] + lift) - lift
+    flux_upper = jnp.where(top, 0.0, 0.5 * above * above)
+    gap = jnp.zeros((48, PLANES), jnp.float32)
+    planar = jnp.concatenate([rhs_lower, rhs_upper, gap, flux_lower, flux_upper, gap], axis=0)
+    gap = jnp.zeros((48, 256), jnp.float32)
+    keep_lower = jnp.where(bottom, 0.0, 1.0)
+    keep_upper = jnp.where(top, 0.0, 1.0)
+    lane = lax.broadcasted_iota(jnp.int32, (128, 128), 1)
     for parity in range(2):
-        if parity == 0:
-            folded = [rhs[:, :HALF] + rhs[:, HALF:], flux[:, :HALF] + flux[:, HALF:]]
-        else:
-            folded = [rhs[:, :HALF] - rhs[:, HALF:], flux[:, :HALF] - flux[:, HALF:]]
-        planar = jnp.concatenate(folded, axis=1)
-        change = dot_split(
-            (forward_high_ref[parity], forward_low_ref[parity]), halves(planar), ((1,), (1,))
-        )
+        projected = project(planar, parity, high_ref, low_ref)
+        change = tendency(parity, projected[:, 0:128], projected[:, 128:256])
+        modal = jnp.concatenate(
+            [keep_lower * below_ref[parity], keep_upper * above_ref[parity], gap], axis=0
+        ).T
         for t in range(2):
             first = 16 * parity + 8 * t
-            modal = jnp.concatenate(
-                [modal_ref[s, first : first + 8, :] for s in range(GRID)], axis=0
-            )
-            rows = change[128 * t : 128 * t + 128]
-            for s in range(GRID):
-                part = slice(8 * s, 8 * s + 8)
-                out_ref[s, first : first + 8, 0:128] = modal[part, :128] + rows[part, :128]
-                out_ref[s, first : first + 8, 128:200] = modal[part, 128:200] + rows[part, 128:200]
+            extra = change[t] + modal[128 * t : 128 * t + 128]
+            lower = jnp.where(lane < 40, extra, 0.0)
+            upper = pltpu.roll(jnp.where(lane < 40, 0.0, extra), 120, 1)
+            for half, added in ((0, lower), (1, upper)):
+                lanes = slice(128 * half, 128 * half + 128)
+                total = inside_ref[parity, 128 * t : 128 * t + 128, lanes] + added
+                for s in range(GRID):
+                    out_ref[s, first : first + 8, lanes] = total[8 * s : 8 * s + 8]
+
+
+def at_ends():
+    plane = lax.axis_index("plane")
+    return plane == 0, plane == GRID - 1
 
 
 def local_operator(values, shift):
@@ -273,12 +323,17 @@
     return out
 
 
-def store_joined(values, joined_ref, low_ref, high_ref):
+def join_columns(values):
     values = list(values)
     for j in range(5):
         joint = values[j * 5 + 4] + pltpu.roll(values[j * 5], 127, 1)
         values[j * 5 + 4] = joint
         values[j * 5] = pltpu.roll(joint, 1, 1)
+    return values
+
+
+def store_joined(values, joined_ref, low_ref, high_ref):
+    values = join_columns(values)
     for n in range(25):
         joined_ref[n] = values[n]
     for i in range(5):
@@ -286,23 +341,25 @@
         high_ref[i] = values[20 + i]
 
 
-def assembled(scalar_ref, joined_ref, below_ref, above_ref):
+def assembled(joined_ref, below_ref, above_ref):
     values = [joined_ref[n] for n in range(25)]
+    bottom, top = at_ends()
     for i in range(5):
-        values[i] = values[i] + jnp.where(scalar_ref[0] == 1, 0.0, below_ref[i])
-        values[20 + i] = values[20 + i] + jnp.where(scalar_ref[1] == 1, 0.0, above_ref[i])
+        values[i] = values[i] + jnp.where(bottom, 0.0, below_ref[i])
+        values[20 + i] = values[20 + i] + jnp.where(top, 0.0, above_ref[i])
     return values
 
 
-def mode_terms(scalar_ref):
+def mode_terms():
     row = lax.broadcasted_iota(jnp.int32, (32, 128), 0)
-    mode_pair = 16 * scalar_ref[2] + 2 * (row & 7) + (row >> 4)
+    mode_pair = 16 * lax.axis_index("span") + 2 * (row & 7) + (row >> 4)
     ratio = mode_pair.astype(jnp.float32) * (1.0 / KMODES)
     shift = 1.0 + SPAN_STIFF * ratio * ratio
     return shift, 0.2 * shift + 0.15
 
 
-def inner(scalar_ref, left, right):
+def inner(left, right):
+    bottom, top = at_ends()
     total = None
     for j in range(5):
         part = None
@@ -311,73 +368,74 @@
             term = term if 0 < i < 4 else 0.5 * term
             part = term if part is None else part + term
         if j == 0:
-            part = jnp.where(scalar_ref[0] == 1, 1.0, 0.5) * part
+            part = jnp.where(bottom, 1.0, 0.5) * part
         elif j == 4:
-            part = jnp.where(scalar_ref[1] == 1, 1.0, 0.5) * part
+            part = jnp.where(top, 1.0, 0.5) * part
         total = part if total is None else total + part
     return total
 
 
-def load_kernel(modal_ref, joined_ref, low_ref, high_ref):
-    predicted = []
+def first_kernel(modal_ref, vector_ref, next_ref, low_ref, high_ref):
+    shift, _ = mode_terms()
+    values = []
     for half in range(2):
-        predicted += exchange_chunks(
+        values += exchange_chunks(
             [modal_ref[s, :, 128 * half : 128 * half + 128] for s in range(GRID)]
         )
-    weighted = [float(WEIGHTS[n // 5] * WEIGHTS[n % 5]) * predicted[n] for n in range(25)]
-    store_joined(weighted, joined_ref, low_ref, high_ref)
-
-
-def first_kernel(
-    scalar_ref, joined_ref, below_ref, above_ref, vector_ref, next_ref, low_ref, high_ref
-):
-    shift, _ = mode_terms(scalar_ref)
-    vector = assembled(scalar_ref, joined_ref, below_ref, above_ref)
+    values = [float(WEIGHTS[n // 5] * WEIGHTS[n % 5]) * values[n] for n in range(25)]
+    vector = join_columns(values)
     for n in range(25):
         vector_ref[n] = vector[n]
     store_joined(local_operator(vector, shift), next_ref, low_ref, high_ref)
 
 
 def second_kernel(
-    scalar_ref, joined_ref, below_ref, above_ref, before_ref, vector_ref, next_ref, low_ref,
+    joined_ref, below_ref, above_ref, before_ref, vector_ref, next_ref, low_ref,
     high_ref,
 ):
-    shift, center = mode_terms(scalar_ref)
-    applied = assembled(scalar_ref, joined_ref, below_ref, above_ref)
+    shift, center = mode_terms()
+    applied = assembled(joined_ref, below_ref, above_ref)
     vector = [applied[n] - center * before_ref[n] for n in range(25)]
     for n in range(25):
         vector_ref[n] = vector[n]
     store_joined(local_operator(vector, shift), next_ref, low_ref, high_ref)
 
 
+def pack_moments(moments, first, packed):
+    lane = lax.broadcasted_iota(jnp.int32, (32, 128), 1)
+    for n, moment in enumerate(moments):
+        packed = jnp.where(lane == first + n, jnp.sum(moment, axis=1, keepdims=True), packed)
+    return packed
+
+
+def early_kernel(first_ref, second_ref, packed_ref):
+    first = [first_ref[n] for n in range(25)]
+    second = [second_ref[n] for n in range(25)]
+    moments = [
+        inner(first, first),
+        inner(first, second),
+        inner(second, second),
+    ]
+    packed_ref[...] = pack_moments(moments, 0, jnp.zeros((32, 128), jnp.float32))
+
+
 def third_kernel(
-    scalar_ref, joined_ref, below_ref, above_ref, first_ref, second_ref, vector_ref, sums_ref,
+    joined_ref, below_ref, above_ref, second_ref, packed_ref, vector_ref, sums_ref,
     turn_ref,
 ):
-    shift, center = mode_terms(scalar_ref)
-    applied = assembled(scalar_ref, joined_ref, below_ref, above_ref)
-    first = [first_ref[n] for n in range(25)]
+    shift, center = mode_terms()
+    applied = assembled(joined_ref, below_ref, above_ref)
     second = [second_ref[n] for n in range(25)]
     third = [applied[n] - center * second[n] for n in range(25)]
     for n in range(25):
         vector_ref[n] = third[n]
-    fourth = inner(scalar_ref, third, third)
+    fourth = inner(third, third)
     local = local_operator(third, shift)
     fifth = -center * fourth
     for n in range(25):
         fifth = fifth + local[n] * third[n]
-    moments = [
-        inner(scalar_ref, first, first),
-        inner(scalar_ref, first, second),
-        inner(scalar_ref, second, second),
-        inner(scalar_ref, second, third),
-        fourth,
-        fifth,
-    ]
-    lane = lax.broadcasted_iota(jnp.int32, (32, 128), 1)
-    packed = jnp.zeros((32, 128), jnp.float32)
-    for n, moment in enumerate(moments):
-        packed = jnp.where(lane == n, jnp.sum(moment, axis=1, keepdims=True), packed)
+    moments = [inner(second, third), fourth, fifth]
+    packed = pack_moments(moments, 3, packed_ref[...])
     turn_ref[...] = jnp.zeros((128, 128), jnp.float32)
     for t in range(4):
         turn_ref[pl.ds(t, 8, stride=4), :] = packed[8 * t : 8 * t + 8]
@@ -410,13 +468,13 @@
             out_ref[j, :, 128 * i : 128 * i + 128] = column_ref[first : first + 32, :]
 
 
-def combine_kernel(scalar_ref, sums_ref, first_ref, second_ref, third_ref, out_ref, turn_ref):
+def combine_kernel(sums_ref, first_ref, second_ref, third_ref, out_ref, turn_ref):
     total = sums_ref[0]
     for p in range(1, GRID):
         total = total + sums_ref[p]
     moment = [total[n : n + 1] for n in range(6)]
     lane = lax.broadcasted_iota(jnp.int32, (1, 128), 1)
-    mode_pair = 16 * scalar_ref[2] + (lane >> 1)
+    mode_pair = 16 * lax.axis_index("span") + (lane >> 1)
     ratio = mode_pair.astype(jnp.float32) * (1.0 / KMODES)
     center = 0.2 * (1.0 + SPAN_STIFF * ratio * ratio) + 0.15
 
@@ -460,17 +518,18 @@
         )
 
 
-def call(kernel, name, out_shapes, *args, smem=(), scratch=()):
+def call(kernel, name, out_shapes, *args, smem=(), anywhere=(), scratch=()):
     vmem = pl.BlockSpec(memory_space=pltpu.VMEM)
-    scalar = pl.BlockSpec(memory_space=pltpu.SMEM)
+    spaces = {n: pl.BlockSpec(memory_space=pltpu.SMEM) for n in smem}
+    spaces |= {n: pl.BlockSpec(memory_space=pltpu.HBM) for n in anywhere}
     return pl.pallas_call(
         kernel,
         name=name,
         out_shape=[jax.ShapeDtypeStruct(s, jnp.float32) for s in out_shapes],
-        in_specs=[scalar if n in smem else vmem for n in range(len(args))],
+        in_specs=[spaces.get(n, vmem) for n in range(len(args))],
         out_specs=[vmem] * len(out_shapes),
         scratch_shapes=list(scratch),
-        compiler_params=pltpu.CompilerParams(vmem_limit_bytes=48 * 1024 * 1024),
+        compiler_params=pltpu.CompilerParams(vmem_limit_bytes=16 * 1024 * 1024),
     )(*args)
 
 
@@ -481,48 +540,45 @@
 
 
 def on_device(state, wall_tag):
-    (inverse_high, inverse_low), (forward_high, forward_low) = transform_tables()
-    span = lax.axis_index("span")
-    plane = lax.axis_index("plane")
-    last = lax.axis_size("plane") - 1
-    scalars = jnp.stack([(plane == 0).astype(jnp.int32), (plane == last).astype(jnp.int32), span])
-    tags = lax.dynamic_slice_in_dim(wall_tag, span * 8, 8)
-    mirror = jnp.broadcast_to(jnp.where(tags == 1, -1.0, 1.0).astype(jnp.float32)[:, None], (8, 128))
-
+    high_table, low_table = wave_table()
     (packed,) = call(
         pack_kernel, "pack", [(16, 32, 256)], jnp.transpose(state, (1, 0, 2)),
-        scratch=[pltpu.VMEM((800, 128), jnp.float32)],
+        anywhere=(0,),
+        scratch=[
+            pltpu.VMEM((800, 128), jnp.float32), pltpu.VMEM((5, 32, 640), jnp.float32),
+            pltpu.VMEM((640, 640), jnp.bfloat16), pltpu.SemaphoreType.DMA(()),
+        ],
     )
     modal = lax.all_to_all(packed, "span", 0, 0, tiled=True)
     nodal, low, high = call(
         turn_kernel, "turn", [(2, 256, 256), (2, 40, 256), (2, 40, 256)], modal
     )
     below, above = from_neighbours(low, high)
-    field, rhs = call(
-        volume_kernel, "volume", [(200, PLANES), (200, PLANES)], nodal, inverse_high, inverse_low,
-        scratch=[pltpu.VMEM((40, PLANES), jnp.float32)],
+    rows = (40, PLANES)
+    field, rhs, rhs_low, rhs_high = call(
+        volume_kernel, "volume", [(200, PLANES), (200, PLANES), rows, rows], nodal, high_table,
+        low_table, scratch=[pltpu.VMEM(rows, jnp.float32)],
+    )
+    rhs_below, rhs_above = from_neighbours(rhs_low, rhs_high)
+    (inside,) = call(
+        inside_kernel, "inside", [(2, 256, 256)], modal, field, rhs, high_table, low_table
     )
     (sent,) = call(
-        forward_kernel, "forward", [(16, 32, 256)], modal, field, rhs, below, above, mirror, scalars,
-        inverse_high, inverse_low, forward_high, forward_low, smem=(6,),
-        scratch=[pltpu.VMEM((80, PLANES), jnp.float32)],
-    )
-    predicted = lax.all_to_all(sent, "span", 0, 0, tiled=True)
+        facing_kernel, "facing", [(16, 32, 256)], wall_tag, inside, field, below, above, rhs_below,
+        rhs_above, high_table, low_table, smem=(0,), scratch=[pltpu.VMEM((80, PLANES), jnp.float32)],
+    )
+    load = lax.all_to_all(sent, "span", 0, 0, tiled=True)
     nodes, trace = (25, 32, 128), (5, 32, 128)
-    joined, low, high = call(load_kernel, "load", [nodes, trace, trace], predicted)
-    below, above = from_neighbours(low, high)
-    first, joined, low, high = call(
-        first_kernel, "first", [nodes, nodes, trace, trace], scalars, joined, below, above, smem=(0,)
-    )
+    first, joined, low, high = call(first_kernel, "first", [nodes, nodes, trace, trace], load)
     below, above = from_neighbours(low, high)
     second, joined, low, high = call(
-        second_kernel, "second", [nodes, nodes, trace, trace], scalars, joined, below, above, first,
-        smem=(0,),
+        second_kernel, "second", [nodes, nodes, trace, trace], joined, below, above, first
     )
     below, above = from_neighbours(low, high)
+    (packed,) = call(early_kernel, "early", [(32, 128)], first, second)
     third, sums = call(
-        third_kernel, "third", [nodes, (16, 8, 128)], scalars, joined, below, above, first, second,
-        smem=(0,), scratch=[pltpu.VMEM((128, 128), jnp.float32)],
+        third_kernel, "third", [nodes, (16, 8, 128)], joined, below, above, second, packed,
+        scratch=[pltpu.VMEM((128, 128), jnp.float32)],
     )
     sums = lax.all_to_all(sums, "plane", 0, 0, tiled=True)
     columns = [
@@ -533,7 +589,7 @@
         for vector in (first, second, third)
     ]
     (columns,) = call(
-        combine_kernel, "combine", [(5, 32, 640)], scalars, sums, *columns, smem=(0,),
+        combine_kernel, "combine", [(5, 32, 640)], sums, *columns,
         scratch=[pltpu.VMEM((128, 128), jnp.float32)],
     )
     return jnp.transpose(columns, (1, 0, 2))

time: 83.8 us -> 79.4 us (0.947)
  blocking collectives: 13.4 us -> 30.1 us
  waiting for transfers between devices: 23.1 us -> 10.7 us
  starting transfers between devices: 31.1 us -> 23.4 us
  Pallas kernels: 14.6 us -> 13 us
    all_to_all x1 -> x2, blocking collectives: 13.4 us -> 30.1 us  [the longest x1 17.9 us: on_device(): modal = lax.all_to_all(packed, 'span', 0, 0, tiled=True)]
    all_to_all x1 -> x0, waiting for transfers between devices: 10.3 us -> none  [on_device(): modal = lax.all_to_all(packed, 'span', 0, 0, tiled=True)]
    all_to_all x1 -> x0, starting transfers between devices: 7.71 us -> none  [on_device(): modal = lax.all_to_all(packed, 'span', 0, 0, tiled=True)]
    ppermute x4, starting transfers between devices: 4.53 us -> 7.68 us  [from_neighbours(): lax.ppermute(high, 'plane', [(p, (p + 1) % GRID) for p in range(GRID)])]
    pallas_call x12 -> x13, Pallas kernels: 14.6 us -> 13 us  [call(): pl.pallas_call(kernel, name=name, out_shape=[jax.ShapeDtypeStruct(s, jnp....]
    ppermute x4, starting transfers between devices: 6.9 us -> 5.32 us  [from_neighbours(): lax.ppermute(low, 'plane', [(p, (p - 1) % GRID) for p in range(GRID)])]
    all_to_all x1, starting transfers between devices: 11.9 us -> 10.4 us  [on_device(): sums = lax.all_to_all(sums, 'plane', 0, 0, tiled=True)]
    ppermute x4, waiting for transfers between devices: 5.61 us -> 4.48 us  [from_neighbours(): lax.ppermute(low, 'plane', [(p, (p - 1) % GRID) for p in range(GRID)])]
  transfers between devices with their start and end apart: 10 -> 9, of which waited for: 9 -> 6; matrix products, arithmetic and copies ran while one was open for 0% -> 0% of each run, Pallas kernels for 5% -> 5%
where the time goes in v2:
time: 79.4 us; the launch traced here: 79.1 us
  blocking collectives  30.1 us (38%)
  starting transfers between devices  23.4 us (29%)
  Pallas kernels  13 us (16%)
  waiting for transfers between devices  10.7 us (13%)
  local copies, waits for them, and re-layouts  1.8 us (2%)
    all_to_all x1, blocking collectives, on_device(): modal = lax.all_to_all(packed, 'span', 0, 0, tiled=True)  17.9 us
    pallas_call x13, Pallas kernels, call(): pl.pallas_call(kernel, name=name, out_shape=[jax.ShapeDtypeStruct(s, jnp....  13 us
    all_to_all x1, blocking collectives, on_device(): load = lax.all_to_all(sent, 'span', 0, 0, tiled=True)  12.3 us
    all_to_all x1, starting transfers between devices, on_device(): sums = lax.all_to_all(sums, 'plane', 0, 0, tiled=True)  10.4 us
    ppermute x4, starting transfers between devices, from_neighbours(): lax.ppermute(high, 'plane', [(p, (p + 1) % GRID) for p in range(GRID)])  7.68 us
    ppermute x4, starting transfers between devices, from_neighbours(): lax.ppermute(low, 'plane', [(p, (p - 1) % GRID) for p in range(GRID)])  5.32 us
    all_to_all x1, waiting for transfers between devices, on_device(): sums = lax.all_to_all(sums, 'plane', 0, 0, tiled=True)  4.96 us
    ppermute x4, waiting for transfers between devices, from_neighbours(): lax.ppermute(low, 'plane', [(p, (p - 1) % GRID) for p in range(GRID)])  4.48 us
  transfers between devices with their start and end apart: 9, of which 6 were waited for; matrix products, arithmetic and copies ran while one was open for 0% of the time, Pallas kernels for 5%

profile of v2, /device:TPU:1, one launch (start us, length us, event | category | flops | bytes accessed | tf_op | source)
XLA Modules:
  0.0 79.1 jit_solution(17721144765616930526)
XLA Ops:
  0.0 1.0 %copy-done.2 = f32[32,5,640]{2,0,1:T(8,128)S(1)} copy-done((f32[32,5,640]{2,0,1:T(8,128)S(1)}, f32[32,5,640]{2,0,1:T(8,128)}, u32[]{:S(2)}) %copy-start.2) | copy-done | bytes 409624
  1.0 1.7 %pack.1 = f32[16,32,256]{2,1,0:T(8,128)S(1)} custom-call(f32[5,32,640]{2,1,0:T(8,128)S(1)} %bitcast.2), custom_call_target="tpu_custom_call" | custom-call | tf_op jit(solution)/shard_map/pack/pallas_call | solution.py:525
  2.7 17.9 %all_to_all.15.modal_ref = f32[16,32,256]{2,1,0:T(8,128)S(1)} all-to-all(f32[16,32,256]{2,1,0:T(8,128)S(1)} %pack.1), channel_id=1, replica_groups=mesh['span'=16,'plane'=16] {'span'}, dimensions={0} | all-to-all | bytes 1048576 | tf_op jit(solution)/shard_map/all_to_all | solution.py:552
  20.8 0.8 copy-done
  21.6 1.5 %volume.1 = (f32[200,768]{1,0:T(8,128)S(1)}, f32[200,768]{1,0:T(8,128)S(1)}, f32[40,768]{1,0:T(8,128)S(1)}, f32[40,768]{1,0:T(8,128)S(1)}) custom-call(f32[2,256,256]{2,1,0:T(8,128)S(1)} %get-tuple-element.22.nodal_ref, bf16[2,256,384]{2,1,0:T(8,128)(2,1)S(1)} %copy-done.1, bf16[2,256,384]{2,1,0:T(8,128)(2,1)S(1)} %copy-done), custom_call_target="tpu_custom_call" | custom-call | tf_op jit(solution)/shard_map/volume/pallas_call | solution.py:525
  23.1 3.6 %collective-permute-start.2 = (f32[40,768]{1,0:T(8,128)S(1)}, f32[40,768]{1,0:T(8,128)S(1)}, u32[]{:S(2)}, u32[]{:S(2)}) collective-permute-start(f32[40,768]{1,0:T(8,128)S(1)} %get-tuple-element.27), channel_id=1, source_target_pairs={{0,1},{1,2},{2,3},{3,4},{4,5},{5,6},{6,7},{7,8},{8,9},{9,10},{10,1... | collective-permute-start | bytes 368648 | tf_op jit(solution)/shard_map/ppermute | solution.py:537
  26.7 1.7 %collective-permute-start = (f32[2,40,256]{2,1,0:T(8,128)S(1)}, f32[2,40,256]{2,1,0:T(8,128)S(1)}, u32[]{:S(2)}, u32[]{:S(2)}) collective-permute-start(f32[2,40,256]{2,1,0:T(8,128)S(1)} %get-tuple-element.25), channel_id=1, source_target_pairs={{0,1},{1,2},{2,3},{3,4},{4,5},{5,6},{6,7},{7,8},{8,9},{9,10},{10,1... | collective-permute-start | bytes 245768 | tf_op jit(solution)/shard_map/ppermute | solution.py:537
  29.1 1.0 %inside.1.inside_ref = f32[2,256,256]{2,1,0:T(8,128)S(1)} custom-call(f32[16,32,256]{2,1,0:T(8,128)S(1)} %all_to_all.15.modal_ref, f32[200,768]{1,0:T(8,128)S(1)} %get-tuple-element.23.field_ref, f32[200,768]{1,0:T(8,128)S(1)} %get-tuple-element.24.rhs_ref, bf16[2,256,384]{2,1,0:T(8,128)(2,1)S(1)} %copy-done.1, bf16[2,256,384]{2,1,0:T(8,128)(2,1)S(1)} %copy-done), custom_call_target="tpu_custom_call" | custom-call | tf_op jit(solution)/shard_map/inside/pallas_call | solution.py:525
  30.1 2.1 %collective-permute-done.1.above_ref = f32[2,40,256]{2,1,0:T(8,128)S(1)} collective-permute-done((f32[2,40,256]{2,1,0:T(8,128)S(1)}, f32[2,40,256]{2,1,0:T(8,128)S(1)}, u32[]{:S(2)}, u32[]{:S(2)}) %collective-permute-start.1) | collective-permute-done | bytes 81952 | tf_op jit(solution)/shard_map/ppermute | solution.py:538
  32.3 1.8 %facing.1 = f32[16,32,256]{2,1,0:T(8,128)S(1)} custom-call(s32[128]{0:T(128)S(1)} %copy-done.3, f32[2,256,256]{2,1,0:T(8,128)S(1)} %inside.1.inside_ref, f32[200,768]{1,0:T(8,128)S(1)} %get-tuple-element.23.field_ref, f32[2,40,256]{2,1,0:T(8,128)S(1)} %collective-permute-done.below_ref, f32[2,40,256]{2,1,0:T(8,128)S(1)} %collective-permute-done.1.above_ref, ...), custom_call_target="tpu_custom_call" | custom-call | tf_op jit(solution)/shard_map/facing/pallas_call | solution.py:525
  34.1 12.3 %all_to_all.16.modal_ref = f32[16,32,256]{2,1,0:T(8,128)S(1)} all-to-all(f32[16,32,256]{2,1,0:T(8,128)S(1)} %facing.1), channel_id=1, replica_groups=mesh['span'=16,'plane'=16] {'span'}, dimensions={0} | all-to-all | bytes 1048576 | tf_op jit(solution)/shard_map/all_to_all | solution.py:570
  46.3 1.1 %first.1 = (f32[25,32,128]{2,1,0:T(8,128)S(1)}, f32[25,32,128]{2,1,0:T(8,128)S(1)}, f32[5,32,128]{2,1,0:T(8,128)S(1)}, f32[5,32,128]{2,1,0:T(8,128)S(1)}) custom-call(f32[16,32,256]{2,1,0:T(8,128)S(1)} %all_to_all.16.modal_ref), custom_call_target="tpu_custom_call" | custom-call | tf_op jit(solution)/shard_map/first/pallas_call | solution.py:525
  47.4 2.3 %collective-permute-start.4 = (f32[5,32,128]{2,1,0:T(8,128)S(1)}, f32[5,32,128]{2,1,0:T(8,128)S(1)}, u32[]{:S(2)}, u32[]{:S(2)}) collective-permute-start(f32[5,32,128]{2,1,0:T(8,128)S(1)} %get-tuple-element.30), channel_id=1, source_target_pairs={{0,1},{1,2},{2,3},{3,4},{4,5},{5,6},{6,7},{7,8},{8,9},{9,10},{10,1... | collective-permute-start | bytes 245768 | tf_op jit(solution)/shard_map/ppermute | solution.py:537
  49.7 1.0 %collective-permute-start.5 = (f32[5,32,128]{2,1,0:T(8,128)S(1)}, f32[5,32,128]{2,1,0:T(8,128)S(1)}, u32[]{:S(2)}, u32[]{:S(2)}) collective-permute-start(f32[5,32,128]{2,1,0:T(8,128)S(1)} %get-tuple-element.31), channel_id=1, source_target_pairs={{0,15},{1,0},{2,1},{3,2},{4,3},{5,4},{6,5},{7,6},{8,7},{9,8},{10,9... | collective-permute-start | bytes 245768 | tf_op jit(solution)/shard_map/ppermute | solution.py:538
  50.7 0.8 collective-permute-done.4.below_ref
  51.4 2.2 %collective-permute-done.5.above_ref = f32[5,32,128]{2,1,0:T(8,128)S(1)} collective-permute-done((f32[5,32,128]{2,1,0:T(8,128)S(1)}, f32[5,32,128]{2,1,0:T(8,128)S(1)}, u32[]{:S(2)}, u32[]{:S(2)}) %collective-permute-start.5) | collective-permute-done | bytes 81952 | tf_op jit(solution)/shard_map/ppermute | solution.py:538
  54.0 3.7 %collective-permute-start.7 = (f32[5,32,128]{2,1,0:T(8,128)S(1)}, f32[5,32,128]{2,1,0:T(8,128)S(1)}, u32[]{:S(2)}, u32[]{:S(2)}) collective-permute-start(f32[5,32,128]{2,1,0:T(8,128)S(1)} %get-tuple-element.35), channel_id=1, source_target_pairs={{0,15},{1,0},{2,1},{3,2},{4,3},{5,4},{6,5},{7,6},{8,7},{9,8},{10,9... | collective-permute-start | bytes 245768 | tf_op jit(solution)/shard_map/ppermute | solution.py:538
  58.6 1.2 %third.1 = (f32[25,32,128]{2,1,0:T(8,128)S(1)}, f32[16,8,128]{2,1,0:T(8,128)}) custom-call(f32[25,32,128]{2,1,0:T(8,128)S(1)} %get-tuple-element.33.joined_ref, f32[5,32,128]{2,1,0:T(8,128)S(1)} %collective-permute-done.6.below_ref, f32[5,32,128]{2,1,0:T(8,128)S(1)} %collective-permute-done.7.above_ref, ...), custom_call_target="tpu_custom_call" | custom-call | tf_op jit(solution)/shard_map/third/pallas_call | solution.py:525
  59.9 10.4 %all-to-all-start.2 = ((f32[16,8,128]{2,1,0:T(8,128)}), f32[16,8,128]{2,1,0:T(8,128)S(1)}, u32[]{:S(2)}, u32[]{:S(2)}) async-start(f32[16,8,128]{2,1,0:T(8,128)} %get-tuple-element.37), calls=%async_computation.2 | async-start | bytes 131072 | tf_op jit(solution)/shard_map/all_to_all | solution.py:583
  70.3 0.9 %natural.3.first_ref = f32[5,32,640]{2,1,0:T(8,128)S(1)} custom-call(f32[25,32,128]{2,1,0:T(8,128)S(1)} %get-tuple-element.32.before_ref.first_ref.vector_ref), custom_call_target="tpu_custom_call" | custom-call | tf_op jit(solution)/shard_map/natural/pallas_call | solution.py:525
  71.2 0.9 %natural.4.second_ref = f32[5,32,640]{2,1,0:T(8,128)S(1)} custom-call(f32[25,32,128]{2,1,0:T(8,128)S(1)} %get-tuple-element.36.second_ref.vector_ref), custom_call_target="tpu_custom_call" | custom-call | tf_op jit(solution)/shard_map/natural/pallas_call | solution.py:525
  72.2 0.9 %natural.5.third_ref = f32[5,32,640]{2,1,0:T(8,128)S(1)} custom-call(f32[25,32,128]{2,1,0:T(8,128)S(1)} %get-tuple-element.38.vector_ref), custom_call_target="tpu_custom_call" | custom-call | tf_op jit(solution)/shard_map/natural/pallas_call | solution.py:525
  73.1 5.0 %all-to-all-done.2.sums_ref = f32[16,8,128]{2,1,0:T(8,128)S(1)} async-done(((f32[16,8,128]{2,1,0:T(8,128)}), f32[16,8,128]{2,1,0:T(8,128)S(1)}, u32[]{:S(2)}, u32[]{:S(2)}) %all-to-all-start.2) | async-done | bytes 65568 | tf_op jit(solution)/shard_map/all_to_all | solution.py:583
  78.1 1.1 %combine.1 = f32[5,32,640]{2,1,0:T(8,128)} custom-call(f32[16,8,128]{2,1,0:T(8,128)S(1)} %all-to-all-done.2.sums_ref, f32[5,32,640]{2,1,0:T(8,128)S(1)} %natural.3.first_ref, f32[5,32,640]{2,1,0:T(8,128)S(1)} %natural.4.second_ref, f32[5,32,640]{2,1,0:T(8,128)S(1)} %natural.5.third_ref), custom_call_target="tpu_custom_call" | custom-call | tf_op jit(solution)/shard_map/combine/pallas_call | solution.py:525
  (17 shorter events, 2.2 us)
Async XLA Ops:
  0.0 1.0 %copy-start.2 = (f32[32,5,640]{2,0,1:T(8,128)S(1)}, f32[32,5,640]{2,0,1:T(8,128)}, u32[]{:S(2)}) copy-start(f32[32,5,640]{2,0,1:T(8,128)} %param.4) | copy-start | bytes 1228804
  2.7 18.1 %copy-start.1 = (bf16[2,256,384]{2,1,0:T(8,128)(2,1)S(1)}, bf16[2,256,384]{2,1,0:T(8,128)(2,1)}, u32[]{:S(2)}) copy-start(bf16[2,256,384]{2,1,0:T(8,128)(2,1)} %constant.4.clone.high_ref) | copy-start | bytes 1179652
  20.6 1.0 %copy-start = (bf16[2,256,384]{2,1,0:T(8,128)(2,1)S(1)}, bf16[2,256,384]{2,1,0:T(8,128)(2,1)}, u32[]{:S(2)}) copy-start(bf16[2,256,384]{2,1,0:T(8,128)(2,1)} %constant.5.clone.low_ref) | copy-start | bytes 1179652
  23.1 9.2 %collective-permute-start.2 = (f32[40,768]{1,0:T(8,128)S(1)}, f32[40,768]{1,0:T(8,128)S(1)}, u32[]{:S(2)}, u32[]{:S(2)}) collective-permute-start(f32[40,768]{1,0:T(8,128)S(1)} %get-tuple-element.27), channel_id=1, source_target_pairs={{0,1},{1,2},{2,3},{3,4},{4,5},{5,6},{6,7},{7,8},{8,9},{9,10},{10,1... | collective-permute-start | bytes 368648 | tf_op jit(solution)/shard_map/ppermute | solution.py:537
  26.7 5.6 %collective-permute-start.3 = (f32[40,768]{1,0:T(8,128)S(1)}, f32[40,768]{1,0:T(8,128)S(1)}, u32[]{:S(2)}, u32[]{:S(2)}) collective-permute-start(f32[40,768]{1,0:T(8,128)S(1)} %get-tuple-element.28), channel_id=1, source_target_pairs={{0,15},{1,0},{2,1},{3,2},{4,3},{5,4},{6,5},{7,6},{8,7},{9,8},{10,9... | collective-permute-start | bytes 368648 | tf_op jit(solution)/shard_map/ppermute | solution.py:538
  26.7 3.5 %collective-permute-start = (f32[2,40,256]{2,1,0:T(8,128)S(1)}, f32[2,40,256]{2,1,0:T(8,128)S(1)}, u32[]{:S(2)}, u32[]{:S(2)}) collective-permute-start(f32[2,40,256]{2,1,0:T(8,128)S(1)} %get-tuple-element.25), channel_id=1, source_target_pairs={{0,1},{1,2},{2,3},{3,4},{4,5},{5,6},{6,7},{7,8},{8,9},{9,10},{10,1... | collective-permute-start | bytes 245768 | tf_op jit(solution)/shard_map/ppermute | solution.py:537
  28.4 3.9 %collective-permute-start.1 = (f32[2,40,256]{2,1,0:T(8,128)S(1)}, f32[2,40,256]{2,1,0:T(8,128)S(1)}, u32[]{:S(2)}, u32[]{:S(2)}) collective-permute-start(f32[2,40,256]{2,1,0:T(8,128)S(1)} %get-tuple-element.26), channel_id=1, source_target_pairs={{0,15},{1,0},{2,1},{3,2},{4,3},{5,4},{6,5},{7,6},{8,7},{9,8},{10,9... | collective-permute-start | bytes 245768 | tf_op jit(solution)/shard_map/ppermute | solution.py:538
  29.1 3.2 %copy-start.3 = (s32[128]{0:T(128)S(1)}, s32[128]{0:T(128)}, u32[]{:S(2)}) copy-start(s32[128]{0:T(128)} %tag_ref.1) | copy-start | bytes 1540
  47.4 4.0 %collective-permute-start.4 = (f32[5,32,128]{2,1,0:T(8,128)S(1)}, f32[5,32,128]{2,1,0:T(8,128)S(1)}, u32[]{:S(2)}, u32[]{:S(2)}) collective-permute-start(f32[5,32,128]{2,1,0:T(8,128)S(1)} %get-tuple-element.30), channel_id=1, source_target_pairs={{0,1},{1,2},{2,3},{3,4},{4,5},{5,6},{6,7},{7,8},{8,9},{9,10},{10,1... | collective-permute-start | bytes 245768 | tf_op jit(solution)/shard_map/ppermute | solution.py:537
  49.7 3.9 %collective-permute-start.5 = (f32[5,32,128]{2,1,0:T(8,128)S(1)}, f32[5,32,128]{2,1,0:T(8,128)S(1)}, u32[]{:S(2)}, u32[]{:S(2)}) collective-permute-start(f32[5,32,128]{2,1,0:T(8,128)S(1)} %get-tuple-element.31), channel_id=1, source_target_pairs={{0,15},{1,0},{2,1},{3,2},{4,3},{5,4},{6,5},{7,6},{8,7},{9,8},{10,9... | collective-permute-start | bytes 245768 | tf_op jit(solution)/shard_map/ppermute | solution.py:538
  54.0 4.5 %collective-permute-start.6 = (f32[5,32,128]{2,1,0:T(8,128)S(1)}, f32[5,32,128]{2,1,0:T(8,128)S(1)}, u32[]{:S(2)}, u32[]{:S(2)}) collective-permute-start(f32[5,32,128]{2,1,0:T(8,128)S(1)} %get-tuple-element.34), channel_id=1, source_target_pairs={{0,1},{1,2},{2,3},{3,4},{4,5},{5,6},{6,7},{7,8},{8,9},{9,10},{10,1... | collective-permute-start | bytes 245768 | tf_op jit(solution)/shard_map/ppermute | solution.py:537
  54.0 4.6 %collective-permute-start.7 = (f32[5,32,128]{2,1,0:T(8,128)S(1)}, f32[5,32,128]{2,1,0:T(8,128)S(1)}, u32[]{:S(2)}, u32[]{:S(2)}) collective-permute-start(f32[5,32,128]{2,1,0:T(8,128)S(1)} %get-tuple-element.35), channel_id=1, source_target_pairs={{0,15},{1,0},{2,1},{3,2},{4,3},{5,4},{6,5},{7,6},{8,7},{9,8},{10,9... | collective-permute-start | bytes 245768 | tf_op jit(solution)/shard_map/ppermute | solution.py:538
  59.9 18.2 %all-to-all-start.2 = ((f32[16,8,128]{2,1,0:T(8,128)}), f32[16,8,128]{2,1,0:T(8,128)S(1)}, u32[]{:S(2)}, u32[]{:S(2)}) async-start(f32[16,8,128]{2,1,0:T(8,128)} %get-tuple-element.37), calls=%async_computation.2 | async-start | bytes 131072 | tf_op jit(solution)/shard_map/all_to_all | solution.py:583

commit v3 on v2

--- a/solution.py
+++ b/solution.py
@@ -38,7 +38,7 @@
 def split_table(table):
     high = table.astype(np.float32).astype(jnp.bfloat16)
     low = (table - high.astype(np.float64)).astype(np.float32).astype(jnp.bfloat16)
-    return jnp.asarray(high), jnp.asarray(low)
+    return jnp.asarray(np.stack([high, low]))
 
 
 def wave_table():
@@ -100,7 +100,7 @@
     return values
 
 
-def pack_kernel(state_hbm, out_ref, chunk_ref, state_ref, order_ref, arrived):
+def pack_kernel(state_hbm, out_hbm, chunk_ref, state_ref, order_ref, packed_ref, arrived, sent):
     copy = pltpu.make_async_copy(state_hbm, state_ref, arrived)
     copy.start()
     order_ref[...] = column_order()
@@ -108,8 +108,8 @@
     stacked = jnp.concatenate([state_ref[j] for j in range(5)], axis=0)
     order = order_ref[...]
     contract = ((1,), (0,))
-    high, middle, low = thirds(stacked)
-    nodes = dot(low, order, contract) + dot(middle, order, contract) + dot(high, order, contract)
+    high, low = halves(stacked)
+    nodes = dot(low, order, contract) + dot(high, order, contract)
     for i in range(5):
         chunk_ref[160 * i : 160 * i + 160, :] = nodes[:, 128 * i : 128 * i + 128]
     chunk = [
@@ -126,47 +126,50 @@
         chunk.append(jnp.where(lane == 0, left, jnp.where(lane == 7, right, 0.0)))
     zero = jnp.zeros((32, 128), jnp.float32)
     chunk = chunk + [zero, zero]
+    copies = []
     for half in range(2):
         block = exchange_chunks(chunk[16 * half : 16 * half + 16])
         for d in range(GRID):
-            out_ref[d, :, 128 * half : 128 * half + 128] = block[d]
-
-
-def turn_kernel(modal_ref, nodal_ref, low_ref, high_ref):
+            packed_ref[half, d] = block[d]
+        lanes = pl.ds(128 * half, 128)
+        copies.append(
+            pltpu.make_async_copy(packed_ref.at[half], out_hbm.at[:, :, lanes], sent.at[half])
+        )
+        copies[half].start()
+    for copy in copies:
+        copy.wait()
+
+
+def synthesize(nodal, table_ref):
+    part = [
+        dot_split(
+            halves(nodal[parity]), (table_ref[0, parity], table_ref[1, parity]), ((1,), (0,))
+        )
+        for parity in range(2)
+    ]
+    scale = 1.0 / math.sqrt(KMODES)
+    return scale * (part[0] + part[1]), scale * (part[0] - part[1])
+
+
+def two_point(left, right):
+    mean = (left * left + left * right + right * right) * (1.0 / 6.0)
+    speed = jnp.maximum(jnp.abs(left), jnp.abs(right))
+    return mean - 0.5 * speed * (right - left)
+
+
+def volume_kernel(modal_ref, table_ref, field_ref, rhs_ref, low_ref, high_ref, side_ref):
+    nodal = []
     for parity in range(2):
         rows = [
             modal_ref[s, 16 * parity + 8 * t : 16 * parity + 8 * t + 8, :]
             for t in range(2)
             for s in range(GRID)
         ]
-        turned = jnp.concatenate(rows, axis=0).T
-        nodal_ref[parity] = turned
-        low_ref[parity] = turned[0:40]
-        high_ref[parity] = turned[160:200]
-
-
-def synthesize(nodal, high_ref, low_ref):
-    part = [
-        dot_split(
-            halves(nodal[parity]), (high_ref[parity], low_ref[parity]), ((1,), (0,))
-        )
-        for parity in range(2)
-    ]
-    scale = 1.0 / math.sqrt(KMODES)
-    return scale * (part[0] + part[1]), scale * (part[0] - part[1])
-
-
-def two_point(left, right):
-    mean = (left * left + left * right + right * right) * (1.0 / 6.0)
-    speed = jnp.maximum(jnp.abs(left), jnp.abs(right))
-    return mean - 0.5 * speed * (right - left)
-
-
-def volume_kernel(
-    nodal_ref, high_ref, low_ref, field_ref, rhs_ref, rhs_low_ref, rhs_high_ref, side_ref
-):
-    nodal = [nodal_ref[0], nodal_ref[1]]
-    pair = synthesize(nodal, high_ref, low_ref)
+        nodal.append(jnp.concatenate(rows, axis=0).T)
+        lanes = slice(PLANES + 256 * parity, PLANES + 256 * parity + 256)
+        low_ref[:, lanes] = nodal[parity][0:40]
+        high_ref[:, lanes] = nodal[parity][160:200]
+    pair = synthesize(nodal, table_ref)
     for q in range(2):
         field_ref[:, HALF * q : HALF * q + HALF] = pair[q][0:200]
         side_ref[:, HALF * q : HALF * q + HALF] = pair[q][200:240]
@@ -203,17 +206,17 @@
                         total = total - 10.0 * two_point(f[n], right)
                 rhs_ref[8 * n : 8 * n + 8, lanes] = total
                 if j == 0:
-                    rhs_low_ref[8 * i : 8 * i + 8, lanes] = total
+                    low_ref[8 * i : 8 * i + 8, lanes] = total
                 elif j == 4:
-                    rhs_high_ref[8 * i : 8 * i + 8, lanes] = total
+                    high_ref[8 * i : 8 * i + 8, lanes] = total
         return carry
 
     lax.fori_loop(0, PLANES // 128, column, 0)
 
 
-def project(planar, parity, high_ref, low_ref):
+def project(planar, parity, table_ref):
     folded = planar[:, :HALF] + planar[:, HALF:] if parity == 0 else planar[:, :HALF] - planar[:, HALF:]
-    return dot_split((high_ref[parity], low_ref[parity]), halves(folded), ((1,), (1,)))
+    return dot_split((table_ref[0, parity], table_ref[1, parity]), halves(folded), ((1,), (1,)))
 
 
 def tendency(parity, from_rhs, from_flux):
@@ -226,7 +229,7 @@
     )
 
 
-def inside_kernel(modal_ref, field_ref, rhs_ref, high_ref, low_ref, out_ref):
+def inside_kernel(modal_ref, field_ref, rhs_ref, table_ref, out_ref):
     field = field_ref[...]
     flux = 0.5 * field * field
     rhs = rhs_ref[...]
@@ -234,8 +237,8 @@
     flux = jnp.concatenate([flux, tail], axis=0)
     rhs = jnp.concatenate([rhs, tail], axis=0)
     for parity in range(2):
-        from_rhs = project(rhs, parity, high_ref, low_ref)
-        from_flux = project(flux, parity, high_ref, low_ref)
+        from_rhs = project(rhs, parity, table_ref)
+        from_flux = project(flux, parity, table_ref)
         for half in range(2):
             lanes = slice(128 * half, 128 * half + 128)
             change = tendency(parity, from_rhs[:, lanes], from_flux[:, lanes])
@@ -248,8 +251,7 @@
 
 
 def facing_kernel(
-    tag_ref, inside_ref, field_ref, below_ref, above_ref, rhs_below_ref, rhs_above_ref, high_ref,
-    low_ref, out_ref, outer_ref,
+    tag_ref, inside_ref, field_ref, below_ref, above_ref, table_ref, out_ref, outer_ref
 ):
     bottom, top = at_ends()
     span = lax.axis_index("span")
@@ -257,10 +259,14 @@
     mirror = jnp.ones((8, 128), jnp.float32)
     for e in range(8):
         mirror = jnp.where((row == e) & (tag_ref[8 * span + e] == 1), -1.0, mirror)
+    below_modal, above_modal = [
+        [ref[:, PLANES + 256 * parity : PLANES + 256 * parity + 256] for parity in range(2)]
+        for ref in (below_ref, above_ref)
+    ]
     outer = [
-        jnp.concatenate([below_ref[parity], above_ref[parity]], axis=0) for parity in range(2)
+        jnp.concatenate([below_modal[parity], above_modal[parity]], axis=0) for parity in range(2)
     ]
-    pair = synthesize(outer, high_ref, low_ref)
+    pair = synthesize(outer, table_ref)
     for q in range(2):
         outer_ref[:, HALF * q : HALF * q + HALF] = pair[q]
     mirror = jnp.concatenate([mirror] * 6, axis=1)
@@ -268,12 +274,12 @@
     inside = field_ref[0:40, :]
     below = outer_ref[0:40, :]
     lift = 10.0 * two_point(jnp.where(bottom, mirror * inside, below), inside)
-    rhs_lower = lift + jnp.where(bottom, 0.0, rhs_below_ref[...] - lift)
+    rhs_lower = lift + jnp.where(bottom, 0.0, below_ref[:, 0:PLANES] - lift)
     flux_lower = jnp.where(bottom, 0.0, 0.5 * below * below)
     inside = field_ref[160:200, :]
     above = outer_ref[40:80, :]
     lift = 10.0 * two_point(inside, jnp.where(top, inside, above))
-    rhs_upper = jnp.where(top, 0.0, rhs_above_ref[...] + lift) - lift
+    rhs_upper = jnp.where(top, 0.0, above_ref[:, 0:PLANES] + lift) - lift
     flux_upper = jnp.where(top, 0.0, 0.5 * above * above)
     gap = jnp.zeros((48, PLANES), jnp.float32)
     planar = jnp.concatenate([rhs_lower, rhs_upper, gap, flux_lower, flux_upper, gap], axis=0)
@@ -282,10 +288,10 @@
     keep_upper = jnp.where(top, 0.0, 1.0)
     lane = lax.broadcasted_iota(jnp.int32, (128, 128), 1)
     for parity in range(2):
-        projected = project(planar, parity, high_ref, low_ref)
+        projected = project(planar, parity, table_ref)
         change = tendency(parity, projected[:, 0:128], projected[:, 128:256])
         modal = jnp.concatenate(
-            [keep_lower * below_ref[parity], keep_upper * above_ref[parity], gap], axis=0
+            [keep_lower * below_modal[parity], keep_upper * above_modal[parity], gap], axis=0
         ).T
         for t in range(2):
             first = 16 * parity + 8 * t
@@ -518,7 +524,7 @@
         )
 
 
-def call(kernel, name, out_shapes, *args, smem=(), anywhere=(), scratch=()):
+def call(kernel, name, out_shapes, *args, smem=(), anywhere=(), scratch=(), limit=16):
     vmem = pl.BlockSpec(memory_space=pltpu.VMEM)
     spaces = {n: pl.BlockSpec(memory_space=pltpu.SMEM) for n in smem}
     spaces |= {n: pl.BlockSpec(memory_space=pltpu.HBM) for n in anywhere}
@@ -527,9 +533,9 @@
         name=name,
         out_shape=[jax.ShapeDtypeStruct(s, jnp.float32) for s in out_shapes],
         in_specs=[spaces.get(n, vmem) for n in range(len(args))],
-        out_specs=[vmem] * len(out_shapes),
+        out_specs=[pl.BlockSpec(memory_space=pltpu.HBM) if anywhere else vmem] * len(out_shapes),
         scratch_shapes=list(scratch),
-        compiler_params=pltpu.CompilerParams(vmem_limit_bytes=16 * 1024 * 1024),
+        compiler_params=pltpu.CompilerParams(vmem_limit_bytes=limit * 1024 * 1024),
     )(*args)
 
 
@@ -540,32 +546,27 @@
 
 
 def on_device(state, wall_tag):
-    high_table, low_table = wave_table()
+    table = wave_table()
     (packed,) = call(
         pack_kernel, "pack", [(16, 32, 256)], jnp.transpose(state, (1, 0, 2)),
-        anywhere=(0,),
+        anywhere=(0,), limit=60,
         scratch=[
             pltpu.VMEM((800, 128), jnp.float32), pltpu.VMEM((5, 32, 640), jnp.float32),
-            pltpu.VMEM((640, 640), jnp.bfloat16), pltpu.SemaphoreType.DMA(()),
+            pltpu.VMEM((640, 640), jnp.bfloat16), pltpu.VMEM((2, 16, 32, 128), jnp.float32),
+            pltpu.SemaphoreType.DMA(()), pltpu.SemaphoreType.DMA((2,)),
         ],
     )
     modal = lax.all_to_all(packed, "span", 0, 0, tiled=True)
-    nodal, low, high = call(
-        turn_kernel, "turn", [(2, 256, 256), (2, 40, 256), (2, 40, 256)], modal
+    trace = (40, PLANES + 512)
+    field, rhs, low, high = call(
+        volume_kernel, "volume", [(200, PLANES), (200, PLANES), trace, trace], modal, table,
+        scratch=[pltpu.VMEM((40, PLANES), jnp.float32)],
     )
     below, above = from_neighbours(low, high)
-    rows = (40, PLANES)
-    field, rhs, rhs_low, rhs_high = call(
-        volume_kernel, "volume", [(200, PLANES), (200, PLANES), rows, rows], nodal, high_table,
-        low_table, scratch=[pltpu.VMEM(rows, jnp.float32)],
-    )
-    rhs_below, rhs_above = from_neighbours(rhs_low, rhs_high)
-    (inside,) = call(
-        inside_kernel, "inside", [(2, 256, 256)], modal, field, rhs, high_table, low_table
-    )
+    (inside,) = call(inside_kernel, "inside", [(2, 256, 256)], modal, field, rhs, table)
     (sent,) = call(
-        facing_kernel, "facing", [(16, 32, 256)], wall_tag, inside, field, below, above, rhs_below,
-        rhs_above, high_table, low_table, smem=(0,), scratch=[pltpu.VMEM((80, PLANES), jnp.float32)],
+        facing_kernel, "facing", [(16, 32, 256)], wall_tag, inside, field, below, above, table,
+        smem=(0,), scratch=[pltpu.VMEM((80, PLANES), jnp.float32)],
     )
     load = lax.all_to_all(sent, "span", 0, 0, tiled=True)
     nodes, trace = (25, 32, 128), (5, 32, 128)

time: 79.4 us -> 78.5 us (0.989)
  starting transfers between devices: 23.4 us -> 19.2 us
  waiting for transfers between devices: 10.7 us -> 13.5 us
  local copies, waits for them, and re-layouts: 1.8 us -> 0.01 us
  blocking collectives: 30.1 us -> 31.4 us
  Pallas kernels: 13 us -> 14.1 us
    ppermute x4 -> x3, starting transfers between devices: 7.68 us -> 4.53 us  [from_neighbours(): lax.ppermute(high, 'plane', [(p, (p + 1) % GRID) for p in range(GRID)])]
    unnamed x8 -> x4, local copies, waits for them, and re-layouts: 1.8 us -> 0.01 us
    ppermute x4 -> x3, starting transfers between devices: 5.32 us -> 3.59 us  [from_neighbours(): lax.ppermute(low, 'plane', [(p, (p - 1) % GRID) for p in range(GRID)])]
    ppermute x4 -> x3, waiting for transfers between devices: 1.3 us -> 2.91 us  [from_neighbours(): lax.ppermute(high, 'plane', [(p, (p + 1) % GRID) for p in range(GRID)])]
    all_to_all x1, blocking collectives: 12.3 us -> 13.4 us  [on_device(): load = lax.all_to_all(sent, 'span', 0, 0, tiled=True)]
    ppermute x4 -> x3, waiting for transfers between devices: 4.48 us -> 5.63 us  [from_neighbours(): lax.ppermute(low, 'plane', [(p, (p - 1) % GRID) for p in range(GRID)])]
    pallas_call x13 -> x12, Pallas kernels: 13 us -> 14.1 us  [call(): pl.pallas_call(kernel, name=name, out_shape=[jax.ShapeDtypeStruct(s, jnp....]
  transfers between devices with their start and end apart: 9 -> 7, of which waited for: 6 -> 7; matrix products, arithmetic and copies ran while one was open for 0% -> 0% of each run, Pallas kernels for 5% -> 5%
where the time goes in v3:
time: 78.5 us; the launch traced here: 78.2 us
  blocking collectives  31.4 us (40%)
  starting transfers between devices  19.2 us (24%)
  Pallas kernels  14.1 us (18%)
  waiting for transfers between devices  13.5 us (17%)
    all_to_all x1, blocking collectives, on_device(): modal = lax.all_to_all(packed, 'span', 0, 0, tiled=True)  17.9 us
    pallas_call x12, Pallas kernels, call(): pl.pallas_call(kernel, name=name, out_shape=[jax.ShapeDtypeStruct(s, jnp....  14.1 us
    all_to_all x1, blocking collectives, on_device(): load = lax.all_to_all(sent, 'span', 0, 0, tiled=True)  13.4 us
    all_to_all x1, starting transfers between devices, on_device(): sums = lax.all_to_all(sums, 'plane', 0, 0, tiled=True)  11.1 us
    ppermute x3, waiting for transfers between devices, from_neighbours(): lax.ppermute(low, 'plane', [(p, (p - 1) % GRID) for p in range(GRID)])  5.63 us
    all_to_all x1, waiting for transfers between devices, on_device(): sums = lax.all_to_all(sums, 'plane', 0, 0, tiled=True)  4.96 us
    ppermute x3, starting transfers between devices, from_neighbours(): lax.ppermute(high, 'plane', [(p, (p + 1) % GRID) for p in range(GRID)])  4.53 us
    ppermute x3, starting transfers between devices, from_neighbours(): lax.ppermute(low, 'plane', [(p, (p - 1) % GRID) for p in range(GRID)])  3.59 us
  transfers between devices with their start and end apart: 7, of which 7 were waited for; matrix products, arithmetic and copies ran while one was open for 0% of the time, Pallas kernels for 5%

profile of v3, /device:TPU:1, one launch (start us, length us, event | category | flops | bytes accessed | tf_op | source)
XLA Modules:
  0.0 78.2 jit_solution(9410815618182649346)
XLA Ops:
  0.0 2.9 %pack.1 = f32[16,32,256]{2,1,0:T(8,128)} custom-call(f32[5,32,640]{2,1,0:T(8,128)} %bitcast.2), custom_call_target="tpu_custom_call" | custom-call | tf_op jit(solution)/shard_map/pack/pallas_call | solution.py:531
  2.9 17.9 %all_to_all.15.modal_ref = f32[16,32,256]{2,1,0:T(8,128)S(1)} all-to-all(f32[16,32,256]{2,1,0:T(8,128)} %pack.1), channel_id=1, replica_groups=mesh['span'=16,'plane'=16] {'span'}, dimensions={0} | all-to-all | bytes 1048576 | tf_op jit(solution)/shard_map/all_to_all | solution.py:559
  20.9 1.6 %volume.1 = (f32[200,768]{1,0:T(8,128)S(1)}, f32[200,768]{1,0:T(8,128)S(1)}, f32[40,1280]{1,0:T(8,128)S(1)}, f32[40,1280]{1,0:T(8,128)S(1)}) custom-call(f32[16,32,256]{2,1,0:T(8,128)S(1)} %all_to_all.15.modal_ref, bf16[2,2,256,384]{3,2,1,0:T(8,128)(2,1)S(1)} %copy-done), custom_call_target="tpu_custom_call" | custom-call | tf_op jit(solution)/shard_map/volume/pallas_call | solution.py:531
  22.4 3.6 %collective-permute-start = (f32[40,1280]{1,0:T(8,128)S(1)}, f32[40,1280]{1,0:T(8,128)S(1)}, u32[]{:S(2)}, u32[]{:S(2)}) collective-permute-start(f32[40,1280]{1,0:T(8,128)S(1)} %get-tuple-element.21), channel_id=1, source_target_pairs={{0,1},{1,2},{2,3},{3,4},{4,5},{5,6},{6,7},{7,8},{8,9},{9,10},{10,1... | collective-permute-start | bytes 614408 | tf_op jit(solution)/shard_map/ppermute | solution.py:543
  26.1 1.1 %inside.1.inside_ref = f32[2,256,256]{2,1,0:T(8,128)S(1)} custom-call(f32[16,32,256]{2,1,0:T(8,128)S(1)} %all_to_all.15.modal_ref, f32[200,768]{1,0:T(8,128)S(1)} %get-tuple-element.19.field_ref, f32[200,768]{1,0:T(8,128)S(1)} %get-tuple-element.20.rhs_ref, bf16[2,2,256,384]{3,2,1,0:T(8,128)(2,1)S(1)} %copy-done), custom_call_target="tpu_custom_call" | custom-call | tf_op jit(solution)/shard_map/inside/pallas_call | solution.py:531
  27.1 1.6 %collective-permute-done.below_ref = f32[40,1280]{1,0:T(8,128)S(1)} collective-permute-done((f32[40,1280]{1,0:T(8,128)S(1)}, f32[40,1280]{1,0:T(8,128)S(1)}, u32[]{:S(2)}, u32[]{:S(2)}) %collective-permute-start) | collective-permute-done | bytes 204832 | tf_op jit(solution)/shard_map/ppermute | solution.py:543
  28.8 2.7 %collective-permute-done.1.above_ref = f32[40,1280]{1,0:T(8,128)S(1)} collective-permute-done((f32[40,1280]{1,0:T(8,128)S(1)}, f32[40,1280]{1,0:T(8,128)S(1)}, u32[]{:S(2)}, u32[]{:S(2)}) %collective-permute-start.1) | collective-permute-done | bytes 204832 | tf_op jit(solution)/shard_map/ppermute | solution.py:544
  31.5 1.8 %facing.1 = f32[16,32,256]{2,1,0:T(8,128)S(1)} custom-call(s32[128]{0:T(128)S(1)} %copy-done.1, f32[2,256,256]{2,1,0:T(8,128)S(1)} %inside.1.inside_ref, f32[200,768]{1,0:T(8,128)S(1)} %get-tuple-element.19.field_ref, f32[40,1280]{1,0:T(8,128)S(1)} %collective-permute-done.below_ref, f32[40,1280]{1,0:T(8,128)S(1)} %collective-permute-done.1.above_ref, ...), custom_call_target="tpu_custom_call" | custom-call | tf_op jit(solution)/shard_map/facing/pallas_call | solution.py:531
  33.2 13.4 %all_to_all.16.modal_ref = f32[16,32,256]{2,1,0:T(8,128)S(1)} all-to-all(f32[16,32,256]{2,1,0:T(8,128)S(1)} %facing.1), channel_id=1, replica_groups=mesh['span'=16,'plane'=16] {'span'}, dimensions={0} | all-to-all | bytes 1048576 | tf_op jit(solution)/shard_map/all_to_all | solution.py:571
  46.7 1.1 %first.1 = (f32[25,32,128]{2,1,0:T(8,128)S(1)}, f32[25,32,128]{2,1,0:T(8,128)S(1)}, f32[5,32,128]{2,1,0:T(8,128)S(1)}, f32[5,32,128]{2,1,0:T(8,128)S(1)}) custom-call(f32[16,32,256]{2,1,0:T(8,128)S(1)} %all_to_all.16.modal_ref), custom_call_target="tpu_custom_call" | custom-call | tf_op jit(solution)/shard_map/first/pallas_call | solution.py:531
  47.8 0.9 %collective-permute-start.2 = (f32[5,32,128]{2,1,0:T(8,128)S(1)}, f32[5,32,128]{2,1,0:T(8,128)S(1)}, u32[]{:S(2)}, u32[]{:S(2)}) collective-permute-start(f32[5,32,128]{2,1,0:T(8,128)S(1)} %get-tuple-element.24), channel_id=1, source_target_pairs={{0,1},{1,2},{2,3},{3,4},{4,5},{5,6},{6,7},{7,8},{8,9},{9,10},{10,1... | collective-permute-start | bytes 245768 | tf_op jit(solution)/shard_map/ppermute | solution.py:543
  48.7 1.2 %collective-permute-start.3 = (f32[5,32,128]{2,1,0:T(8,128)S(1)}, f32[5,32,128]{2,1,0:T(8,128)S(1)}, u32[]{:S(2)}, u32[]{:S(2)}) collective-permute-start(f32[5,32,128]{2,1,0:T(8,128)S(1)} %get-tuple-element.25), channel_id=1, source_target_pairs={{0,15},{1,0},{2,1},{3,2},{4,3},{5,4},{6,5},{7,6},{8,7},{9,8},{10,9... | collective-permute-start | bytes 245768 | tf_op jit(solution)/shard_map/ppermute | solution.py:544
  49.9 0.8 collective-permute-done.2.below_ref
  50.6 1.9 %collective-permute-done.3.above_ref = f32[5,32,128]{2,1,0:T(8,128)S(1)} collective-permute-done((f32[5,32,128]{2,1,0:T(8,128)S(1)}, f32[5,32,128]{2,1,0:T(8,128)S(1)}, u32[]{:S(2)}, u32[]{:S(2)}) %collective-permute-start.3) | collective-permute-done | bytes 81952 | tf_op jit(solution)/shard_map/ppermute | solution.py:544
  53.0 2.4 %collective-permute-start.5 = (f32[5,32,128]{2,1,0:T(8,128)S(1)}, f32[5,32,128]{2,1,0:T(8,128)S(1)}, u32[]{:S(2)}, u32[]{:S(2)}) collective-permute-start(f32[5,32,128]{2,1,0:T(8,128)S(1)} %get-tuple-element.29), channel_id=1, source_target_pairs={{0,15},{1,0},{2,1},{3,2},{4,3},{5,4},{6,5},{7,6},{8,7},{9,8},{10,9... | collective-permute-start | bytes 245768 | tf_op jit(solution)/shard_map/ppermute | solution.py:544
  55.6 0.5 collective-permute-done.4.below_ref
  56.1 1.0 %collective-permute-done.5.above_ref = f32[5,32,128]{2,1,0:T(8,128)S(1)} collective-permute-done((f32[5,32,128]{2,1,0:T(8,128)S(1)}, f32[5,32,128]{2,1,0:T(8,128)S(1)}, u32[]{:S(2)}, u32[]{:S(2)}) %collective-permute-start.5) | collective-permute-done | bytes 81952 | tf_op jit(solution)/shard_map/ppermute | solution.py:544
  57.1 1.2 %third.1 = (f32[25,32,128]{2,1,0:T(8,128)S(1)}, f32[16,8,128]{2,1,0:T(8,128)}) custom-call(f32[25,32,128]{2,1,0:T(8,128)S(1)} %get-tuple-element.27.joined_ref, f32[5,32,128]{2,1,0:T(8,128)S(1)} %collective-permute-done.4.below_ref, f32[5,32,128]{2,1,0:T(8,128)S(1)} %collective-permute-done.5.above_ref, ...), custom_call_target="tpu_custom_call" | custom-call | tf_op jit(solution)/shard_map/third/pallas_call | solution.py:531
  58.3 11.1 %all-to-all-start.2 = ((f32[16,8,128]{2,1,0:T(8,128)}), f32[16,8,128]{2,1,0:T(8,128)S(1)}, u32[]{:S(2)}, u32[]{:S(2)}) async-start(f32[16,8,128]{2,1,0:T(8,128)} %get-tuple-element.31), calls=%async_computation.2 | async-start | bytes 131072 | tf_op jit(solution)/shard_map/all_to_all | solution.py:584
  69.4 0.9 %natural.3.first_ref = f32[5,32,640]{2,1,0:T(8,128)S(1)} custom-call(f32[25,32,128]{2,1,0:T(8,128)S(1)} %get-tuple-element.26.before_ref.first_ref.vector_ref), custom_call_target="tpu_custom_call" | custom-call | tf_op jit(solution)/shard_map/natural/pallas_call | solution.py:531
  70.3 0.9 %natural.4.second_ref = f32[5,32,640]{2,1,0:T(8,128)S(1)} custom-call(f32[25,32,128]{2,1,0:T(8,128)S(1)} %get-tuple-element.30.second_ref.vector_ref), custom_call_target="tpu_custom_call" | custom-call | tf_op jit(solution)/shard_map/natural/pallas_call | solution.py:531
  71.3 0.9 %natural.5.third_ref = f32[5,32,640]{2,1,0:T(8,128)S(1)} custom-call(f32[25,32,128]{2,1,0:T(8,128)S(1)} %get-tuple-element.32.vector_ref), custom_call_target="tpu_custom_call" | custom-call | tf_op jit(solution)/shard_map/natural/pallas_call | solution.py:531
  72.2 5.0 %all-to-all-done.2.sums_ref = f32[16,8,128]{2,1,0:T(8,128)S(1)} async-done(((f32[16,8,128]{2,1,0:T(8,128)}), f32[16,8,128]{2,1,0:T(8,128)S(1)}, u32[]{:S(2)}, u32[]{:S(2)}) %all-to-all-start.2) | async-done | bytes 65568 | tf_op jit(solution)/shard_map/all_to_all | solution.py:584
  77.2 1.1 %combine.1 = f32[5,32,640]{2,1,0:T(8,128)} custom-call(f32[16,8,128]{2,1,0:T(8,128)S(1)} %all-to-all-done.2.sums_ref, f32[5,32,640]{2,1,0:T(8,128)S(1)} %natural.3.first_ref, f32[5,32,640]{2,1,0:T(8,128)S(1)} %natural.4.second_ref, f32[5,32,640]{2,1,0:T(8,128)S(1)} %natural.5.third_ref), custom_call_target="tpu_custom_call" | custom-call | tf_op jit(solution)/shard_map/combine/pallas_call | solution.py:531
  (8 shorter events, 0.6 us)
Async XLA Ops:
  0.0 20.9 %copy-start = (bf16[2,2,256,384]{3,2,1,0:T(8,128)(2,1)S(1)}, bf16[2,2,256,384]{3,2,1,0:T(8,128)(2,1)}, u32[]{:S(2)}) copy-start(bf16[2,2,256,384]{3,2,1,0:T(8,128)(2,1)} %constant.2.clone.table_ref) | copy-start | bytes 2359300
  22.4 6.3 %collective-permute-start = (f32[40,1280]{1,0:T(8,128)S(1)}, f32[40,1280]{1,0:T(8,128)S(1)}, u32[]{:S(2)}, u32[]{:S(2)}) collective-permute-start(f32[40,1280]{1,0:T(8,128)S(1)} %get-tuple-element.21), channel_id=1, source_target_pairs={{0,1},{1,2},{2,3},{3,4},{4,5},{5,6},{6,7},{7,8},{8,9},{9,10},{10,1... | collective-permute-start | bytes 614408 | tf_op jit(solution)/shard_map/ppermute | solution.py:543
  26.0 5.4 %collective-permute-start.1 = (f32[40,1280]{1,0:T(8,128)S(1)}, f32[40,1280]{1,0:T(8,128)S(1)}, u32[]{:S(2)}, u32[]{:S(2)}) collective-permute-start(f32[40,1280]{1,0:T(8,128)S(1)} %get-tuple-element.22), channel_id=1, source_target_pairs={{0,15},{1,0},{2,1},{3,2},{4,3},{5,4},{6,5},{7,6},{8,7},{9,8},{10,9... | collective-permute-start | bytes 614408 | tf_op jit(solution)/shard_map/ppermute | solution.py:544
  26.1 5.4 %copy-start.1 = (s32[128]{0:T(128)S(1)}, s32[128]{0:T(128)}, u32[]{:S(2)}) copy-start(s32[128]{0:T(128)} %tag_ref.1) | copy-start | bytes 1540
  47.8 2.9 %collective-permute-start.2 = (f32[5,32,128]{2,1,0:T(8,128)S(1)}, f32[5,32,128]{2,1,0:T(8,128)S(1)}, u32[]{:S(2)}, u32[]{:S(2)}) collective-permute-start(f32[5,32,128]{2,1,0:T(8,128)S(1)} %get-tuple-element.24), channel_id=1, source_target_pairs={{0,1},{1,2},{2,3},{3,4},{4,5},{5,6},{6,7},{7,8},{8,9},{9,10},{10,1... | collective-permute-start | bytes 245768 | tf_op jit(solution)/shard_map/ppermute | solution.py:543
  48.7 3.9 %collective-permute-start.3 = (f32[5,32,128]{2,1,0:T(8,128)S(1)}, f32[5,32,128]{2,1,0:T(8,128)S(1)}, u32[]{:S(2)}, u32[]{:S(2)}) collective-permute-start(f32[5,32,128]{2,1,0:T(8,128)S(1)} %get-tuple-element.25), channel_id=1, source_target_pairs={{0,15},{1,0},{2,1},{3,2},{4,3},{5,4},{6,5},{7,6},{8,7},{9,8},{10,9... | collective-permute-start | bytes 245768 | tf_op jit(solution)/shard_map/ppermute | solution.py:544
  52.9 3.2 %collective-permute-start.4 = (f32[5,32,128]{2,1,0:T(8,128)S(1)}, f32[5,32,128]{2,1,0:T(8,128)S(1)}, u32[]{:S(2)}, u32[]{:S(2)}) collective-permute-start(f32[5,32,128]{2,1,0:T(8,128)S(1)} %get-tuple-element.28), channel_id=1, source_target_pairs={{0,1},{1,2},{2,3},{3,4},{4,5},{5,6},{6,7},{7,8},{8,9},{9,10},{10,1... | collective-permute-start | bytes 245768 | tf_op jit(solution)/shard_map/ppermute | solution.py:543
  53.0 4.1 %collective-permute-start.5 = (f32[5,32,128]{2,1,0:T(8,128)S(1)}, f32[5,32,128]{2,1,0:T(8,128)S(1)}, u32[]{:S(2)}, u32[]{:S(2)}) collective-permute-start(f32[5,32,128]{2,1,0:T(8,128)S(1)} %get-tuple-element.29), channel_id=1, source_target_pairs={{0,15},{1,0},{2,1},{3,2},{4,3},{5,4},{6,5},{7,6},{8,7},{9,8},{10,9... | collective-permute-start | bytes 245768 | tf_op jit(solution)/shard_map/ppermute | solution.py:544
  58.3 18.9 %all-to-all-start.2 = ((f32[16,8,128]{2,1,0:T(8,128)}), f32[16,8,128]{2,1,0:T(8,128)S(1)}, u32[]{:S(2)}, u32[]{:S(2)}) async-start(f32[16,8,128]{2,1,0:T(8,128)} %get-tuple-element.31), calls=%async_computation.2 | async-start | bytes 131072 | tf_op jit(solution)/shard_map/all_to_all | solution.py:584

commit v4 on v3

--- a/solution.py
+++ b/solution.py
@@ -100,7 +100,7 @@
     return values
 
 
-def pack_kernel(state_hbm, out_hbm, chunk_ref, state_ref, order_ref, packed_ref, arrived, sent):
+def pack_kernel(state_hbm, out_ref, chunk_ref, state_ref, order_ref, arrived):
     copy = pltpu.make_async_copy(state_hbm, state_ref, arrived)
     copy.start()
     order_ref[...] = column_order()
@@ -126,18 +126,10 @@
         chunk.append(jnp.where(lane == 0, left, jnp.where(lane == 7, right, 0.0)))
     zero = jnp.zeros((32, 128), jnp.float32)
     chunk = chunk + [zero, zero]
-    copies = []
     for half in range(2):
         block = exchange_chunks(chunk[16 * half : 16 * half + 16])
         for d in range(GRID):
-            packed_ref[half, d] = block[d]
-        lanes = pl.ds(128 * half, 128)
-        copies.append(
-            pltpu.make_async_copy(packed_ref.at[half], out_hbm.at[:, :, lanes], sent.at[half])
-        )
-        copies[half].start()
-    for copy in copies:
-        copy.wait()
+            out_ref[d, :, 128 * half : 128 * half + 128] = block[d]
 
 
 def synthesize(nodal, table_ref):
@@ -157,7 +149,7 @@
     return mean - 0.5 * speed * (right - left)
 
 
-def volume_kernel(modal_ref, table_ref, field_ref, rhs_ref, low_ref, high_ref, side_ref):
+def volume_kernel(modal_ref, table_ref, field_ref, rhs_ref, cross_ref, chip_ref, side_ref):
     nodal = []
     for parity in range(2):
         rows = [
@@ -167,8 +159,9 @@
         ]
         nodal.append(jnp.concatenate(rows, axis=0).T)
         lanes = slice(PLANES + 256 * parity, PLANES + 256 * parity + 256)
-        low_ref[:, lanes] = nodal[parity][0:40]
-        high_ref[:, lanes] = nodal[parity][160:200]
+        cross_ref[:, lanes], chip_ref[:, lanes] = to_partners(
+            nodal[parity][0:40], nodal[parity][160:200]
+        )
     pair = synthesize(nodal, table_ref)
     for q in range(2):
         field_ref[:, HALF * q : HALF * q + HALF] = pair[q][0:200]
@@ -179,6 +172,7 @@
         lanes = pl.ds(pl.multiple_of(block * 128, 128), 128)
         f = [field_ref[8 * n : 8 * n + 8, lanes] for n in range(25)]
         square = [v * v for v in f]
+        low = []
         for j in range(5):
             for i in range(5):
                 n = j * 5 + i
@@ -206,9 +200,10 @@
                         total = total - 10.0 * two_point(f[n], right)
                 rhs_ref[8 * n : 8 * n + 8, lanes] = total
                 if j == 0:
-                    low_ref[8 * i : 8 * i + 8, lanes] = total
+                    low.append(total)
                 elif j == 4:
-                    high_ref[8 * i : 8 * i + 8, lanes] = total
+                    rows = slice(8 * i, 8 * i + 8)
+                    cross_ref[rows, lanes], chip_ref[rows, lanes] = to_partners(low[i], total)
         return carry
 
     lax.fori_loop(0, PLANES // 128, column, 0)
@@ -251,7 +246,7 @@
 
 
 def facing_kernel(
-    tag_ref, inside_ref, field_ref, below_ref, above_ref, table_ref, out_ref, outer_ref
+    tag_ref, inside_ref, field_ref, cross_ref, chip_ref, table_ref, out_ref, outer_ref
 ):
     bottom, top = at_ends()
     span = lax.axis_index("span")
@@ -259,9 +254,10 @@
     mirror = jnp.ones((8, 128), jnp.float32)
     for e in range(8):
         mirror = jnp.where((row == e) & (tag_ref[8 * span + e] == 1), -1.0, mirror)
+    below_trace, above_trace = from_partners(cross_ref[...], chip_ref[...])
     below_modal, above_modal = [
-        [ref[:, PLANES + 256 * parity : PLANES + 256 * parity + 256] for parity in range(2)]
-        for ref in (below_ref, above_ref)
+        [trace[:, PLANES + 256 * parity : PLANES + 256 * parity + 256] for parity in range(2)]
+        for trace in (below_trace, above_trace)
     ]
     outer = [
         jnp.concatenate([below_modal[parity], above_modal[parity]], axis=0) for parity in range(2)
@@ -274,12 +270,12 @@
     inside = field_ref[0:40, :]
     below = outer_ref[0:40, :]
     lift = 10.0 * two_point(jnp.where(bottom, mirror * inside, below), inside)
-    rhs_lower = lift + jnp.where(bottom, 0.0, below_ref[:, 0:PLANES] - lift)
+    rhs_lower = lift + jnp.where(bottom, 0.0, below_trace[:, 0:PLANES] - lift)
     flux_lower = jnp.where(bottom, 0.0, 0.5 * below * below)
     inside = field_ref[160:200, :]
     above = outer_ref[40:80, :]
     lift = 10.0 * two_point(inside, jnp.where(top, inside, above))
-    rhs_upper = jnp.where(top, 0.0, above_ref[:, 0:PLANES] + lift) - lift
+    rhs_upper = jnp.where(top, 0.0, above_trace[:, 0:PLANES] + lift) - lift
     flux_upper = jnp.where(top, 0.0, 0.5 * above * above)
     gap = jnp.zeros((48, PLANES), jnp.float32)
     planar = jnp.concatenate([rhs_lower, rhs_upper, gap, flux_lower, flux_upper, gap], axis=0)
@@ -310,6 +306,16 @@
     return plane == 0, plane == GRID - 1
 
 
+def to_partners(low, high):
+    odd = lax.axis_index("plane") % 2 == 1
+    return jnp.where(odd, high, low), jnp.where(odd, low, high)
+
+
+def from_partners(cross, chip):
+    odd = lax.axis_index("plane") % 2 == 1
+    return jnp.where(odd, chip, cross), jnp.where(odd, cross, chip)
+
+
 def local_operator(values, shift):
     out = []
     for j in range(5):
@@ -338,21 +344,21 @@
     return values
 
 
-def store_joined(values, joined_ref, low_ref, high_ref):
+def store_joined(values, joined_ref, cross_ref, chip_ref):
     values = join_columns(values)
     for n in range(25):
         joined_ref[n] = values[n]
     for i in range(5):
-        low_ref[i] = values[i]
-        high_ref[i] = values[20 + i]
-
-
-def assembled(joined_ref, below_ref, above_ref):
+        cross_ref[i], chip_ref[i] = to_partners(values[i], values[20 + i])
+
+
+def assembled(joined_ref, cross_ref, chip_ref):
     values = [joined_ref[n] for n in range(25)]
     bottom, top = at_ends()
     for i in range(5):
-        values[i] = values[i] + jnp.where(bottom, 0.0, below_ref[i])
-        values[20 + i] = values[20 + i] + jnp.where(top, 0.0, above_ref[i])
+        below, above = from_partners(cross_ref[i], chip_ref[i])
+        values[i] = values[i] + jnp.where(bottom, 0.0, below)
+        values[20 + i] = values[20 + i] + jnp.where(top, 0.0, above)
     return values
 
 
@@ -381,7 +387,7 @@
     return total
 
 
-def first_kernel(modal_ref, vector_ref, next_ref, low_ref, high_ref):
+def first_kernel(modal_ref, vector_ref, next_ref, cross_ref, chip_ref):
     shift, _ = mode_terms()
     values = []
     for half in range(2):
@@ -392,19 +398,18 @@
     vector = join_columns(values)
     for n in range(25):
         vector_ref[n] = vector[n]
-    store_joined(local_operator(vector, shift), next_ref, low_ref, high_ref)
+    store_joined(local_operator(vector, shift), next_ref, cross_ref, chip_ref)
 
 
 def second_kernel(
-    joined_ref, below_ref, above_ref, before_ref, vector_ref, next_ref, low_ref,
-    high_ref,
+    joined_ref, cross_in_ref, chip_in_ref, before_ref, vector_ref, next_ref, cross_ref, chip_ref
 ):
     shift, center = mode_terms()
-    applied = assembled(joined_ref, below_ref, above_ref)
+    applied = assembled(joined_ref, cross_in_ref, chip_in_ref)
     vector = [applied[n] - center * before_ref[n] for n in range(25)]
     for n in range(25):
         vector_ref[n] = vector[n]
-    store_joined(local_operator(vector, shift), next_ref, low_ref, high_ref)
+    store_joined(local_operator(vector, shift), next_ref, cross_ref, chip_ref)
 
 
 def pack_moments(moments, first, packed):
@@ -426,11 +431,11 @@
 
 
 def third_kernel(
-    joined_ref, below_ref, above_ref, second_ref, packed_ref, vector_ref, sums_ref,
+    joined_ref, cross_in_ref, chip_in_ref, second_ref, packed_ref, vector_ref, sums_ref,
     turn_ref,
 ):
     shift, center = mode_terms()
-    applied = assembled(joined_ref, below_ref, above_ref)
+    applied = assembled(joined_ref, cross_in_ref, chip_in_ref)
     second = [second_ref[n] for n in range(25)]
     third = [applied[n] - center * second[n] for n in range(25)]
     for n in range(25):
@@ -533,52 +538,53 @@
         name=name,
         out_shape=[jax.ShapeDtypeStruct(s, jnp.float32) for s in out_shapes],
         in_specs=[spaces.get(n, vmem) for n in range(len(args))],
-        out_specs=[pl.BlockSpec(memory_space=pltpu.HBM) if anywhere else vmem] * len(out_shapes),
+        out_specs=[vmem] * len(out_shapes),
         scratch_shapes=list(scratch),
         compiler_params=pltpu.CompilerParams(vmem_limit_bytes=limit * 1024 * 1024),
     )(*args)
 
 
-def from_neighbours(low, high):
-    below = lax.ppermute(high, "plane", [(p, (p + 1) % GRID) for p in range(GRID)])
-    above = lax.ppermute(low, "plane", [(p, (p - 1) % GRID) for p in range(GRID)])
-    return below, above
+def swap_traces(cross, chip):
+    partner = [(p, (p + 1) % GRID if p % 2 else (p - 1) % GRID) for p in range(GRID)]
+    cross = lax.ppermute(cross, "plane", partner)
+    chip = lax.ppermute(chip, "plane", [(p, p ^ 1) for p in range(GRID)])
+    return cross, chip
 
 
 def on_device(state, wall_tag):
     table = wave_table()
     (packed,) = call(
-        pack_kernel, "pack", [(16, 32, 256)], jnp.transpose(state, (1, 0, 2)),
-        anywhere=(0,), limit=60,
+        pack_kernel, "pack", [(16, 32, 256)],
+        pltpu.with_memory_space_constraint(jnp.transpose(state, (1, 0, 2)), pltpu.HBM),
+        anywhere=(0,),
         scratch=[
             pltpu.VMEM((800, 128), jnp.float32), pltpu.VMEM((5, 32, 640), jnp.float32),
-            pltpu.VMEM((640, 640), jnp.bfloat16), pltpu.VMEM((2, 16, 32, 128), jnp.float32),
-            pltpu.SemaphoreType.DMA(()), pltpu.SemaphoreType.DMA((2,)),
+            pltpu.VMEM((640, 640), jnp.bfloat16), pltpu.SemaphoreType.DMA(()),
         ],
     )
     modal = lax.all_to_all(packed, "span", 0, 0, tiled=True)
     trace = (40, PLANES + 512)
-    field, rhs, low, high = call(
+    field, rhs, cross, chip = call(
         volume_kernel, "volume", [(200, PLANES), (200, PLANES), trace, trace], modal, table,
         scratch=[pltpu.VMEM((40, PLANES), jnp.float32)],
     )
-    below, above = from_neighbours(low, high)
+    cross, chip = swap_traces(cross, chip)
     (inside,) = call(inside_kernel, "inside", [(2, 256, 256)], modal, field, rhs, table)
     (sent,) = call(
-        facing_kernel, "facing", [(16, 32, 256)], wall_tag, inside, field, below, above, table,
+        facing_kernel, "facing", [(16, 32, 256)], wall_tag, inside, field, cross, chip, table,
         smem=(0,), scratch=[pltpu.VMEM((80, PLANES), jnp.float32)],
     )
     load = lax.all_to_all(sent, "span", 0, 0, tiled=True)
     nodes, trace = (25, 32, 128), (5, 32, 128)
-    first, joined, low, high = call(first_kernel, "first", [nodes, nodes, trace, trace], load)
-    below, above = from_neighbours(low, high)
-    second, joined, low, high = call(
-        second_kernel, "second", [nodes, nodes, trace, trace], joined, below, above, first
-    )
-    below, above = from_neighbours(low, high)
+    first, joined, cross, chip = call(first_kernel, "first", [nodes, nodes, trace, trace], load)
+    cross, chip = swap_traces(cross, chip)
+    second, joined, cross, chip = call(
+        second_kernel, "second", [nodes, nodes, trace, trace], joined, cross, chip, first
+    )
+    cross, chip = swap_traces(cross, chip)
     (packed,) = call(early_kernel, "early", [(32, 128)], first, second)
     third, sums = call(
-        third_kernel, "third", [nodes, (16, 8, 128)], joined, below, above, second, packed,
+        third_kernel, "third", [nodes, (16, 8, 128)], joined, cross, chip, second, packed,
         scratch=[pltpu.VMEM((128, 128), jnp.float32)],
     )
     sums = lax.all_to_all(sums, "plane", 0, 0, tiled=True)

time: 78.5 us -> 75.9 us (0.967)
  waiting for transfers between devices: 13.5 us -> 6.91 us
  starting transfers between devices: 19.2 us -> 25.4 us
  blocking collectives: 31.4 us -> 29.9 us
    ppermute x6, starting transfers between devices: 8.12 us -> 16.8 us  [the longest x3 9.28 us: swap_traces(): cross = lax.ppermute(cross, 'plane', partner)]
    ppermute x6, waiting for transfers between devices: 8.54 us -> 1.94 us  [the longest x3 1.49 us: swap_traces(): chip = lax.ppermute(chip, 'plane', [(p, p ^ 1) for p in range(GRID)])]
    all_to_all x1, starting transfers between devices: 11.1 us -> 8.53 us  [on_device(): sums = lax.all_to_all(sums, 'plane', 0, 0, tiled=True)]
    all_to_all x1, blocking collectives: 13.4 us -> 12.2 us  [on_device(): load = lax.all_to_all(sent, 'span', 0, 0, tiled=True)]
  transfers between devices with their start and end apart: 7 -> 7, of which waited for: 7 -> 5; matrix products, arithmetic and copies ran while one was open for 0% -> 0% of each run, Pallas kernels for 5% -> 5%
where the time goes in v4:
time: 75.9 us; the launch traced here: 75.6 us
  blocking collectives  29.9 us (39%)
  starting transfers between devices  25.4 us (33%)
  Pallas kernels  13.4 us (18%)
  waiting for transfers between devices  6.91 us (9%)
    all_to_all x1, blocking collectives, on_device(): modal = lax.all_to_all(packed, 'span', 0, 0, tiled=True)  17.7 us
    pallas_call x12, Pallas kernels, call(): pl.pallas_call(kernel, name=name, out_shape=[jax.ShapeDtypeStruct(s, jnp....  13.4 us
    all_to_all x1, blocking collectives, on_device(): load = lax.all_to_all(sent, 'span', 0, 0, tiled=True)  12.2 us
    ppermute x3, starting transfers between devices, swap_traces(): cross = lax.ppermute(cross, 'plane', partner)  9.28 us
    all_to_all x1, starting transfers between devices, on_device(): sums = lax.all_to_all(sums, 'plane', 0, 0, tiled=True)  8.53 us
    ppermute x3, starting transfers between devices, swap_traces(): chip = lax.ppermute(chip, 'plane', [(p, p ^ 1) for p in range(GRID)])  7.54 us
    all_to_all x1, waiting for transfers between devices, on_device(): sums = lax.all_to_all(sums, 'plane', 0, 0, tiled=True)  4.97 us
  transfers between devices with their start and end apart: 7, of which 5 were waited for; matrix products, arithmetic and copies ran while one was open for 0% of the time, Pallas kernels for 5%

profile of v4, /device:TPU:1, one launch (start us, length us, event | category | flops | bytes accessed | tf_op | source)
XLA Modules:
  0.0 75.6 jit_solution(10229511235849882515)
XLA Ops:
  0.0 2.2 %pack.1 = f32[16,32,256]{2,1,0:T(8,128)S(1)} custom-call(f32[5,32,640]{2,1,0:T(8,128)} %bitcast.2), custom_call_target="tpu_custom_call" | custom-call | tf_op jit(solution)/shard_map/pack/pallas_call | solution.py:536
  2.2 17.7 %all_to_all.15.modal_ref = f32[16,32,256]{2,1,0:T(8,128)S(1)} all-to-all(f32[16,32,256]{2,1,0:T(8,128)S(1)} %pack.1), channel_id=1, replica_groups=mesh['span'=16,'plane'=16] {'span'}, dimensions={0} | all-to-all | bytes 1048576 | tf_op jit(solution)/shard_map/all_to_all | solution.py:565
  19.9 1.5 %volume.1 = (f32[200,768]{1,0:T(8,128)S(1)}, f32[200,768]{1,0:T(8,128)S(1)}, f32[40,1280]{1,0:T(8,128)S(1)}, f32[40,1280]{1,0:T(8,128)S(1)}) custom-call(f32[16,32,256]{2,1,0:T(8,128)S(1)} %all_to_all.15.modal_ref, bf16[2,2,256,384]{3,2,1,0:T(8,128)(2,1)S(1)} %copy-done), custom_call_target="tpu_custom_call" | custom-call | tf_op jit(solution)/shard_map/volume/pallas_call | solution.py:536
  21.5 3.7 %collective-permute-start = (f32[40,1280]{1,0:T(8,128)S(1)}, f32[40,1280]{1,0:T(8,128)S(1)}, u32[]{:S(2)}, u32[]{:S(2)}) collective-permute-start(f32[40,1280]{1,0:T(8,128)S(1)} %get-tuple-element.21), channel_id=1, source_target_pairs={{0,15},{1,2},{2,1},{3,4},{4,3},{5,6},{6,5},{7,8},{8,7},{9,10},{10,... | collective-permute-start | bytes 614408 | tf_op jit(solution)/shard_map/ppermute | solution.py:549
  25.2 2.4 %collective-permute-start.1 = (f32[40,1280]{1,0:T(8,128)S(1)}, f32[40,1280]{1,0:T(8,128)S(1)}, u32[]{:S(2)}, u32[]{:S(2)}) collective-permute-start(f32[40,1280]{1,0:T(8,128)S(1)} %get-tuple-element.22), channel_id=1, source_target_pairs={{0,1},{1,0},{2,3},{3,2},{4,5},{5,4},{6,7},{7,6},{8,9},{9,8},{10,11... | collective-permute-start | bytes 614408 | tf_op jit(solution)/shard_map/ppermute | solution.py:550
  27.6 1.1 %inside.1.inside_ref = f32[2,256,256]{2,1,0:T(8,128)S(1)} custom-call(f32[16,32,256]{2,1,0:T(8,128)S(1)} %all_to_all.15.modal_ref, f32[200,768]{1,0:T(8,128)S(1)} %get-tuple-element.19.field_ref, f32[200,768]{1,0:T(8,128)S(1)} %get-tuple-element.20.rhs_ref, bf16[2,2,256,384]{3,2,1,0:T(8,128)(2,1)S(1)} %copy-done), custom_call_target="tpu_custom_call" | custom-call | tf_op jit(solution)/shard_map/inside/pallas_call | solution.py:536
  28.6 0.3 collective-permute-done.cross_ref
  28.9 1.8 %facing.1 = f32[16,32,256]{2,1,0:T(8,128)S(1)} custom-call(s32[128]{0:T(128)S(1)} %copy-done.1, f32[2,256,256]{2,1,0:T(8,128)S(1)} %inside.1.inside_ref, f32[200,768]{1,0:T(8,128)S(1)} %get-tuple-element.19.field_ref, f32[40,1280]{1,0:T(8,128)S(1)} %collective-permute-done.cross_ref, f32[40,1280]{1,0:T(8,128)S(1)} %collective-permute-done.1.chip_ref, ...), custom_call_target="tpu_custom_call" | custom-call | tf_op jit(solution)/shard_map/facing/pallas_call | solution.py:536
  30.7 12.2 %all_to_all.16.modal_ref = f32[16,32,256]{2,1,0:T(8,128)S(1)} all-to-all(f32[16,32,256]{2,1,0:T(8,128)S(1)} %facing.1), channel_id=1, replica_groups=mesh['span'=16,'plane'=16] {'span'}, dimensions={0} | all-to-all | bytes 1048576 | tf_op jit(solution)/shard_map/all_to_all | solution.py:577
  42.9 1.1 %first.1 = (f32[25,32,128]{2,1,0:T(8,128)S(1)}, f32[25,32,128]{2,1,0:T(8,128)S(1)}, f32[5,32,128]{2,1,0:T(8,128)S(1)}, f32[5,32,128]{2,1,0:T(8,128)S(1)}) custom-call(f32[16,32,256]{2,1,0:T(8,128)S(1)} %all_to_all.16.modal_ref), custom_call_target="tpu_custom_call" | custom-call | tf_op jit(solution)/shard_map/first/pallas_call | solution.py:536
  44.0 4.6 %collective-permute-start.2 = (f32[5,32,128]{2,1,0:T(8,128)S(1)}, f32[5,32,128]{2,1,0:T(8,128)S(1)}, u32[]{:S(2)}, u32[]{:S(2)}) collective-permute-start(f32[5,32,128]{2,1,0:T(8,128)S(1)} %get-tuple-element.24), channel_id=1, source_target_pairs={{0,15},{1,2},{2,1},{3,4},{4,3},{5,6},{6,5},{7,8},{8,7},{9,10},{10,... | collective-permute-start | bytes 245768 | tf_op jit(solution)/shard_map/ppermute | solution.py:549
  48.6 2.0 %collective-permute-start.3 = (f32[5,32,128]{2,1,0:T(8,128)S(1)}, f32[5,32,128]{2,1,0:T(8,128)S(1)}, u32[]{:S(2)}, u32[]{:S(2)}) collective-permute-start(f32[5,32,128]{2,1,0:T(8,128)S(1)} %get-tuple-element.25), channel_id=1, source_target_pairs={{0,1},{1,0},{2,3},{3,2},{4,5},{5,4},{6,7},{7,6},{8,9},{9,8},{10,11... | collective-permute-start | bytes 245768 | tf_op jit(solution)/shard_map/ppermute | solution.py:550
  50.7 0.8 %collective-permute-done.3.chip_in_ref = f32[5,32,128]{2,1,0:T(8,128)S(1)} collective-permute-done((f32[5,32,128]{2,1,0:T(8,128)S(1)}, f32[5,32,128]{2,1,0:T(8,128)S(1)}, u32[]{:S(2)}, u32[]{:S(2)}) %collective-permute-start.3) | collective-permute-done | bytes 81952 | tf_op jit(solution)/shard_map/ppermute | solution.py:550
  51.5 0.4 second.1
  51.9 1.0 %collective-permute-start.4 = (f32[5,32,128]{2,1,0:T(8,128)S(1)}, f32[5,32,128]{2,1,0:T(8,128)S(1)}, u32[]{:S(2)}, u32[]{:S(2)}) collective-permute-start(f32[5,32,128]{2,1,0:T(8,128)S(1)} %get-tuple-element.28), channel_id=1, source_target_pairs={{0,15},{1,2},{2,1},{3,4},{4,3},{5,6},{6,5},{7,8},{8,7},{9,10},{10,... | collective-permute-start | bytes 245768 | tf_op jit(solution)/shard_map/ppermute | solution.py:549
  52.9 3.2 %collective-permute-start.5 = (f32[5,32,128]{2,1,0:T(8,128)S(1)}, f32[5,32,128]{2,1,0:T(8,128)S(1)}, u32[]{:S(2)}, u32[]{:S(2)}) collective-permute-start(f32[5,32,128]{2,1,0:T(8,128)S(1)} %get-tuple-element.29), channel_id=1, source_target_pairs={{0,1},{1,0},{2,3},{3,2},{4,5},{5,4},{6,7},{7,6},{8,9},{9,8},{10,11... | collective-permute-start | bytes 245768 | tf_op jit(solution)/shard_map/ppermute | solution.py:550
  56.3 0.7 collective-permute-done.5.chip_in_ref
  57.0 1.2 %third.1 = (f32[25,32,128]{2,1,0:T(8,128)S(1)}, f32[16,8,128]{2,1,0:T(8,128)}) custom-call(f32[25,32,128]{2,1,0:T(8,128)S(1)} %get-tuple-element.27.joined_ref, f32[5,32,128]{2,1,0:T(8,128)S(1)} %collective-permute-done.4.cross_in_ref, f32[5,32,128]{2,1,0:T(8,128)S(1)} %collective-permute-done.5.chip_in_ref, ...), custom_call_target="tpu_custom_call" | custom-call | tf_op jit(solution)/shard_map/third/pallas_call | solution.py:536
  58.3 8.5 %all-to-all-start.2 = ((f32[16,8,128]{2,1,0:T(8,128)}), f32[16,8,128]{2,1,0:T(8,128)S(1)}, u32[]{:S(2)}, u32[]{:S(2)}) async-start(f32[16,8,128]{2,1,0:T(8,128)} %get-tuple-element.31), calls=%async_computation.2 | async-start | bytes 131072 | tf_op jit(solution)/shard_map/all_to_all | solution.py:590
  66.8 0.9 %natural.3.first_ref = f32[5,32,640]{2,1,0:T(8,128)S(1)} custom-call(f32[25,32,128]{2,1,0:T(8,128)S(1)} %get-tuple-element.26.before_ref.first_ref.vector_ref), custom_call_target="tpu_custom_call" | custom-call | tf_op jit(solution)/shard_map/natural/pallas_call | solution.py:536
  67.7 0.9 %natural.4.second_ref = f32[5,32,640]{2,1,0:T(8,128)S(1)} custom-call(f32[25,32,128]{2,1,0:T(8,128)S(1)} %get-tuple-element.30.second_ref.vector_ref), custom_call_target="tpu_custom_call" | custom-call | tf_op jit(solution)/shard_map/natural/pallas_call | solution.py:536
  68.7 0.9 %natural.5.third_ref = f32[5,32,640]{2,1,0:T(8,128)S(1)} custom-call(f32[25,32,128]{2,1,0:T(8,128)S(1)} %get-tuple-element.32.vector_ref), custom_call_target="tpu_custom_call" | custom-call | tf_op jit(solution)/shard_map/natural/pallas_call | solution.py:536
  69.6 5.0 %all-to-all-done.2.sums_ref = f32[16,8,128]{2,1,0:T(8,128)S(1)} async-done(((f32[16,8,128]{2,1,0:T(8,128)}), f32[16,8,128]{2,1,0:T(8,128)S(1)}, u32[]{:S(2)}, u32[]{:S(2)}) %all-to-all-start.2) | async-done | bytes 65568 | tf_op jit(solution)/shard_map/all_to_all | solution.py:590
  74.6 1.1 %combine.1 = f32[5,32,640]{2,1,0:T(8,128)} custom-call(f32[16,8,128]{2,1,0:T(8,128)S(1)} %all-to-all-done.2.sums_ref, f32[5,32,640]{2,1,0:T(8,128)S(1)} %natural.3.first_ref, f32[5,32,640]{2,1,0:T(8,128)S(1)} %natural.4.second_ref, f32[5,32,640]{2,1,0:T(8,128)S(1)} %natural.5.third_ref), custom_call_target="tpu_custom_call" | custom-call | tf_op jit(solution)/shard_map/combine/pallas_call | solution.py:536
  (8 shorter events, 0.4 us)
Async XLA Ops:
  0.0 19.9 %copy-start = (bf16[2,2,256,384]{3,2,1,0:T(8,128)(2,1)S(1)}, bf16[2,2,256,384]{3,2,1,0:T(8,128)(2,1)}, u32[]{:S(2)}) copy-start(bf16[2,2,256,384]{3,2,1,0:T(8,128)(2,1)} %constant.2.clone.table_ref) | copy-start | bytes 2359300
  21.5 7.4 %collective-permute-start = (f32[40,1280]{1,0:T(8,128)S(1)}, f32[40,1280]{1,0:T(8,128)S(1)}, u32[]{:S(2)}, u32[]{:S(2)}) collective-permute-start(f32[40,1280]{1,0:T(8,128)S(1)} %get-tuple-element.21), channel_id=1, source_target_pairs={{0,15},{1,2},{2,1},{3,4},{4,3},{5,6},{6,5},{7,8},{8,7},{9,10},{10,... | collective-permute-start | bytes 614408 | tf_op jit(solution)/shard_map/ppermute | solution.py:549
  25.2 3.7 %collective-permute-start.1 = (f32[40,1280]{1,0:T(8,128)S(1)}, f32[40,1280]{1,0:T(8,128)S(1)}, u32[]{:S(2)}, u32[]{:S(2)}) collective-permute-start(f32[40,1280]{1,0:T(8,128)S(1)} %get-tuple-element.22), channel_id=1, source_target_pairs={{0,1},{1,0},{2,3},{3,2},{4,5},{5,4},{6,7},{7,6},{8,9},{9,8},{10,11... | collective-permute-start | bytes 614408 | tf_op jit(solution)/shard_map/ppermute | solution.py:550
  27.6 1.4 %copy-start.1 = (s32[128]{0:T(128)S(1)}, s32[128]{0:T(128)}, u32[]{:S(2)}) copy-start(s32[128]{0:T(128)} %tag_ref.1) | copy-start | bytes 1540
  44.0 6.7 %collective-permute-start.2 = (f32[5,32,128]{2,1,0:T(8,128)S(1)}, f32[5,32,128]{2,1,0:T(8,128)S(1)}, u32[]{:S(2)}, u32[]{:S(2)}) collective-permute-start(f32[5,32,128]{2,1,0:T(8,128)S(1)} %get-tuple-element.24), channel_id=1, source_target_pairs={{0,15},{1,2},{2,1},{3,4},{4,3},{5,6},{6,5},{7,8},{8,7},{9,10},{10,... | collective-permute-start | bytes 245768 | tf_op jit(solution)/shard_map/ppermute | solution.py:549
  48.6 2.9 %collective-permute-start.3 = (f32[5,32,128]{2,1,0:T(8,128)S(1)}, f32[5,32,128]{2,1,0:T(8,128)S(1)}, u32[]{:S(2)}, u32[]{:S(2)}) collective-permute-start(f32[5,32,128]{2,1,0:T(8,128)S(1)} %get-tuple-element.25), channel_id=1, source_target_pairs={{0,1},{1,0},{2,3},{3,2},{4,5},{5,4},{6,7},{7,6},{8,9},{9,8},{10,11... | collective-permute-start | bytes 245768 | tf_op jit(solution)/shard_map/ppermute | solution.py:550
  51.9 4.4 %collective-permute-start.4 = (f32[5,32,128]{2,1,0:T(8,128)S(1)}, f32[5,32,128]{2,1,0:T(8,128)S(1)}, u32[]{:S(2)}, u32[]{:S(2)}) collective-permute-start(f32[5,32,128]{2,1,0:T(8,128)S(1)} %get-tuple-element.28), channel_id=1, source_target_pairs={{0,15},{1,2},{2,1},{3,4},{4,3},{5,6},{6,5},{7,8},{8,7},{9,10},{10,... | collective-permute-start | bytes 245768 | tf_op jit(solution)/shard_map/ppermute | solution.py:549
  52.9 4.1 %collective-permute-start.5 = (f32[5,32,128]{2,1,0:T(8,128)S(1)}, f32[5,32,128]{2,1,0:T(8,128)S(1)}, u32[]{:S(2)}, u32[]{:S(2)}) collective-permute-start(f32[5,32,128]{2,1,0:T(8,128)S(1)} %get-tuple-element.29), channel_id=1, source_target_pairs={{0,1},{1,0},{2,3},{3,2},{4,5},{5,4},{6,7},{7,6},{8,9},{9,8},{10,11... | collective-permute-start | bytes 245768 | tf_op jit(solution)/shard_map/ppermute | solution.py:550
  58.3 16.3 %all-to-all-start.2 = ((f32[16,8,128]{2,1,0:T(8,128)}), f32[16,8,128]{2,1,0:T(8,128)S(1)}, u32[]{:S(2)}, u32[]{:S(2)}) async-start(f32[16,8,128]{2,1,0:T(8,128)} %get-tuple-element.31), calls=%async_computation.2 | async-start | bytes 131072 | tf_op jit(solution)/shard_map/all_to_all | solution.py:590

commit v5 on v4

--- a/solution.py
+++ b/solution.py
@@ -7,6 +7,7 @@
 from jax.experimental import pallas as pl
 from jax.experimental.pallas import tpu as pltpu
 from jax.sharding import PartitionSpec as P
+
 
 KMODES = 256
 PLANES = 768
@@ -63,14 +64,6 @@
     return high, low
 
 
-def thirds(value):
-    high = value.astype(jnp.bfloat16)
-    rest = value - high.astype(jnp.float32)
-    middle = rest.astype(jnp.bfloat16)
-    low = (rest - middle.astype(jnp.float32)).astype(jnp.bfloat16)
-    return high, middle, low
-
-
 def dot_split(left, right, contract):
     (left_high, left_low), (right_high, right_low) = left, right
     return (
@@ -80,11 +73,34 @@
     )
 
 
-def column_order():
-    column = lax.broadcasted_iota(jnp.int32, (640, 128), 0)
-    element = lax.broadcasted_iota(jnp.int32, (640, 128), 1)
-    tiles = [jnp.where(column == 5 * element + i, 1.0, 0.0).astype(jnp.bfloat16) for i in range(5)]
-    return jnp.concatenate(tiles, axis=1)
+def lanes_of(values, index):
+    return jnp.take_along_axis(values, index, axis=1)
+
+
+def split_columns(tiles):
+    lane = lax.broadcasted_iota(jnp.int32, tiles[0].shape, 1)
+    out = []
+    for i in range(5):
+        column = 5 * lane + i
+        picked = lanes_of(tiles[0], column & 127)
+        for t in range(1, 5):
+            picked = jnp.where(column >= 128 * t, lanes_of(tiles[t], column & 127), picked)
+        out.append(picked)
+    return out
+
+
+def merge_columns(tiles):
+    lane = lax.broadcasted_iota(jnp.int32, tiles[0].shape, 1)
+    out = []
+    for t in range(5):
+        column = lane + 128 * t
+        element = (column * 13108) >> 16
+        node = column - 5 * element
+        picked = lanes_of(tiles[0], element)
+        for i in range(1, 5):
+            picked = jnp.where(node == i, lanes_of(tiles[i], element), picked)
+        out.append(picked)
+    return out
 
 
 def exchange_chunks(values):
@@ -92,32 +108,37 @@
     lane = lax.broadcasted_iota(jnp.int32, values[0].shape, 1)
     for bit in (1, 2, 4, 8):
         upper = (lane & (8 * bit)) != 0
+        other = lane ^ (8 * bit)
         for a in range(16):
             if a & bit == 0:
                 first, second = values[a], values[a | bit]
-                values[a] = jnp.where(upper, pltpu.roll(second, 8 * bit, 1), first)
-                values[a | bit] = jnp.where(upper, second, pltpu.roll(first, 128 - 8 * bit, 1))
+                moved = jnp.where(upper, first, second)
+                if bit == 8:
+                    moved = pltpu.roll(moved, 64, 1)
+                else:
+                    moved = lanes_of(moved, other)
+                values[a] = jnp.where(upper, moved, first)
+                values[a | bit] = jnp.where(upper, second, moved)
     return values
 
 
-def pack_kernel(state_hbm, out_ref, chunk_ref, state_ref, order_ref, arrived):
-    copy = pltpu.make_async_copy(state_hbm, state_ref, arrived)
-    copy.start()
-    order_ref[...] = column_order()
-    copy.wait()
-    stacked = jnp.concatenate([state_ref[j] for j in range(5)], axis=0)
-    order = order_ref[...]
-    contract = ((1,), (0,))
-    high, low = halves(stacked)
-    nodes = dot(low, order, contract) + dot(high, order, contract)
-    for i in range(5):
-        chunk_ref[160 * i : 160 * i + 160, :] = nodes[:, 128 * i : 128 * i + 128]
+def pack_kernel(state_hbm, out_ref, chunk_ref, state_ref, arrived):
+    copies = [
+        pltpu.make_async_copy(state_hbm.at[j], state_ref.at[j], arrived.at[j]) for j in range(5)
+    ]
+    for copy in copies:
+        copy.start()
+    for j in range(5):
+        copies[j].wait()
+        tiles = split_columns([state_ref[j, :, 128 * t : 128 * t + 128] for t in range(5)])
+        for i in range(5):
+            first = 32 * (5 * j + i)
+            chunk_ref[first : first + 32, :] = tiles[i]
     chunk = [
         jnp.concatenate(
-            [chunk_ref[pl.ds(160 * i + 32 * j + t, 8, stride=4), :] for t in range(4)], axis=0
+            [chunk_ref[pl.ds(32 * n + t, 8, stride=4), :] for t in range(4)], axis=0
         )
-        for j in range(5)
-        for i in range(5)
+        for n in range(25)
     ]
     lane = lax.broadcasted_iota(jnp.int32, (32, 128), 1) & 7
     for j in range(5):
@@ -149,19 +170,20 @@
     return mean - 0.5 * speed * (right - left)
 
 
-def volume_kernel(modal_ref, table_ref, field_ref, rhs_ref, cross_ref, chip_ref, side_ref):
-    nodal = []
+def turn_kernel(modal_ref, nodal_ref, cross_ref, chip_ref):
     for parity in range(2):
         rows = [
             modal_ref[s, 16 * parity + 8 * t : 16 * parity + 8 * t + 8, :]
             for t in range(2)
             for s in range(GRID)
         ]
-        nodal.append(jnp.concatenate(rows, axis=0).T)
-        lanes = slice(PLANES + 256 * parity, PLANES + 256 * parity + 256)
-        cross_ref[:, lanes], chip_ref[:, lanes] = to_partners(
-            nodal[parity][0:40], nodal[parity][160:200]
-        )
+        nodal = jnp.concatenate(rows, axis=0).T
+        nodal_ref[parity] = nodal
+        cross_ref[parity], chip_ref[parity] = to_partners(nodal[0:40], nodal[160:200])
+
+
+def volume_kernel(nodal_ref, table_ref, field_ref, rhs_ref, cross_ref, chip_ref, side_ref):
+    nodal = [nodal_ref[0], nodal_ref[1]]
     pair = synthesize(nodal, table_ref)
     for q in range(2):
         field_ref[:, HALF * q : HALF * q + HALF] = pair[q][0:200]
@@ -245,8 +267,8 @@
                 out_ref[parity, 128 * t : 128 * t + 128, lanes] = modal + change[t]
 
 
-def facing_kernel(
-    tag_ref, inside_ref, field_ref, cross_ref, chip_ref, table_ref, out_ref, outer_ref
+def lift_kernel(
+    tag_ref, field_ref, cross_ref, chip_ref, table_ref, lift_ref, flux_ref, modal_ref, outer_ref
 ):
     bottom, top = at_ends()
     span = lax.axis_index("span")
@@ -254,14 +276,16 @@
     mirror = jnp.ones((8, 128), jnp.float32)
     for e in range(8):
         mirror = jnp.where((row == e) & (tag_ref[8 * span + e] == 1), -1.0, mirror)
-    below_trace, above_trace = from_partners(cross_ref[...], chip_ref[...])
-    below_modal, above_modal = [
-        [trace[:, PLANES + 256 * parity : PLANES + 256 * parity + 256] for parity in range(2)]
-        for trace in (below_trace, above_trace)
-    ]
-    outer = [
-        jnp.concatenate([below_modal[parity], above_modal[parity]], axis=0) for parity in range(2)
-    ]
+    keep_lower = jnp.where(bottom, 0.0, 1.0)
+    keep_upper = jnp.where(top, 0.0, 1.0)
+    gap = jnp.zeros((48, 256), jnp.float32)
+    outer = []
+    for parity in range(2):
+        below, above = from_partners(cross_ref[parity], chip_ref[parity])
+        outer.append(jnp.concatenate([below, above], axis=0))
+        modal_ref[parity] = jnp.concatenate(
+            [keep_lower * below, keep_upper * above, gap], axis=0
+        ).T
     pair = synthesize(outer, table_ref)
     for q in range(2):
         outer_ref[:, HALF * q : HALF * q + HALF] = pair[q]
@@ -269,34 +293,38 @@
     mirror = jnp.concatenate([mirror] * 5, axis=0)
     inside = field_ref[0:40, :]
     below = outer_ref[0:40, :]
-    lift = 10.0 * two_point(jnp.where(bottom, mirror * inside, below), inside)
-    rhs_lower = lift + jnp.where(bottom, 0.0, below_trace[:, 0:PLANES] - lift)
-    flux_lower = jnp.where(bottom, 0.0, 0.5 * below * below)
+    lift_ref[0:40, :] = 10.0 * two_point(jnp.where(bottom, mirror * inside, below), inside)
+    flux_ref[0:40, :] = keep_lower * (0.5 * below * below)
     inside = field_ref[160:200, :]
     above = outer_ref[40:80, :]
-    lift = 10.0 * two_point(inside, jnp.where(top, inside, above))
-    rhs_upper = jnp.where(top, 0.0, above_trace[:, 0:PLANES] + lift) - lift
-    flux_upper = jnp.where(top, 0.0, 0.5 * above * above)
+    lift_ref[40:80, :] = 10.0 * two_point(inside, jnp.where(top, inside, above))
+    flux_ref[40:80, :] = keep_upper * (0.5 * above * above)
+
+
+def facing_kernel(
+    inside_ref, lift_ref, flux_ref, facing_ref, cross_ref, chip_ref, table_ref, out_ref
+):
+    bottom, top = at_ends()
+    below, above = from_partners(cross_ref[...], chip_ref[...])
+    lift = lift_ref[0:40, :]
+    rhs_lower = lift + jnp.where(bottom, 0.0, below - lift)
+    lift = lift_ref[40:80, :]
+    rhs_upper = jnp.where(top, 0.0, above + lift) - lift
     gap = jnp.zeros((48, PLANES), jnp.float32)
-    planar = jnp.concatenate([rhs_lower, rhs_upper, gap, flux_lower, flux_upper, gap], axis=0)
-    gap = jnp.zeros((48, 256), jnp.float32)
-    keep_lower = jnp.where(bottom, 0.0, 1.0)
-    keep_upper = jnp.where(top, 0.0, 1.0)
+    planar = jnp.concatenate([rhs_lower, rhs_upper, gap, flux_ref[...], gap], axis=0)
     lane = lax.broadcasted_iota(jnp.int32, (128, 128), 1)
     for parity in range(2):
         projected = project(planar, parity, table_ref)
         change = tendency(parity, projected[:, 0:128], projected[:, 128:256])
-        modal = jnp.concatenate(
-            [keep_lower * below_modal[parity], keep_upper * above_modal[parity], gap], axis=0
-        ).T
         for t in range(2):
             first = 16 * parity + 8 * t
-            extra = change[t] + modal[128 * t : 128 * t + 128]
+            rows = slice(128 * t, 128 * t + 128)
+            extra = change[t] + facing_ref[parity, rows, :]
             lower = jnp.where(lane < 40, extra, 0.0)
             upper = pltpu.roll(jnp.where(lane < 40, 0.0, extra), 120, 1)
             for half, added in ((0, lower), (1, upper)):
                 lanes = slice(128 * half, 128 * half + 128)
-                total = inside_ref[parity, 128 * t : 128 * t + 128, lanes] + added
+                total = inside_ref[parity, rows, lanes] + added
                 for s in range(GRID):
                     out_ref[s, first : first + 8, lanes] = total[8 * s : 8 * s + 8]
 
@@ -447,39 +475,26 @@
         fifth = fifth + local[n] * third[n]
     moments = [inner(second, third), fourth, fifth]
     packed = pack_moments(moments, 3, packed_ref[...])
-    turn_ref[...] = jnp.zeros((128, 128), jnp.float32)
     for t in range(4):
         turn_ref[pl.ds(t, 8, stride=4), :] = packed[8 * t : 8 * t + 8]
     turned = turn_ref[...].T[0:8]
     for p in range(GRID):
-        sums_ref[p] = turned
+        sums_ref[p, :, 0:32] = turned
 
 
 def natural_kernel(vector_ref, out_ref, column_ref):
-    order = column_order()
-    stacked = jnp.concatenate(
-        [
-            jnp.concatenate([vector_ref[j * 5 + i] for i in range(5)], axis=1) for j in range(5)
-        ],
-        axis=0,
-    )
-    contract = ((1,), (1,))
-    high, middle, low = thirds(stacked)
-    columns = dot(low, order, contract) + dot(middle, order, contract) + dot(high, order, contract)
-    for i in range(5):
-        for j in range(5):
+    for j in range(5):
+        tiles = merge_columns([vector_ref[j * 5 + i] for i in range(5)])
+        for i in range(5):
+            first = 32 * (5 * j + i)
             for t in range(4):
-                first = 32 * j + 8 * t
-                column_ref[pl.ds(160 * i + 32 * j + t, 8, stride=4), :] = columns[
-                    first : first + 8, 128 * i : 128 * i + 128
-                ]
-    for j in range(5):
-        for i in range(5):
-            first = 160 * i + 32 * j
+                column_ref[pl.ds(first + t, 8, stride=4), :] = tiles[i][8 * t : 8 * t + 8]
             out_ref[j, :, 128 * i : 128 * i + 128] = column_ref[first : first + 32, :]
 
 
-def combine_kernel(sums_ref, first_ref, second_ref, third_ref, out_ref, turn_ref):
+def combine_kernel(
+    sums_ref, first_ref, second_ref, third_ref, out_hbm, turn_ref, result_ref, sent
+):
     total = sums_ref[0]
     for p in range(1, GRID):
         total = total + sums_ref[p]
@@ -518,29 +533,34 @@
             norm = fresh
             padded = direction + [0.0]
             direction = [residual[a] + ratio * padded[a] for a in range(len(residual))]
-    turn_ref[...] = jnp.zeros((128, 128), jnp.float32)
+    turn_ref[...] = jnp.zeros((8, 128), jnp.float32)
     for a in range(3):
         turn_ref[a : a + 1, :] = result[a]
     turned = turn_ref[...].T[0:32]
     weight = [turned[:, a : a + 1] for a in range(3)]
+    copies = []
     for j in range(5):
-        out_ref[j] = (
+        result_ref[j] = (
             weight[0] * first_ref[j] + weight[1] * second_ref[j] + weight[2] * third_ref[j]
         )
-
-
-def call(kernel, name, out_shapes, *args, smem=(), anywhere=(), scratch=(), limit=16):
+        copies.append(pltpu.make_async_copy(result_ref.at[j], out_hbm.at[j], sent.at[j]))
+        copies[j].start()
+    for copy in copies:
+        copy.wait()
+
+
+def call(kernel, out_shapes, *args, smem=(), anywhere=(), scratch=(), out_space=pltpu.VMEM, covers=True):
     vmem = pl.BlockSpec(memory_space=pltpu.VMEM)
     spaces = {n: pl.BlockSpec(memory_space=pltpu.SMEM) for n in smem}
     spaces |= {n: pl.BlockSpec(memory_space=pltpu.HBM) for n in anywhere}
     return pl.pallas_call(
         kernel,
-        name=name,
         out_shape=[jax.ShapeDtypeStruct(s, jnp.float32) for s in out_shapes],
         in_specs=[spaces.get(n, vmem) for n in range(len(args))],
-        out_specs=[vmem] * len(out_shapes),
+        out_specs=[pl.BlockSpec(memory_space=out_space)] * len(out_shapes),
         scratch_shapes=list(scratch),
-        compiler_params=pltpu.CompilerParams(vmem_limit_bytes=limit * 1024 * 1024),
+        cost_estimate=None if covers else pl.CostEstimate(flops=0, bytes_accessed=0, transcendentals=0),
+        compiler_params=pltpu.CompilerParams(vmem_limit_bytes=16 * 1024 * 1024),
     )(*args)
 
 
@@ -554,57 +574,66 @@
 def on_device(state, wall_tag):
     table = wave_table()
     (packed,) = call(
-        pack_kernel, "pack", [(16, 32, 256)],
+        pack_kernel, [(16, 32, 256)],
         pltpu.with_memory_space_constraint(jnp.transpose(state, (1, 0, 2)), pltpu.HBM),
         anywhere=(0,),
         scratch=[
             pltpu.VMEM((800, 128), jnp.float32), pltpu.VMEM((5, 32, 640), jnp.float32),
-            pltpu.VMEM((640, 640), jnp.bfloat16), pltpu.SemaphoreType.DMA(()),
+            pltpu.SemaphoreType.DMA((5,)),
         ],
     )
     modal = lax.all_to_all(packed, "span", 0, 0, tiled=True)
-    trace = (40, PLANES + 512)
+    trace, rows = (2, 40, 256), (40, PLANES)
+    nodal, cross, chip = call(turn_kernel, [(2, 256, 256), trace, trace], modal)
+    modal_traces = swap_traces(cross, chip)
     field, rhs, cross, chip = call(
-        volume_kernel, "volume", [(200, PLANES), (200, PLANES), trace, trace], modal, table,
-        scratch=[pltpu.VMEM((40, PLANES), jnp.float32)],
-    )
-    cross, chip = swap_traces(cross, chip)
-    (inside,) = call(inside_kernel, "inside", [(2, 256, 256)], modal, field, rhs, table)
-    (sent,) = call(
-        facing_kernel, "facing", [(16, 32, 256)], wall_tag, inside, field, cross, chip, table,
-        smem=(0,), scratch=[pltpu.VMEM((80, PLANES), jnp.float32)],
-    )
+        volume_kernel, [(200, PLANES), (200, PLANES), rows, rows], nodal, table,
+        scratch=[pltpu.VMEM(rows, jnp.float32)],
+    )
+    rhs_traces = swap_traces(cross, chip)
+    (inside,) = call(inside_kernel, [(2, 256, 256)], modal, field, rhs, table, covers=False)
+    lift, flux, facing = call(
+        lift_kernel, [(80, PLANES), (80, PLANES), (2, 256, 128)], wall_tag, field,
+        *modal_traces, table, smem=(0,), scratch=[pltpu.VMEM((80, PLANES), jnp.float32)],
+        covers=False,
+    )
+    (sent,) = call(facing_kernel, [(16, 32, 256)], inside, lift, flux, facing, *rhs_traces, table)
     load = lax.all_to_all(sent, "span", 0, 0, tiled=True)
     nodes, trace = (25, 32, 128), (5, 32, 128)
-    first, joined, cross, chip = call(first_kernel, "first", [nodes, nodes, trace, trace], load)
+    first, joined, cross, chip = call(first_kernel, [nodes, nodes, trace, trace], load)
     cross, chip = swap_traces(cross, chip)
     second, joined, cross, chip = call(
-        second_kernel, "second", [nodes, nodes, trace, trace], joined, cross, chip, first
+        second_kernel, [nodes, nodes, trace, trace], joined, cross, chip, first
     )
     cross, chip = swap_traces(cross, chip)
-    (packed,) = call(early_kernel, "early", [(32, 128)], first, second)
+    (packed,) = call(early_kernel, [(32, 128)], first, second)
     third, sums = call(
-        third_kernel, "third", [nodes, (16, 8, 128)], joined, cross, chip, second, packed,
-        scratch=[pltpu.VMEM((128, 128), jnp.float32)],
+        third_kernel, [nodes, (16, 8, 128)], joined, cross, chip, second, packed,
+        scratch=[pltpu.VMEM((32, 128), jnp.float32)],
     )
     sums = lax.all_to_all(sums, "plane", 0, 0, tiled=True)
     columns = [
         call(
-            natural_kernel, "natural", [(5, 32, 640)], vector,
+            natural_kernel, [(5, 32, 640)], vector,
             scratch=[pltpu.VMEM((800, 128), jnp.float32)],
         )[0]
         for vector in (first, second, third)
     ]
     (columns,) = call(
-        combine_kernel, "combine", [(5, 32, 640)], sums, *columns,
-        scratch=[pltpu.VMEM((128, 128), jnp.float32)],
+        combine_kernel, [(5, 32, 640)], sums, *columns, out_space=pltpu.HBM,
+        scratch=[
+            pltpu.VMEM((8, 128), jnp.float32), pltpu.VMEM((5, 32, 640), jnp.float32),
+            pltpu.SemaphoreType.DMA((5,)),
+        ],
     )
     return jnp.transpose(columns, (1, 0, 2))
 
 
 def solution(mesh):
-    in_specs = (P("span", "plane", None), P())
-    out_specs = P("span", "plane", None)
     return jax.shard_map(
-        on_device, mesh=mesh, in_specs=in_specs, out_specs=out_specs, check_vma=False
-    )
+        on_device,
+        mesh=mesh,
+        in_specs=(P("span", "plane", None), P()),
+        out_specs=P("span", "plane", None),
+        check_vma=False,
+    )

time: 75.9 us -> 77 us (1.014)
  blocking collectives: 29.9 us -> 31.4 us
  starting transfers between devices: 25.4 us -> 23.9 us
  waiting for transfers between devices: 6.91 us -> 8.36 us
    ppermute x3 -> x4, starting transfers between devices: 9.28 us -> 6.66 us  [swap_traces(): cross = lax.ppermute(cross, 'plane', partner)]
    ppermute x3 -> x4, waiting for transfers between devices: 0.45 us -> 2.02 us  [swap_traces(): cross = lax.ppermute(cross, 'plane', partner)]
    all_to_all x1, blocking collectives: 12.2 us -> 13.5 us  [on_device(): load = lax.all_to_all(sent, 'span', 0, 0, tiled=True)]
    ppermute x3 -> x4, starting transfers between devices: 7.54 us -> 8.47 us  [swap_traces(): chip = lax.ppermute(chip, 'plane', [(p, p ^ 1) for p in range(GRID)])]
    ppermute x3 -> x4, waiting for transfers between devices: 1.49 us -> 0.72 us  [swap_traces(): chip = lax.ppermute(chip, 'plane', [(p, p ^ 1) for p in range(GRID)])]
    pallas_call x12 -> x14, Pallas kernels: 13.4 us -> 13 us  [call(): pl.pallas_call(kernel, out_shape=[jax.ShapeDtypeStruct(s, jnp.float32) fo...]
  transfers between devices with their start and end apart: 7 -> 9, of which waited for: 5 -> 4; matrix products, arithmetic and copies ran while one was open for 0% -> 0% of each run, Pallas kernels for 5% -> 6%
where the time goes in v5:
time: 77 us; the launch traced here: 76.7 us
  blocking collectives  31.4 us (41%)
  starting transfers between devices  23.9 us (31%)
  Pallas kernels  13 us (17%)
  waiting for transfers between devices  8.36 us (11%)
    all_to_all x1, blocking collectives, on_device(): modal = lax.all_to_all(packed, 'span', 0, 0, tiled=True)  17.9 us
    all_to_all x1, blocking collectives, on_device(): load = lax.all_to_all(sent, 'span', 0, 0, tiled=True)  13.5 us
    pallas_call x14, Pallas kernels, call(): pl.pallas_call(kernel, out_shape=[jax.ShapeDtypeStruct(s, jnp.float32) fo...  13 us
    all_to_all x1, starting transfers between devices, on_device(): sums = lax.all_to_all(sums, 'plane', 0, 0, tiled=True)  8.74 us
    ppermute x4, starting transfers between devices, swap_traces(): chip = lax.ppermute(chip, 'plane', [(p, p ^ 1) for p in range(GRID)])  8.47 us
    ppermute x4, starting transfers between devices, swap_traces(): cross = lax.ppermute(cross, 'plane', partner)  6.66 us
    all_to_all x1, waiting for transfers between devices, on_device(): sums = lax.all_to_all(sums, 'plane', 0, 0, tiled=True)  5.62 us
    ppermute x4, waiting for transfers between devices, swap_traces(): cross = lax.ppermute(cross, 'plane', partner)  2.02 us
  transfers between devices with their start and end apart: 9, of which 4 were waited for; matrix products, arithmetic and copies ran while one was open for 0% of the time, Pallas kernels for 6%

profile of v5, /device:TPU:1, one launch (start us, length us, event | category | flops | bytes accessed | tf_op | source)
XLA Modules:
  0.0 76.7 jit_solution(10374343629142075924)
XLA Ops:
  0.0 2.5 %shard_map.37 = f32[16,32,256]{2,1,0:T(8,128)S(1)} custom-call(f32[5,32,640]{2,1,0:T(8,128)} %bitcast.2), custom_call_target="tpu_custom_call" | custom-call | tf_op jit(solution)/shard_map/pallas_call | solution.py:556
  2.5 17.9 %all_to_all.15.modal_ref = f32[16,32,256]{2,1,0:T(8,128)S(1)} all-to-all(f32[16,32,256]{2,1,0:T(8,128)S(1)} %shard_map.37), channel_id=1, replica_groups=mesh['span'=16,'plane'=16] {'span'}, dimensions={0} | all-to-all | bytes 1048576 | tf_op jit(solution)/shard_map/all_to_all | solution.py:585
  20.6 1.5 %shard_map.39 = (f32[200,768]{1,0:T(8,128)S(1)}, f32[200,768]{1,0:T(8,128)S(1)}, f32[40,768]{1,0:T(8,128)S(1)}, f32[40,768]{1,0:T(8,128)S(1)}) custom-call(f32[2,256,256]{2,1,0:T(8,128)S(1)} %get-tuple-element.25.nodal_ref, bf16[2,2,256,384]{3,2,1,0:T(8,128)(2,1)S(1)} %copy-done), custom_call_target="tpu_custom_call" | custom-call | tf_op jit(solution)/shard_map/pallas_call | solution.py:556
  22.1 3.7 %collective-permute-start.2 = (f32[40,768]{1,0:T(8,128)S(1)}, f32[40,768]{1,0:T(8,128)S(1)}, u32[]{:S(2)}, u32[]{:S(2)}) collective-permute-start(f32[40,768]{1,0:T(8,128)S(1)} %get-tuple-element.33), channel_id=1, source_target_pairs={{0,15},{1,2},{2,1},{3,4},{4,3},{5,6},{6,5},{7,8},{8,7},{9,10},{10,... | collective-permute-start | bytes 368648 | tf_op jit(solution)/shard_map/ppermute | solution.py:569
  25.8 2.4 %collective-permute-start.3 = (f32[40,768]{1,0:T(8,128)S(1)}, f32[40,768]{1,0:T(8,128)S(1)}, u32[]{:S(2)}, u32[]{:S(2)}) collective-permute-start(f32[40,768]{1,0:T(8,128)S(1)} %get-tuple-element.34), channel_id=1, source_target_pairs={{0,1},{1,0},{2,3},{3,2},{4,5},{5,4},{6,7},{7,6},{8,9},{9,8},{10,11... | collective-permute-start | bytes 368648 | tf_op jit(solution)/shard_map/ppermute | solution.py:570
  28.2 2.2 %collective-permute-start.1 = (f32[2,40,256]{2,1,0:T(8,128)S(1)}, f32[2,40,256]{2,1,0:T(8,128)S(1)}, u32[]{:S(2)}, u32[]{:S(2)}) collective-permute-start(f32[2,40,256]{2,1,0:T(8,128)S(1)} %get-tuple-element.29), channel_id=1, source_target_pairs={{0,1},{1,0},{2,3},{3,2},{4,5},{5,4},{6,7},{7,6},{8,9},{9,8},{10,11... | collective-permute-start | bytes 245768 | tf_op jit(solution)/shard_map/ppermute | solution.py:570
  30.3 1.1 %shard_map.40.inside_ref = f32[2,256,256]{2,1,0:T(8,128)S(1)} custom-call(f32[16,32,256]{2,1,0:T(8,128)S(1)} %all_to_all.15.modal_ref, f32[200,768]{1,0:T(8,128)S(1)} %get-tuple-element.26.field_ref, f32[200,768]{1,0:T(8,128)S(1)} %get-tuple-element.27.rhs_ref, bf16[2,2,256,384]{3,2,1,0:T(8,128)(2,1)S(1)} %copy-done), custom_call_target="tpu_custom_call" | custom-call | tf_op jit(solution)/shard_map/pallas_call | solution.py:556
  31.4 0.9 %collective-permute-done.cross_ref = f32[2,40,256]{2,1,0:T(8,128)S(1)} collective-permute-done((f32[2,40,256]{2,1,0:T(8,128)S(1)}, f32[2,40,256]{2,1,0:T(8,128)S(1)}, u32[]{:S(2)}, u32[]{:S(2)}) %collective-permute-start) | collective-permute-done | bytes 81952 | tf_op jit(solution)/shard_map/ppermute | solution.py:569
  32.3 1.0 %shard_map.41 = (f32[80,768]{1,0:T(8,128)S(1)}, f32[80,768]{1,0:T(8,128)S(1)}, f32[2,256,128]{2,1,0:T(8,128)S(1)}) custom-call(s32[128]{0:T(128)S(1)} %copy-done.1, f32[200,768]{1,0:T(8,128)S(1)} %get-tuple-element.26.field_ref, f32[2,40,256]{2,1,0:T(8,128)S(1)} %collective-permute-done.cross_ref, f32[2,40,256]{2,1,0:T(8,128)S(1)} %collective-permute-done.1.chip_ref, ...), custom_call_target="tpu_custom_call" | custom-call | tf_op jit(solution)/shard_map/pallas_call | solution.py:556
  33.4 0.8 shard_map.42
  34.1 13.5 %all_to_all.16.modal_ref = f32[16,32,256]{2,1,0:T(8,128)S(1)} all-to-all(f32[16,32,256]{2,1,0:T(8,128)S(1)} %shard_map.42), channel_id=1, replica_groups=mesh['span'=16,'plane'=16] {'span'}, dimensions={0} | all-to-all | bytes 1048576 | tf_op jit(solution)/shard_map/all_to_all | solution.py:601
  47.6 0.9 %shard_map.43 = (f32[25,32,128]{2,1,0:T(8,128)S(1)}, f32[25,32,128]{2,1,0:T(8,128)S(1)}, f32[5,32,128]{2,1,0:T(8,128)S(1)}, f32[5,32,128]{2,1,0:T(8,128)S(1)}) custom-call(f32[16,32,256]{2,1,0:T(8,128)S(1)} %all_to_all.16.modal_ref), custom_call_target="tpu_custom_call" | custom-call | tf_op jit(solution)/shard_map/pallas_call | solution.py:556
  48.5 1.5 %collective-permute-start.4 = (f32[5,32,128]{2,1,0:T(8,128)S(1)}, f32[5,32,128]{2,1,0:T(8,128)S(1)}, u32[]{:S(2)}, u32[]{:S(2)}) collective-permute-start(f32[5,32,128]{2,1,0:T(8,128)S(1)} %get-tuple-element.36), channel_id=1, source_target_pairs={{0,15},{1,2},{2,1},{3,4},{4,3},{5,6},{6,5},{7,8},{8,7},{9,10},{10,... | collective-permute-start | bytes 245768 | tf_op jit(solution)/shard_map/ppermute | solution.py:569
  50.0 1.4 %collective-permute-start.5 = (f32[5,32,128]{2,1,0:T(8,128)S(1)}, f32[5,32,128]{2,1,0:T(8,128)S(1)}, u32[]{:S(2)}, u32[]{:S(2)}) collective-permute-start(f32[5,32,128]{2,1,0:T(8,128)S(1)} %get-tuple-element.37), channel_id=1, source_target_pairs={{0,1},{1,0},{2,3},{3,2},{4,5},{5,4},{6,7},{7,6},{8,9},{9,8},{10,11... | collective-permute-start | bytes 245768 | tf_op jit(solution)/shard_map/ppermute | solution.py:570
  51.4 1.1 %collective-permute-done.4.cross_in_ref = f32[5,32,128]{2,1,0:T(8,128)S(1)} collective-permute-done((f32[5,32,128]{2,1,0:T(8,128)S(1)}, f32[5,32,128]{2,1,0:T(8,128)S(1)}, u32[]{:S(2)}, u32[]{:S(2)}) %collective-permute-start.4) | collective-permute-done | bytes 81952 | tf_op jit(solution)/shard_map/ppermute | solution.py:569
  52.9 1.5 %collective-permute-start.6 = (f32[5,32,128]{2,1,0:T(8,128)S(1)}, f32[5,32,128]{2,1,0:T(8,128)S(1)}, u32[]{:S(2)}, u32[]{:S(2)}) collective-permute-start(f32[5,32,128]{2,1,0:T(8,128)S(1)} %get-tuple-element.40), channel_id=1, source_target_pairs={{0,15},{1,2},{2,1},{3,4},{4,3},{5,6},{6,5},{7,8},{8,7},{9,10},{10,... | collective-permute-start | bytes 245768 | tf_op jit(solution)/shard_map/ppermute | solution.py:569
  54.4 2.6 %collective-permute-start.7 = (f32[5,32,128]{2,1,0:T(8,128)S(1)}, f32[5,32,128]{2,1,0:T(8,128)S(1)}, u32[]{:S(2)}, u32[]{:S(2)}) collective-permute-start(f32[5,32,128]{2,1,0:T(8,128)S(1)} %get-tuple-element.41), channel_id=1, source_target_pairs={{0,1},{1,0},{2,3},{3,2},{4,5},{5,4},{6,7},{7,6},{8,9},{9,8},{10,11... | collective-permute-start | bytes 245768 | tf_op jit(solution)/shard_map/ppermute | solution.py:570
  57.9 1.2 %shard_map.46 = (f32[25,32,128]{2,1,0:T(8,128)S(1)}, f32[16,8,128]{2,1,0:T(8,128)}) custom-call(f32[25,32,128]{2,1,0:T(8,128)S(1)} %get-tuple-element.39.joined_ref, f32[5,32,128]{2,1,0:T(8,128)S(1)} %collective-permute-done.6.cross_in_ref, f32[5,32,128]{2,1,0:T(8,128)S(1)} %collective-permute-done.7.chip_in_ref, ...), custom_call_target="tpu_custom_call" | custom-call | tf_op jit(solution)/shard_map/pallas_call | solution.py:556
  59.1 8.7 %all-to-all-start.2 = ((f32[16,8,128]{2,1,0:T(8,128)}), f32[16,8,128]{2,1,0:T(8,128)S(1)}, u32[]{:S(2)}, u32[]{:S(2)}) async-start(f32[16,8,128]{2,1,0:T(8,128)} %get-tuple-element.43), calls=%async_computation.2 | async-start | bytes 131072 | tf_op jit(solution)/shard_map/all_to_all | solution.py:614
  67.9 0.7 shard_map.47.first_ref
  68.6 0.7 shard_map.48.second_ref
  69.3 0.7 shard_map.49.third_ref
  70.0 5.6 %all-to-all-done.2.sums_ref = f32[16,8,128]{2,1,0:T(8,128)S(1)} async-done(((f32[16,8,128]{2,1,0:T(8,128)}), f32[16,8,128]{2,1,0:T(8,128)S(1)}, u32[]{:S(2)}, u32[]{:S(2)}) %all-to-all-start.2) | async-done | bytes 65568 | tf_op jit(solution)/shard_map/all_to_all | solution.py:614
  75.6 1.1 %shard_map.50 = f32[5,32,640]{2,1,0:T(8,128)} custom-call(f32[16,8,128]{2,1,0:T(8,128)S(1)} %all-to-all-done.2.sums_ref, f32[5,32,640]{2,1,0:T(8,128)S(1)} %shard_map.47.first_ref, f32[5,32,640]{2,1,0:T(8,128)S(1)} %shard_map.48.second_ref, f32[5,32,640]{2,1,0:T(8,128)S(1)} %shard_map.49.third_ref), custom_call_target="tpu_custom_call" | custom-call | tf_op jit(solution)/shard_map/pallas_call | solution.py:556
  (14 shorter events, 1.6 us)
Async XLA Ops:
  2.5 18.1 %copy-start = (bf16[2,2,256,384]{3,2,1,0:T(8,128)(2,1)S(1)}, bf16[2,2,256,384]{3,2,1,0:T(8,128)(2,1)}, u32[]{:S(2)}) copy-start(bf16[2,2,256,384]{3,2,1,0:T(8,128)(2,1)} %constant.2.clone.table_ref) | copy-start | bytes 2359300
  22.1 11.2 %collective-permute-start.2 = (f32[40,768]{1,0:T(8,128)S(1)}, f32[40,768]{1,0:T(8,128)S(1)}, u32[]{:S(2)}, u32[]{:S(2)}) collective-permute-start(f32[40,768]{1,0:T(8,128)S(1)} %get-tuple-element.33), channel_id=1, source_target_pairs={{0,15},{1,2},{2,1},{3,4},{4,3},{5,6},{6,5},{7,8},{8,7},{9,10},{10,... | collective-permute-start | bytes 368648 | tf_op jit(solution)/shard_map/ppermute | solution.py:569
  25.8 7.6 %collective-permute-start.3 = (f32[40,768]{1,0:T(8,128)S(1)}, f32[40,768]{1,0:T(8,128)S(1)}, u32[]{:S(2)}, u32[]{:S(2)}) collective-permute-start(f32[40,768]{1,0:T(8,128)S(1)} %get-tuple-element.34), channel_id=1, source_target_pairs={{0,1},{1,0},{2,3},{3,2},{4,5},{5,4},{6,7},{7,6},{8,9},{9,8},{10,11... | collective-permute-start | bytes 368648 | tf_op jit(solution)/shard_map/ppermute | solution.py:570
  28.2 4.2 %collective-permute-start = (f32[2,40,256]{2,1,0:T(8,128)S(1)}, f32[2,40,256]{2,1,0:T(8,128)S(1)}, u32[]{:S(2)}, u32[]{:S(2)}) collective-permute-start(f32[2,40,256]{2,1,0:T(8,128)S(1)} %get-tuple-element.28), channel_id=1, source_target_pairs={{0,15},{1,2},{2,1},{3,4},{4,3},{5,6},{6,5},{7,8},{8,7},{9,10},{10,... | collective-permute-start | bytes 245768 | tf_op jit(solution)/shard_map/ppermute | solution.py:569
  28.2 4.2 %collective-permute-start.1 = (f32[2,40,256]{2,1,0:T(8,128)S(1)}, f32[2,40,256]{2,1,0:T(8,128)S(1)}, u32[]{:S(2)}, u32[]{:S(2)}) collective-permute-start(f32[2,40,256]{2,1,0:T(8,128)S(1)} %get-tuple-element.29), channel_id=1, source_target_pairs={{0,1},{1,0},{2,3},{3,2},{4,5},{5,4},{6,7},{7,6},{8,9},{9,8},{10,11... | collective-permute-start | bytes 245768 | tf_op jit(solution)/shard_map/ppermute | solution.py:570
  30.3 2.0 %copy-start.1 = (s32[128]{0:T(128)S(1)}, s32[128]{0:T(128)}, u32[]{:S(2)}) copy-start(s32[128]{0:T(128)} %tag_ref.1) | copy-start | bytes 1540
  48.5 4.0 %collective-permute-start.4 = (f32[5,32,128]{2,1,0:T(8,128)S(1)}, f32[5,32,128]{2,1,0:T(8,128)S(1)}, u32[]{:S(2)}, u32[]{:S(2)}) collective-permute-start(f32[5,32,128]{2,1,0:T(8,128)S(1)} %get-tuple-element.36), channel_id=1, source_target_pairs={{0,15},{1,2},{2,1},{3,4},{4,3},{5,6},{6,5},{7,8},{8,7},{9,10},{10,... | collective-permute-start | bytes 245768 | tf_op jit(solution)/shard_map/ppermute | solution.py:569
  50.0 2.5 %collective-permute-start.5 = (f32[5,32,128]{2,1,0:T(8,128)S(1)}, f32[5,32,128]{2,1,0:T(8,128)S(1)}, u32[]{:S(2)}, u32[]{:S(2)}) collective-permute-start(f32[5,32,128]{2,1,0:T(8,128)S(1)} %get-tuple-element.37), channel_id=1, source_target_pairs={{0,1},{1,0},{2,3},{3,2},{4,5},{5,4},{6,7},{7,6},{8,9},{9,8},{10,11... | collective-permute-start | bytes 245768 | tf_op jit(solution)/shard_map/ppermute | solution.py:570
  52.9 4.3 %collective-permute-start.6 = (f32[5,32,128]{2,1,0:T(8,128)S(1)}, f32[5,32,128]{2,1,0:T(8,128)S(1)}, u32[]{:S(2)}, u32[]{:S(2)}) collective-permute-start(f32[5,32,128]{2,1,0:T(8,128)S(1)} %get-tuple-element.40), channel_id=1, source_target_pairs={{0,15},{1,2},{2,1},{3,4},{4,3},{5,6},{6,5},{7,8},{8,7},{9,10},{10,... | collective-permute-start | bytes 245768 | tf_op jit(solution)/shard_map/ppermute | solution.py:569
  54.4 3.5 %collective-permute-start.7 = (f32[5,32,128]{2,1,0:T(8,128)S(1)}, f32[5,32,128]{2,1,0:T(8,128)S(1)}, u32[]{:S(2)}, u32[]{:S(2)}) collective-permute-start(f32[5,32,128]{2,1,0:T(8,128)S(1)} %get-tuple-element.41), channel_id=1, source_target_pairs={{0,1},{1,0},{2,3},{3,2},{4,5},{5,4},{6,7},{7,6},{8,9},{9,8},{10,11... | collective-permute-start | bytes 245768 | tf_op jit(solution)/shard_map/ppermute | solution.py:570
  59.1 16.5 %all-to-all-start.2 = ((f32[16,8,128]{2,1,0:T(8,128)}), f32[16,8,128]{2,1,0:T(8,128)S(1)}, u32[]{:S(2)}, u32[]{:S(2)}) async-start(f32[16,8,128]{2,1,0:T(8,128)} %get-tuple-element.43), calls=%async_computation.2 | async-start | bytes 131072 | tf_op jit(solution)/shard_map/all_to_all | solution.py:614

commit v6 on v5

--- a/solution.py
+++ b/solution.py
@@ -75,18 +75,6 @@
 
 def lanes_of(values, index):
     return jnp.take_along_axis(values, index, axis=1)
-
-
-def split_columns(tiles):
-    lane = lax.broadcasted_iota(jnp.int32, tiles[0].shape, 1)
-    out = []
-    for i in range(5):
-        column = 5 * lane + i
-        picked = lanes_of(tiles[0], column & 127)
-        for t in range(1, 5):
-            picked = jnp.where(column >= 128 * t, lanes_of(tiles[t], column & 127), picked)
-        out.append(picked)
-    return out
 
 
 def merge_columns(tiles):
@@ -122,35 +110,87 @@
     return values
 
 
-def pack_kernel(state_hbm, out_ref, chunk_ref, state_ref, arrived):
-    copies = [
-        pltpu.make_async_copy(state_hbm.at[j], state_ref.at[j], arrived.at[j]) for j in range(5)
-    ]
-    for copy in copies:
-        copy.start()
-    for j in range(5):
-        copies[j].wait()
-        tiles = split_columns([state_ref[j, :, 128 * t : 128 * t + 128] for t in range(5)])
-        for i in range(5):
-            first = 32 * (5 * j + i)
-            chunk_ref[first : first + 32, :] = tiles[i]
+def column_order():
+    column = lax.broadcasted_iota(jnp.int32, (640, 128), 0)
+    element = lax.broadcasted_iota(jnp.int32, (640, 128), 1)
+    tiles = [jnp.where(column == 5 * element + i, 1.0, 0.0).astype(jnp.bfloat16) for i in range(5)]
+    return jnp.concatenate(tiles, axis=1)
+
+
+def pack_rows(out_ref, d, whole, rest, count):
+    out_ref[d, 0:32, :] = whole
+    lane = lax.broadcasted_iota(jnp.int32, (8, 128), 1)
+    free = 16 - count
+    for g in range(3):
+        tile = rest[8 * g : 8 * g + 8]
+        if g * free < count:
+            shift = 8 * (count - g * free)
+            tile = jnp.where(lane < 8 * count, tile, pltpu.roll(rest[24:32], shift % 128, 1))
+        out_ref[d, 32 + 8 * g : 40 + 8 * g, :] = tile
+
+
+def unpack_last(tiles, count):
+    lane = lax.broadcasted_iota(jnp.int32, (8, 128), 1)
+    free = 16 - count
+    last = pltpu.roll(tiles[0], 128 - 8 * count, 1)
+    for g in range(1, 3):
+        if g * free < count:
+            shift = 8 * (count - g * free)
+            last = jnp.where(lane < 8 * g * free, last, pltpu.roll(tiles[g], (128 - shift) % 128, 1))
+    return last
+
+
+def pack_kernel(state_hbm, out_ref, chunk_ref, state_ref, order_ref, arrived):
+    copy = pltpu.make_async_copy(state_hbm, state_ref, arrived)
+    copy.start()
+    order_ref[...] = column_order()
+    copy.wait()
+    stacked = jnp.concatenate([state_ref[j] for j in range(5)], axis=0)
+    order = order_ref[...]
+    contract = ((1,), (0,))
+    high, low = halves(stacked)
+    nodes = dot(low, order, contract) + dot(high, order, contract)
+    for i in range(5):
+        chunk_ref[160 * i : 160 * i + 160, :] = nodes[:, 128 * i : 128 * i + 128]
     chunk = [
         jnp.concatenate(
-            [chunk_ref[pl.ds(32 * n + t, 8, stride=4), :] for t in range(4)], axis=0
+            [chunk_ref[pl.ds(160 * i + 32 * j + t, 8, stride=4), :] for t in range(4)], axis=0
         )
-        for n in range(25)
+        for j in range(5)
+        for i in range(5)
     ]
     lane = lax.broadcasted_iota(jnp.int32, (32, 128), 1) & 7
+    sides = [jnp.zeros((32, 128), jnp.float32), jnp.zeros((32, 128), jnp.float32)]
     for j in range(5):
-        left = pltpu.roll(chunk[j * 5 + 4], 1, 1)
-        right = pltpu.roll(chunk[j * 5], 127, 1)
-        chunk.append(jnp.where(lane == 0, left, jnp.where(lane == 7, right, 0.0)))
-    zero = jnp.zeros((32, 128), jnp.float32)
-    chunk = chunk + [zero, zero]
-    for half in range(2):
-        block = exchange_chunks(chunk[16 * half : 16 * half + 16])
-        for d in range(GRID):
-            out_ref[d, :, 128 * half : 128 * half + 128] = block[d]
+        at = j & 3
+        side = jnp.where(lane == at, pltpu.roll(chunk[j * 5 + 4], 1 + at, 1), sides[j // 4])
+        sides[j // 4] = jnp.where(lane == 7 - at, pltpu.roll(chunk[j * 5], 127 - at, 1), side)
+    chunk = chunk + sides
+    whole = exchange_chunks(chunk[:16])
+    rest = exchange_chunks(chunk[16:] + [jnp.zeros((32, 128), jnp.float32)] * 5)
+    for d in range(GRID):
+        pack_rows(out_ref, d, whole[d], rest[d], 11)
+
+
+def turn(modal_ref, cross_ref, chip_ref):
+    last = [
+        unpack_last([modal_ref[s, 32 + 8 * g : 40 + 8 * g, :] for g in range(3)], 11)
+        for s in range(GRID)
+    ]
+    nodal = []
+    for parity in range(2):
+        whole, rest = [], []
+        for t in range(2):
+            group = 2 * parity + t
+            for s in range(GRID):
+                whole.append(modal_ref[s, 8 * group : 8 * group + 8, :])
+                rest.append(
+                    last[s] if group == 3 else modal_ref[s, 32 + 8 * group : 40 + 8 * group, :]
+                )
+        turned = [jnp.concatenate(part, axis=0).T for part in (whole, rest)]
+        nodal.append(jnp.concatenate([turned[0], turned[1][0:88]], axis=0))
+        cross_ref[parity], chip_ref[parity] = to_partners(turned[0][0:40], turned[1][32:72])
+    return nodal
 
 
 def synthesize(nodal, table_ref):
@@ -170,24 +210,15 @@
     return mean - 0.5 * speed * (right - left)
 
 
-def turn_kernel(modal_ref, nodal_ref, cross_ref, chip_ref):
-    for parity in range(2):
-        rows = [
-            modal_ref[s, 16 * parity + 8 * t : 16 * parity + 8 * t + 8, :]
-            for t in range(2)
-            for s in range(GRID)
-        ]
-        nodal = jnp.concatenate(rows, axis=0).T
-        nodal_ref[parity] = nodal
-        cross_ref[parity], chip_ref[parity] = to_partners(nodal[0:40], nodal[160:200])
-
-
-def volume_kernel(nodal_ref, table_ref, field_ref, rhs_ref, cross_ref, chip_ref, side_ref):
-    nodal = [nodal_ref[0], nodal_ref[1]]
+def volume_kernel(
+    modal_ref, table_ref, field_ref, rhs_ref, modal_cross_ref, modal_chip_ref, cross_ref, chip_ref,
+    side_ref,
+):
+    nodal = turn(modal_ref, modal_cross_ref, modal_chip_ref)
     pair = synthesize(nodal, table_ref)
     for q in range(2):
         field_ref[:, HALF * q : HALF * q + HALF] = pair[q][0:200]
-        side_ref[:, HALF * q : HALF * q + HALF] = pair[q][200:240]
+        side_ref[:, HALF * q : HALF * q + HALF] = pair[q][200:216]
     row = lax.broadcasted_iota(jnp.int32, (8, 128), 0)
 
     def column(block, carry):
@@ -213,7 +244,10 @@
                 if own:
                     total = total + (5.0 * own) * square[n]
                 if i == 0 or i == 4:
-                    side = side_ref[8 * j : 8 * j + 8, lanes]
+                    at = j & 3
+                    side = side_ref[8 * (j // 4) : 8 * (j // 4) + 8, lanes]
+                    if at:
+                        side = pltpu.roll(side, 8 - at if i == 0 else at, 0)
                     if i == 0:
                         left = jnp.where(row == 0, side, pltpu.roll(f[j * 5 + 4], 1, 0))
                         total = total + 10.0 * two_point(left, f[n])
@@ -247,6 +281,10 @@
 
 
 def inside_kernel(modal_ref, field_ref, rhs_ref, table_ref, out_ref):
+    last = [
+        unpack_last([modal_ref[s, 32 + 8 * g : 40 + 8 * g, :] for g in range(3)], 11)
+        for s in range(GRID)
+    ]
     field = field_ref[...]
     flux = 0.5 * field * field
     rhs = rhs_ref[...]
@@ -260,9 +298,10 @@
             lanes = slice(128 * half, 128 * half + 128)
             change = tendency(parity, from_rhs[:, lanes], from_flux[:, lanes])
             for t in range(2):
-                first = 16 * parity + 8 * t
+                first = 16 * parity + 8 * t + 32 * half
                 modal = jnp.concatenate(
-                    [modal_ref[s, first : first + 8, lanes] for s in range(GRID)], axis=0
+                    last if first == 56 else [modal_ref[s, first : first + 8, :] for s in range(GRID)],
+                    axis=0,
                 )
                 out_ref[parity, 128 * t : 128 * t + 128, lanes] = modal + change[t]
 
@@ -313,20 +352,26 @@
     gap = jnp.zeros((48, PLANES), jnp.float32)
     planar = jnp.concatenate([rhs_lower, rhs_upper, gap, flux_ref[...], gap], axis=0)
     lane = lax.broadcasted_iota(jnp.int32, (128, 128), 1)
+    whole, rest = [], []
     for parity in range(2):
         projected = project(planar, parity, table_ref)
         change = tendency(parity, projected[:, 0:128], projected[:, 128:256])
         for t in range(2):
-            first = 16 * parity + 8 * t
             rows = slice(128 * t, 128 * t + 128)
             extra = change[t] + facing_ref[parity, rows, :]
             lower = jnp.where(lane < 40, extra, 0.0)
             upper = pltpu.roll(jnp.where(lane < 40, 0.0, extra), 120, 1)
-            for half, added in ((0, lower), (1, upper)):
-                lanes = slice(128 * half, 128 * half + 128)
-                total = inside_ref[parity, rows, lanes] + added
-                for s in range(GRID):
-                    out_ref[s, first : first + 8, lanes] = total[8 * s : 8 * s + 8]
+            whole.append(inside_ref[parity, rows, 0:128] + lower)
+            rest.append(inside_ref[parity, rows, 128:256] + upper)
+    for s in range(GRID):
+        part = slice(8 * s, 8 * s + 8)
+        pack_rows(
+            out_ref,
+            s,
+            jnp.concatenate([group[part] for group in whole], axis=0),
+            jnp.concatenate([group[part] for group in rest], axis=0),
+            9,
+        )
 
 
 def at_ends():
@@ -417,11 +462,12 @@
 
 def first_kernel(modal_ref, vector_ref, next_ref, cross_ref, chip_ref):
     shift, _ = mode_terms()
-    values = []
-    for half in range(2):
-        values += exchange_chunks(
-            [modal_ref[s, :, 128 * half : 128 * half + 128] for s in range(GRID)]
-        )
+    values = exchange_chunks([modal_ref[s, 0:32, :] for s in range(GRID)])
+    rest = []
+    for s in range(GRID):
+        tiles = [modal_ref[s, 32 + 8 * g : 40 + 8 * g, :] for g in range(3)]
+        rest.append(jnp.concatenate(tiles + [unpack_last(tiles, 9)], axis=0))
+    values += exchange_chunks(rest)
     values = [float(WEIGHTS[n // 5] * WEIGHTS[n % 5]) * values[n] for n in range(25)]
     vector = join_columns(values)
     for n in range(25):
@@ -574,22 +620,21 @@
 def on_device(state, wall_tag):
     table = wave_table()
     (packed,) = call(
-        pack_kernel, [(16, 32, 256)],
+        pack_kernel, [(16, 56, 128)],
         pltpu.with_memory_space_constraint(jnp.transpose(state, (1, 0, 2)), pltpu.HBM),
         anywhere=(0,),
         scratch=[
             pltpu.VMEM((800, 128), jnp.float32), pltpu.VMEM((5, 32, 640), jnp.float32),
-            pltpu.SemaphoreType.DMA((5,)),
+            pltpu.VMEM((640, 640), jnp.bfloat16), pltpu.SemaphoreType.DMA(()),
         ],
     )
     modal = lax.all_to_all(packed, "span", 0, 0, tiled=True)
     trace, rows = (2, 40, 256), (40, PLANES)
-    nodal, cross, chip = call(turn_kernel, [(2, 256, 256), trace, trace], modal)
-    modal_traces = swap_traces(cross, chip)
-    field, rhs, cross, chip = call(
-        volume_kernel, [(200, PLANES), (200, PLANES), rows, rows], nodal, table,
-        scratch=[pltpu.VMEM(rows, jnp.float32)],
-    )
+    field, rhs, *modal_traces, cross, chip = call(
+        volume_kernel, [(200, PLANES), (200, PLANES), trace, trace, rows, rows], modal,
+        table, scratch=[pltpu.VMEM((16, PLANES), jnp.float32)],
+    )
+    modal_traces = swap_traces(*modal_traces)
     rhs_traces = swap_traces(cross, chip)
     (inside,) = call(inside_kernel, [(2, 256, 256)], modal, field, rhs, table, covers=False)
     lift, flux, facing = call(
@@ -597,7 +642,7 @@
         *modal_traces, table, smem=(0,), scratch=[pltpu.VMEM((80, PLANES), jnp.float32)],
         covers=False,
     )
-    (sent,) = call(facing_kernel, [(16, 32, 256)], inside, lift, flux, facing, *rhs_traces, table)
+    (sent,) = call(facing_kernel, [(16, 56, 128)], inside, lift, flux, facing, *rhs_traces, table)
     load = lax.all_to_all(sent, "span", 0, 0, tiled=True)
     nodes, trace = (25, 32, 128), (5, 32, 128)
     first, joined, cross, chip = call(first_kernel, [nodes, nodes, trace, trace], load)

time: 77 us -> 75 us (0.974)
  blocking collectives: 31.4 us -> 28.9 us
  starting transfers between devices: 23.9 us -> 25 us
    all_to_all x1, blocking collectives: 13.5 us -> 11.9 us  [on_device(): load = lax.all_to_all(sent, 'span', 0, 0, tiled=True)]
    ppermute x4, starting transfers between devices: 6.66 us -> 7.64 us  [swap_traces(): cross = lax.ppermute(cross, 'plane', partner)]
    all_to_all x1, blocking collectives: 17.9 us -> 17 us  [on_device(): modal = lax.all_to_all(packed, 'span', 0, 0, tiled=True)]
    pallas_call x14 -> x13, Pallas kernels: 13 us -> 12.6 us  [call(): pl.pallas_call(kernel, out_shape=[jax.ShapeDtypeStruct(s, jnp.float32) fo...]
  transfers between devices with their start and end apart: 9 -> 9, of which waited for: 4 -> 5; matrix products, arithmetic and copies ran while one was open for 0% -> 0% of each run, Pallas kernels for 6% -> 6%
where the time goes in v6:
time: 75 us; the launch traced here: 74.8 us
  blocking collectives  28.9 us (39%)
  starting transfers between devices  25 us (33%)
  Pallas kernels  12.6 us (17%)
  waiting for transfers between devices  8.14 us (11%)
    all_to_all x1, blocking collectives, on_device(): modal = lax.all_to_all(packed, 'span', 0, 0, tiled=True)  17 us
    pallas_call x13, Pallas kernels, call(): pl.pallas_call(kernel, out_shape=[jax.ShapeDtypeStruct(s, jnp.float32) fo...  12.6 us
    all_to_all x1, blocking collectives, on_device(): load = lax.all_to_all(sent, 'span', 0, 0, tiled=True)  11.9 us
    ppermute x4, starting transfers between devices, swap_traces(): chip = lax.ppermute(chip, 'plane', [(p, p ^ 1) for p in range(GRID)])  8.74 us
    all_to_all x1, starting transfers between devices, on_device(): sums = lax.all_to_all(sums, 'plane', 0, 0, tiled=True)  8.61 us
    ppermute x4, starting transfers between devices, swap_traces(): cross = lax.ppermute(cross, 'plane', partner)  7.64 us
    all_to_all x1, waiting for transfers between devices, on_device(): sums = lax.all_to_all(sums, 'plane', 0, 0, tiled=True)  5.62 us
    ppermute x4, waiting for transfers between devices, swap_traces(): cross = lax.ppermute(cross, 'plane', partner)  1.51 us
  transfers between devices with their start and end apart: 9, of which 5 were waited for; matrix products, arithmetic and copies ran while one was open for 0% of the time, Pallas kernels for 6%

profile of v6, /device:TPU:1, one launch (start us, length us, event | category | flops | bytes accessed | tf_op | source)
XLA Modules:
  0.0 74.8 jit_solution(8068502479650080904)
XLA Ops:
  0.0 2.1 %shard_map.37 = f32[16,56,128]{2,1,0:T(8,128)S(1)} custom-call(f32[5,32,640]{2,1,0:T(8,128)} %bitcast.2), custom_call_target="tpu_custom_call" | custom-call | tf_op jit(solution)/shard_map/pallas_call | solution.py:602
  2.2 17.0 %all_to_all.15.modal_ref = f32[16,56,128]{2,1,0:T(8,128)S(1)} all-to-all(f32[16,56,128]{2,1,0:T(8,128)S(1)} %shard_map.37), channel_id=1, replica_groups=mesh['span'=16,'plane'=16] {'span'}, dimensions={0} | all-to-all | bytes 917504 | tf_op jit(solution)/shard_map/all_to_all | solution.py:631
  19.2 1.5 %shard_map.38 = (f32[200,768]{1,0:T(8,128)S(1)}, f32[200,768]{1,0:T(8,128)S(1)}, f32[2,40,256]{2,1,0:T(8,128)S(1)}, f32[2,40,256]{2,1,0:T(8,128)S(1)}, f32[40,768]{1,0:T(8,128)S(1)}, /*index=5*/f32[40,768]{1,0:T(8,128)S(1)}) custom-call(f32[16,56,128]{2,1,0:T(8,128)S(1)} %all_to_all.15.modal_ref, bf16[2,2,256,384]{3,2,1,0:T(8,128)(2,1)S(1)} %copy-done), custom_call_target="tpu_custom_call" | custom-call | tf_op jit(solution)/shard_map/pallas_call | solution.py:602
  20.7 3.7 %collective-permute-start.2 = (f32[40,768]{1,0:T(8,128)S(1)}, f32[40,768]{1,0:T(8,128)S(1)}, u32[]{:S(2)}, u32[]{:S(2)}) collective-permute-start(f32[40,768]{1,0:T(8,128)S(1)} %get-tuple-element.31), channel_id=1, source_target_pairs={{0,15},{1,2},{2,1},{3,4},{4,3},{5,6},{6,5},{7,8},{8,7},{9,10},{10,... | collective-permute-start | bytes 368648 | tf_op jit(solution)/shard_map/ppermute | solution.py:615
  24.4 2.3 %collective-permute-start.3 = (f32[40,768]{1,0:T(8,128)S(1)}, f32[40,768]{1,0:T(8,128)S(1)}, u32[]{:S(2)}, u32[]{:S(2)}) collective-permute-start(f32[40,768]{1,0:T(8,128)S(1)} %get-tuple-element.32), channel_id=1, source_target_pairs={{0,1},{1,0},{2,3},{3,2},{4,5},{5,4},{6,7},{7,6},{8,9},{9,8},{10,11... | collective-permute-start | bytes 368648 | tf_op jit(solution)/shard_map/ppermute | solution.py:616
  26.7 2.2 %collective-permute-start.1 = (f32[2,40,256]{2,1,0:T(8,128)S(1)}, f32[2,40,256]{2,1,0:T(8,128)S(1)}, u32[]{:S(2)}, u32[]{:S(2)}) collective-permute-start(f32[2,40,256]{2,1,0:T(8,128)S(1)} %get-tuple-element.27), channel_id=1, source_target_pairs={{0,1},{1,0},{2,3},{3,2},{4,5},{5,4},{6,7},{7,6},{8,9},{9,8},{10,11... | collective-permute-start | bytes 245768 | tf_op jit(solution)/shard_map/ppermute | solution.py:616
  29.0 1.1 %shard_map.39.inside_ref = f32[2,256,256]{2,1,0:T(8,128)S(1)} custom-call(f32[16,56,128]{2,1,0:T(8,128)S(1)} %all_to_all.15.modal_ref, f32[200,768]{1,0:T(8,128)S(1)} %get-tuple-element.24.field_ref, f32[200,768]{1,0:T(8,128)S(1)} %get-tuple-element.25.rhs_ref, bf16[2,2,256,384]{3,2,1,0:T(8,128)(2,1)S(1)} %copy-done), custom_call_target="tpu_custom_call" | custom-call | tf_op jit(solution)/shard_map/pallas_call | solution.py:602
  30.0 0.9 %collective-permute-done.cross_ref = f32[2,40,256]{2,1,0:T(8,128)S(1)} collective-permute-done((f32[2,40,256]{2,1,0:T(8,128)S(1)}, f32[2,40,256]{2,1,0:T(8,128)S(1)}, u32[]{:S(2)}, u32[]{:S(2)}) %collective-permute-start) | collective-permute-done | bytes 81952 | tf_op jit(solution)/shard_map/ppermute | solution.py:615
  30.9 1.0 %shard_map.40 = (f32[80,768]{1,0:T(8,128)S(1)}, f32[80,768]{1,0:T(8,128)S(1)}, f32[2,256,128]{2,1,0:T(8,128)S(1)}) custom-call(s32[128]{0:T(128)S(1)} %copy-done.1, f32[200,768]{1,0:T(8,128)S(1)} %get-tuple-element.24.field_ref, f32[2,40,256]{2,1,0:T(8,128)S(1)} %collective-permute-done.cross_ref, f32[2,40,256]{2,1,0:T(8,128)S(1)} %collective-permute-done.1.chip_ref, ...), custom_call_target="tpu_custom_call" | custom-call | tf_op jit(solution)/shard_map/pallas_call | solution.py:602
  31.9 0.8 %shard_map.41 = f32[16,56,128]{2,1,0:T(8,128)S(1)} custom-call(f32[2,256,256]{2,1,0:T(8,128)S(1)} %shard_map.39.inside_ref, f32[80,768]{1,0:T(8,128)S(1)} %get-tuple-element.28.lift_ref, f32[80,768]{1,0:T(8,128)S(1)} %get-tuple-element.29.flux_ref, f32[2,256,128]{2,1,0:T(8,128)S(1)} %get-tuple-element.30.facing_ref, ...), custom_call_target="tpu_custom_call" | custom-call | tf_op jit(solution)/shard_map/pallas_call | solution.py:602
  32.8 11.9 %all_to_all.16.modal_ref = f32[16,56,128]{2,1,0:T(8,128)S(1)} all-to-all(f32[16,56,128]{2,1,0:T(8,128)S(1)} %shard_map.41), channel_id=1, replica_groups=mesh['span'=16,'plane'=16] {'span'}, dimensions={0} | all-to-all | bytes 917504 | tf_op jit(solution)/shard_map/all_to_all | solution.py:646
  44.7 1.0 %shard_map.42 = (f32[25,32,128]{2,1,0:T(8,128)S(1)}, f32[25,32,128]{2,1,0:T(8,128)S(1)}, f32[5,32,128]{2,1,0:T(8,128)S(1)}, f32[5,32,128]{2,1,0:T(8,128)S(1)}) custom-call(f32[16,56,128]{2,1,0:T(8,128)S(1)} %all_to_all.16.modal_ref), custom_call_target="tpu_custom_call" | custom-call | tf_op jit(solution)/shard_map/pallas_call | solution.py:602
  45.7 2.4 %collective-permute-start.4 = (f32[5,32,128]{2,1,0:T(8,128)S(1)}, f32[5,32,128]{2,1,0:T(8,128)S(1)}, u32[]{:S(2)}, u32[]{:S(2)}) collective-permute-start(f32[5,32,128]{2,1,0:T(8,128)S(1)} %get-tuple-element.34), channel_id=1, source_target_pairs={{0,15},{1,2},{2,1},{3,4},{4,3},{5,6},{6,5},{7,8},{8,7},{9,10},{10,... | collective-permute-start | bytes 245768 | tf_op jit(solution)/shard_map/ppermute | solution.py:615
  48.1 1.5 %collective-permute-start.5 = (f32[5,32,128]{2,1,0:T(8,128)S(1)}, f32[5,32,128]{2,1,0:T(8,128)S(1)}, u32[]{:S(2)}, u32[]{:S(2)}) collective-permute-start(f32[5,32,128]{2,1,0:T(8,128)S(1)} %get-tuple-element.35), channel_id=1, source_target_pairs={{0,1},{1,0},{2,3},{3,2},{4,5},{5,4},{6,7},{7,6},{8,9},{9,8},{10,11... | collective-permute-start | bytes 245768 | tf_op jit(solution)/shard_map/ppermute | solution.py:616
  50.9 1.5 %collective-permute-start.6 = (f32[5,32,128]{2,1,0:T(8,128)S(1)}, f32[5,32,128]{2,1,0:T(8,128)S(1)}, u32[]{:S(2)}, u32[]{:S(2)}) collective-permute-start(f32[5,32,128]{2,1,0:T(8,128)S(1)} %get-tuple-element.38), channel_id=1, source_target_pairs={{0,15},{1,2},{2,1},{3,4},{4,3},{5,6},{6,5},{7,8},{8,7},{9,10},{10,... | collective-permute-start | bytes 245768 | tf_op jit(solution)/shard_map/ppermute | solution.py:615
  52.4 2.7 %collective-permute-start.7 = (f32[5,32,128]{2,1,0:T(8,128)S(1)}, f32[5,32,128]{2,1,0:T(8,128)S(1)}, u32[]{:S(2)}, u32[]{:S(2)}) collective-permute-start(f32[5,32,128]{2,1,0:T(8,128)S(1)} %get-tuple-element.39), channel_id=1, source_target_pairs={{0,1},{1,0},{2,3},{3,2},{4,5},{5,4},{6,7},{7,6},{8,9},{9,8},{10,11... | collective-permute-start | bytes 245768 | tf_op jit(solution)/shard_map/ppermute | solution.py:616
  55.3 0.7 collective-permute-done.7.chip_in_ref
  56.1 1.2 %shard_map.45 = (f32[25,32,128]{2,1,0:T(8,128)S(1)}, f32[16,8,128]{2,1,0:T(8,128)}) custom-call(f32[25,32,128]{2,1,0:T(8,128)S(1)} %get-tuple-element.37.joined_ref, f32[5,32,128]{2,1,0:T(8,128)S(1)} %collective-permute-done.6.cross_in_ref, f32[5,32,128]{2,1,0:T(8,128)S(1)} %collective-permute-done.7.chip_in_ref, ...), custom_call_target="tpu_custom_call" | custom-call | tf_op jit(solution)/shard_map/pallas_call | solution.py:602
  57.3 8.6 %all-to-all-start.2 = ((f32[16,8,128]{2,1,0:T(8,128)}), f32[16,8,128]{2,1,0:T(8,128)S(1)}, u32[]{:S(2)}, u32[]{:S(2)}) async-start(f32[16,8,128]{2,1,0:T(8,128)} %get-tuple-element.41), calls=%async_computation.2 | async-start | bytes 131072 | tf_op jit(solution)/shard_map/all_to_all | solution.py:659
  65.9 0.7 shard_map.46.first_ref
  66.6 0.7 shard_map.47.second_ref
  67.3 0.7 shard_map.48.third_ref
  68.1 5.6 %all-to-all-done.2.sums_ref = f32[16,8,128]{2,1,0:T(8,128)S(1)} async-done(((f32[16,8,128]{2,1,0:T(8,128)}), f32[16,8,128]{2,1,0:T(8,128)S(1)}, u32[]{:S(2)}, u32[]{:S(2)}) %all-to-all-start.2) | async-done | bytes 65568 | tf_op jit(solution)/shard_map/all_to_all | solution.py:659
  73.7 1.1 %shard_map.49 = f32[5,32,640]{2,1,0:T(8,128)} custom-call(f32[16,8,128]{2,1,0:T(8,128)S(1)} %all-to-all-done.2.sums_ref, f32[5,32,640]{2,1,0:T(8,128)S(1)} %shard_map.46.first_ref, f32[5,32,640]{2,1,0:T(8,128)S(1)} %shard_map.47.second_ref, f32[5,32,640]{2,1,0:T(8,128)S(1)} %shard_map.48.third_ref), custom_call_target="tpu_custom_call" | custom-call | tf_op jit(solution)/shard_map/pallas_call | solution.py:602
  (13 shorter events, 1.6 us)
Async XLA Ops:
  0.0 19.2 %copy-start = (bf16[2,2,256,384]{3,2,1,0:T(8,128)(2,1)S(1)}, bf16[2,2,256,384]{3,2,1,0:T(8,128)(2,1)}, u32[]{:S(2)}) copy-start(bf16[2,2,256,384]{3,2,1,0:T(8,128)(2,1)} %constant.2.clone.table_ref) | copy-start | bytes 2359300
  20.7 11.2 %collective-permute-start.2 = (f32[40,768]{1,0:T(8,128)S(1)}, f32[40,768]{1,0:T(8,128)S(1)}, u32[]{:S(2)}, u32[]{:S(2)}) collective-permute-start(f32[40,768]{1,0:T(8,128)S(1)} %get-tuple-element.31), channel_id=1, source_target_pairs={{0,15},{1,2},{2,1},{3,4},{4,3},{5,6},{6,5},{7,8},{8,7},{9,10},{10,... | collective-permute-start | bytes 368648 | tf_op jit(solution)/shard_map/ppermute | solution.py:615
  24.4 7.5 %collective-permute-start.3 = (f32[40,768]{1,0:T(8,128)S(1)}, f32[40,768]{1,0:T(8,128)S(1)}, u32[]{:S(2)}, u32[]{:S(2)}) collective-permute-start(f32[40,768]{1,0:T(8,128)S(1)} %get-tuple-element.32), channel_id=1, source_target_pairs={{0,1},{1,0},{2,3},{3,2},{4,5},{5,4},{6,7},{7,6},{8,9},{9,8},{10,11... | collective-permute-start | bytes 368648 | tf_op jit(solution)/shard_map/ppermute | solution.py:616
  26.7 4.2 %collective-permute-start = (f32[2,40,256]{2,1,0:T(8,128)S(1)}, f32[2,40,256]{2,1,0:T(8,128)S(1)}, u32[]{:S(2)}, u32[]{:S(2)}) collective-permute-start(f32[2,40,256]{2,1,0:T(8,128)S(1)} %get-tuple-element.26), channel_id=1, source_target_pairs={{0,15},{1,2},{2,1},{3,4},{4,3},{5,6},{6,5},{7,8},{8,7},{9,10},{10,... | collective-permute-start | bytes 245768 | tf_op jit(solution)/shard_map/ppermute | solution.py:615
  26.7 4.2 %collective-permute-start.1 = (f32[2,40,256]{2,1,0:T(8,128)S(1)}, f32[2,40,256]{2,1,0:T(8,128)S(1)}, u32[]{:S(2)}, u32[]{:S(2)}) collective-permute-start(f32[2,40,256]{2,1,0:T(8,128)S(1)} %get-tuple-element.27), channel_id=1, source_target_pairs={{0,1},{1,0},{2,3},{3,2},{4,5},{5,4},{6,7},{7,6},{8,9},{9,8},{10,11... | collective-permute-start | bytes 245768 | tf_op jit(solution)/shard_map/ppermute | solution.py:616
  29.0 1.9 %copy-start.1 = (s32[128]{0:T(128)S(1)}, s32[128]{0:T(128)}, u32[]{:S(2)}) copy-start(s32[128]{0:T(128)} %tag_ref.1) | copy-start | bytes 1540
  45.7 4.5 %collective-permute-start.4 = (f32[5,32,128]{2,1,0:T(8,128)S(1)}, f32[5,32,128]{2,1,0:T(8,128)S(1)}, u32[]{:S(2)}, u32[]{:S(2)}) collective-permute-start(f32[5,32,128]{2,1,0:T(8,128)S(1)} %get-tuple-element.34), channel_id=1, source_target_pairs={{0,15},{1,2},{2,1},{3,4},{4,3},{5,6},{6,5},{7,8},{8,7},{9,10},{10,... | collective-permute-start | bytes 245768 | tf_op jit(solution)/shard_map/ppermute | solution.py:615
  48.1 2.4 %collective-permute-start.5 = (f32[5,32,128]{2,1,0:T(8,128)S(1)}, f32[5,32,128]{2,1,0:T(8,128)S(1)}, u32[]{:S(2)}, u32[]{:S(2)}) collective-permute-start(f32[5,32,128]{2,1,0:T(8,128)S(1)} %get-tuple-element.35), channel_id=1, source_target_pairs={{0,1},{1,0},{2,3},{3,2},{4,5},{5,4},{6,7},{7,6},{8,9},{9,8},{10,11... | collective-permute-start | bytes 245768 | tf_op jit(solution)/shard_map/ppermute | solution.py:616
  50.9 4.4 %collective-permute-start.6 = (f32[5,32,128]{2,1,0:T(8,128)S(1)}, f32[5,32,128]{2,1,0:T(8,128)S(1)}, u32[]{:S(2)}, u32[]{:S(2)}) collective-permute-start(f32[5,32,128]{2,1,0:T(8,128)S(1)} %get-tuple-element.38), channel_id=1, source_target_pairs={{0,15},{1,2},{2,1},{3,4},{4,3},{5,6},{6,5},{7,8},{8,7},{9,10},{10,... | collective-permute-start | bytes 245768 | tf_op jit(solution)/shard_map/ppermute | solution.py:615
  52.4 3.6 %collective-permute-start.7 = (f32[5,32,128]{2,1,0:T(8,128)S(1)}, f32[5,32,128]{2,1,0:T(8,128)S(1)}, u32[]{:S(2)}, u32[]{:S(2)}) collective-permute-start(f32[5,32,128]{2,1,0:T(8,128)S(1)} %get-tuple-element.39), channel_id=1, source_target_pairs={{0,1},{1,0},{2,3},{3,2},{4,5},{5,4},{6,7},{7,6},{8,9},{9,8},{10,11... | collective-permute-start | bytes 245768 | tf_op jit(solution)/shard_map/ppermute | solution.py:616
  57.3 16.4 %all-to-all-start.2 = ((f32[16,8,128]{2,1,0:T(8,128)}), f32[16,8,128]{2,1,0:T(8,128)S(1)}, u32[]{:S(2)}, u32[]{:S(2)}) async-start(f32[16,8,128]{2,1,0:T(8,128)} %get-tuple-element.41), calls=%async_computation.2 | async-start | bytes 131072 | tf_op jit(solution)/shard_map/all_to_all | solution.py:659

commit v7 on v6

--- a/solution.py
+++ b/solution.py
@@ -374,6 +374,25 @@
         )
 
 
+def energy(values, shift):
+    total = None
+    for j in range(5):
+        for i in range(5):
+            n = j * 5 + i
+            mass = float(WEIGHTS[j] * WEIGHTS[i])
+            diagonal = VISCOUS * float(WEIGHTS[j] * STIFFNESS[i][i] + WEIGHTS[i] * STIFFNESS[j][j])
+            value = (shift * mass + diagonal) * values[n]
+            for other in range(i + 1, 5):
+                weight = 2.0 * VISCOUS * float(WEIGHTS[j] * STIFFNESS[i][other])
+                value = value + weight * values[j * 5 + other]
+            for other in range(j + 1, 5):
+                weight = 2.0 * VISCOUS * float(WEIGHTS[i] * STIFFNESS[j][other])
+                value = value + weight * values[other * 5 + i]
+            term = value * values[n]
+            total = term if total is None else total + term
+    return total
+
+
 def at_ends():
     plane = lax.axis_index("plane")
     return plane == 0, plane == GRID - 1
@@ -421,17 +440,19 @@
     values = join_columns(values)
     for n in range(25):
         joined_ref[n] = values[n]
-    for i in range(5):
+    for i in range(4):
         cross_ref[i], chip_ref[i] = to_partners(values[i], values[20 + i])
 
 
 def assembled(joined_ref, cross_ref, chip_ref):
     values = [joined_ref[n] for n in range(25)]
     bottom, top = at_ends()
-    for i in range(5):
+    for i in range(4):
         below, above = from_partners(cross_ref[i], chip_ref[i])
         values[i] = values[i] + jnp.where(bottom, 0.0, below)
         values[20 + i] = values[20 + i] + jnp.where(top, 0.0, above)
+    values[4] = pltpu.roll(values[0], 127, 1)
+    values[24] = pltpu.roll(values[20], 127, 1)
     return values
 
 
@@ -493,14 +514,17 @@
     return packed
 
 
-def early_kernel(first_ref, second_ref, packed_ref):
+def early_kernel(first_ref, second_ref, joined_ref, packed_ref):
+    _, center = mode_terms()
     first = [first_ref[n] for n in range(25)]
     second = [second_ref[n] for n in range(25)]
-    moments = [
-        inner(first, first),
-        inner(first, second),
-        inner(second, second),
-    ]
+    square = inner(second, second)
+    product = None
+    for n in range(25):
+        term = second[n] * joined_ref[n]
+        term = term if 0 < n % 5 < 4 else 0.5 * term
+        product = term if product is None else product + term
+    moments = [inner(first, first), inner(first, second), square, product - center * square]
     packed_ref[...] = pack_moments(moments, 0, jnp.zeros((32, 128), jnp.float32))
 
 
@@ -515,12 +539,8 @@
     for n in range(25):
         vector_ref[n] = third[n]
     fourth = inner(third, third)
-    local = local_operator(third, shift)
-    fifth = -center * fourth
-    for n in range(25):
-        fifth = fifth + local[n] * third[n]
-    moments = [inner(second, third), fourth, fifth]
-    packed = pack_moments(moments, 3, packed_ref[...])
+    moments = [fourth, energy(third, shift) - center * fourth]
+    packed = pack_moments(moments, 4, packed_ref[...])
     for t in range(4):
         turn_ref[pl.ds(t, 8, stride=4), :] = packed[8 * t : 8 * t + 8]
     turned = turn_ref[...].T[0:8]
@@ -538,12 +558,16 @@
             out_ref[j, :, 128 * i : 128 * i + 128] = column_ref[first : first + 32, :]
 
 
+def tree(terms):
+    while len(terms) > 1:
+        terms = [sum(terms[n + 1 : n + 2], terms[n]) for n in range(0, len(terms), 2)]
+    return terms[0]
+
+
 def combine_kernel(
     sums_ref, first_ref, second_ref, third_ref, out_hbm, turn_ref, result_ref, sent
 ):
-    total = sums_ref[0]
-    for p in range(1, GRID):
-        total = total + sums_ref[p]
+    total = tree([sums_ref[p] for p in range(GRID)])
     moment = [total[n : n + 1] for n in range(6)]
     lane = lax.broadcasted_iota(jnp.int32, (1, 128), 1)
     mode_pair = 16 * lax.axis_index("span") + (lane >> 1)
@@ -551,12 +575,19 @@
     center = 0.2 * (1.0 + SPAN_STIFF * ratio * ratio) + 0.15
 
     def product(left, right):
-        terms = None
-        for a in range(len(left)):
-            for b in range(len(right)):
-                term = left[a] * right[b] * moment[a + b]
-                terms = term if terms is None else terms + term
-        return terms
+        return tree(
+            [
+                tree(
+                    [
+                        left[a] * right[power - a]
+                        for a in range(len(left))
+                        if 0 <= power - a < len(right)
+                    ]
+                )
+                * moment[power]
+                for power in range(len(left) + len(right) - 1)
+            ]
+        )
 
     def operator(c):
         shifted = [center * v for v in c] + [0.0]
@@ -612,8 +643,8 @@
 
 def swap_traces(cross, chip):
     partner = [(p, (p + 1) % GRID if p % 2 else (p - 1) % GRID) for p in range(GRID)]
+    chip = lax.ppermute(chip, "plane", [(p, p ^ 1) for p in range(GRID)])
     cross = lax.ppermute(cross, "plane", partner)
-    chip = lax.ppermute(chip, "plane", [(p, p ^ 1) for p in range(GRID)])
     return cross, chip
 
 
@@ -644,14 +675,14 @@
     )
     (sent,) = call(facing_kernel, [(16, 56, 128)], inside, lift, flux, facing, *rhs_traces, table)
     load = lax.all_to_all(sent, "span", 0, 0, tiled=True)
-    nodes, trace = (25, 32, 128), (5, 32, 128)
+    nodes, trace = (25, 32, 128), (4, 32, 128)
     first, joined, cross, chip = call(first_kernel, [nodes, nodes, trace, trace], load)
     cross, chip = swap_traces(cross, chip)
     second, joined, cross, chip = call(
         second_kernel, [nodes, nodes, trace, trace], joined, cross, chip, first
     )
     cross, chip = swap_traces(cross, chip)
-    (packed,) = call(early_kernel, [(32, 128)], first, second)
+    (packed,) = call(early_kernel, [(32, 128)], first, second, joined)
     third, sums = call(
         third_kernel, [nodes, (16, 8, 128)], joined, cross, chip, second, packed,
         scratch=[pltpu.VMEM((32, 128), jnp.float32)],

time: 75 us -> 74.5 us (level)
  no operation moved by 1% of the time
where the time goes in v7:
time: 74.5 us; the launch traced here: 74.2 us
  blocking collectives  28.9 us (39%)
  starting transfers between devices  24.7 us (33%)
  Pallas kernels  12.5 us (17%)
  waiting for transfers between devices  8.03 us (11%)
    all_to_all x1, blocking collectives, on_device(): modal = lax.all_to_all(packed, 'span', 0, 0, tiled=True)  17 us
    pallas_call x13, Pallas kernels, call(): pl.pallas_call(kernel, out_shape=[jax.ShapeDtypeStruct(s, jnp.float32) fo...  12.5 us
    all_to_all x1, blocking collectives, on_device(): load = lax.all_to_all(sent, 'span', 0, 0, tiled=True)  11.9 us
    ppermute x4, starting transfers between devices, swap_traces(): chip = lax.ppermute(chip, 'plane', [(p, p ^ 1) for p in range(GRID)])  8.58 us
    all_to_all x1, starting transfers between devices, on_device(): sums = lax.all_to_all(sums, 'plane', 0, 0, tiled=True)  8.46 us
    ppermute x4, starting transfers between devices, swap_traces(): cross = lax.ppermute(cross, 'plane', partner)  7.67 us
    all_to_all x1, waiting for transfers between devices, on_device(): sums = lax.all_to_all(sums, 'plane', 0, 0, tiled=True)  5.62 us
  transfers between devices with their start and end apart: 9, of which 5 were waited for; matrix products, arithmetic and copies ran while one was open for 0% of the time, Pallas kernels for 6%

profile of v7, /device:TPU:1, one launch (start us, length us, event | category | flops | bytes accessed | tf_op | source)
XLA Modules:
  0.0 74.2 jit_solution(3177579362605837502)
XLA Ops:
  0.0 2.1 %shard_map.37 = f32[16,56,128]{2,1,0:T(8,128)S(1)} custom-call(f32[5,32,640]{2,1,0:T(8,128)} %bitcast.2), custom_call_target="tpu_custom_call" | custom-call | tf_op jit(solution)/shard_map/pallas_call | solution.py:633
  2.2 17.0 %all_to_all.15.modal_ref = f32[16,56,128]{2,1,0:T(8,128)S(1)} all-to-all(f32[16,56,128]{2,1,0:T(8,128)S(1)} %shard_map.37), channel_id=1, replica_groups=mesh['span'=16,'plane'=16] {'span'}, dimensions={0} | all-to-all | bytes 917504 | tf_op jit(solution)/shard_map/all_to_all | solution.py:662
  19.2 1.5 %shard_map.38 = (f32[200,768]{1,0:T(8,128)S(1)}, f32[200,768]{1,0:T(8,128)S(1)}, f32[2,40,256]{2,1,0:T(8,128)S(1)}, f32[2,40,256]{2,1,0:T(8,128)S(1)}, f32[40,768]{1,0:T(8,128)S(1)}, /*index=5*/f32[40,768]{1,0:T(8,128)S(1)}) custom-call(f32[16,56,128]{2,1,0:T(8,128)S(1)} %all_to_all.15.modal_ref, bf16[2,2,256,384]{3,2,1,0:T(8,128)(2,1)S(1)} %copy-done), custom_call_target="tpu_custom_call" | custom-call | tf_op jit(solution)/shard_map/pallas_call | solution.py:633
  20.7 3.7 %collective-permute-start.2 = (f32[40,768]{1,0:T(8,128)S(1)}, f32[40,768]{1,0:T(8,128)S(1)}, u32[]{:S(2)}, u32[]{:S(2)}) collective-permute-start(f32[40,768]{1,0:T(8,128)S(1)} %get-tuple-element.31), channel_id=1, source_target_pairs={{0,15},{1,2},{2,1},{3,4},{4,3},{5,6},{6,5},{7,8},{8,7},{9,10},{10,... | collective-permute-start | bytes 368648 | tf_op jit(solution)/shard_map/ppermute | solution.py:647
  24.4 2.3 %collective-permute-start.3 = (f32[40,768]{1,0:T(8,128)S(1)}, f32[40,768]{1,0:T(8,128)S(1)}, u32[]{:S(2)}, u32[]{:S(2)}) collective-permute-start(f32[40,768]{1,0:T(8,128)S(1)} %get-tuple-element.32), channel_id=1, source_target_pairs={{0,1},{1,0},{2,3},{3,2},{4,5},{5,4},{6,7},{7,6},{8,9},{9,8},{10,11... | collective-permute-start | bytes 368648 | tf_op jit(solution)/shard_map/ppermute | solution.py:646
  26.7 2.2 %collective-permute-start.1 = (f32[2,40,256]{2,1,0:T(8,128)S(1)}, f32[2,40,256]{2,1,0:T(8,128)S(1)}, u32[]{:S(2)}, u32[]{:S(2)}) collective-permute-start(f32[2,40,256]{2,1,0:T(8,128)S(1)} %get-tuple-element.27), channel_id=1, source_target_pairs={{0,1},{1,0},{2,3},{3,2},{4,5},{5,4},{6,7},{7,6},{8,9},{9,8},{10,11... | collective-permute-start | bytes 245768 | tf_op jit(solution)/shard_map/ppermute | solution.py:646
  29.0 1.1 %shard_map.39.inside_ref = f32[2,256,256]{2,1,0:T(8,128)S(1)} custom-call(f32[16,56,128]{2,1,0:T(8,128)S(1)} %all_to_all.15.modal_ref, f32[200,768]{1,0:T(8,128)S(1)} %get-tuple-element.24.field_ref, f32[200,768]{1,0:T(8,128)S(1)} %get-tuple-element.25.rhs_ref, bf16[2,2,256,384]{3,2,1,0:T(8,128)(2,1)S(1)} %copy-done), custom_call_target="tpu_custom_call" | custom-call | tf_op jit(solution)/shard_map/pallas_call | solution.py:633
  30.0 0.9 %collective-permute-done.cross_ref = f32[2,40,256]{2,1,0:T(8,128)S(1)} collective-permute-done((f32[2,40,256]{2,1,0:T(8,128)S(1)}, f32[2,40,256]{2,1,0:T(8,128)S(1)}, u32[]{:S(2)}, u32[]{:S(2)}) %collective-permute-start) | collective-permute-done | bytes 81952 | tf_op jit(solution)/shard_map/ppermute | solution.py:647
  30.9 1.0 %shard_map.40 = (f32[80,768]{1,0:T(8,128)S(1)}, f32[80,768]{1,0:T(8,128)S(1)}, f32[2,256,128]{2,1,0:T(8,128)S(1)}) custom-call(s32[128]{0:T(128)S(1)} %copy-done.1, f32[200,768]{1,0:T(8,128)S(1)} %get-tuple-element.24.field_ref, f32[2,40,256]{2,1,0:T(8,128)S(1)} %collective-permute-done.cross_ref, f32[2,40,256]{2,1,0:T(8,128)S(1)} %collective-permute-done.1.chip_ref, ...), custom_call_target="tpu_custom_call" | custom-call | tf_op jit(solution)/shard_map/pallas_call | solution.py:633
  31.9 0.8 %shard_map.41 = f32[16,56,128]{2,1,0:T(8,128)S(1)} custom-call(f32[2,256,256]{2,1,0:T(8,128)S(1)} %shard_map.39.inside_ref, f32[80,768]{1,0:T(8,128)S(1)} %get-tuple-element.28.lift_ref, f32[80,768]{1,0:T(8,128)S(1)} %get-tuple-element.29.flux_ref, f32[2,256,128]{2,1,0:T(8,128)S(1)} %get-tuple-element.30.facing_ref, ...), custom_call_target="tpu_custom_call" | custom-call | tf_op jit(solution)/shard_map/pallas_call | solution.py:633
  32.8 11.9 %all_to_all.16.modal_ref = f32[16,56,128]{2,1,0:T(8,128)S(1)} all-to-all(f32[16,56,128]{2,1,0:T(8,128)S(1)} %shard_map.41), channel_id=1, replica_groups=mesh['span'=16,'plane'=16] {'span'}, dimensions={0} | all-to-all | bytes 917504 | tf_op jit(solution)/shard_map/all_to_all | solution.py:677
  44.7 1.0 %shard_map.42 = (f32[25,32,128]{2,1,0:T(8,128)S(1)}, f32[25,32,128]{2,1,0:T(8,128)S(1)}, f32[4,32,128]{2,1,0:T(8,128)S(1)}, f32[4,32,128]{2,1,0:T(8,128)S(1)}) custom-call(f32[16,56,128]{2,1,0:T(8,128)S(1)} %all_to_all.16.modal_ref), custom_call_target="tpu_custom_call" | custom-call | tf_op jit(solution)/shard_map/pallas_call | solution.py:633
  45.7 2.4 %collective-permute-start.4 = (f32[4,32,128]{2,1,0:T(8,128)S(1)}, f32[4,32,128]{2,1,0:T(8,128)S(1)}, u32[]{:S(2)}, u32[]{:S(2)}) collective-permute-start(f32[4,32,128]{2,1,0:T(8,128)S(1)} %get-tuple-element.34), channel_id=1, source_target_pairs={{0,15},{1,2},{2,1},{3,4},{4,3},{5,6},{6,5},{7,8},{8,7},{9,10},{10,... | collective-permute-start | bytes 196616 | tf_op jit(solution)/shard_map/ppermute | solution.py:647
  48.1 1.5 %collective-permute-start.5 = (f32[4,32,128]{2,1,0:T(8,128)S(1)}, f32[4,32,128]{2,1,0:T(8,128)S(1)}, u32[]{:S(2)}, u32[]{:S(2)}) collective-permute-start(f32[4,32,128]{2,1,0:T(8,128)S(1)} %get-tuple-element.35), channel_id=1, source_target_pairs={{0,1},{1,0},{2,3},{3,2},{4,5},{5,4},{6,7},{7,6},{8,9},{9,8},{10,11... | collective-permute-start | bytes 196616 | tf_op jit(solution)/shard_map/ppermute | solution.py:646
  50.9 1.5 %collective-permute-start.6 = (f32[4,32,128]{2,1,0:T(8,128)S(1)}, f32[4,32,128]{2,1,0:T(8,128)S(1)}, u32[]{:S(2)}, u32[]{:S(2)}) collective-permute-start(f32[4,32,128]{2,1,0:T(8,128)S(1)} %get-tuple-element.38), channel_id=1, source_target_pairs={{0,15},{1,2},{2,1},{3,4},{4,3},{5,6},{6,5},{7,8},{8,7},{9,10},{10,... | collective-permute-start | bytes 196616 | tf_op jit(solution)/shard_map/ppermute | solution.py:647
  52.4 2.5 %collective-permute-start.7 = (f32[4,32,128]{2,1,0:T(8,128)S(1)}, f32[4,32,128]{2,1,0:T(8,128)S(1)}, u32[]{:S(2)}, u32[]{:S(2)}) collective-permute-start(f32[4,32,128]{2,1,0:T(8,128)S(1)} %get-tuple-element.39), channel_id=1, source_target_pairs={{0,1},{1,0},{2,3},{3,2},{4,5},{5,4},{6,7},{7,6},{8,9},{9,8},{10,11... | collective-permute-start | bytes 196616 | tf_op jit(solution)/shard_map/ppermute | solution.py:646
  55.3 0.6 collective-permute-done.7.chip_in_ref
  55.9 1.1 %shard_map.45 = (f32[25,32,128]{2,1,0:T(8,128)S(1)}, f32[16,8,128]{2,1,0:T(8,128)}) custom-call(f32[25,32,128]{2,1,0:T(8,128)S(1)} %get-tuple-element.37.joined_ref, f32[4,32,128]{2,1,0:T(8,128)S(1)} %collective-permute-done.6.cross_in_ref, f32[4,32,128]{2,1,0:T(8,128)S(1)} %collective-permute-done.7.chip_in_ref, ...), custom_call_target="tpu_custom_call" | custom-call | tf_op jit(solution)/shard_map/pallas_call | solution.py:633
  56.9 8.5 %all-to-all-start.2 = ((f32[16,8,128]{2,1,0:T(8,128)}), f32[16,8,128]{2,1,0:T(8,128)S(1)}, u32[]{:S(2)}, u32[]{:S(2)}) async-start(f32[16,8,128]{2,1,0:T(8,128)} %get-tuple-element.41), calls=%async_computation.2 | async-start | bytes 131072 | tf_op jit(solution)/shard_map/all_to_all | solution.py:690
  65.4 0.7 shard_map.46.first_ref
  66.1 0.7 shard_map.47.second_ref
  66.8 0.7 shard_map.48.third_ref
  67.6 5.6 %all-to-all-done.2.sums_ref = f32[16,8,128]{2,1,0:T(8,128)S(1)} async-done(((f32[16,8,128]{2,1,0:T(8,128)}), f32[16,8,128]{2,1,0:T(8,128)S(1)}, u32[]{:S(2)}, u32[]{:S(2)}) %all-to-all-start.2) | async-done | bytes 65568 | tf_op jit(solution)/shard_map/all_to_all | solution.py:690
  73.2 1.1 %shard_map.49 = f32[5,32,640]{2,1,0:T(8,128)} custom-call(f32[16,8,128]{2,1,0:T(8,128)S(1)} %all-to-all-done.2.sums_ref, f32[5,32,640]{2,1,0:T(8,128)S(1)} %shard_map.46.first_ref, f32[5,32,640]{2,1,0:T(8,128)S(1)} %shard_map.47.second_ref, f32[5,32,640]{2,1,0:T(8,128)S(1)} %shard_map.48.third_ref), custom_call_target="tpu_custom_call" | custom-call | tf_op jit(solution)/shard_map/pallas_call | solution.py:633
  (13 shorter events, 1.6 us)
Async XLA Ops:
  0.0 19.2 %copy-start = (bf16[2,2,256,384]{3,2,1,0:T(8,128)(2,1)S(1)}, bf16[2,2,256,384]{3,2,1,0:T(8,128)(2,1)}, u32[]{:S(2)}) copy-start(bf16[2,2,256,384]{3,2,1,0:T(8,128)(2,1)} %constant.2.clone.table_ref) | copy-start | bytes 2359300
  20.7 11.2 %collective-permute-start.2 = (f32[40,768]{1,0:T(8,128)S(1)}, f32[40,768]{1,0:T(8,128)S(1)}, u32[]{:S(2)}, u32[]{:S(2)}) collective-permute-start(f32[40,768]{1,0:T(8,128)S(1)} %get-tuple-element.31), channel_id=1, source_target_pairs={{0,15},{1,2},{2,1},{3,4},{4,3},{5,6},{6,5},{7,8},{8,7},{9,10},{10,... | collective-permute-start | bytes 368648 | tf_op jit(solution)/shard_map/ppermute | solution.py:647
  24.4 7.5 %collective-permute-start.3 = (f32[40,768]{1,0:T(8,128)S(1)}, f32[40,768]{1,0:T(8,128)S(1)}, u32[]{:S(2)}, u32[]{:S(2)}) collective-permute-start(f32[40,768]{1,0:T(8,128)S(1)} %get-tuple-element.32), channel_id=1, source_target_pairs={{0,1},{1,0},{2,3},{3,2},{4,5},{5,4},{6,7},{7,6},{8,9},{9,8},{10,11... | collective-permute-start | bytes 368648 | tf_op jit(solution)/shard_map/ppermute | solution.py:646
  26.7 4.2 %collective-permute-start = (f32[2,40,256]{2,1,0:T(8,128)S(1)}, f32[2,40,256]{2,1,0:T(8,128)S(1)}, u32[]{:S(2)}, u32[]{:S(2)}) collective-permute-start(f32[2,40,256]{2,1,0:T(8,128)S(1)} %get-tuple-element.26), channel_id=1, source_target_pairs={{0,15},{1,2},{2,1},{3,4},{4,3},{5,6},{6,5},{7,8},{8,7},{9,10},{10,... | collective-permute-start | bytes 245768 | tf_op jit(solution)/shard_map/ppermute | solution.py:647
  26.7 4.2 %collective-permute-start.1 = (f32[2,40,256]{2,1,0:T(8,128)S(1)}, f32[2,40,256]{2,1,0:T(8,128)S(1)}, u32[]{:S(2)}, u32[]{:S(2)}) collective-permute-start(f32[2,40,256]{2,1,0:T(8,128)S(1)} %get-tuple-element.27), channel_id=1, source_target_pairs={{0,1},{1,0},{2,3},{3,2},{4,5},{5,4},{6,7},{7,6},{8,9},{9,8},{10,11... | collective-permute-start | bytes 245768 | tf_op jit(solution)/shard_map/ppermute | solution.py:646
  29.0 1.9 %copy-start.1 = (s32[128]{0:T(128)S(1)}, s32[128]{0:T(128)}, u32[]{:S(2)}) copy-start(s32[128]{0:T(128)} %tag_ref.1) | copy-start | bytes 1540
  45.7 4.3 %collective-permute-start.4 = (f32[4,32,128]{2,1,0:T(8,128)S(1)}, f32[4,32,128]{2,1,0:T(8,128)S(1)}, u32[]{:S(2)}, u32[]{:S(2)}) collective-permute-start(f32[4,32,128]{2,1,0:T(8,128)S(1)} %get-tuple-element.34), channel_id=1, source_target_pairs={{0,15},{1,2},{2,1},{3,4},{4,3},{5,6},{6,5},{7,8},{8,7},{9,10},{10,... | collective-permute-start | bytes 196616 | tf_op jit(solution)/shard_map/ppermute | solution.py:647
  48.1 2.4 %collective-permute-start.5 = (f32[4,32,128]{2,1,0:T(8,128)S(1)}, f32[4,32,128]{2,1,0:T(8,128)S(1)}, u32[]{:S(2)}, u32[]{:S(2)}) collective-permute-start(f32[4,32,128]{2,1,0:T(8,128)S(1)} %get-tuple-element.35), channel_id=1, source_target_pairs={{0,1},{1,0},{2,3},{3,2},{4,5},{5,4},{6,7},{7,6},{8,9},{9,8},{10,11... | collective-permute-start | bytes 196616 | tf_op jit(solution)/shard_map/ppermute | solution.py:646
  50.9 4.4 %collective-permute-start.6 = (f32[4,32,128]{2,1,0:T(8,128)S(1)}, f32[4,32,128]{2,1,0:T(8,128)S(1)}, u32[]{:S(2)}, u32[]{:S(2)}) collective-permute-start(f32[4,32,128]{2,1,0:T(8,128)S(1)} %get-tuple-element.38), channel_id=1, source_target_pairs={{0,15},{1,2},{2,1},{3,4},{4,3},{5,6},{6,5},{7,8},{8,7},{9,10},{10,... | collective-permute-start | bytes 196616 | tf_op jit(solution)/shard_map/ppermute | solution.py:647
  52.4 3.4 %collective-permute-start.7 = (f32[4,32,128]{2,1,0:T(8,128)S(1)}, f32[4,32,128]{2,1,0:T(8,128)S(1)}, u32[]{:S(2)}, u32[]{:S(2)}) collective-permute-start(f32[4,32,128]{2,1,0:T(8,128)S(1)} %get-tuple-element.39), channel_id=1, source_target_pairs={{0,1},{1,0},{2,3},{3,2},{4,5},{5,4},{6,7},{7,6},{8,9},{9,8},{10,11... | collective-permute-start | bytes 196616 | tf_op jit(solution)/shard_map/ppermute | solution.py:646
  56.9 16.2 %all-to-all-start.2 = ((f32[16,8,128]{2,1,0:T(8,128)}), f32[16,8,128]{2,1,0:T(8,128)S(1)}, u32[]{:S(2)}, u32[]{:S(2)}) async-start(f32[16,8,128]{2,1,0:T(8,128)} %get-tuple-element.41), calls=%async_computation.2 | async-start | bytes 131072 | tf_op jit(solution)/shard_map/all_to_all | solution.py:690

commit v8 on v7

--- a/solution.py
+++ b/solution.py
@@ -189,7 +189,8 @@
                 )
         turned = [jnp.concatenate(part, axis=0).T for part in (whole, rest)]
         nodal.append(jnp.concatenate([turned[0], turned[1][0:88]], axis=0))
-        cross_ref[parity], chip_ref[parity] = to_partners(turned[0][0:40], turned[1][32:72])
+        lanes = slice(PLANES + 256 * parity, PLANES + 256 * parity + 256)
+        cross_ref[:, lanes], chip_ref[:, lanes] = to_partners(turned[0][0:40], turned[1][32:72])
     return nodal
 
 
@@ -210,11 +211,8 @@
     return mean - 0.5 * speed * (right - left)
 
 
-def volume_kernel(
-    modal_ref, table_ref, field_ref, rhs_ref, modal_cross_ref, modal_chip_ref, cross_ref, chip_ref,
-    side_ref,
-):
-    nodal = turn(modal_ref, modal_cross_ref, modal_chip_ref)
+def volume_kernel(modal_ref, table_ref, field_ref, rhs_ref, cross_ref, chip_ref, side_ref):
+    nodal = turn(modal_ref, cross_ref, chip_ref)
     pair = synthesize(nodal, table_ref)
     for q in range(2):
         field_ref[:, HALF * q : HALF * q + HALF] = pair[q][0:200]
@@ -306,8 +304,8 @@
                 out_ref[parity, 128 * t : 128 * t + 128, lanes] = modal + change[t]
 
 
-def lift_kernel(
-    tag_ref, field_ref, cross_ref, chip_ref, table_ref, lift_ref, flux_ref, modal_ref, outer_ref
+def lift_faces(
+    tag_ref, field_ref, below_trace, above_trace, table_ref, lift_ref, flux_ref, modal_ref, outer_ref
 ):
     bottom, top = at_ends()
     span = lax.axis_index("span")
@@ -320,7 +318,8 @@
     gap = jnp.zeros((48, 256), jnp.float32)
     outer = []
     for parity in range(2):
-        below, above = from_partners(cross_ref[parity], chip_ref[parity])
+        lanes = slice(PLANES + 256 * parity, PLANES + 256 * parity + 256)
+        below, above = below_trace[:, lanes], above_trace[:, lanes]
         outer.append(jnp.concatenate([below, above], axis=0))
         modal_ref[parity] = jnp.concatenate(
             [keep_lower * below, keep_upper * above, gap], axis=0
@@ -341,10 +340,15 @@
 
 
 def facing_kernel(
-    inside_ref, lift_ref, flux_ref, facing_ref, cross_ref, chip_ref, table_ref, out_ref
+    tag_ref, inside_ref, field_ref, cross_ref, chip_ref, table_ref, out_ref, lift_ref, flux_ref,
+    facing_ref, outer_ref,
 ):
     bottom, top = at_ends()
     below, above = from_partners(cross_ref[...], chip_ref[...])
+    lift_faces(
+        tag_ref, field_ref, below, above, table_ref, lift_ref, flux_ref, facing_ref, outer_ref
+    )
+    below, above = below[:, 0:PLANES], above[:, 0:PLANES]
     lift = lift_ref[0:40, :]
     rhs_lower = lift + jnp.where(bottom, 0.0, below - lift)
     lift = lift_ref[40:80, :]
@@ -507,14 +511,13 @@
     store_joined(local_operator(vector, shift), next_ref, cross_ref, chip_ref)
 
 
-def pack_moments(moments, first, packed):
-    lane = lax.broadcasted_iota(jnp.int32, (32, 128), 1)
-    for n, moment in enumerate(moments):
-        packed = jnp.where(lane == first + n, jnp.sum(moment, axis=1, keepdims=True), packed)
-    return packed
-
-
-def early_kernel(first_ref, second_ref, joined_ref, packed_ref):
+def mode_sums(moment, turn_ref):
+    for t in range(4):
+        turn_ref[pl.ds(t, 8, stride=4), :] = moment[8 * t : 8 * t + 8]
+    return jnp.sum(turn_ref[...].T, axis=0, keepdims=True)
+
+
+def early_kernel(first_ref, second_ref, joined_ref, packed_ref, turn_ref):
     _, center = mode_terms()
     first = [first_ref[n] for n in range(25)]
     second = [second_ref[n] for n in range(25)]
@@ -525,7 +528,9 @@
         term = term if 0 < n % 5 < 4 else 0.5 * term
         product = term if product is None else product + term
     moments = [inner(first, first), inner(first, second), square, product - center * square]
-    packed_ref[...] = pack_moments(moments, 0, jnp.zeros((32, 128), jnp.float32))
+    packed_ref[...] = jnp.zeros((8, 128), jnp.float32)
+    for n, moment in enumerate(moments):
+        packed_ref[n : n + 1, 0:32] = mode_sums(moment, turn_ref.at[n])
 
 
 def third_kernel(
@@ -540,12 +545,12 @@
         vector_ref[n] = third[n]
     fourth = inner(third, third)
     moments = [fourth, energy(third, shift) - center * fourth]
-    packed = pack_moments(moments, 4, packed_ref[...])
-    for t in range(4):
-        turn_ref[pl.ds(t, 8, stride=4), :] = packed[8 * t : 8 * t + 8]
-    turned = turn_ref[...].T[0:8]
-    for p in range(GRID):
-        sums_ref[p, :, 0:32] = turned
+    sums_ref[0] = packed_ref[...]
+    for n, moment in enumerate(moments):
+        sums_ref[0, 4 + n : 5 + n, 0:32] = mode_sums(moment, turn_ref.at[n])
+    sums = sums_ref[0]
+    for p in range(1, GRID):
+        sums_ref[p] = sums
 
 
 def natural_kernel(vector_ref, out_ref, column_ref):
@@ -626,7 +631,7 @@
         copy.wait()
 
 
-def call(kernel, out_shapes, *args, smem=(), anywhere=(), scratch=(), out_space=pltpu.VMEM, covers=True):
+def call(kernel, out_shapes, *args, smem=(), anywhere=(), scratch=(), out_space=pltpu.VMEM):
     vmem = pl.BlockSpec(memory_space=pltpu.VMEM)
     spaces = {n: pl.BlockSpec(memory_space=pltpu.SMEM) for n in smem}
     spaces |= {n: pl.BlockSpec(memory_space=pltpu.HBM) for n in anywhere}
@@ -636,7 +641,6 @@
         in_specs=[spaces.get(n, vmem) for n in range(len(args))],
         out_specs=[pl.BlockSpec(memory_space=out_space)] * len(out_shapes),
         scratch_shapes=list(scratch),
-        cost_estimate=None if covers else pl.CostEstimate(flops=0, bytes_accessed=0, transcendentals=0),
         compiler_params=pltpu.CompilerParams(vmem_limit_bytes=16 * 1024 * 1024),
     )(*args)
 
@@ -660,20 +664,21 @@
         ],
     )
     modal = lax.all_to_all(packed, "span", 0, 0, tiled=True)
-    trace, rows = (2, 40, 256), (40, PLANES)
-    field, rhs, *modal_traces, cross, chip = call(
-        volume_kernel, [(200, PLANES), (200, PLANES), trace, trace, rows, rows], modal,
-        table, scratch=[pltpu.VMEM((16, PLANES), jnp.float32)],
-    )
-    modal_traces = swap_traces(*modal_traces)
-    rhs_traces = swap_traces(cross, chip)
-    (inside,) = call(inside_kernel, [(2, 256, 256)], modal, field, rhs, table, covers=False)
-    lift, flux, facing = call(
-        lift_kernel, [(80, PLANES), (80, PLANES), (2, 256, 128)], wall_tag, field,
-        *modal_traces, table, smem=(0,), scratch=[pltpu.VMEM((80, PLANES), jnp.float32)],
-        covers=False,
-    )
-    (sent,) = call(facing_kernel, [(16, 56, 128)], inside, lift, flux, facing, *rhs_traces, table)
+    trace = (40, PLANES + 512)
+    field, rhs, cross, chip = call(
+        volume_kernel, [(200, PLANES), (200, PLANES), trace, trace], modal, table,
+        scratch=[pltpu.VMEM((16, PLANES), jnp.float32)],
+    )
+    cross, chip = swap_traces(cross, chip)
+    (inside,) = call(inside_kernel, [(2, 256, 256)], modal, field, rhs, table)
+    (sent,) = call(
+        facing_kernel, [(16, 56, 128)], wall_tag, inside, field, cross, chip, table,
+        smem=(0,),
+        scratch=[
+            pltpu.VMEM((80, PLANES), jnp.float32), pltpu.VMEM((80, PLANES), jnp.float32),
+            pltpu.VMEM((2, 256, 128), jnp.float32), pltpu.VMEM((80, PLANES), jnp.float32),
+        ],
+    )
     load = lax.all_to_all(sent, "span", 0, 0, tiled=True)
     nodes, trace = (25, 32, 128), (4, 32, 128)
     first, joined, cross, chip = call(first_kernel, [nodes, nodes, trace, trace], load)
@@ -682,10 +687,13 @@
         second_kernel, [nodes, nodes, trace, trace], joined, cross, chip, first
     )
     cross, chip = swap_traces(cross, chip)
-    (packed,) = call(early_kernel, [(32, 128)], first, second, joined)
+    (packed,) = call(
+        early_kernel, [(8, 128)], first, second, joined,
+        scratch=[pltpu.VMEM((4, 32, 128), jnp.float32)],
+    )
     third, sums = call(
         third_kernel, [nodes, (16, 8, 128)], joined, cross, chip, second, packed,
-        scratch=[pltpu.VMEM((32, 128), jnp.float32)],
+        scratch=[pltpu.VMEM((2, 32, 128), jnp.float32)],
     )
     sums = lax.all_to_all(sums, "plane", 0, 0, tiled=True)
     columns = [

time: 74.5 us -> 74.1 us (level)
    ppermute x4 -> x3, starting transfers between devices: 7.67 us -> 8.95 us  [swap_traces(): cross = lax.ppermute(cross, 'plane', partner)]
    ppermute x4 -> x3, waiting for transfers between devices: 1.34 us -> 0.35 us  [swap_traces(): cross = lax.ppermute(cross, 'plane', partner)]
    ppermute x4 -> x3, starting transfers between devices: 8.58 us -> 7.76 us  [swap_traces(): chip = lax.ppermute(chip, 'plane', [(p, p ^ 1) for p in range(GRID)])]
    ppermute x4 -> x3, waiting for transfers between devices: 1.08 us -> 1.51 us  [swap_traces(): chip = lax.ppermute(chip, 'plane', [(p, p ^ 1) for p in range(GRID)])]
    pallas_call x13 -> x12, Pallas kernels: 12.5 us -> 12.5 us  [call(): pl.pallas_call(kernel, out_shape=[jax.ShapeDtypeStruct(s, jnp.float32) fo...]
  transfers between devices with their start and end apart: 9 -> 7, of which waited for: 5 -> 4; matrix products, arithmetic and copies ran while one was open for 0% -> 0% of each run, Pallas kernels for 6% -> 5%
where the time goes in v8:
time: 74.1 us; the launch traced here: 73.9 us
  blocking collectives  28.6 us (39%)
  starting transfers between devices  25.3 us (34%)
  Pallas kernels  12.5 us (17%)
  waiting for transfers between devices  7.47 us (10%)
    all_to_all x1, blocking collectives, on_device(): modal = lax.all_to_all(packed, 'span', 0, 0, tiled=True)  17 us
    pallas_call x12, Pallas kernels, call(): pl.pallas_call(kernel, out_shape=[jax.ShapeDtypeStruct(s, jnp.float32) fo...  12.5 us
    all_to_all x1, blocking collectives, on_device(): load = lax.all_to_all(sent, 'span', 0, 0, tiled=True)  11.6 us
    ppermute x3, starting transfers between devices, swap_traces(): cross = lax.ppermute(cross, 'plane', partner)  8.95 us
    all_to_all x1, starting transfers between devices, on_device(): sums = lax.all_to_all(sums, 'plane', 0, 0, tiled=True)  8.56 us
    ppermute x3, starting transfers between devices, swap_traces(): chip = lax.ppermute(chip, 'plane', [(p, p ^ 1) for p in range(GRID)])  7.76 us
    all_to_all x1, waiting for transfers between devices, on_device(): sums = lax.all_to_all(sums, 'plane', 0, 0, tiled=True)  5.62 us
    ppermute x3, waiting for transfers between devices, swap_traces(): chip = lax.ppermute(chip, 'plane', [(p, p ^ 1) for p in range(GRID)])  1.51 us
  transfers between devices with their start and end apart: 7, of which 4 were waited for; matrix products, arithmetic and copies ran while one was open for 0% of the time, Pallas kernels for 5%

profile of v8, /device:TPU:1, one launch (start us, length us, event | category | flops | bytes accessed | tf_op | source)
XLA Modules:
  0.0 73.9 jit_solution(14109714525774106641)
XLA Ops:
  0.0 2.1 %shard_map.37 = f32[16,56,128]{2,1,0:T(8,128)S(1)} custom-call(f32[5,32,640]{2,1,0:T(8,128)} %bitcast.2), custom_call_target="tpu_custom_call" | custom-call | tf_op jit(solution)/shard_map/pallas_call | solution.py:638
  2.2 17.0 %all_to_all.15.modal_ref = f32[16,56,128]{2,1,0:T(8,128)S(1)} all-to-all(f32[16,56,128]{2,1,0:T(8,128)S(1)} %shard_map.37), channel_id=1, replica_groups=mesh['span'=16,'plane'=16] {'span'}, dimensions={0} | all-to-all | bytes 917504 | tf_op jit(solution)/shard_map/all_to_all | solution.py:666
  19.2 1.5 %shard_map.38 = (f32[200,768]{1,0:T(8,128)S(1)}, f32[200,768]{1,0:T(8,128)S(1)}, f32[40,1280]{1,0:T(8,128)S(1)}, f32[40,1280]{1,0:T(8,128)S(1)}) custom-call(f32[16,56,128]{2,1,0:T(8,128)S(1)} %all_to_all.15.modal_ref, bf16[2,2,256,384]{3,2,1,0:T(8,128)(2,1)S(1)} %copy-done), custom_call_target="tpu_custom_call" | custom-call | tf_op jit(solution)/shard_map/pallas_call | solution.py:638
  20.7 3.7 %collective-permute-start = (f32[40,1280]{1,0:T(8,128)S(1)}, f32[40,1280]{1,0:T(8,128)S(1)}, u32[]{:S(2)}, u32[]{:S(2)}) collective-permute-start(f32[40,1280]{1,0:T(8,128)S(1)} %get-tuple-element.21), channel_id=1, source_target_pairs={{0,15},{1,2},{2,1},{3,4},{4,3},{5,6},{6,5},{7,8},{8,7},{9,10},{10,... | collective-permute-start | bytes 614408 | tf_op jit(solution)/shard_map/ppermute | solution.py:651
  24.4 2.3 %collective-permute-start.1 = (f32[40,1280]{1,0:T(8,128)S(1)}, f32[40,1280]{1,0:T(8,128)S(1)}, u32[]{:S(2)}, u32[]{:S(2)}) collective-permute-start(f32[40,1280]{1,0:T(8,128)S(1)} %get-tuple-element.22), channel_id=1, source_target_pairs={{0,1},{1,0},{2,3},{3,2},{4,5},{5,4},{6,7},{7,6},{8,9},{9,8},{10,11... | collective-permute-start | bytes 614408 | tf_op jit(solution)/shard_map/ppermute | solution.py:650
  26.7 1.1 %shard_map.39.inside_ref = f32[2,256,256]{2,1,0:T(8,128)S(1)} custom-call(f32[16,56,128]{2,1,0:T(8,128)S(1)} %all_to_all.15.modal_ref, f32[200,768]{1,0:T(8,128)S(1)} %get-tuple-element.19.field_ref, f32[200,768]{1,0:T(8,128)S(1)} %get-tuple-element.20.rhs_ref, bf16[2,2,256,384]{3,2,1,0:T(8,128)(2,1)S(1)} %copy-done), custom_call_target="tpu_custom_call" | custom-call | tf_op jit(solution)/shard_map/pallas_call | solution.py:638
  27.8 0.3 collective-permute-done.cross_ref
  28.2 1.8 %shard_map.40 = f32[16,56,128]{2,1,0:T(8,128)S(1)} custom-call(s32[128]{0:T(128)S(1)} %copy-done.1, f32[2,256,256]{2,1,0:T(8,128)S(1)} %shard_map.39.inside_ref, f32[200,768]{1,0:T(8,128)S(1)} %get-tuple-element.19.field_ref, f32[40,1280]{1,0:T(8,128)S(1)} %collective-permute-done.cross_ref, f32[40,1280]{1,0:T(8,128)S(1)} %collective-permute-done.1.chip_ref, ...), custom_call_target="tpu_custom_call" | custom-call | tf_op jit(solution)/shard_map/pallas_call | solution.py:638
  30.0 11.6 %all_to_all.16.modal_ref = f32[16,56,128]{2,1,0:T(8,128)S(1)} all-to-all(f32[16,56,128]{2,1,0:T(8,128)S(1)} %shard_map.40), channel_id=1, replica_groups=mesh['span'=16,'plane'=16] {'span'}, dimensions={0} | all-to-all | bytes 917504 | tf_op jit(solution)/shard_map/all_to_all | solution.py:682
  41.6 1.0 %shard_map.41 = (f32[25,32,128]{2,1,0:T(8,128)S(1)}, f32[25,32,128]{2,1,0:T(8,128)S(1)}, f32[4,32,128]{2,1,0:T(8,128)S(1)}, f32[4,32,128]{2,1,0:T(8,128)S(1)}) custom-call(f32[16,56,128]{2,1,0:T(8,128)S(1)} %all_to_all.16.modal_ref), custom_call_target="tpu_custom_call" | custom-call | tf_op jit(solution)/shard_map/pallas_call | solution.py:638
  42.6 4.5 %collective-permute-start.2 = (f32[4,32,128]{2,1,0:T(8,128)S(1)}, f32[4,32,128]{2,1,0:T(8,128)S(1)}, u32[]{:S(2)}, u32[]{:S(2)}) collective-permute-start(f32[4,32,128]{2,1,0:T(8,128)S(1)} %get-tuple-element.24), channel_id=1, source_target_pairs={{0,15},{1,2},{2,1},{3,4},{4,3},{5,6},{6,5},{7,8},{8,7},{9,10},{10,... | collective-permute-start | bytes 196616 | tf_op jit(solution)/shard_map/ppermute | solution.py:651
  47.1 2.1 %collective-permute-start.3 = (f32[4,32,128]{2,1,0:T(8,128)S(1)}, f32[4,32,128]{2,1,0:T(8,128)S(1)}, u32[]{:S(2)}, u32[]{:S(2)}) collective-permute-start(f32[4,32,128]{2,1,0:T(8,128)S(1)} %get-tuple-element.25), channel_id=1, source_target_pairs={{0,1},{1,0},{2,3},{3,2},{4,5},{5,4},{6,7},{7,6},{8,9},{9,8},{10,11... | collective-permute-start | bytes 196616 | tf_op jit(solution)/shard_map/ppermute | solution.py:650
  49.2 0.9 %collective-permute-done.3.chip_in_ref = f32[4,32,128]{2,1,0:T(8,128)S(1)} collective-permute-done((f32[4,32,128]{2,1,0:T(8,128)S(1)}, f32[4,32,128]{2,1,0:T(8,128)S(1)}, u32[]{:S(2)}, u32[]{:S(2)}) %collective-permute-start.3) | collective-permute-done | bytes 65568 | tf_op jit(solution)/shard_map/ppermute | solution.py:650
  50.1 0.4 shard_map.42
  50.5 0.8 %collective-permute-start.4 = (f32[4,32,128]{2,1,0:T(8,128)S(1)}, f32[4,32,128]{2,1,0:T(8,128)S(1)}, u32[]{:S(2)}, u32[]{:S(2)}) collective-permute-start(f32[4,32,128]{2,1,0:T(8,128)S(1)} %get-tuple-element.28), channel_id=1, source_target_pairs={{0,15},{1,2},{2,1},{3,4},{4,3},{5,6},{6,5},{7,8},{8,7},{9,10},{10,... | collective-permute-start | bytes 196616 | tf_op jit(solution)/shard_map/ppermute | solution.py:651
  51.2 3.3 %collective-permute-start.5 = (f32[4,32,128]{2,1,0:T(8,128)S(1)}, f32[4,32,128]{2,1,0:T(8,128)S(1)}, u32[]{:S(2)}, u32[]{:S(2)}) collective-permute-start(f32[4,32,128]{2,1,0:T(8,128)S(1)} %get-tuple-element.29), channel_id=1, source_target_pairs={{0,1},{1,0},{2,3},{3,2},{4,5},{5,4},{6,7},{7,6},{8,9},{9,8},{10,11... | collective-permute-start | bytes 196616 | tf_op jit(solution)/shard_map/ppermute | solution.py:650
  54.9 0.6 collective-permute-done.5.chip_in_ref
  55.5 1.0 %shard_map.44 = (f32[25,32,128]{2,1,0:T(8,128)S(1)}, f32[16,8,128]{2,1,0:T(8,128)}) custom-call(f32[25,32,128]{2,1,0:T(8,128)S(1)} %get-tuple-element.27.joined_ref, f32[4,32,128]{2,1,0:T(8,128)S(1)} %collective-permute-done.4.cross_in_ref, f32[4,32,128]{2,1,0:T(8,128)S(1)} %collective-permute-done.5.chip_in_ref, ...), custom_call_target="tpu_custom_call" | custom-call | tf_op jit(solution)/shard_map/pallas_call | solution.py:638
  56.5 8.6 %all-to-all-start.2 = ((f32[16,8,128]{2,1,0:T(8,128)}), f32[16,8,128]{2,1,0:T(8,128)S(1)}, u32[]{:S(2)}, u32[]{:S(2)}) async-start(f32[16,8,128]{2,1,0:T(8,128)} %get-tuple-element.31), calls=%async_computation.2 | async-start | bytes 131072 | tf_op jit(solution)/shard_map/all_to_all | solution.py:698
  65.1 0.7 shard_map.45.first_ref
  65.8 0.7 shard_map.46.second_ref
  66.5 0.7 shard_map.47.third_ref
  67.2 5.6 %all-to-all-done.2.sums_ref = f32[16,8,128]{2,1,0:T(8,128)S(1)} async-done(((f32[16,8,128]{2,1,0:T(8,128)}), f32[16,8,128]{2,1,0:T(8,128)S(1)}, u32[]{:S(2)}, u32[]{:S(2)}) %all-to-all-start.2) | async-done | bytes 65568 | tf_op jit(solution)/shard_map/all_to_all | solution.py:698
  72.8 1.1 %shard_map.48 = f32[5,32,640]{2,1,0:T(8,128)} custom-call(f32[16,8,128]{2,1,0:T(8,128)S(1)} %all-to-all-done.2.sums_ref, f32[5,32,640]{2,1,0:T(8,128)S(1)} %shard_map.45.first_ref, f32[5,32,640]{2,1,0:T(8,128)S(1)} %shard_map.46.second_ref, f32[5,32,640]{2,1,0:T(8,128)S(1)} %shard_map.47.third_ref), custom_call_target="tpu_custom_call" | custom-call | tf_op jit(solution)/shard_map/pallas_call | solution.py:638
  (8 shorter events, 0.3 us)
Async XLA Ops:
  0.0 19.2 %copy-start = (bf16[2,2,256,384]{3,2,1,0:T(8,128)(2,1)S(1)}, bf16[2,2,256,384]{3,2,1,0:T(8,128)(2,1)}, u32[]{:S(2)}) copy-start(bf16[2,2,256,384]{3,2,1,0:T(8,128)(2,1)} %constant.2.clone.table_ref) | copy-start | bytes 2359300
  20.7 7.5 %collective-permute-start = (f32[40,1280]{1,0:T(8,128)S(1)}, f32[40,1280]{1,0:T(8,128)S(1)}, u32[]{:S(2)}, u32[]{:S(2)}) collective-permute-start(f32[40,1280]{1,0:T(8,128)S(1)} %get-tuple-element.21), channel_id=1, source_target_pairs={{0,15},{1,2},{2,1},{3,4},{4,3},{5,6},{6,5},{7,8},{8,7},{9,10},{10,... | collective-permute-start | bytes 614408 | tf_op jit(solution)/shard_map/ppermute | solution.py:651
  24.4 3.7 %collective-permute-start.1 = (f32[40,1280]{1,0:T(8,128)S(1)}, f32[40,1280]{1,0:T(8,128)S(1)}, u32[]{:S(2)}, u32[]{:S(2)}) collective-permute-start(f32[40,1280]{1,0:T(8,128)S(1)} %get-tuple-element.22), channel_id=1, source_target_pairs={{0,1},{1,0},{2,3},{3,2},{4,5},{5,4},{6,7},{7,6},{8,9},{9,8},{10,11... | collective-permute-start | bytes 614408 | tf_op jit(solution)/shard_map/ppermute | solution.py:650
  26.7 1.4 %copy-start.1 = (s32[128]{0:T(128)S(1)}, s32[128]{0:T(128)}, u32[]{:S(2)}) copy-start(s32[128]{0:T(128)} %tag_ref.1) | copy-start | bytes 1540
  42.6 6.6 %collective-permute-start.2 = (f32[4,32,128]{2,1,0:T(8,128)S(1)}, f32[4,32,128]{2,1,0:T(8,128)S(1)}, u32[]{:S(2)}, u32[]{:S(2)}) collective-permute-start(f32[4,32,128]{2,1,0:T(8,128)S(1)} %get-tuple-element.24), channel_id=1, source_target_pairs={{0,15},{1,2},{2,1},{3,4},{4,3},{5,6},{6,5},{7,8},{8,7},{9,10},{10,... | collective-permute-start | bytes 196616 | tf_op jit(solution)/shard_map/ppermute | solution.py:651
  47.1 3.0 %collective-permute-start.3 = (f32[4,32,128]{2,1,0:T(8,128)S(1)}, f32[4,32,128]{2,1,0:T(8,128)S(1)}, u32[]{:S(2)}, u32[]{:S(2)}) collective-permute-start(f32[4,32,128]{2,1,0:T(8,128)S(1)} %get-tuple-element.25), channel_id=1, source_target_pairs={{0,1},{1,0},{2,3},{3,2},{4,5},{5,4},{6,7},{7,6},{8,9},{9,8},{10,11... | collective-permute-start | bytes 196616 | tf_op jit(solution)/shard_map/ppermute | solution.py:650
  50.5 4.4 %collective-permute-start.4 = (f32[4,32,128]{2,1,0:T(8,128)S(1)}, f32[4,32,128]{2,1,0:T(8,128)S(1)}, u32[]{:S(2)}, u32[]{:S(2)}) collective-permute-start(f32[4,32,128]{2,1,0:T(8,128)S(1)} %get-tuple-element.28), channel_id=1, source_target_pairs={{0,15},{1,2},{2,1},{3,4},{4,3},{5,6},{6,5},{7,8},{8,7},{9,10},{10,... | collective-permute-start | bytes 196616 | tf_op jit(solution)/shard_map/ppermute | solution.py:651
  51.2 4.2 %collective-permute-start.5 = (f32[4,32,128]{2,1,0:T(8,128)S(1)}, f32[4,32,128]{2,1,0:T(8,128)S(1)}, u32[]{:S(2)}, u32[]{:S(2)}) collective-permute-start(f32[4,32,128]{2,1,0:T(8,128)S(1)} %get-tuple-element.29), channel_id=1, source_target_pairs={{0,1},{1,0},{2,3},{3,2},{4,5},{5,4},{6,7},{7,6},{8,9},{9,8},{10,11... | collective-permute-start | bytes 196616 | tf_op jit(solution)/shard_map/ppermute | solution.py:650
  56.5 16.3 %all-to-all-start.2 = ((f32[16,8,128]{2,1,0:T(8,128)}), f32[16,8,128]{2,1,0:T(8,128)S(1)}, u32[]{:S(2)}, u32[]{:S(2)}) async-start(f32[16,8,128]{2,1,0:T(8,128)} %get-tuple-element.31), calls=%async_computation.2 | async-start | bytes 131072 | tf_op jit(solution)/shard_map/all_to_all | solution.py:698

commit v9 on v7

--- a/solution.py
+++ b/solution.py
@@ -210,59 +210,70 @@
     return mean - 0.5 * speed * (right - left)
 
 
+def row_rhs(field_ref, side_ref, lanes, rows):
+    row = lax.broadcasted_iota(jnp.int32, (8, 128), 0)
+    f = [field_ref[8 * n : 8 * n + 8, lanes] for n in range(25)]
+    square = [v * v for v in f]
+    out = {}
+    for j in rows:
+        for i in range(5):
+            n = j * 5 + i
+            plain = None
+            power = None
+            for other in range(5):
+                terms = [(DIFFER[i][other], j * 5 + other), (DIFFER[j][other], other * 5 + i)]
+                for weight, m in terms:
+                    if weight == 0.0:
+                        continue
+                    weight = float(weight) / -3.0
+                    plain = weight * f[m] if plain is None else plain + weight * f[m]
+                    power = weight * square[m] if power is None else power + weight * square[m]
+            total = power + f[n] * plain
+            own = (i == 4) + (j == 4) - (i == 0) - (j == 0)
+            if own:
+                total = total + (5.0 * own) * square[n]
+            if i == 0 or i == 4:
+                at = j & 3
+                side = side_ref[8 * (j // 4) : 8 * (j // 4) + 8, lanes]
+                if at:
+                    side = pltpu.roll(side, 8 - at if i == 0 else at, 0)
+                if i == 0:
+                    left = jnp.where(row == 0, side, pltpu.roll(f[j * 5 + 4], 1, 0))
+                    total = total + 10.0 * two_point(left, f[n])
+                else:
+                    right = jnp.where(row == 7, side, pltpu.roll(f[j * 5], 7, 0))
+                    total = total - 10.0 * two_point(f[n], right)
+            out[n] = total
+    return out
+
+
+def each_lane_block(body):
+    def step(block, carry):
+        body(pl.ds(pl.multiple_of(block * 128, 128), 128))
+        return carry
+
+    lax.fori_loop(0, PLANES // 128, step, 0)
+
+
 def volume_kernel(
-    modal_ref, table_ref, field_ref, rhs_ref, modal_cross_ref, modal_chip_ref, cross_ref, chip_ref,
-    side_ref,
+    modal_ref, table_ref, field_ref, side_ref, edge_ref, modal_cross_ref, modal_chip_ref, cross_ref,
+    chip_ref,
 ):
     nodal = turn(modal_ref, modal_cross_ref, modal_chip_ref)
     pair = synthesize(nodal, table_ref)
     for q in range(2):
         field_ref[:, HALF * q : HALF * q + HALF] = pair[q][0:200]
         side_ref[:, HALF * q : HALF * q + HALF] = pair[q][200:216]
-    row = lax.broadcasted_iota(jnp.int32, (8, 128), 0)
-
-    def column(block, carry):
-        lanes = pl.ds(pl.multiple_of(block * 128, 128), 128)
-        f = [field_ref[8 * n : 8 * n + 8, lanes] for n in range(25)]
-        square = [v * v for v in f]
-        low = []
-        for j in range(5):
-            for i in range(5):
-                n = j * 5 + i
-                plain = None
-                power = None
-                for other in range(5):
-                    terms = [(DIFFER[i][other], j * 5 + other), (DIFFER[j][other], other * 5 + i)]
-                    for weight, m in terms:
-                        if weight == 0.0:
-                            continue
-                        weight = float(weight) / -3.0
-                        plain = weight * f[m] if plain is None else plain + weight * f[m]
-                        power = weight * square[m] if power is None else power + weight * square[m]
-                total = power + f[n] * plain
-                own = (i == 4) + (j == 4) - (i == 0) - (j == 0)
-                if own:
-                    total = total + (5.0 * own) * square[n]
-                if i == 0 or i == 4:
-                    at = j & 3
-                    side = side_ref[8 * (j // 4) : 8 * (j // 4) + 8, lanes]
-                    if at:
-                        side = pltpu.roll(side, 8 - at if i == 0 else at, 0)
-                    if i == 0:
-                        left = jnp.where(row == 0, side, pltpu.roll(f[j * 5 + 4], 1, 0))
-                        total = total + 10.0 * two_point(left, f[n])
-                    else:
-                        right = jnp.where(row == 7, side, pltpu.roll(f[j * 5], 7, 0))
-                        total = total - 10.0 * two_point(f[n], right)
-                rhs_ref[8 * n : 8 * n + 8, lanes] = total
-                if j == 0:
-                    low.append(total)
-                elif j == 4:
-                    rows = slice(8 * i, 8 * i + 8)
-                    cross_ref[rows, lanes], chip_ref[rows, lanes] = to_partners(low[i], total)
-        return carry
-
-    lax.fori_loop(0, PLANES // 128, column, 0)
+
+    def body(lanes):
+        total = row_rhs(field_ref, side_ref, lanes, (0, 4))
+        for i in range(5):
+            rows = slice(8 * i, 8 * i + 8)
+            edge_ref[rows, lanes] = total[i]
+            edge_ref[40 + 8 * i : 48 + 8 * i, lanes] = total[20 + i]
+            cross_ref[rows, lanes], chip_ref[rows, lanes] = to_partners(total[i], total[20 + i])
+
+    each_lane_block(body)
 
 
 def project(planar, parity, table_ref):
@@ -280,14 +291,21 @@
     )
 
 
-def inside_kernel(modal_ref, field_ref, rhs_ref, table_ref, out_ref):
+def inside_kernel(modal_ref, field_ref, side_ref, edge_ref, table_ref, out_ref, rhs_ref):
     last = [
         unpack_last([modal_ref[s, 32 + 8 * g : 40 + 8 * g, :] for g in range(3)], 11)
         for s in range(GRID)
     ]
+
+    def body(lanes):
+        total = row_rhs(field_ref, side_ref, lanes, (1, 2, 3))
+        for n in range(5, 20):
+            rhs_ref[8 * n - 40 : 8 * n - 32, lanes] = total[n]
+
+    each_lane_block(body)
     field = field_ref[...]
     flux = 0.5 * field * field
-    rhs = rhs_ref[...]
+    rhs = jnp.concatenate([edge_ref[0:40, :], rhs_ref[...], edge_ref[40:80, :]], axis=0)
     tail = jnp.zeros((56, PLANES), jnp.float32)
     flux = jnp.concatenate([flux, tail], axis=0)
     rhs = jnp.concatenate([rhs, tail], axis=0)
@@ -507,14 +525,13 @@
     store_joined(local_operator(vector, shift), next_ref, cross_ref, chip_ref)
 
 
-def pack_moments(moments, first, packed):
-    lane = lax.broadcasted_iota(jnp.int32, (32, 128), 1)
-    for n, moment in enumerate(moments):
-        packed = jnp.where(lane == first + n, jnp.sum(moment, axis=1, keepdims=True), packed)
-    return packed
-
-
-def early_kernel(first_ref, second_ref, joined_ref, packed_ref):
+def mode_sums(moment, turn_ref):
+    for t in range(4):
+        turn_ref[pl.ds(t, 8, stride=4), :] = moment[8 * t : 8 * t + 8]
+    return jnp.sum(turn_ref[...].T, axis=0, keepdims=True)
+
+
+def early_kernel(first_ref, second_ref, joined_ref, packed_ref, turn_ref):
     _, center = mode_terms()
     first = [first_ref[n] for n in range(25)]
     second = [second_ref[n] for n in range(25)]
@@ -525,7 +542,9 @@
         term = term if 0 < n % 5 < 4 else 0.5 * term
         product = term if product is None else product + term
     moments = [inner(first, first), inner(first, second), square, product - center * square]
-    packed_ref[...] = pack_moments(moments, 0, jnp.zeros((32, 128), jnp.float32))
+    packed_ref[...] = jnp.zeros((8, 128), jnp.float32)
+    for n, moment in enumerate(moments):
+        packed_ref[n : n + 1, 0:32] = mode_sums(moment, turn_ref.at[n])
 
 
 def third_kernel(
@@ -540,12 +559,12 @@
         vector_ref[n] = third[n]
     fourth = inner(third, third)
     moments = [fourth, energy(third, shift) - center * fourth]
-    packed = pack_moments(moments, 4, packed_ref[...])
-    for t in range(4):
-        turn_ref[pl.ds(t, 8, stride=4), :] = packed[8 * t : 8 * t + 8]
-    turned = turn_ref[...].T[0:8]
-    for p in range(GRID):
-        sums_ref[p, :, 0:32] = turned
+    sums_ref[0] = packed_ref[...]
+    for n, moment in enumerate(moments):
+        sums_ref[0, 4 + n : 5 + n, 0:32] = mode_sums(moment, turn_ref.at[n])
+    sums = sums_ref[0]
+    for p in range(1, GRID):
+        sums_ref[p] = sums
 
 
 def natural_kernel(vector_ref, out_ref, column_ref):
@@ -661,13 +680,16 @@
     )
     modal = lax.all_to_all(packed, "span", 0, 0, tiled=True)
     trace, rows = (2, 40, 256), (40, PLANES)
-    field, rhs, *modal_traces, cross, chip = call(
-        volume_kernel, [(200, PLANES), (200, PLANES), trace, trace, rows, rows], modal,
-        table, scratch=[pltpu.VMEM((16, PLANES), jnp.float32)],
+    field, side, edge, *modal_traces, cross, chip = call(
+        volume_kernel,
+        [(200, PLANES), (16, PLANES), (80, PLANES), trace, trace, rows, rows], modal, table,
     )
     modal_traces = swap_traces(*modal_traces)
     rhs_traces = swap_traces(cross, chip)
-    (inside,) = call(inside_kernel, [(2, 256, 256)], modal, field, rhs, table, covers=False)
+    (inside,) = call(
+        inside_kernel, [(2, 256, 256)], modal, field, side, edge, table, covers=False,
+        scratch=[pltpu.VMEM((120, PLANES), jnp.float32)],
+    )
     lift, flux, facing = call(
         lift_kernel, [(80, PLANES), (80, PLANES), (2, 256, 128)], wall_tag, field,
         *modal_traces, table, smem=(0,), scratch=[pltpu.VMEM((80, PLANES), jnp.float32)],
@@ -682,10 +704,13 @@
         second_kernel, [nodes, nodes, trace, trace], joined, cross, chip, first
     )
     cross, chip = swap_traces(cross, chip)
-    (packed,) = call(early_kernel, [(32, 128)], first, second, joined)
+    (packed,) = call(
+        early_kernel, [(8, 128)], first, second, joined,
+        scratch=[pltpu.VMEM((4, 32, 128), jnp.float32)],
+    )
     third, sums = call(
         third_kernel, [nodes, (16, 8, 128)], joined, cross, chip, second, packed,
-        scratch=[pltpu.VMEM((32, 128), jnp.float32)],
+        scratch=[pltpu.VMEM((2, 32, 128), jnp.float32)],
     )
     sums = lax.all_to_all(sums, "plane", 0, 0, tiled=True)
     columns = [

time: 74.5 us -> 73.9 us (level)
  transfers between devices with their start and end apart: 9 -> 9, of which waited for: 5 -> 5; matrix products, arithmetic and copies ran while one was open for 0% -> 0% of each run, Pallas kernels for 6% -> 7%
where the time goes in v9:
time: 73.9 us; the launch traced here: 73.7 us
  blocking collectives  28.9 us (39%)
  starting transfers between devices  24.7 us (33%)
  Pallas kernels  12.6 us (17%)
  waiting for transfers between devices  7.34 us (10%)
    all_to_all x1, blocking collectives, on_device(): modal = lax.all_to_all(packed, 'span', 0, 0, tiled=True)  17 us
    pallas_call x13, Pallas kernels, call(): pl.pallas_call(kernel, out_shape=[jax.ShapeDtypeStruct(s, jnp.float32) fo...  12.6 us
    all_to_all x1, blocking collectives, on_device(): load = lax.all_to_all(sent, 'span', 0, 0, tiled=True)  11.9 us
    all_to_all x1, starting transfers between devices, on_device(): sums = lax.all_to_all(sums, 'plane', 0, 0, tiled=True)  8.43 us
    ppermute x4, starting transfers between devices, swap_traces(): chip = lax.ppermute(chip, 'plane', [(p, p ^ 1) for p in range(GRID)])  8.36 us
    ppermute x4, starting transfers between devices, swap_traces(): cross = lax.ppermute(cross, 'plane', partner)  7.88 us
    all_to_all x1, waiting for transfers between devices, on_device(): sums = lax.all_to_all(sums, 'plane', 0, 0, tiled=True)  5.62 us
  transfers between devices with their start and end apart: 9, of which 5 were waited for; matrix products, arithmetic and copies ran while one was open for 0% of the time, Pallas kernels for 7%

profile of v9, /device:TPU:1, one launch (start us, length us, event | category | flops | bytes accessed | tf_op | source)
XLA Modules:
  0.0 73.7 jit_solution(8983036228091451769)
XLA Ops:
  0.0 2.1 %shard_map.37 = f32[16,56,128]{2,1,0:T(8,128)S(1)} custom-call(f32[5,32,640]{2,1,0:T(8,128)} %bitcast.2), custom_call_target="tpu_custom_call" | custom-call | tf_op jit(solution)/shard_map/pallas_call | solution.py:652
  2.2 17.0 %all_to_all.15.modal_ref = f32[16,56,128]{2,1,0:T(8,128)S(1)} all-to-all(f32[16,56,128]{2,1,0:T(8,128)S(1)} %shard_map.37), channel_id=1, replica_groups=mesh['span'=16,'plane'=16] {'span'}, dimensions={0} | all-to-all | bytes 917504 | tf_op jit(solution)/shard_map/all_to_all | solution.py:681
  19.2 1.0 %shard_map.38 = (f32[200,768]{1,0:T(8,128)S(1)}, f32[16,768]{1,0:T(8,128)S(1)}, f32[80,768]{1,0:T(8,128)S(1)}, f32[2,40,256]{2,1,0:T(8,128)S(1)}, f32[2,40,256]{...) custom-call(f32[16,56,128]{2,1,0:T(8,128)S(1)} %all_to_all.15.modal_ref, ...), custom_call_target="tpu_custom_call" | custom-call | tf_op jit(solution)/shard_map/pallas_call | solution.py:652
  20.2 3.7 %collective-permute-start.2 = (f32[40,768]{1,0:T(8,128)S(1)}, f32[40,768]{1,0:T(8,128)S(1)}, u32[]{:S(2)}, u32[]{:S(2)}) collective-permute-start(f32[40,768]{1,0:T(8,128)S(1)} %get-tuple-element.33), channel_id=1, source_target_pairs={{0,15},{1,2},{2,1},{3,4},{4,3},{5,6},{6,5},{7,8},{8,7},{9,10},{10,... | collective-permute-start | bytes 368648 | tf_op jit(solution)/shard_map/ppermute | solution.py:666
  23.9 2.3 %collective-permute-start.3 = (f32[40,768]{1,0:T(8,128)S(1)}, f32[40,768]{1,0:T(8,128)S(1)}, u32[]{:S(2)}, u32[]{:S(2)}) collective-permute-start(f32[40,768]{1,0:T(8,128)S(1)} %get-tuple-element.34), channel_id=1, source_target_pairs={{0,1},{1,0},{2,3},{3,2},{4,5},{5,4},{6,7},{7,6},{8,9},{9,8},{10,11... | collective-permute-start | bytes 368648 | tf_op jit(solution)/shard_map/ppermute | solution.py:665
  26.2 2.2 %collective-permute-start.1 = (f32[2,40,256]{2,1,0:T(8,128)S(1)}, f32[2,40,256]{2,1,0:T(8,128)S(1)}, u32[]{:S(2)}, u32[]{:S(2)}) collective-permute-start(f32[2,40,256]{2,1,0:T(8,128)S(1)} %get-tuple-element.29), channel_id=1, source_target_pairs={{0,1},{1,0},{2,3},{3,2},{4,5},{5,4},{6,7},{7,6},{8,9},{9,8},{10,11... | collective-permute-start | bytes 245768 | tf_op jit(solution)/shard_map/ppermute | solution.py:665
  28.5 1.7 %shard_map.39.inside_ref = f32[2,256,256]{2,1,0:T(8,128)S(1)} custom-call(f32[16,56,128]{2,1,0:T(8,128)S(1)} %all_to_all.15.modal_ref, f32[200,768]{1,0:T(8,128)S(1)} %get-tuple-element.25.field_ref, f32[16,768]{1,0:T(8,128)S(1)} %get-tuple-element.26.side_ref, f32[80,768]{1,0:T(8,128)S(1)} %get-tuple-element.27.edge_ref, bf16[2,2,256,384]{3,2,1,0:T(8,128)(2,1)S(1)} %copy-done), custom_call_target="tpu_custom_call" | custom-call | tf_op jit(solution)/shard_map/pallas_call | solution.py:652
  30.4 1.0 %shard_map.40 = (f32[80,768]{1,0:T(8,128)S(1)}, f32[80,768]{1,0:T(8,128)S(1)}, f32[2,256,128]{2,1,0:T(8,128)S(1)}) custom-call(s32[128]{0:T(128)S(1)} %copy-done.1, f32[200,768]{1,0:T(8,128)S(1)} %get-tuple-element.25.field_ref, f32[2,40,256]{2,1,0:T(8,128)S(1)} %collective-permute-done.cross_ref, f32[2,40,256]{2,1,0:T(8,128)S(1)} %collective-permute-done.1.chip_ref, ...), custom_call_target="tpu_custom_call" | custom-call | tf_op jit(solution)/shard_map/pallas_call | solution.py:652
  31.4 0.8 %shard_map.41 = f32[16,56,128]{2,1,0:T(8,128)S(1)} custom-call(f32[2,256,256]{2,1,0:T(8,128)S(1)} %shard_map.39.inside_ref, f32[80,768]{1,0:T(8,128)S(1)} %get-tuple-element.30.lift_ref, f32[80,768]{1,0:T(8,128)S(1)} %get-tuple-element.31.flux_ref, f32[2,256,128]{2,1,0:T(8,128)S(1)} %get-tuple-element.32.facing_ref, ...), custom_call_target="tpu_custom_call" | custom-call | tf_op jit(solution)/shard_map/pallas_call | solution.py:652
  32.3 11.9 %all_to_all.16.modal_ref = f32[16,56,128]{2,1,0:T(8,128)S(1)} all-to-all(f32[16,56,128]{2,1,0:T(8,128)S(1)} %shard_map.41), channel_id=1, replica_groups=mesh['span'=16,'plane'=16] {'span'}, dimensions={0} | all-to-all | bytes 917504 | tf_op jit(solution)/shard_map/all_to_all | solution.py:699
  44.2 1.0 %shard_map.42 = (f32[25,32,128]{2,1,0:T(8,128)S(1)}, f32[25,32,128]{2,1,0:T(8,128)S(1)}, f32[4,32,128]{2,1,0:T(8,128)S(1)}, f32[4,32,128]{2,1,0:T(8,128)S(1)}) custom-call(f32[16,56,128]{2,1,0:T(8,128)S(1)} %all_to_all.16.modal_ref), custom_call_target="tpu_custom_call" | custom-call | tf_op jit(solution)/shard_map/pallas_call | solution.py:652
  45.2 2.6 %collective-permute-start.4 = (f32[4,32,128]{2,1,0:T(8,128)S(1)}, f32[4,32,128]{2,1,0:T(8,128)S(1)}, u32[]{:S(2)}, u32[]{:S(2)}) collective-permute-start(f32[4,32,128]{2,1,0:T(8,128)S(1)} %get-tuple-element.36), channel_id=1, source_target_pairs={{0,15},{1,2},{2,1},{3,4},{4,3},{5,6},{6,5},{7,8},{8,7},{9,10},{10,... | collective-permute-start | bytes 196616 | tf_op jit(solution)/shard_map/ppermute | solution.py:666
  47.8 1.3 %collective-permute-start.5 = (f32[4,32,128]{2,1,0:T(8,128)S(1)}, f32[4,32,128]{2,1,0:T(8,128)S(1)}, u32[]{:S(2)}, u32[]{:S(2)}) collective-permute-start(f32[4,32,128]{2,1,0:T(8,128)S(1)} %get-tuple-element.37), channel_id=1, source_target_pairs={{0,1},{1,0},{2,3},{3,2},{4,5},{5,4},{6,7},{7,6},{8,9},{9,8},{10,11... | collective-permute-start | bytes 196616 | tf_op jit(solution)/shard_map/ppermute | solution.py:665
  49.1 0.7 collective-permute-done.4.cross_in_ref
  50.4 1.6 %collective-permute-start.6 = (f32[4,32,128]{2,1,0:T(8,128)S(1)}, f32[4,32,128]{2,1,0:T(8,128)S(1)}, u32[]{:S(2)}, u32[]{:S(2)}) collective-permute-start(f32[4,32,128]{2,1,0:T(8,128)S(1)} %get-tuple-element.40), channel_id=1, source_target_pairs={{0,15},{1,2},{2,1},{3,4},{4,3},{5,6},{6,5},{7,8},{8,7},{9,10},{10,... | collective-permute-start | bytes 196616 | tf_op jit(solution)/shard_map/ppermute | solution.py:666
  52.0 2.5 %collective-permute-start.7 = (f32[4,32,128]{2,1,0:T(8,128)S(1)}, f32[4,32,128]{2,1,0:T(8,128)S(1)}, u32[]{:S(2)}, u32[]{:S(2)}) collective-permute-start(f32[4,32,128]{2,1,0:T(8,128)S(1)} %get-tuple-element.41), channel_id=1, source_target_pairs={{0,1},{1,0},{2,3},{3,2},{4,5},{5,4},{6,7},{7,6},{8,9},{9,8},{10,11... | collective-permute-start | bytes 196616 | tf_op jit(solution)/shard_map/ppermute | solution.py:665
  54.8 0.6 collective-permute-done.7.chip_in_ref
  55.4 1.0 %shard_map.45 = (f32[25,32,128]{2,1,0:T(8,128)S(1)}, f32[16,8,128]{2,1,0:T(8,128)}) custom-call(f32[25,32,128]{2,1,0:T(8,128)S(1)} %get-tuple-element.39.joined_ref, f32[4,32,128]{2,1,0:T(8,128)S(1)} %collective-permute-done.6.cross_in_ref, f32[4,32,128]{2,1,0:T(8,128)S(1)} %collective-permute-done.7.chip_in_ref, ...), custom_call_target="tpu_custom_call" | custom-call | tf_op jit(solution)/shard_map/pallas_call | solution.py:652
  56.4 8.4 %all-to-all-start.2 = ((f32[16,8,128]{2,1,0:T(8,128)}), f32[16,8,128]{2,1,0:T(8,128)S(1)}, u32[]{:S(2)}, u32[]{:S(2)}) async-start(f32[16,8,128]{2,1,0:T(8,128)} %get-tuple-element.43), calls=%async_computation.2 | async-start | bytes 131072 | tf_op jit(solution)/shard_map/all_to_all | solution.py:715
  64.8 0.7 shard_map.46.first_ref
  65.5 0.7 shard_map.47.second_ref
  66.3 0.7 shard_map.48.third_ref
  67.0 5.6 %all-to-all-done.2.sums_ref = f32[16,8,128]{2,1,0:T(8,128)S(1)} async-done(((f32[16,8,128]{2,1,0:T(8,128)}), f32[16,8,128]{2,1,0:T(8,128)S(1)}, u32[]{:S(2)}, u32[]{:S(2)}) %all-to-all-start.2) | async-done | bytes 65568 | tf_op jit(solution)/shard_map/all_to_all | solution.py:715
  72.6 1.1 %shard_map.49 = f32[5,32,640]{2,1,0:T(8,128)} custom-call(f32[16,8,128]{2,1,0:T(8,128)S(1)} %all-to-all-done.2.sums_ref, f32[5,32,640]{2,1,0:T(8,128)S(1)} %shard_map.46.first_ref, f32[5,32,640]{2,1,0:T(8,128)S(1)} %shard_map.47.second_ref, f32[5,32,640]{2,1,0:T(8,128)S(1)} %shard_map.48.third_ref), custom_call_target="tpu_custom_call" | custom-call | tf_op jit(solution)/shard_map/pallas_call | solution.py:652
  (13 shorter events, 1.2 us)
Async XLA Ops:
  0.0 19.2 %copy-start = (bf16[2,2,256,384]{3,2,1,0:T(8,128)(2,1)S(1)}, bf16[2,2,256,384]{3,2,1,0:T(8,128)(2,1)}, u32[]{:S(2)}) copy-start(bf16[2,2,256,384]{3,2,1,0:T(8,128)(2,1)} %constant.2.clone.table_ref) | copy-start | bytes 2359300
  20.2 11.2 %collective-permute-start.2 = (f32[40,768]{1,0:T(8,128)S(1)}, f32[40,768]{1,0:T(8,128)S(1)}, u32[]{:S(2)}, u32[]{:S(2)}) collective-permute-start(f32[40,768]{1,0:T(8,128)S(1)} %get-tuple-element.33), channel_id=1, source_target_pairs={{0,15},{1,2},{2,1},{3,4},{4,3},{5,6},{6,5},{7,8},{8,7},{9,10},{10,... | collective-permute-start | bytes 368648 | tf_op jit(solution)/shard_map/ppermute | solution.py:666
  23.9 7.5 %collective-permute-start.3 = (f32[40,768]{1,0:T(8,128)S(1)}, f32[40,768]{1,0:T(8,128)S(1)}, u32[]{:S(2)}, u32[]{:S(2)}) collective-permute-start(f32[40,768]{1,0:T(8,128)S(1)} %get-tuple-element.34), channel_id=1, source_target_pairs={{0,1},{1,0},{2,3},{3,2},{4,5},{5,4},{6,7},{7,6},{8,9},{9,8},{10,11... | collective-permute-start | bytes 368648 | tf_op jit(solution)/shard_map/ppermute | solution.py:665
  26.2 4.2 %collective-permute-start = (f32[2,40,256]{2,1,0:T(8,128)S(1)}, f32[2,40,256]{2,1,0:T(8,128)S(1)}, u32[]{:S(2)}, u32[]{:S(2)}) collective-permute-start(f32[2,40,256]{2,1,0:T(8,128)S(1)} %get-tuple-element.28), channel_id=1, source_target_pairs={{0,15},{1,2},{2,1},{3,4},{4,3},{5,6},{6,5},{7,8},{8,7},{9,10},{10,... | collective-permute-start | bytes 245768 | tf_op jit(solution)/shard_map/ppermute | solution.py:666
  26.2 4.2 %collective-permute-start.1 = (f32[2,40,256]{2,1,0:T(8,128)S(1)}, f32[2,40,256]{2,1,0:T(8,128)S(1)}, u32[]{:S(2)}, u32[]{:S(2)}) collective-permute-start(f32[2,40,256]{2,1,0:T(8,128)S(1)} %get-tuple-element.29), channel_id=1, source_target_pairs={{0,1},{1,0},{2,3},{3,2},{4,5},{5,4},{6,7},{7,6},{8,9},{9,8},{10,11... | collective-permute-start | bytes 245768 | tf_op jit(solution)/shard_map/ppermute | solution.py:665
  28.5 1.9 %copy-start.1 = (s32[128]{0:T(128)S(1)}, s32[128]{0:T(128)}, u32[]{:S(2)}) copy-start(s32[128]{0:T(128)} %tag_ref.1) | copy-start | bytes 1540
  45.2 4.5 %collective-permute-start.4 = (f32[4,32,128]{2,1,0:T(8,128)S(1)}, f32[4,32,128]{2,1,0:T(8,128)S(1)}, u32[]{:S(2)}, u32[]{:S(2)}) collective-permute-start(f32[4,32,128]{2,1,0:T(8,128)S(1)} %get-tuple-element.36), channel_id=1, source_target_pairs={{0,15},{1,2},{2,1},{3,4},{4,3},{5,6},{6,5},{7,8},{8,7},{9,10},{10,... | collective-permute-start | bytes 196616 | tf_op jit(solution)/shard_map/ppermute | solution.py:666
  47.8 2.2 %collective-permute-start.5 = (f32[4,32,128]{2,1,0:T(8,128)S(1)}, f32[4,32,128]{2,1,0:T(8,128)S(1)}, u32[]{:S(2)}, u32[]{:S(2)}) collective-permute-start(f32[4,32,128]{2,1,0:T(8,128)S(1)} %get-tuple-element.37), channel_id=1, source_target_pairs={{0,1},{1,0},{2,3},{3,2},{4,5},{5,4},{6,7},{7,6},{8,9},{9,8},{10,11... | collective-permute-start | bytes 196616 | tf_op jit(solution)/shard_map/ppermute | solution.py:665
  50.4 4.4 %collective-permute-start.6 = (f32[4,32,128]{2,1,0:T(8,128)S(1)}, f32[4,32,128]{2,1,0:T(8,128)S(1)}, u32[]{:S(2)}, u32[]{:S(2)}) collective-permute-start(f32[4,32,128]{2,1,0:T(8,128)S(1)} %get-tuple-element.40), channel_id=1, source_target_pairs={{0,15},{1,2},{2,1},{3,4},{4,3},{5,6},{6,5},{7,8},{8,7},{9,10},{10,... | collective-permute-start | bytes 196616 | tf_op jit(solution)/shard_map/ppermute | solution.py:666
  52.0 3.4 %collective-permute-start.7 = (f32[4,32,128]{2,1,0:T(8,128)S(1)}, f32[4,32,128]{2,1,0:T(8,128)S(1)}, u32[]{:S(2)}, u32[]{:S(2)}) collective-permute-start(f32[4,32,128]{2,1,0:T(8,128)S(1)} %get-tuple-element.41), channel_id=1, source_target_pairs={{0,1},{1,0},{2,3},{3,2},{4,5},{5,4},{6,7},{7,6},{8,9},{9,8},{10,11... | collective-permute-start | bytes 196616 | tf_op jit(solution)/shard_map/ppermute | solution.py:665
  56.4 16.2 %all-to-all-start.2 = ((f32[16,8,128]{2,1,0:T(8,128)}), f32[16,8,128]{2,1,0:T(8,128)S(1)}, u32[]{:S(2)}, u32[]{:S(2)}) async-start(f32[16,8,128]{2,1,0:T(8,128)} %get-tuple-element.43), calls=%async_computation.2 | async-start | bytes 131072 | tf_op jit(solution)/shard_map/all_to_all | solution.py:715

commit v10 on v9

--- a/solution.py
+++ b/solution.py
@@ -547,16 +547,39 @@
         packed_ref[n : n + 1, 0:32] = mode_sums(moment, turn_ref.at[n])
 
 
+def store_natural(tiles, out_ref, row, column_ref):
+    columns = merge_columns(tiles)
+    for i in range(5):
+        first = 32 * (5 * row + i)
+        for t in range(4):
+            column_ref[pl.ds(first + t, 8, stride=4), :] = columns[i][8 * t : 8 * t + 8]
+        out_ref[row, :, 128 * i : 128 * i + 128] = column_ref[first : first + 32, :]
+
+
+def natural_kernel(vector_ref, out_ref, column_ref):
+    for j in range(5):
+        store_natural([vector_ref[j * 5 + i] for i in range(5)], out_ref, j, column_ref)
+
+
+def inner_kernel(joined_ref, second_ref, out_ref, column_ref):
+    _, center = mode_terms()
+    for j in range(1, 4):
+        tiles = [
+            joined_ref[n] - center * second_ref[n] for n in range(5 * j, 5 * j + 5)
+        ]
+        store_natural(tiles, out_ref, j - 1, column_ref)
+
+
 def third_kernel(
-    joined_ref, cross_in_ref, chip_in_ref, second_ref, packed_ref, vector_ref, sums_ref,
-    turn_ref,
+    joined_ref, cross_in_ref, chip_in_ref, second_ref, packed_ref, edge_ref, sums_ref, turn_ref,
+    column_ref,
 ):
     shift, center = mode_terms()
     applied = assembled(joined_ref, cross_in_ref, chip_in_ref)
     second = [second_ref[n] for n in range(25)]
     third = [applied[n] - center * second[n] for n in range(25)]
-    for n in range(25):
-        vector_ref[n] = third[n]
+    for row in range(2):
+        store_natural(third[20 * row : 20 * row + 5], edge_ref, row, column_ref)
     fourth = inner(third, third)
     moments = [fourth, energy(third, shift) - center * fourth]
     sums_ref[0] = packed_ref[...]
@@ -567,16 +590,6 @@
         sums_ref[p] = sums
 
 
-def natural_kernel(vector_ref, out_ref, column_ref):
-    for j in range(5):
-        tiles = merge_columns([vector_ref[j * 5 + i] for i in range(5)])
-        for i in range(5):
-            first = 32 * (5 * j + i)
-            for t in range(4):
-                column_ref[pl.ds(first + t, 8, stride=4), :] = tiles[i][8 * t : 8 * t + 8]
-            out_ref[j, :, 128 * i : 128 * i + 128] = column_ref[first : first + 32, :]
-
-
 def tree(terms):
     while len(terms) > 1:
         terms = [sum(terms[n + 1 : n + 2], terms[n]) for n in range(0, len(terms), 2)]
@@ -584,7 +597,7 @@
 
 
 def combine_kernel(
-    sums_ref, first_ref, second_ref, third_ref, out_hbm, turn_ref, result_ref, sent
+    sums_ref, first_ref, second_ref, inner_ref, edge_ref, out_hbm, turn_ref, result_ref, sent
 ):
     total = tree([sums_ref[p] for p in range(GRID)])
     moment = [total[n : n + 1] for n in range(6)]
@@ -636,9 +649,8 @@
     weight = [turned[:, a : a + 1] for a in range(3)]
     copies = []
     for j in range(5):
-        result_ref[j] = (
-            weight[0] * first_ref[j] + weight[1] * second_ref[j] + weight[2] * third_ref[j]
-        )
+        third = inner_ref[j - 1] if 0 < j < 4 else edge_ref[j // 4]
+        result_ref[j] = weight[0] * first_ref[j] + weight[1] * second_ref[j] + weight[2] * third
         copies.append(pltpu.make_async_copy(result_ref.at[j], out_hbm.at[j], sent.at[j]))
         copies[j].start()
     for copy in copies:
@@ -708,20 +720,25 @@
         early_kernel, [(8, 128)], first, second, joined,
         scratch=[pltpu.VMEM((4, 32, 128), jnp.float32)],
     )
-    third, sums = call(
-        third_kernel, [nodes, (16, 8, 128)], joined, cross, chip, second, packed,
-        scratch=[pltpu.VMEM((2, 32, 128), jnp.float32)],
-    )
-    sums = lax.all_to_all(sums, "plane", 0, 0, tiled=True)
-    columns = [
+    natural = [
         call(
             natural_kernel, [(5, 32, 640)], vector,
             scratch=[pltpu.VMEM((800, 128), jnp.float32)],
         )[0]
-        for vector in (first, second, third)
+        for vector in (first, second)
     ]
+    (inside,) = call(
+        inner_kernel, [(3, 32, 640)], joined, second,
+        scratch=[pltpu.VMEM((480, 128), jnp.float32)],
+    )
+    edges, sums = call(
+        third_kernel, [(2, 32, 640), (16, 8, 128)], joined, cross, chip, second, packed,
+        scratch=[pltpu.VMEM((2, 32, 128), jnp.float32), pltpu.VMEM((320, 128), jnp.float32)],
+    )
+    sums = lax.all_to_all(sums, "plane", 0, 0, tiled=True)
     (columns,) = call(
-        combine_kernel, [(5, 32, 640)], sums, *columns, out_space=pltpu.HBM,
+        combine_kernel, [(5, 32, 640)], sums, *natural, inside, edges,
+        out_space=pltpu.HBM,
         scratch=[
             pltpu.VMEM((8, 128), jnp.float32), pltpu.VMEM((5, 32, 640), jnp.float32),
             pltpu.SemaphoreType.DMA((5,)),

time: 73.9 us -> 74 us (level)
  no operation moved by 1% of the time
where the time goes in v10:
time: 74 us; the launch traced here: 73.7 us
  blocking collectives  28.9 us (39%)
  starting transfers between devices  24.7 us (33%)
  Pallas kernels  12.5 us (17%)
  waiting for transfers between devices  7.58 us (10%)
    all_to_all x1, blocking collectives, on_device(): modal = lax.all_to_all(packed, 'span', 0, 0, tiled=True)  17 us
    pallas_call x13, Pallas kernels, call(): pl.pallas_call(kernel, out_shape=[jax.ShapeDtypeStruct(s, jnp.float32) fo...  12.5 us
    all_to_all x1, blocking collectives, on_device(): load = lax.all_to_all(sent, 'span', 0, 0, tiled=True)  11.9 us
    all_to_all x1, starting transfers between devices, on_device(): sums = lax.all_to_all(sums, 'plane', 0, 0, tiled=True)  8.43 us
    ppermute x4, starting transfers between devices, swap_traces(): chip = lax.ppermute(chip, 'plane', [(p, p ^ 1) for p in range(GRID)])  8.36 us
    ppermute x4, starting transfers between devices, swap_traces(): cross = lax.ppermute(cross, 'plane', partner)  7.88 us
    all_to_all x1, waiting for transfers between devices, on_device(): sums = lax.all_to_all(sums, 'plane', 0, 0, tiled=True)  5.87 us
  transfers between devices with their start and end apart: 9, of which 5 were waited for; matrix products, arithmetic and copies ran while one was open for 0% of the time, Pallas kernels for 7%

profile of v10, /device:TPU:1, one launch (start us, length us, event | category | flops | bytes accessed | tf_op | source)
XLA Modules:
  0.0 73.7 jit_solution(13405804382186614909)
XLA Ops:
  0.0 2.1 %shard_map.37 = f32[16,56,128]{2,1,0:T(8,128)S(1)} custom-call(f32[5,32,640]{2,1,0:T(8,128)} %bitcast.2), custom_call_target="tpu_custom_call" | custom-call | tf_op jit(solution)/shard_map/pallas_call | solution.py:664
  2.2 17.0 %all_to_all.15.modal_ref = f32[16,56,128]{2,1,0:T(8,128)S(1)} all-to-all(f32[16,56,128]{2,1,0:T(8,128)S(1)} %shard_map.37), channel_id=1, replica_groups=mesh['span'=16,'plane'=16] {'span'}, dimensions={0} | all-to-all | bytes 917504 | tf_op jit(solution)/shard_map/all_to_all | solution.py:693
  19.2 1.0 %shard_map.38 = (f32[200,768]{1,0:T(8,128)S(1)}, f32[16,768]{1,0:T(8,128)S(1)}, f32[80,768]{1,0:T(8,128)S(1)}, f32[2,40,256]{2,1,0:T(8,128)S(1)}, f32[2,40,256]{...) custom-call(f32[16,56,128]{2,1,0:T(8,128)S(1)} %all_to_all.15.modal_ref, ...), custom_call_target="tpu_custom_call" | custom-call | tf_op jit(solution)/shard_map/pallas_call | solution.py:664
  20.2 3.7 %collective-permute-start.2 = (f32[40,768]{1,0:T(8,128)S(1)}, f32[40,768]{1,0:T(8,128)S(1)}, u32[]{:S(2)}, u32[]{:S(2)}) collective-permute-start(f32[40,768]{1,0:T(8,128)S(1)} %get-tuple-element.33), channel_id=1, source_target_pairs={{0,15},{1,2},{2,1},{3,4},{4,3},{5,6},{6,5},{7,8},{8,7},{9,10},{10,... | collective-permute-start | bytes 368648 | tf_op jit(solution)/shard_map/ppermute | solution.py:678
  23.9 2.3 %collective-permute-start.3 = (f32[40,768]{1,0:T(8,128)S(1)}, f32[40,768]{1,0:T(8,128)S(1)}, u32[]{:S(2)}, u32[]{:S(2)}) collective-permute-start(f32[40,768]{1,0:T(8,128)S(1)} %get-tuple-element.34), channel_id=1, source_target_pairs={{0,1},{1,0},{2,3},{3,2},{4,5},{5,4},{6,7},{7,6},{8,9},{9,8},{10,11... | collective-permute-start | bytes 368648 | tf_op jit(solution)/shard_map/ppermute | solution.py:677
  26.2 2.2 %collective-permute-start.1 = (f32[2,40,256]{2,1,0:T(8,128)S(1)}, f32[2,40,256]{2,1,0:T(8,128)S(1)}, u32[]{:S(2)}, u32[]{:S(2)}) collective-permute-start(f32[2,40,256]{2,1,0:T(8,128)S(1)} %get-tuple-element.29), channel_id=1, source_target_pairs={{0,1},{1,0},{2,3},{3,2},{4,5},{5,4},{6,7},{7,6},{8,9},{9,8},{10,11... | collective-permute-start | bytes 245768 | tf_op jit(solution)/shard_map/ppermute | solution.py:677
  28.5 1.7 %shard_map.39.inside_ref = f32[2,256,256]{2,1,0:T(8,128)S(1)} custom-call(f32[16,56,128]{2,1,0:T(8,128)S(1)} %all_to_all.15.modal_ref, f32[200,768]{1,0:T(8,128)S(1)} %get-tuple-element.25.field_ref, f32[16,768]{1,0:T(8,128)S(1)} %get-tuple-element.26.side_ref, f32[80,768]{1,0:T(8,128)S(1)} %get-tuple-element.27.edge_ref, bf16[2,2,256,384]{3,2,1,0:T(8,128)(2,1)S(1)} %copy-done), custom_call_target="tpu_custom_call" | custom-call | tf_op jit(solution)/shard_map/pallas_call | solution.py:664
  30.4 1.0 %shard_map.40 = (f32[80,768]{1,0:T(8,128)S(1)}, f32[80,768]{1,0:T(8,128)S(1)}, f32[2,256,128]{2,1,0:T(8,128)S(1)}) custom-call(s32[128]{0:T(128)S(1)} %copy-done.1, f32[200,768]{1,0:T(8,128)S(1)} %get-tuple-element.25.field_ref, f32[2,40,256]{2,1,0:T(8,128)S(1)} %collective-permute-done.cross_ref, f32[2,40,256]{2,1,0:T(8,128)S(1)} %collective-permute-done.1.chip_ref, ...), custom_call_target="tpu_custom_call" | custom-call | tf_op jit(solution)/shard_map/pallas_call | solution.py:664
  31.4 0.8 %shard_map.41 = f32[16,56,128]{2,1,0:T(8,128)S(1)} custom-call(f32[2,256,256]{2,1,0:T(8,128)S(1)} %shard_map.39.inside_ref, f32[80,768]{1,0:T(8,128)S(1)} %get-tuple-element.30.lift_ref, f32[80,768]{1,0:T(8,128)S(1)} %get-tuple-element.31.flux_ref, f32[2,256,128]{2,1,0:T(8,128)S(1)} %get-tuple-element.32.facing_ref, ...), custom_call_target="tpu_custom_call" | custom-call | tf_op jit(solution)/shard_map/pallas_call | solution.py:664
  32.3 11.9 %all_to_all.16.modal_ref = f32[16,56,128]{2,1,0:T(8,128)S(1)} all-to-all(f32[16,56,128]{2,1,0:T(8,128)S(1)} %shard_map.41), channel_id=1, replica_groups=mesh['span'=16,'plane'=16] {'span'}, dimensions={0} | all-to-all | bytes 917504 | tf_op jit(solution)/shard_map/all_to_all | solution.py:711
  44.2 1.0 %shard_map.42 = (f32[25,32,128]{2,1,0:T(8,128)S(1)}, f32[25,32,128]{2,1,0:T(8,128)S(1)}, f32[4,32,128]{2,1,0:T(8,128)S(1)}, f32[4,32,128]{2,1,0:T(8,128)S(1)}) custom-call(f32[16,56,128]{2,1,0:T(8,128)S(1)} %all_to_all.16.modal_ref), custom_call_target="tpu_custom_call" | custom-call | tf_op jit(solution)/shard_map/pallas_call | solution.py:664
  45.2 2.6 %collective-permute-start.4 = (f32[4,32,128]{2,1,0:T(8,128)S(1)}, f32[4,32,128]{2,1,0:T(8,128)S(1)}, u32[]{:S(2)}, u32[]{:S(2)}) collective-permute-start(f32[4,32,128]{2,1,0:T(8,128)S(1)} %get-tuple-element.36), channel_id=1, source_target_pairs={{0,15},{1,2},{2,1},{3,4},{4,3},{5,6},{6,5},{7,8},{8,7},{9,10},{10,... | collective-permute-start | bytes 196616 | tf_op jit(solution)/shard_map/ppermute | solution.py:678
  47.8 1.3 %collective-permute-start.5 = (f32[4,32,128]{2,1,0:T(8,128)S(1)}, f32[4,32,128]{2,1,0:T(8,128)S(1)}, u32[]{:S(2)}, u32[]{:S(2)}) collective-permute-start(f32[4,32,128]{2,1,0:T(8,128)S(1)} %get-tuple-element.37), channel_id=1, source_target_pairs={{0,1},{1,0},{2,3},{3,2},{4,5},{5,4},{6,7},{7,6},{8,9},{9,8},{10,11... | collective-permute-start | bytes 196616 | tf_op jit(solution)/shard_map/ppermute | solution.py:677
  49.1 0.7 collective-permute-done.4.cross_in_ref
  50.4 1.6 %collective-permute-start.6 = (f32[4,32,128]{2,1,0:T(8,128)S(1)}, f32[4,32,128]{2,1,0:T(8,128)S(1)}, u32[]{:S(2)}, u32[]{:S(2)}) collective-permute-start(f32[4,32,128]{2,1,0:T(8,128)S(1)} %get-tuple-element.40), channel_id=1, source_target_pairs={{0,15},{1,2},{2,1},{3,4},{4,3},{5,6},{6,5},{7,8},{8,7},{9,10},{10,... | collective-permute-start | bytes 196616 | tf_op jit(solution)/shard_map/ppermute | solution.py:678
  52.0 2.5 %collective-permute-start.7 = (f32[4,32,128]{2,1,0:T(8,128)S(1)}, f32[4,32,128]{2,1,0:T(8,128)S(1)}, u32[]{:S(2)}, u32[]{:S(2)}) collective-permute-start(f32[4,32,128]{2,1,0:T(8,128)S(1)} %get-tuple-element.41), channel_id=1, source_target_pairs={{0,1},{1,0},{2,3},{3,2},{4,5},{5,4},{6,7},{7,6},{8,9},{9,8},{10,11... | collective-permute-start | bytes 196616 | tf_op jit(solution)/shard_map/ppermute | solution.py:677
  54.8 0.6 collective-permute-done.7.chip_in_ref
  55.4 1.1 %shard_map.45 = (f32[2,32,640]{2,1,0:T(8,128)S(1)}, f32[16,8,128]{2,1,0:T(8,128)}) custom-call(f32[25,32,128]{2,1,0:T(8,128)S(1)} %get-tuple-element.39.joined_ref, f32[4,32,128]{2,1,0:T(8,128)S(1)} %collective-permute-done.6.cross_in_ref, f32[4,32,128]{2,1,0:T(8,128)S(1)} %collective-permute-done.7.chip_in_ref, ...), custom_call_target="tpu_custom_call" | custom-call | tf_op jit(solution)/shard_map/pallas_call | solution.py:664
  56.4 8.4 %all-to-all-start.2 = ((f32[16,8,128]{2,1,0:T(8,128)}), f32[16,8,128]{2,1,0:T(8,128)S(1)}, u32[]{:S(2)}, u32[]{:S(2)}) async-start(f32[16,8,128]{2,1,0:T(8,128)} %get-tuple-element.43), calls=%async_computation.2 | async-start | bytes 131072 | tf_op jit(solution)/shard_map/all_to_all | solution.py:738
  64.9 0.7 shard_map.46.first_ref
  65.6 0.7 shard_map.47.second_ref
  66.3 0.5 shard_map.48.inner_ref
  66.8 5.9 %all-to-all-done.2.sums_ref = f32[16,8,128]{2,1,0:T(8,128)S(1)} async-done(((f32[16,8,128]{2,1,0:T(8,128)}), f32[16,8,128]{2,1,0:T(8,128)S(1)}, u32[]{:S(2)}, u32[]{:S(2)}) %all-to-all-start.2) | async-done | bytes 65568 | tf_op jit(solution)/shard_map/all_to_all | solution.py:738
  72.7 1.1 %shard_map.49 = f32[5,32,640]{2,1,0:T(8,128)} custom-call(f32[16,8,128]{2,1,0:T(8,128)S(1)} %all-to-all-done.2.sums_ref, f32[5,32,640]{2,1,0:T(8,128)S(1)} %shard_map.46.first_ref, f32[5,32,640]{2,1,0:T(8,128)S(1)} %shard_map.47.second_ref, f32[3,32,640]{2,1,0:T(8,128)S(1)} %shard_map.48.inner_ref, f32[2,32,640]{2,1,0:T(8,128)S(1)} %get-tuple-element.44.edge_ref), custom_call_target="tpu_custom_call" | custom-call | tf_op jit(solution)/shard_map/pallas_call | solution.py:664
  (13 shorter events, 1.2 us)
Async XLA Ops:
  0.0 19.2 %copy-start = (bf16[2,2,256,384]{3,2,1,0:T(8,128)(2,1)S(1)}, bf16[2,2,256,384]{3,2,1,0:T(8,128)(2,1)}, u32[]{:S(2)}) copy-start(bf16[2,2,256,384]{3,2,1,0:T(8,128)(2,1)} %constant.2.clone.table_ref) | copy-start | bytes 2359300
  20.2 11.2 %collective-permute-start.2 = (f32[40,768]{1,0:T(8,128)S(1)}, f32[40,768]{1,0:T(8,128)S(1)}, u32[]{:S(2)}, u32[]{:S(2)}) collective-permute-start(f32[40,768]{1,0:T(8,128)S(1)} %get-tuple-element.33), channel_id=1, source_target_pairs={{0,15},{1,2},{2,1},{3,4},{4,3},{5,6},{6,5},{7,8},{8,7},{9,10},{10,... | collective-permute-start | bytes 368648 | tf_op jit(solution)/shard_map/ppermute | solution.py:678
  23.9 7.5 %collective-permute-start.3 = (f32[40,768]{1,0:T(8,128)S(1)}, f32[40,768]{1,0:T(8,128)S(1)}, u32[]{:S(2)}, u32[]{:S(2)}) collective-permute-start(f32[40,768]{1,0:T(8,128)S(1)} %get-tuple-element.34), channel_id=1, source_target_pairs={{0,1},{1,0},{2,3},{3,2},{4,5},{5,4},{6,7},{7,6},{8,9},{9,8},{10,11... | collective-permute-start | bytes 368648 | tf_op jit(solution)/shard_map/ppermute | solution.py:677
  26.2 4.2 %collective-permute-start = (f32[2,40,256]{2,1,0:T(8,128)S(1)}, f32[2,40,256]{2,1,0:T(8,128)S(1)}, u32[]{:S(2)}, u32[]{:S(2)}) collective-permute-start(f32[2,40,256]{2,1,0:T(8,128)S(1)} %get-tuple-element.28), channel_id=1, source_target_pairs={{0,15},{1,2},{2,1},{3,4},{4,3},{5,6},{6,5},{7,8},{8,7},{9,10},{10,... | collective-permute-start | bytes 245768 | tf_op jit(solution)/shard_map/ppermute | solution.py:678
  26.2 4.2 %collective-permute-start.1 = (f32[2,40,256]{2,1,0:T(8,128)S(1)}, f32[2,40,256]{2,1,0:T(8,128)S(1)}, u32[]{:S(2)}, u32[]{:S(2)}) collective-permute-start(f32[2,40,256]{2,1,0:T(8,128)S(1)} %get-tuple-element.29), channel_id=1, source_target_pairs={{0,1},{1,0},{2,3},{3,2},{4,5},{5,4},{6,7},{7,6},{8,9},{9,8},{10,11... | collective-permute-start | bytes 245768 | tf_op jit(solution)/shard_map/ppermute | solution.py:677
  28.5 1.9 %copy-start.1 = (s32[128]{0:T(128)S(1)}, s32[128]{0:T(128)}, u32[]{:S(2)}) copy-start(s32[128]{0:T(128)} %tag_ref.1) | copy-start | bytes 1540
  45.2 4.5 %collective-permute-start.4 = (f32[4,32,128]{2,1,0:T(8,128)S(1)}, f32[4,32,128]{2,1,0:T(8,128)S(1)}, u32[]{:S(2)}, u32[]{:S(2)}) collective-permute-start(f32[4,32,128]{2,1,0:T(8,128)S(1)} %get-tuple-element.36), channel_id=1, source_target_pairs={{0,15},{1,2},{2,1},{3,4},{4,3},{5,6},{6,5},{7,8},{8,7},{9,10},{10,... | collective-permute-start | bytes 196616 | tf_op jit(solution)/shard_map/ppermute | solution.py:678
  47.8 2.2 %collective-permute-start.5 = (f32[4,32,128]{2,1,0:T(8,128)S(1)}, f32[4,32,128]{2,1,0:T(8,128)S(1)}, u32[]{:S(2)}, u32[]{:S(2)}) collective-permute-start(f32[4,32,128]{2,1,0:T(8,128)S(1)} %get-tuple-element.37), channel_id=1, source_target_pairs={{0,1},{1,0},{2,3},{3,2},{4,5},{5,4},{6,7},{7,6},{8,9},{9,8},{10,11... | collective-permute-start | bytes 196616 | tf_op jit(solution)/shard_map/ppermute | solution.py:677
  50.4 4.4 %collective-permute-start.6 = (f32[4,32,128]{2,1,0:T(8,128)S(1)}, f32[4,32,128]{2,1,0:T(8,128)S(1)}, u32[]{:S(2)}, u32[]{:S(2)}) collective-permute-start(f32[4,32,128]{2,1,0:T(8,128)S(1)} %get-tuple-element.40), channel_id=1, source_target_pairs={{0,15},{1,2},{2,1},{3,4},{4,3},{5,6},{6,5},{7,8},{8,7},{9,10},{10,... | collective-permute-start | bytes 196616 | tf_op jit(solution)/shard_map/ppermute | solution.py:678
  52.0 3.4 %collective-permute-start.7 = (f32[4,32,128]{2,1,0:T(8,128)S(1)}, f32[4,32,128]{2,1,0:T(8,128)S(1)}, u32[]{:S(2)}, u32[]{:S(2)}) collective-permute-start(f32[4,32,128]{2,1,0:T(8,128)S(1)} %get-tuple-element.41), channel_id=1, source_target_pairs={{0,1},{1,0},{2,3},{3,2},{4,5},{5,4},{6,7},{7,6},{8,9},{9,8},{10,11... | collective-permute-start | bytes 196616 | tf_op jit(solution)/shard_map/ppermute | solution.py:677
  56.4 16.2 %all-to-all-start.2 = ((f32[16,8,128]{2,1,0:T(8,128)}), f32[16,8,128]{2,1,0:T(8,128)S(1)}, u32[]{:S(2)}, u32[]{:S(2)}) async-start(f32[16,8,128]{2,1,0:T(8,128)} %get-tuple-element.43), calls=%async_computation.2 | async-start | bytes 131072 | tf_op jit(solution)/shard_map/all_to_all | solution.py:738

commit v11 on v10

--- a/solution.py
+++ b/solution.py
@@ -324,8 +324,19 @@
                 out_ref[parity, 128 * t : 128 * t + 128, lanes] = modal + change[t]
 
 
+def project_rows(planar, parity, table_ref):
+    folded = planar[:, :HALF] + planar[:, HALF:] if parity == 0 else planar[:, :HALF] - planar[:, HALF:]
+    return dot_split(halves(folded), (table_ref[0, parity], table_ref[1, parity]), ((1,), (1,)))
+
+
+def wave_factors(parity):
+    k = 2 * lax.broadcasted_iota(jnp.int32, (80, 128), 1) + parity
+    scale = jnp.where(k == 0, 1.0, 2.0) * (math.sqrt(KMODES) / PLANES * STEP_SIZE)
+    return scale, scale * (k.astype(jnp.float32) * (1.0 / KMODES))
+
+
 def lift_kernel(
-    tag_ref, field_ref, cross_ref, chip_ref, table_ref, lift_ref, flux_ref, modal_ref, outer_ref
+    tag_ref, field_ref, cross_ref, chip_ref, table_ref, lift_ref, base_ref, outer_ref
 ):
     bottom, top = at_ends()
     span = lax.axis_index("span")
@@ -335,14 +346,11 @@
         mirror = jnp.where((row == e) & (tag_ref[8 * span + e] == 1), -1.0, mirror)
     keep_lower = jnp.where(bottom, 0.0, 1.0)
     keep_upper = jnp.where(top, 0.0, 1.0)
-    gap = jnp.zeros((48, 256), jnp.float32)
-    outer = []
+    outer, modal = [], []
     for parity in range(2):
         below, above = from_partners(cross_ref[parity], chip_ref[parity])
         outer.append(jnp.concatenate([below, above], axis=0))
-        modal_ref[parity] = jnp.concatenate(
-            [keep_lower * below, keep_upper * above, gap], axis=0
-        ).T
+        modal.append(jnp.concatenate([keep_lower * below, keep_upper * above], axis=0))
     pair = synthesize(outer, table_ref)
     for q in range(2):
         outer_ref[:, HALF * q : HALF * q + HALF] = pair[q]
@@ -351,36 +359,40 @@
     inside = field_ref[0:40, :]
     below = outer_ref[0:40, :]
     lift_ref[0:40, :] = 10.0 * two_point(jnp.where(bottom, mirror * inside, below), inside)
-    flux_ref[0:40, :] = keep_lower * (0.5 * below * below)
+    flux_lower = keep_lower * (0.5 * below * below)
     inside = field_ref[160:200, :]
     above = outer_ref[40:80, :]
     lift_ref[40:80, :] = 10.0 * two_point(inside, jnp.where(top, inside, above))
-    flux_ref[40:80, :] = keep_upper * (0.5 * above * above)
-
-
-def facing_kernel(
-    inside_ref, lift_ref, flux_ref, facing_ref, cross_ref, chip_ref, table_ref, out_ref
-):
+    flux = jnp.concatenate([flux_lower, keep_upper * (0.5 * above * above)], axis=0)
+    for parity in range(2):
+        from_flux = project_rows(flux, parity, table_ref)
+        _, ratio = wave_factors(parity)
+        base_ref[parity, :, 0:128] = modal[parity][:, 0:128] - ratio * from_flux[:, 128:256]
+        base_ref[parity, :, 128:256] = modal[parity][:, 128:256] + ratio * from_flux[:, 0:128]
+
+
+def facing_kernel(inside_ref, lift_ref, base_ref, cross_ref, chip_ref, table_ref, out_ref):
     bottom, top = at_ends()
     below, above = from_partners(cross_ref[...], chip_ref[...])
     lift = lift_ref[0:40, :]
     rhs_lower = lift + jnp.where(bottom, 0.0, below - lift)
     lift = lift_ref[40:80, :]
     rhs_upper = jnp.where(top, 0.0, above + lift) - lift
-    gap = jnp.zeros((48, PLANES), jnp.float32)
-    planar = jnp.concatenate([rhs_lower, rhs_upper, gap, flux_ref[...], gap], axis=0)
+    rhs = jnp.concatenate([rhs_lower, rhs_upper], axis=0)
+    gap = jnp.zeros((48, 128), jnp.float32)
     lane = lax.broadcasted_iota(jnp.int32, (128, 128), 1)
     whole, rest = [], []
     for parity in range(2):
-        projected = project(planar, parity, table_ref)
-        change = tendency(parity, projected[:, 0:128], projected[:, 128:256])
+        from_rhs = project_rows(rhs, parity, table_ref)
+        scale, _ = wave_factors(parity)
         for t in range(2):
-            rows = slice(128 * t, 128 * t + 128)
-            extra = change[t] + facing_ref[parity, rows, :]
+            waves = slice(128 * t, 128 * t + 128)
+            nodal = base_ref[parity, :, waves] + scale * from_rhs[:, waves]
+            extra = jnp.concatenate([nodal, gap], axis=0).T
             lower = jnp.where(lane < 40, extra, 0.0)
             upper = pltpu.roll(jnp.where(lane < 40, 0.0, extra), 120, 1)
-            whole.append(inside_ref[parity, rows, 0:128] + lower)
-            rest.append(inside_ref[parity, rows, 128:256] + upper)
+            whole.append(inside_ref[parity, waves, 0:128] + lower)
+            rest.append(inside_ref[parity, waves, 128:256] + upper)
     for s in range(GRID):
         part = slice(8 * s, 8 * s + 8)
         pack_rows(
@@ -426,9 +438,10 @@
     return jnp.where(odd, chip, cross), jnp.where(odd, cross, chip)
 
 
-def local_operator(values, shift):
+def local_operator(values, shift, rows):
     out = []
-    for j in range(5):
+    for j in rows:
+        line = []
         for i in range(5):
             n = j * 5 + i
             mass = float(WEIGHTS[j] * WEIGHTS[i])
@@ -441,29 +454,41 @@
                 if other != j:
                     weight = VISCOUS * float(WEIGHTS[i] * STIFFNESS[j][other])
                     value = value + weight * values[other * 5 + i]
-            out.append(value)
+            line.append(value)
+        out += join_columns(line)
     return out
 
 
-def join_columns(values):
-    values = list(values)
-    for j in range(5):
-        joint = values[j * 5 + 4] + pltpu.roll(values[j * 5], 127, 1)
-        values[j * 5 + 4] = joint
-        values[j * 5] = pltpu.roll(joint, 1, 1)
-    return values
-
-
-def store_joined(values, joined_ref, cross_ref, chip_ref):
-    values = join_columns(values)
-    for n in range(25):
-        joined_ref[n] = values[n]
+def join_columns(line):
+    joint = line[4] + pltpu.roll(line[0], 127, 1)
+    return [pltpu.roll(joint, 1, 1), *line[1:4], joint]
+
+
+def store_edges(values, shift, edge_ref, cross_ref, chip_ref):
+    image = local_operator(values, shift, (0, 4))
+    for n in range(10):
+        edge_ref[n] = image[n]
     for i in range(4):
-        cross_ref[i], chip_ref[i] = to_partners(values[i], values[20 + i])
-
-
-def assembled(joined_ref, cross_ref, chip_ref):
-    values = [joined_ref[n] for n in range(25)]
+        cross_ref[i], chip_ref[i] = to_partners(image[i], image[5 + i])
+
+
+def fill_kernel(vector_ref, inner_ref):
+    shift, _ = mode_terms()
+    image = local_operator([vector_ref[n] for n in range(25)], shift, (1, 2, 3))
+    for n in range(15):
+        inner_ref[n] = image[n]
+
+
+def unassembled(edge_ref, inner_ref):
+    return (
+        [edge_ref[n] for n in range(5)]
+        + [inner_ref[n] for n in range(15)]
+        + [edge_ref[5 + n] for n in range(5)]
+    )
+
+
+def assembled(edge_ref, inner_ref, cross_ref, chip_ref):
+    values = unassembled(edge_ref, inner_ref)
     bottom, top = at_ends()
     for i in range(4):
         below, above = from_partners(cross_ref[i], chip_ref[i])
@@ -499,7 +524,7 @@
     return total
 
 
-def first_kernel(modal_ref, vector_ref, next_ref, cross_ref, chip_ref):
+def first_kernel(modal_ref, vector_ref, edge_ref, cross_ref, chip_ref):
     shift, _ = mode_terms()
     values = exchange_chunks([modal_ref[s, 0:32, :] for s in range(GRID)])
     rest = []
@@ -508,21 +533,24 @@
         rest.append(jnp.concatenate(tiles + [unpack_last(tiles, 9)], axis=0))
     values += exchange_chunks(rest)
     values = [float(WEIGHTS[n // 5] * WEIGHTS[n % 5]) * values[n] for n in range(25)]
-    vector = join_columns(values)
+    vector = []
+    for j in range(5):
+        vector += join_columns(values[5 * j : 5 * j + 5])
     for n in range(25):
         vector_ref[n] = vector[n]
-    store_joined(local_operator(vector, shift), next_ref, cross_ref, chip_ref)
+    store_edges(vector, shift, edge_ref, cross_ref, chip_ref)
 
 
 def second_kernel(
-    joined_ref, cross_in_ref, chip_in_ref, before_ref, vector_ref, next_ref, cross_ref, chip_ref
+    edge_in_ref, inner_ref, cross_in_ref, chip_in_ref, before_ref, vector_ref, edge_ref, cross_ref,
+    chip_ref,
 ):
     shift, center = mode_terms()
-    applied = assembled(joined_ref, cross_in_ref, chip_in_ref)
+    applied = assembled(edge_in_ref, inner_ref, cross_in_ref, chip_in_ref)
     vector = [applied[n] - center * before_ref[n] for n in range(25)]
     for n in range(25):
         vector_ref[n] = vector[n]
-    store_joined(local_operator(vector, shift), next_ref, cross_ref, chip_ref)
+    store_edges(vector, shift, edge_ref, cross_ref, chip_ref)
 
 
 def mode_sums(moment, turn_ref):
@@ -531,14 +559,15 @@
     return jnp.sum(turn_ref[...].T, axis=0, keepdims=True)
 
 
-def early_kernel(first_ref, second_ref, joined_ref, packed_ref, turn_ref):
+def early_kernel(first_ref, second_ref, edge_ref, inner_ref, packed_ref, turn_ref):
     _, center = mode_terms()
     first = [first_ref[n] for n in range(25)]
     second = [second_ref[n] for n in range(25)]
     square = inner(second, second)
     product = None
+    image = unassembled(edge_ref, inner_ref)
     for n in range(25):
-        term = second[n] * joined_ref[n]
+        term = second[n] * image[n]
         term = term if 0 < n % 5 < 4 else 0.5 * term
         product = term if product is None else product + term
     moments = [inner(first, first), inner(first, second), square, product - center * square]
@@ -561,21 +590,21 @@
         store_natural([vector_ref[j * 5 + i] for i in range(5)], out_ref, j, column_ref)
 
 
-def inner_kernel(joined_ref, second_ref, out_ref, column_ref):
+def inner_kernel(inner_ref, second_ref, out_ref, column_ref):
     _, center = mode_terms()
     for j in range(1, 4):
         tiles = [
-            joined_ref[n] - center * second_ref[n] for n in range(5 * j, 5 * j + 5)
+            inner_ref[n - 5] - center * second_ref[n] for n in range(5 * j, 5 * j + 5)
         ]
         store_natural(tiles, out_ref, j - 1, column_ref)
 
 
 def third_kernel(
-    joined_ref, cross_in_ref, chip_in_ref, second_ref, packed_ref, edge_ref, sums_ref, turn_ref,
-    column_ref,
+    edge_in_ref, inner_ref, cross_in_ref, chip_in_ref, second_ref, packed_ref, edge_ref, sums_ref,
+    turn_ref, column_ref,
 ):
     shift, center = mode_terms()
-    applied = assembled(joined_ref, cross_in_ref, chip_in_ref)
+    applied = assembled(edge_in_ref, inner_ref, cross_in_ref, chip_in_ref)
     second = [second_ref[n] for n in range(25)]
     third = [applied[n] - center * second[n] for n in range(25)]
     for row in range(2):
@@ -629,6 +658,7 @@
     direction = residual
     result = [0.0, 0.0, 0.0]
     norm = moment[0]
+    inverse = 1.0 / norm
     for step in range(ITERS):
         applied = operator(direction)
         length = norm / product(direction, applied)
@@ -638,8 +668,9 @@
             padded = residual + [0.0]
             residual = [padded[a] - length * applied[a] for a in range(len(applied))]
             fresh = product(residual, residual)
-            ratio = fresh / norm
+            ratio = fresh * inverse
             norm = fresh
+            inverse = 1.0 / norm
             padded = direction + [0.0]
             direction = [residual[a] + ratio * padded[a] for a in range(len(residual))]
     turn_ref[...] = jnp.zeros((8, 128), jnp.float32)
@@ -702,22 +733,24 @@
         inside_kernel, [(2, 256, 256)], modal, field, side, edge, table, covers=False,
         scratch=[pltpu.VMEM((120, PLANES), jnp.float32)],
     )
-    lift, flux, facing = call(
-        lift_kernel, [(80, PLANES), (80, PLANES), (2, 256, 128)], wall_tag, field,
-        *modal_traces, table, smem=(0,), scratch=[pltpu.VMEM((80, PLANES), jnp.float32)],
-        covers=False,
-    )
-    (sent,) = call(facing_kernel, [(16, 56, 128)], inside, lift, flux, facing, *rhs_traces, table)
+    lift, base = call(
+        lift_kernel, [(80, PLANES), (2, 80, 256)], wall_tag, field, *modal_traces, table,
+        smem=(0,), scratch=[pltpu.VMEM((80, PLANES), jnp.float32)], covers=False,
+    )
+    (sent,) = call(facing_kernel, [(16, 56, 128)], inside, lift, base, *rhs_traces, table)
     load = lax.all_to_all(sent, "span", 0, 0, tiled=True)
     nodes, trace = (25, 32, 128), (4, 32, 128)
-    first, joined, cross, chip = call(first_kernel, [nodes, nodes, trace, trace], load)
+    edges, inner_rows = (10, 32, 128), (15, 32, 128)
+    first, edge, cross, chip = call(first_kernel, [nodes, edges, trace, trace], load)
     cross, chip = swap_traces(cross, chip)
-    second, joined, cross, chip = call(
-        second_kernel, [nodes, nodes, trace, trace], joined, cross, chip, first
+    (filled,) = call(fill_kernel, [inner_rows], first)
+    second, edge, cross, chip = call(
+        second_kernel, [nodes, edges, trace, trace], edge, filled, cross, chip, first
     )
     cross, chip = swap_traces(cross, chip)
+    (filled,) = call(fill_kernel, [inner_rows], second)
     (packed,) = call(
-        early_kernel, [(8, 128)], first, second, joined,
+        early_kernel, [(8, 128)], first, second, edge, filled,
         scratch=[pltpu.VMEM((4, 32, 128), jnp.float32)],
     )
     natural = [
@@ -728,11 +761,12 @@
         for vector in (first, second)
     ]
     (inside,) = call(
-        inner_kernel, [(3, 32, 640)], joined, second,
+        inner_kernel, [(3, 32, 640)], filled, second,
         scratch=[pltpu.VMEM((480, 128), jnp.float32)],
     )
     edges, sums = call(
-        third_kernel, [(2, 32, 640), (16, 8, 128)], joined, cross, chip, second, packed,
+        third_kernel, [(2, 32, 640), (16, 8, 128)], edge, filled, cross, chip, second,
+        packed,
         scratch=[pltpu.VMEM((2, 32, 128), jnp.float32), pltpu.VMEM((320, 128), jnp.float32)],
     )
     sums = lax.all_to_all(sums, "plane", 0, 0, tiled=True)

time: 74 us -> 74.1 us (level)
    pallas_call x13 -> x15, Pallas kernels: 12.5 us -> 13.2 us  [call(): pl.pallas_call(kernel, out_shape=[jax.ShapeDtypeStruct(s, jnp.float32) fo...]
  transfers between devices with their start and end apart: 9 -> 9, of which waited for: 5 -> 5; matrix products, arithmetic and copies ran while one was open for 0% -> 0% of each run, Pallas kernels for 7% -> 8%
where the time goes in v11:
time: 74.1 us; the launch traced here: 73.8 us
  blocking collectives  28.9 us (39%)
  starting transfers between devices  24.6 us (33%)
  Pallas kernels  13.2 us (18%)
  waiting for transfers between devices  6.99 us (9%)
    all_to_all x1, blocking collectives, on_device(): modal = lax.all_to_all(packed, 'span', 0, 0, tiled=True)  17 us
    pallas_call x15, Pallas kernels, call(): pl.pallas_call(kernel, out_shape=[jax.ShapeDtypeStruct(s, jnp.float32) fo...  13.2 us
    all_to_all x1, blocking collectives, on_device(): load = lax.all_to_all(sent, 'span', 0, 0, tiled=True)  11.9 us
    all_to_all x1, starting transfers between devices, on_device(): sums = lax.all_to_all(sums, 'plane', 0, 0, tiled=True)  8.39 us
    ppermute x4, starting transfers between devices, swap_traces(): chip = lax.ppermute(chip, 'plane', [(p, p ^ 1) for p in range(GRID)])  8.34 us
    ppermute x4, starting transfers between devices, swap_traces(): cross = lax.ppermute(cross, 'plane', partner)  7.9 us
    all_to_all x1, waiting for transfers between devices, on_device(): sums = lax.all_to_all(sums, 'plane', 0, 0, tiled=True)  5.86 us
  transfers between devices with their start and end apart: 9, of which 5 were waited for; matrix products, arithmetic and copies ran while one was open for 0% of the time, Pallas kernels for 8%

profile of v11, /device:TPU:1, one launch (start us, length us, event | category | flops | bytes accessed | tf_op | source)
XLA Modules:
  0.0 73.8 jit_solution(3670056204511318565)
XLA Ops:
  0.0 2.1 %shard_map.37 = f32[16,56,128]{2,1,0:T(8,128)S(1)} custom-call(f32[5,32,640]{2,1,0:T(8,128)} %bitcast.2), custom_call_target="tpu_custom_call" | custom-call | tf_op jit(solution)/shard_map/pallas_call | solution.py:695
  2.2 17.0 %all_to_all.15.modal_ref = f32[16,56,128]{2,1,0:T(8,128)S(1)} all-to-all(f32[16,56,128]{2,1,0:T(8,128)S(1)} %shard_map.37), channel_id=1, replica_groups=mesh['span'=16,'plane'=16] {'span'}, dimensions={0} | all-to-all | bytes 917504 | tf_op jit(solution)/shard_map/all_to_all | solution.py:724
  19.2 1.0 %shard_map.38 = (f32[200,768]{1,0:T(8,128)S(1)}, f32[16,768]{1,0:T(8,128)S(1)}, f32[80,768]{1,0:T(8,128)S(1)}, f32[2,40,256]{2,1,0:T(8,128)S(1)}, f32[2,40,256]{...) custom-call(f32[16,56,128]{2,1,0:T(8,128)S(1)} %all_to_all.15.modal_ref, ...), custom_call_target="tpu_custom_call" | custom-call | tf_op jit(solution)/shard_map/pallas_call | solution.py:695
  20.2 3.7 %collective-permute-start.2 = (f32[40,768]{1,0:T(8,128)S(1)}, f32[40,768]{1,0:T(8,128)S(1)}, u32[]{:S(2)}, u32[]{:S(2)}) collective-permute-start(f32[40,768]{1,0:T(8,128)S(1)} %get-tuple-element.31), channel_id=1, source_target_pairs={{0,15},{1,2},{2,1},{3,4},{4,3},{5,6},{6,5},{7,8},{8,7},{9,10},{10,... | collective-permute-start | bytes 368648 | tf_op jit(solution)/shard_map/ppermute | solution.py:709
  23.9 2.3 %collective-permute-start.3 = (f32[40,768]{1,0:T(8,128)S(1)}, f32[40,768]{1,0:T(8,128)S(1)}, u32[]{:S(2)}, u32[]{:S(2)}) collective-permute-start(f32[40,768]{1,0:T(8,128)S(1)} %get-tuple-element.32), channel_id=1, source_target_pairs={{0,1},{1,0},{2,3},{3,2},{4,5},{5,4},{6,7},{7,6},{8,9},{9,8},{10,11... | collective-permute-start | bytes 368648 | tf_op jit(solution)/shard_map/ppermute | solution.py:708
  26.3 2.2 %collective-permute-start.1 = (f32[2,40,256]{2,1,0:T(8,128)S(1)}, f32[2,40,256]{2,1,0:T(8,128)S(1)}, u32[]{:S(2)}, u32[]{:S(2)}) collective-permute-start(f32[2,40,256]{2,1,0:T(8,128)S(1)} %get-tuple-element.28), channel_id=1, source_target_pairs={{0,1},{1,0},{2,3},{3,2},{4,5},{5,4},{6,7},{7,6},{8,9},{9,8},{10,11... | collective-permute-start | bytes 245768 | tf_op jit(solution)/shard_map/ppermute | solution.py:708
  28.5 1.8 %shard_map.39.inside_ref = f32[2,256,256]{2,1,0:T(8,128)S(1)} custom-call(f32[16,56,128]{2,1,0:T(8,128)S(1)} %all_to_all.15.modal_ref, f32[200,768]{1,0:T(8,128)S(1)} %get-tuple-element.24.field_ref, f32[16,768]{1,0:T(8,128)S(1)} %get-tuple-element.25.side_ref, f32[80,768]{1,0:T(8,128)S(1)} %get-tuple-element.26.edge_ref, bf16[2,2,256,384]{3,2,1,0:T(8,128)(2,1)S(1)} %copy-done), custom_call_target="tpu_custom_call" | custom-call | tf_op jit(solution)/shard_map/pallas_call | solution.py:695
  30.4 1.4 %shard_map.40 = (f32[80,768]{1,0:T(8,128)S(1)}, f32[2,80,256]{2,1,0:T(8,128)S(1)}) custom-call(s32[128]{0:T(128)S(1)} %copy-done.1, f32[200,768]{1,0:T(8,128)S(1)} %get-tuple-element.24.field_ref, f32[2,40,256]{2,1,0:T(8,128)S(1)} %collective-permute-done.cross_ref, f32[2,40,256]{2,1,0:T(8,128)S(1)} %collective-permute-done.1.chip_ref, ...), custom_call_target="tpu_custom_call" | custom-call | tf_op jit(solution)/shard_map/pallas_call | solution.py:695
  31.9 0.8 %shard_map.41 = f32[16,56,128]{2,1,0:T(8,128)S(1)} custom-call(f32[2,256,256]{2,1,0:T(8,128)S(1)} %shard_map.39.inside_ref, f32[80,768]{1,0:T(8,128)S(1)} %get-tuple-element.29.lift_ref, f32[2,80,256]{2,1,0:T(8,128)S(1)} %get-tuple-element.30.base_ref, f32[40,768]{1,0:T(8,128)S(1)} %collective-permute-done.2.cross_ref, ...), custom_call_target="tpu_custom_call" | custom-call | tf_op jit(solution)/shard_map/pallas_call | solution.py:695
  32.7 11.9 %all_to_all.16.modal_ref = f32[16,56,128]{2,1,0:T(8,128)S(1)} all-to-all(f32[16,56,128]{2,1,0:T(8,128)S(1)} %shard_map.41), channel_id=1, replica_groups=mesh['span'=16,'plane'=16] {'span'}, dimensions={0} | all-to-all | bytes 917504 | tf_op jit(solution)/shard_map/all_to_all | solution.py:741
  44.6 0.8 %shard_map.42 = (f32[25,32,128]{2,1,0:T(8,128)S(1)}, f32[10,32,128]{2,1,0:T(8,128)S(1)}, f32[4,32,128]{2,1,0:T(8,128)S(1)}, f32[4,32,128]{2,1,0:T(8,128)S(1)}) custom-call(f32[16,56,128]{2,1,0:T(8,128)S(1)} %all_to_all.16.modal_ref), custom_call_target="tpu_custom_call" | custom-call | tf_op jit(solution)/shard_map/pallas_call | solution.py:695
  45.4 2.6 %collective-permute-start.4 = (f32[4,32,128]{2,1,0:T(8,128)S(1)}, f32[4,32,128]{2,1,0:T(8,128)S(1)}, u32[]{:S(2)}, u32[]{:S(2)}) collective-permute-start(f32[4,32,128]{2,1,0:T(8,128)S(1)} %get-tuple-element.35), channel_id=1, source_target_pairs={{0,15},{1,2},{2,1},{3,4},{4,3},{5,6},{6,5},{7,8},{8,7},{9,10},{10,... | collective-permute-start | bytes 196616 | tf_op jit(solution)/shard_map/ppermute | solution.py:709
  48.0 1.3 %collective-permute-start.5 = (f32[4,32,128]{2,1,0:T(8,128)S(1)}, f32[4,32,128]{2,1,0:T(8,128)S(1)}, u32[]{:S(2)}, u32[]{:S(2)}) collective-permute-start(f32[4,32,128]{2,1,0:T(8,128)S(1)} %get-tuple-element.36), channel_id=1, source_target_pairs={{0,1},{1,0},{2,3},{3,2},{4,5},{5,4},{6,7},{7,6},{8,9},{9,8},{10,11... | collective-permute-start | bytes 196616 | tf_op jit(solution)/shard_map/ppermute | solution.py:708
  49.6 0.4 collective-permute-done.4.cross_in_ref
  50.5 1.6 %collective-permute-start.6 = (f32[4,32,128]{2,1,0:T(8,128)S(1)}, f32[4,32,128]{2,1,0:T(8,128)S(1)}, u32[]{:S(2)}, u32[]{:S(2)}) collective-permute-start(f32[4,32,128]{2,1,0:T(8,128)S(1)} %get-tuple-element.39), channel_id=1, source_target_pairs={{0,15},{1,2},{2,1},{3,4},{4,3},{5,6},{6,5},{7,8},{8,7},{9,10},{10,... | collective-permute-start | bytes 196616 | tf_op jit(solution)/shard_map/ppermute | solution.py:709
  52.1 2.5 %collective-permute-start.7 = (f32[4,32,128]{2,1,0:T(8,128)S(1)}, f32[4,32,128]{2,1,0:T(8,128)S(1)}, u32[]{:S(2)}, u32[]{:S(2)}) collective-permute-start(f32[4,32,128]{2,1,0:T(8,128)S(1)} %get-tuple-element.40), channel_id=1, source_target_pairs={{0,1},{1,0},{2,3},{3,2},{4,5},{5,4},{6,7},{7,6},{8,9},{9,8},{10,11... | collective-permute-start | bytes 196616 | tf_op jit(solution)/shard_map/ppermute | solution.py:708
  55.2 0.3 collective-permute-done.7.chip_in_ref
  55.5 1.1 %shard_map.47 = (f32[2,32,640]{2,1,0:T(8,128)S(1)}, f32[16,8,128]{2,1,0:T(8,128)}) custom-call(f32[10,32,128]{2,1,0:T(8,128)S(1)} %get-tuple-element.37.edge_ref.edge_in_ref, f32[15,32,128]{2,1,0:T(8,128)S(1)} %shard_map.45.inner_ref, f32[4,32,128]{2,1,0:T(8,128)S(1)} %collective-permute-done.6.cross_in_ref, ...), custom_call_target="tpu_custom_call" | custom-call | tf_op jit(solution)/shard_map/pallas_call | solution.py:695
  56.6 8.4 %all-to-all-start.2 = ((f32[16,8,128]{2,1,0:T(8,128)}), f32[16,8,128]{2,1,0:T(8,128)S(1)}, u32[]{:S(2)}, u32[]{:S(2)}) async-start(f32[16,8,128]{2,1,0:T(8,128)} %get-tuple-element.41), calls=%async_computation.2 | async-start | bytes 131072 | tf_op jit(solution)/shard_map/all_to_all | solution.py:772
  65.0 0.7 shard_map.48.first_ref
  65.7 0.5 shard_map.50.inner_ref
  66.2 0.7 shard_map.49.second_ref
  66.9 5.9 %all-to-all-done.2.sums_ref = f32[16,8,128]{2,1,0:T(8,128)S(1)} async-done(((f32[16,8,128]{2,1,0:T(8,128)}), f32[16,8,128]{2,1,0:T(8,128)S(1)}, u32[]{:S(2)}, u32[]{:S(2)}) %all-to-all-start.2) | async-done | bytes 65568 | tf_op jit(solution)/shard_map/all_to_all | solution.py:772
  72.7 1.1 %shard_map.51 = f32[5,32,640]{2,1,0:T(8,128)} custom-call(f32[16,8,128]{2,1,0:T(8,128)S(1)} %all-to-all-done.2.sums_ref, f32[5,32,640]{2,1,0:T(8,128)S(1)} %shard_map.48.first_ref, f32[5,32,640]{2,1,0:T(8,128)S(1)} %shard_map.49.second_ref, f32[3,32,640]{2,1,0:T(8,128)S(1)} %shard_map.50.inner_ref, f32[2,32,640]{2,1,0:T(8,128)S(1)} %get-tuple-element.42.edge_ref), custom_call_target="tpu_custom_call" | custom-call | tf_op jit(solution)/shard_map/pallas_call | solution.py:695
  (15 shorter events, 1.6 us)
Async XLA Ops:
  0.0 19.2 %copy-start = (bf16[2,2,256,384]{3,2,1,0:T(8,128)(2,1)S(1)}, bf16[2,2,256,384]{3,2,1,0:T(8,128)(2,1)}, u32[]{:S(2)}) copy-start(bf16[2,2,256,384]{3,2,1,0:T(8,128)(2,1)} %constant.2.clone.table_ref) | copy-start | bytes 2359300
  20.2 11.7 %collective-permute-start.2 = (f32[40,768]{1,0:T(8,128)S(1)}, f32[40,768]{1,0:T(8,128)S(1)}, u32[]{:S(2)}, u32[]{:S(2)}) collective-permute-start(f32[40,768]{1,0:T(8,128)S(1)} %get-tuple-element.31), channel_id=1, source_target_pairs={{0,15},{1,2},{2,1},{3,4},{4,3},{5,6},{6,5},{7,8},{8,7},{9,10},{10,... | collective-permute-start | bytes 368648 | tf_op jit(solution)/shard_map/ppermute | solution.py:709
  23.9 7.9 %collective-permute-start.3 = (f32[40,768]{1,0:T(8,128)S(1)}, f32[40,768]{1,0:T(8,128)S(1)}, u32[]{:S(2)}, u32[]{:S(2)}) collective-permute-start(f32[40,768]{1,0:T(8,128)S(1)} %get-tuple-element.32), channel_id=1, source_target_pairs={{0,1},{1,0},{2,3},{3,2},{4,5},{5,4},{6,7},{7,6},{8,9},{9,8},{10,11... | collective-permute-start | bytes 368648 | tf_op jit(solution)/shard_map/ppermute | solution.py:708
  26.3 4.2 %collective-permute-start = (f32[2,40,256]{2,1,0:T(8,128)S(1)}, f32[2,40,256]{2,1,0:T(8,128)S(1)}, u32[]{:S(2)}, u32[]{:S(2)}) collective-permute-start(f32[2,40,256]{2,1,0:T(8,128)S(1)} %get-tuple-element.27), channel_id=1, source_target_pairs={{0,15},{1,2},{2,1},{3,4},{4,3},{5,6},{6,5},{7,8},{8,7},{9,10},{10,... | collective-permute-start | bytes 245768 | tf_op jit(solution)/shard_map/ppermute | solution.py:709
  26.3 4.2 %collective-permute-start.1 = (f32[2,40,256]{2,1,0:T(8,128)S(1)}, f32[2,40,256]{2,1,0:T(8,128)S(1)}, u32[]{:S(2)}, u32[]{:S(2)}) collective-permute-start(f32[2,40,256]{2,1,0:T(8,128)S(1)} %get-tuple-element.28), channel_id=1, source_target_pairs={{0,1},{1,0},{2,3},{3,2},{4,5},{5,4},{6,7},{7,6},{8,9},{9,8},{10,11... | collective-permute-start | bytes 245768 | tf_op jit(solution)/shard_map/ppermute | solution.py:708
  28.5 2.0 %copy-start.1 = (s32[128]{0:T(128)S(1)}, s32[128]{0:T(128)}, u32[]{:S(2)}) copy-start(s32[128]{0:T(128)} %tag_ref.1) | copy-start | bytes 1540
  45.4 4.6 %collective-permute-start.4 = (f32[4,32,128]{2,1,0:T(8,128)S(1)}, f32[4,32,128]{2,1,0:T(8,128)S(1)}, u32[]{:S(2)}, u32[]{:S(2)}) collective-permute-start(f32[4,32,128]{2,1,0:T(8,128)S(1)} %get-tuple-element.35), channel_id=1, source_target_pairs={{0,15},{1,2},{2,1},{3,4},{4,3},{5,6},{6,5},{7,8},{8,7},{9,10},{10,... | collective-permute-start | bytes 196616 | tf_op jit(solution)/shard_map/ppermute | solution.py:709
  48.0 2.2 %collective-permute-start.5 = (f32[4,32,128]{2,1,0:T(8,128)S(1)}, f32[4,32,128]{2,1,0:T(8,128)S(1)}, u32[]{:S(2)}, u32[]{:S(2)}) collective-permute-start(f32[4,32,128]{2,1,0:T(8,128)S(1)} %get-tuple-element.36), channel_id=1, source_target_pairs={{0,1},{1,0},{2,3},{3,2},{4,5},{5,4},{6,7},{7,6},{8,9},{9,8},{10,11... | collective-permute-start | bytes 196616 | tf_op jit(solution)/shard_map/ppermute | solution.py:708
  50.5 4.7 %collective-permute-start.6 = (f32[4,32,128]{2,1,0:T(8,128)S(1)}, f32[4,32,128]{2,1,0:T(8,128)S(1)}, u32[]{:S(2)}, u32[]{:S(2)}) collective-permute-start(f32[4,32,128]{2,1,0:T(8,128)S(1)} %get-tuple-element.39), channel_id=1, source_target_pairs={{0,15},{1,2},{2,1},{3,4},{4,3},{5,6},{6,5},{7,8},{8,7},{9,10},{10,... | collective-permute-start | bytes 196616 | tf_op jit(solution)/shard_map/ppermute | solution.py:709
  52.1 3.4 %collective-permute-start.7 = (f32[4,32,128]{2,1,0:T(8,128)S(1)}, f32[4,32,128]{2,1,0:T(8,128)S(1)}, u32[]{:S(2)}, u32[]{:S(2)}) collective-permute-start(f32[4,32,128]{2,1,0:T(8,128)S(1)} %get-tuple-element.40), channel_id=1, source_target_pairs={{0,1},{1,0},{2,3},{3,2},{4,5},{5,4},{6,7},{7,6},{8,9},{9,8},{10,11... | collective-permute-start | bytes 196616 | tf_op jit(solution)/shard_map/ppermute | solution.py:708
  56.6 16.2 %all-to-all-start.2 = ((f32[16,8,128]{2,1,0:T(8,128)}), f32[16,8,128]{2,1,0:T(8,128)S(1)}, u32[]{:S(2)}, u32[]{:S(2)}) async-start(f32[16,8,128]{2,1,0:T(8,128)} %get-tuple-element.41), calls=%async_computation.2 | async-start | bytes 131072 | tf_op jit(solution)/shard_map/all_to_all | solution.py:772

commit v12 on v11

--- a/solution.py
+++ b/solution.py
@@ -100,6 +100,10 @@
         for a in range(16):
             if a & bit == 0:
                 first, second = values[a], values[a | bit]
+                if first is None:
+                    continue
+                if second is None:
+                    second = jnp.zeros_like(first)
                 moved = jnp.where(upper, first, second)
                 if bit == 8:
                     moved = pltpu.roll(moved, 64, 1)
@@ -167,7 +171,7 @@
         sides[j // 4] = jnp.where(lane == 7 - at, pltpu.roll(chunk[j * 5], 127 - at, 1), side)
     chunk = chunk + sides
     whole = exchange_chunks(chunk[:16])
-    rest = exchange_chunks(chunk[16:] + [jnp.zeros((32, 128), jnp.float32)] * 5)
+    rest = exchange_chunks(chunk[16:] + [None] * 5)
     for d in range(GRID):
         pack_rows(out_ref, d, whole[d], rest[d], 11)
 
@@ -324,19 +328,8 @@
                 out_ref[parity, 128 * t : 128 * t + 128, lanes] = modal + change[t]
 
 
-def project_rows(planar, parity, table_ref):
-    folded = planar[:, :HALF] + planar[:, HALF:] if parity == 0 else planar[:, :HALF] - planar[:, HALF:]
-    return dot_split(halves(folded), (table_ref[0, parity], table_ref[1, parity]), ((1,), (1,)))
-
-
-def wave_factors(parity):
-    k = 2 * lax.broadcasted_iota(jnp.int32, (80, 128), 1) + parity
-    scale = jnp.where(k == 0, 1.0, 2.0) * (math.sqrt(KMODES) / PLANES * STEP_SIZE)
-    return scale, scale * (k.astype(jnp.float32) * (1.0 / KMODES))
-
-
 def lift_kernel(
-    tag_ref, field_ref, cross_ref, chip_ref, table_ref, lift_ref, base_ref, outer_ref
+    tag_ref, field_ref, cross_ref, chip_ref, table_ref, lift_ref, flux_ref, modal_ref, outer_ref
 ):
     bottom, top = at_ends()
     span = lax.axis_index("span")
@@ -346,11 +339,14 @@
         mirror = jnp.where((row == e) & (tag_ref[8 * span + e] == 1), -1.0, mirror)
     keep_lower = jnp.where(bottom, 0.0, 1.0)
     keep_upper = jnp.where(top, 0.0, 1.0)
-    outer, modal = [], []
+    gap = jnp.zeros((48, 256), jnp.float32)
+    outer = []
     for parity in range(2):
         below, above = from_partners(cross_ref[parity], chip_ref[parity])
         outer.append(jnp.concatenate([below, above], axis=0))
-        modal.append(jnp.concatenate([keep_lower * below, keep_upper * above], axis=0))
+        modal_ref[parity] = jnp.concatenate(
+            [keep_lower * below, keep_upper * above, gap], axis=0
+        ).T
     pair = synthesize(outer, table_ref)
     for q in range(2):
         outer_ref[:, HALF * q : HALF * q + HALF] = pair[q]
@@ -359,40 +355,36 @@
     inside = field_ref[0:40, :]
     below = outer_ref[0:40, :]
     lift_ref[0:40, :] = 10.0 * two_point(jnp.where(bottom, mirror * inside, below), inside)
-    flux_lower = keep_lower * (0.5 * below * below)
+    flux_ref[0:40, :] = keep_lower * (0.5 * below * below)
     inside = field_ref[160:200, :]
     above = outer_ref[40:80, :]
     lift_ref[40:80, :] = 10.0 * two_point(inside, jnp.where(top, inside, above))
-    flux = jnp.concatenate([flux_lower, keep_upper * (0.5 * above * above)], axis=0)
-    for parity in range(2):
-        from_flux = project_rows(flux, parity, table_ref)
-        _, ratio = wave_factors(parity)
-        base_ref[parity, :, 0:128] = modal[parity][:, 0:128] - ratio * from_flux[:, 128:256]
-        base_ref[parity, :, 128:256] = modal[parity][:, 128:256] + ratio * from_flux[:, 0:128]
-
-
-def facing_kernel(inside_ref, lift_ref, base_ref, cross_ref, chip_ref, table_ref, out_ref):
+    flux_ref[40:80, :] = keep_upper * (0.5 * above * above)
+
+
+def facing_kernel(
+    inside_ref, lift_ref, flux_ref, facing_ref, cross_ref, chip_ref, table_ref, out_ref
+):
     bottom, top = at_ends()
     below, above = from_partners(cross_ref[...], chip_ref[...])
     lift = lift_ref[0:40, :]
     rhs_lower = lift + jnp.where(bottom, 0.0, below - lift)
     lift = lift_ref[40:80, :]
     rhs_upper = jnp.where(top, 0.0, above + lift) - lift
-    rhs = jnp.concatenate([rhs_lower, rhs_upper], axis=0)
-    gap = jnp.zeros((48, 128), jnp.float32)
+    gap = jnp.zeros((48, PLANES), jnp.float32)
+    planar = jnp.concatenate([rhs_lower, rhs_upper, gap, flux_ref[...], gap], axis=0)
     lane = lax.broadcasted_iota(jnp.int32, (128, 128), 1)
     whole, rest = [], []
     for parity in range(2):
-        from_rhs = project_rows(rhs, parity, table_ref)
-        scale, _ = wave_factors(parity)
+        projected = project(planar, parity, table_ref)
+        change = tendency(parity, projected[:, 0:128], projected[:, 128:256])
         for t in range(2):
-            waves = slice(128 * t, 128 * t + 128)
-            nodal = base_ref[parity, :, waves] + scale * from_rhs[:, waves]
-            extra = jnp.concatenate([nodal, gap], axis=0).T
+            rows = slice(128 * t, 128 * t + 128)
+            extra = change[t] + facing_ref[parity, rows, :]
             lower = jnp.where(lane < 40, extra, 0.0)
             upper = pltpu.roll(jnp.where(lane < 40, 0.0, extra), 120, 1)
-            whole.append(inside_ref[parity, waves, 0:128] + lower)
-            rest.append(inside_ref[parity, waves, 128:256] + upper)
+            whole.append(inside_ref[parity, rows, 0:128] + lower)
+            rest.append(inside_ref[parity, rows, 128:256] + upper)
     for s in range(GRID):
         part = slice(8 * s, 8 * s + 8)
         pack_rows(
@@ -733,11 +725,12 @@
         inside_kernel, [(2, 256, 256)], modal, field, side, edge, table, covers=False,
         scratch=[pltpu.VMEM((120, PLANES), jnp.float32)],
     )
-    lift, base = call(
-        lift_kernel, [(80, PLANES), (2, 80, 256)], wall_tag, field, *modal_traces, table,
-        smem=(0,), scratch=[pltpu.VMEM((80, PLANES), jnp.float32)], covers=False,
-    )
-    (sent,) = call(facing_kernel, [(16, 56, 128)], inside, lift, base, *rhs_traces, table)
+    lift, flux, facing = call(
+        lift_kernel, [(80, PLANES), (80, PLANES), (2, 256, 128)], wall_tag, field,
+        *modal_traces, table, smem=(0,), scratch=[pltpu.VMEM((80, PLANES), jnp.float32)],
+        covers=False,
+    )
+    (sent,) = call(facing_kernel, [(16, 56, 128)], inside, lift, flux, facing, *rhs_traces, table)
     load = lax.all_to_all(sent, "span", 0, 0, tiled=True)
     nodes, trace = (25, 32, 128), (4, 32, 128)
     edges, inner_rows = (10, 32, 128), (15, 32, 128)

time: 74.1 us -> 73.7 us (level)
  transfers between devices with their start and end apart: 9 -> 9, of which waited for: 5 -> 5; matrix products, arithmetic and copies ran while one was open for 0% -> 0% of each run, Pallas kernels for 8% -> 7%
where the time goes in v12:
time: 73.7 us; the launch traced here: 73.4 us
  blocking collectives  28.9 us (39%)
  starting transfers between devices  24.6 us (33%)
  Pallas kernels  12.8 us (17%)
  waiting for transfers between devices  7.02 us (10%)
    all_to_all x1, blocking collectives, on_device(): modal = lax.all_to_all(packed, 'span', 0, 0, tiled=True)  17 us
    pallas_call x15, Pallas kernels, call(): pl.pallas_call(kernel, out_shape=[jax.ShapeDtypeStruct(s, jnp.float32) fo...  12.8 us
    all_to_all x1, blocking collectives, on_device(): load = lax.all_to_all(sent, 'span', 0, 0, tiled=True)  11.9 us
    all_to_all x1, starting transfers between devices, on_device(): sums = lax.all_to_all(sums, 'plane', 0, 0, tiled=True)  8.43 us
    ppermute x4, starting transfers between devices, swap_traces(): chip = lax.ppermute(chip, 'plane', [(p, p ^ 1) for p in range(GRID)])  8.36 us
    ppermute x4, starting transfers between devices, swap_traces(): cross = lax.ppermute(cross, 'plane', partner)  7.86 us
    all_to_all x1, waiting for transfers between devices, on_device(): sums = lax.all_to_all(sums, 'plane', 0, 0, tiled=True)  5.86 us
  transfers between devices with their start and end apart: 9, of which 5 were waited for; matrix products, arithmetic and copies ran while one was open for 0% of the time, Pallas kernels for 7%

profile of v12, /device:TPU:1, one launch (start us, length us, event | category | flops | bytes accessed | tf_op | source)
XLA Modules:
  0.0 73.4 jit_solution(14622961507263042977)
XLA Ops:
  0.0 2.1 %shard_map.37 = f32[16,56,128]{2,1,0:T(8,128)S(1)} custom-call(f32[5,32,640]{2,1,0:T(8,128)} %bitcast.2), custom_call_target="tpu_custom_call" | custom-call | tf_op jit(solution)/shard_map/pallas_call | solution.py:687
  2.2 17.0 %all_to_all.15.modal_ref = f32[16,56,128]{2,1,0:T(8,128)S(1)} all-to-all(f32[16,56,128]{2,1,0:T(8,128)S(1)} %shard_map.37), channel_id=1, replica_groups=mesh['span'=16,'plane'=16] {'span'}, dimensions={0} | all-to-all | bytes 917504 | tf_op jit(solution)/shard_map/all_to_all | solution.py:716
  19.2 1.0 %shard_map.38 = (f32[200,768]{1,0:T(8,128)S(1)}, f32[16,768]{1,0:T(8,128)S(1)}, f32[80,768]{1,0:T(8,128)S(1)}, f32[2,40,256]{2,1,0:T(8,128)S(1)}, f32[2,40,256]{...) custom-call(f32[16,56,128]{2,1,0:T(8,128)S(1)} %all_to_all.15.modal_ref, ...), custom_call_target="tpu_custom_call" | custom-call | tf_op jit(solution)/shard_map/pallas_call | solution.py:687
  20.2 3.7 %collective-permute-start.2 = (f32[40,768]{1,0:T(8,128)S(1)}, f32[40,768]{1,0:T(8,128)S(1)}, u32[]{:S(2)}, u32[]{:S(2)}) collective-permute-start(f32[40,768]{1,0:T(8,128)S(1)} %get-tuple-element.33), channel_id=1, source_target_pairs={{0,15},{1,2},{2,1},{3,4},{4,3},{5,6},{6,5},{7,8},{8,7},{9,10},{10,... | collective-permute-start | bytes 368648 | tf_op jit(solution)/shard_map/ppermute | solution.py:701
  23.9 2.3 %collective-permute-start.3 = (f32[40,768]{1,0:T(8,128)S(1)}, f32[40,768]{1,0:T(8,128)S(1)}, u32[]{:S(2)}, u32[]{:S(2)}) collective-permute-start(f32[40,768]{1,0:T(8,128)S(1)} %get-tuple-element.34), channel_id=1, source_target_pairs={{0,1},{1,0},{2,3},{3,2},{4,5},{5,4},{6,7},{7,6},{8,9},{9,8},{10,11... | collective-permute-start | bytes 368648 | tf_op jit(solution)/shard_map/ppermute | solution.py:700
  26.2 2.2 %collective-permute-start.1 = (f32[2,40,256]{2,1,0:T(8,128)S(1)}, f32[2,40,256]{2,1,0:T(8,128)S(1)}, u32[]{:S(2)}, u32[]{:S(2)}) collective-permute-start(f32[2,40,256]{2,1,0:T(8,128)S(1)} %get-tuple-element.29), channel_id=1, source_target_pairs={{0,1},{1,0},{2,3},{3,2},{4,5},{5,4},{6,7},{7,6},{8,9},{9,8},{10,11... | collective-permute-start | bytes 245768 | tf_op jit(solution)/shard_map/ppermute | solution.py:700
  28.5 1.7 %shard_map.39.inside_ref = f32[2,256,256]{2,1,0:T(8,128)S(1)} custom-call(f32[16,56,128]{2,1,0:T(8,128)S(1)} %all_to_all.15.modal_ref, f32[200,768]{1,0:T(8,128)S(1)} %get-tuple-element.25.field_ref, f32[16,768]{1,0:T(8,128)S(1)} %get-tuple-element.26.side_ref, f32[80,768]{1,0:T(8,128)S(1)} %get-tuple-element.27.edge_ref, bf16[2,2,256,384]{3,2,1,0:T(8,128)(2,1)S(1)} %copy-done), custom_call_target="tpu_custom_call" | custom-call | tf_op jit(solution)/shard_map/pallas_call | solution.py:687
  30.4 1.0 %shard_map.40 = (f32[80,768]{1,0:T(8,128)S(1)}, f32[80,768]{1,0:T(8,128)S(1)}, f32[2,256,128]{2,1,0:T(8,128)S(1)}) custom-call(s32[128]{0:T(128)S(1)} %copy-done.1, f32[200,768]{1,0:T(8,128)S(1)} %get-tuple-element.25.field_ref, f32[2,40,256]{2,1,0:T(8,128)S(1)} %collective-permute-done.cross_ref, f32[2,40,256]{2,1,0:T(8,128)S(1)} %collective-permute-done.1.chip_ref, ...), custom_call_target="tpu_custom_call" | custom-call | tf_op jit(solution)/shard_map/pallas_call | solution.py:687
  31.4 0.8 %shard_map.41 = f32[16,56,128]{2,1,0:T(8,128)S(1)} custom-call(f32[2,256,256]{2,1,0:T(8,128)S(1)} %shard_map.39.inside_ref, f32[80,768]{1,0:T(8,128)S(1)} %get-tuple-element.30.lift_ref, f32[80,768]{1,0:T(8,128)S(1)} %get-tuple-element.31.flux_ref, f32[2,256,128]{2,1,0:T(8,128)S(1)} %get-tuple-element.32.facing_ref, ...), custom_call_target="tpu_custom_call" | custom-call | tf_op jit(solution)/shard_map/pallas_call | solution.py:687
  32.3 11.9 %all_to_all.16.modal_ref = f32[16,56,128]{2,1,0:T(8,128)S(1)} all-to-all(f32[16,56,128]{2,1,0:T(8,128)S(1)} %shard_map.41), channel_id=1, replica_groups=mesh['span'=16,'plane'=16] {'span'}, dimensions={0} | all-to-all | bytes 917504 | tf_op jit(solution)/shard_map/all_to_all | solution.py:734
  44.2 0.8 %shard_map.42 = (f32[25,32,128]{2,1,0:T(8,128)S(1)}, f32[10,32,128]{2,1,0:T(8,128)S(1)}, f32[4,32,128]{2,1,0:T(8,128)S(1)}, f32[4,32,128]{2,1,0:T(8,128)S(1)}) custom-call(f32[16,56,128]{2,1,0:T(8,128)S(1)} %all_to_all.16.modal_ref), custom_call_target="tpu_custom_call" | custom-call | tf_op jit(solution)/shard_map/pallas_call | solution.py:687
  45.0 2.6 %collective-permute-start.4 = (f32[4,32,128]{2,1,0:T(8,128)S(1)}, f32[4,32,128]{2,1,0:T(8,128)S(1)}, u32[]{:S(2)}, u32[]{:S(2)}) collective-permute-start(f32[4,32,128]{2,1,0:T(8,128)S(1)} %get-tuple-element.37), channel_id=1, source_target_pairs={{0,15},{1,2},{2,1},{3,4},{4,3},{5,6},{6,5},{7,8},{8,7},{9,10},{10,... | collective-permute-start | bytes 196616 | tf_op jit(solution)/shard_map/ppermute | solution.py:701
  47.6 1.3 %collective-permute-start.5 = (f32[4,32,128]{2,1,0:T(8,128)S(1)}, f32[4,32,128]{2,1,0:T(8,128)S(1)}, u32[]{:S(2)}, u32[]{:S(2)}) collective-permute-start(f32[4,32,128]{2,1,0:T(8,128)S(1)} %get-tuple-element.38), channel_id=1, source_target_pairs={{0,1},{1,0},{2,3},{3,2},{4,5},{5,4},{6,7},{7,6},{8,9},{9,8},{10,11... | collective-permute-start | bytes 196616 | tf_op jit(solution)/shard_map/ppermute | solution.py:700
  49.2 0.4 collective-permute-done.4.cross_in_ref
  50.1 1.6 %collective-permute-start.6 = (f32[4,32,128]{2,1,0:T(8,128)S(1)}, f32[4,32,128]{2,1,0:T(8,128)S(1)}, u32[]{:S(2)}, u32[]{:S(2)}) collective-permute-start(f32[4,32,128]{2,1,0:T(8,128)S(1)} %get-tuple-element.41), channel_id=1, source_target_pairs={{0,15},{1,2},{2,1},{3,4},{4,3},{5,6},{6,5},{7,8},{8,7},{9,10},{10,... | collective-permute-start | bytes 196616 | tf_op jit(solution)/shard_map/ppermute | solution.py:701
  51.7 2.5 %collective-permute-start.7 = (f32[4,32,128]{2,1,0:T(8,128)S(1)}, f32[4,32,128]{2,1,0:T(8,128)S(1)}, u32[]{:S(2)}, u32[]{:S(2)}) collective-permute-start(f32[4,32,128]{2,1,0:T(8,128)S(1)} %get-tuple-element.42), channel_id=1, source_target_pairs={{0,1},{1,0},{2,3},{3,2},{4,5},{5,4},{6,7},{7,6},{8,9},{9,8},{10,11... | collective-permute-start | bytes 196616 | tf_op jit(solution)/shard_map/ppermute | solution.py:700
  54.8 0.3 collective-permute-done.7.chip_in_ref
  55.1 1.1 %shard_map.47 = (f32[2,32,640]{2,1,0:T(8,128)S(1)}, f32[16,8,128]{2,1,0:T(8,128)}) custom-call(f32[10,32,128]{2,1,0:T(8,128)S(1)} %get-tuple-element.39.edge_ref.edge_in_ref, f32[15,32,128]{2,1,0:T(8,128)S(1)} %shard_map.45.inner_ref, f32[4,32,128]{2,1,0:T(8,128)S(1)} %collective-permute-done.6.cross_in_ref, ...), custom_call_target="tpu_custom_call" | custom-call | tf_op jit(solution)/shard_map/pallas_call | solution.py:687
  56.2 8.4 %all-to-all-start.2 = ((f32[16,8,128]{2,1,0:T(8,128)}), f32[16,8,128]{2,1,0:T(8,128)S(1)}, u32[]{:S(2)}, u32[]{:S(2)}) async-start(f32[16,8,128]{2,1,0:T(8,128)} %get-tuple-element.43), calls=%async_computation.2 | async-start | bytes 131072 | tf_op jit(solution)/shard_map/all_to_all | solution.py:765
  64.6 0.7 shard_map.48.first_ref
  65.3 0.5 shard_map.50.inner_ref
  65.8 0.7 shard_map.49.second_ref
  66.5 5.9 %all-to-all-done.2.sums_ref = f32[16,8,128]{2,1,0:T(8,128)S(1)} async-done(((f32[16,8,128]{2,1,0:T(8,128)}), f32[16,8,128]{2,1,0:T(8,128)S(1)}, u32[]{:S(2)}, u32[]{:S(2)}) %all-to-all-start.2) | async-done | bytes 65568 | tf_op jit(solution)/shard_map/all_to_all | solution.py:765
  72.4 1.1 %shard_map.51 = f32[5,32,640]{2,1,0:T(8,128)} custom-call(f32[16,8,128]{2,1,0:T(8,128)S(1)} %all-to-all-done.2.sums_ref, f32[5,32,640]{2,1,0:T(8,128)S(1)} %shard_map.48.first_ref, f32[5,32,640]{2,1,0:T(8,128)S(1)} %shard_map.49.second_ref, f32[3,32,640]{2,1,0:T(8,128)S(1)} %shard_map.50.inner_ref, f32[2,32,640]{2,1,0:T(8,128)S(1)} %get-tuple-element.44.edge_ref), custom_call_target="tpu_custom_call" | custom-call | tf_op jit(solution)/shard_map/pallas_call | solution.py:687
  (15 shorter events, 1.6 us)
Async XLA Ops:
  0.0 19.2 %copy-start = (bf16[2,2,256,384]{3,2,1,0:T(8,128)(2,1)S(1)}, bf16[2,2,256,384]{3,2,1,0:T(8,128)(2,1)}, u32[]{:S(2)}) copy-start(bf16[2,2,256,384]{3,2,1,0:T(8,128)(2,1)} %constant.2.clone.table_ref) | copy-start | bytes 2359300
  20.2 11.2 %collective-permute-start.2 = (f32[40,768]{1,0:T(8,128)S(1)}, f32[40,768]{1,0:T(8,128)S(1)}, u32[]{:S(2)}, u32[]{:S(2)}) collective-permute-start(f32[40,768]{1,0:T(8,128)S(1)} %get-tuple-element.33), channel_id=1, source_target_pairs={{0,15},{1,2},{2,1},{3,4},{4,3},{5,6},{6,5},{7,8},{8,7},{9,10},{10,... | collective-permute-start | bytes 368648 | tf_op jit(solution)/shard_map/ppermute | solution.py:701
  23.9 7.5 %collective-permute-start.3 = (f32[40,768]{1,0:T(8,128)S(1)}, f32[40,768]{1,0:T(8,128)S(1)}, u32[]{:S(2)}, u32[]{:S(2)}) collective-permute-start(f32[40,768]{1,0:T(8,128)S(1)} %get-tuple-element.34), channel_id=1, source_target_pairs={{0,1},{1,0},{2,3},{3,2},{4,5},{5,4},{6,7},{7,6},{8,9},{9,8},{10,11... | collective-permute-start | bytes 368648 | tf_op jit(solution)/shard_map/ppermute | solution.py:700
  26.2 4.2 %collective-permute-start = (f32[2,40,256]{2,1,0:T(8,128)S(1)}, f32[2,40,256]{2,1,0:T(8,128)S(1)}, u32[]{:S(2)}, u32[]{:S(2)}) collective-permute-start(f32[2,40,256]{2,1,0:T(8,128)S(1)} %get-tuple-element.28), channel_id=1, source_target_pairs={{0,15},{1,2},{2,1},{3,4},{4,3},{5,6},{6,5},{7,8},{8,7},{9,10},{10,... | collective-permute-start | bytes 245768 | tf_op jit(solution)/shard_map/ppermute | solution.py:701
  26.2 4.2 %collective-permute-start.1 = (f32[2,40,256]{2,1,0:T(8,128)S(1)}, f32[2,40,256]{2,1,0:T(8,128)S(1)}, u32[]{:S(2)}, u32[]{:S(2)}) collective-permute-start(f32[2,40,256]{2,1,0:T(8,128)S(1)} %get-tuple-element.29), channel_id=1, source_target_pairs={{0,1},{1,0},{2,3},{3,2},{4,5},{5,4},{6,7},{7,6},{8,9},{9,8},{10,11... | collective-permute-start | bytes 245768 | tf_op jit(solution)/shard_map/ppermute | solution.py:700
  28.5 1.9 %copy-start.1 = (s32[128]{0:T(128)S(1)}, s32[128]{0:T(128)}, u32[]{:S(2)}) copy-start(s32[128]{0:T(128)} %tag_ref.1) | copy-start | bytes 1540
  45.0 4.5 %collective-permute-start.4 = (f32[4,32,128]{2,1,0:T(8,128)S(1)}, f32[4,32,128]{2,1,0:T(8,128)S(1)}, u32[]{:S(2)}, u32[]{:S(2)}) collective-permute-start(f32[4,32,128]{2,1,0:T(8,128)S(1)} %get-tuple-element.37), channel_id=1, source_target_pairs={{0,15},{1,2},{2,1},{3,4},{4,3},{5,6},{6,5},{7,8},{8,7},{9,10},{10,... | collective-permute-start | bytes 196616 | tf_op jit(solution)/shard_map/ppermute | solution.py:701
  47.6 2.2 %collective-permute-start.5 = (f32[4,32,128]{2,1,0:T(8,128)S(1)}, f32[4,32,128]{2,1,0:T(8,128)S(1)}, u32[]{:S(2)}, u32[]{:S(2)}) collective-permute-start(f32[4,32,128]{2,1,0:T(8,128)S(1)} %get-tuple-element.38), channel_id=1, source_target_pairs={{0,1},{1,0},{2,3},{3,2},{4,5},{5,4},{6,7},{7,6},{8,9},{9,8},{10,11... | collective-permute-start | bytes 196616 | tf_op jit(solution)/shard_map/ppermute | solution.py:700
  50.1 4.7 %collective-permute-start.6 = (f32[4,32,128]{2,1,0:T(8,128)S(1)}, f32[4,32,128]{2,1,0:T(8,128)S(1)}, u32[]{:S(2)}, u32[]{:S(2)}) collective-permute-start(f32[4,32,128]{2,1,0:T(8,128)S(1)} %get-tuple-element.41), channel_id=1, source_target_pairs={{0,15},{1,2},{2,1},{3,4},{4,3},{5,6},{6,5},{7,8},{8,7},{9,10},{10,... | collective-permute-start | bytes 196616 | tf_op jit(solution)/shard_map/ppermute | solution.py:701
  51.7 3.4 %collective-permute-start.7 = (f32[4,32,128]{2,1,0:T(8,128)S(1)}, f32[4,32,128]{2,1,0:T(8,128)S(1)}, u32[]{:S(2)}, u32[]{:S(2)}) collective-permute-start(f32[4,32,128]{2,1,0:T(8,128)S(1)} %get-tuple-element.42), channel_id=1, source_target_pairs={{0,1},{1,0},{2,3},{3,2},{4,5},{5,4},{6,7},{7,6},{8,9},{9,8},{10,11... | collective-permute-start | bytes 196616 | tf_op jit(solution)/shard_map/ppermute | solution.py:700
  56.2 16.2 %all-to-all-start.2 = ((f32[16,8,128]{2,1,0:T(8,128)}), f32[16,8,128]{2,1,0:T(8,128)S(1)}, u32[]{:S(2)}, u32[]{:S(2)}) async-start(f32[16,8,128]{2,1,0:T(8,128)} %get-tuple-element.43), calls=%async_computation.2 | async-start | bytes 131072 | tf_op jit(solution)/shard_map/all_to_all | solution.py:765

commit v13 on v12

--- a/solution.py
+++ b/solution.py
@@ -145,15 +145,19 @@
 
 
 def pack_kernel(state_hbm, out_ref, chunk_ref, state_ref, order_ref, arrived):
-    copy = pltpu.make_async_copy(state_hbm, state_ref, arrived)
-    copy.start()
+    copies = [
+        pltpu.make_async_copy(state_hbm.at[j], state_ref.at[j], arrived.at[j]) for j in range(5)
+    ]
+    for copy in copies:
+        copy.start()
     order_ref[...] = column_order()
-    copy.wait()
+    for copy in copies:
+        copy.wait()
     stacked = jnp.concatenate([state_ref[j] for j in range(5)], axis=0)
     order = order_ref[...]
     contract = ((1,), (0,))
-    high, low = halves(stacked)
-    nodes = dot(low, order, contract) + dot(high, order, contract)
+    both = dot(jnp.concatenate(halves(stacked), axis=0), order, contract)
+    nodes = both[160:] + both[:160]
     for i in range(5):
         chunk_ref[160 * i : 160 * i + 160, :] = nodes[:, 128 * i : 128 * i + 128]
     chunk = [
@@ -282,7 +286,9 @@
 
 def project(planar, parity, table_ref):
     folded = planar[:, :HALF] + planar[:, HALF:] if parity == 0 else planar[:, :HALF] - planar[:, HALF:]
-    return dot_split((table_ref[0, parity], table_ref[1, parity]), halves(folded), ((1,), (1,)))
+    high, low = halves(folded)
+    both = dot(table_ref[:, parity].reshape(512, HALF), high, ((1,), (1,)))
+    return dot(table_ref[0, parity], low, ((1,), (1,))) + both[256:] + both[:256]
 
 
 def tendency(parity, from_rhs, from_flux):
@@ -710,7 +716,7 @@
         anywhere=(0,),
         scratch=[
             pltpu.VMEM((800, 128), jnp.float32), pltpu.VMEM((5, 32, 640), jnp.float32),
-            pltpu.VMEM((640, 640), jnp.bfloat16), pltpu.SemaphoreType.DMA(()),
+            pltpu.VMEM((640, 640), jnp.bfloat16), pltpu.SemaphoreType.DMA((5,)),
         ],
     )
     modal = lax.all_to_all(packed, "span", 0, 0, tiled=True)

time: 73.7 us -> 73.8 us (level)
  no operation moved by 1% of the time
where the time goes in v13:
time: 73.8 us; the launch traced here: 73.5 us
  blocking collectives  28.9 us (39%)
  starting transfers between devices  24.7 us (33%)
  Pallas kernels  12.8 us (17%)
  waiting for transfers between devices  7.04 us (10%)
    all_to_all x1, blocking collectives, on_device(): modal = lax.all_to_all(packed, 'span', 0, 0, tiled=True)  17 us
    pallas_call x15, Pallas kernels, call(): pl.pallas_call(kernel, out_shape=[jax.ShapeDtypeStruct(s, jnp.float32) fo...  12.8 us
    all_to_all x1, blocking collectives, on_device(): load = lax.all_to_all(sent, 'span', 0, 0, tiled=True)  11.9 us
    all_to_all x1, starting transfers between devices, on_device(): sums = lax.all_to_all(sums, 'plane', 0, 0, tiled=True)  8.43 us
    ppermute x4, starting transfers between devices, swap_traces(): chip = lax.ppermute(chip, 'plane', [(p, p ^ 1) for p in range(GRID)])  8.41 us
    ppermute x4, starting transfers between devices, swap_traces(): cross = lax.ppermute(cross, 'plane', partner)  7.82 us
    all_to_all x1, waiting for transfers between devices, on_device(): sums = lax.all_to_all(sums, 'plane', 0, 0, tiled=True)  5.86 us
  transfers between devices with their start and end apart: 9, of which 5 were waited for; matrix products, arithmetic and copies ran while one was open for 0% of the time, Pallas kernels for 7%

profile of v13, /device:TPU:1, one launch (start us, length us, event | category | flops | bytes accessed | tf_op | source)
XLA Modules:
  0.0 73.5 jit_solution(3503669991692210515)
XLA Ops:
  0.0 2.2 %shard_map.37 = f32[16,56,128]{2,1,0:T(8,128)S(1)} custom-call(f32[5,32,640]{2,1,0:T(8,128)} %bitcast.2), custom_call_target="tpu_custom_call" | custom-call | tf_op jit(solution)/shard_map/pallas_call | solution.py:693
  2.2 17.0 %all_to_all.15.modal_ref = f32[16,56,128]{2,1,0:T(8,128)S(1)} all-to-all(f32[16,56,128]{2,1,0:T(8,128)S(1)} %shard_map.37), channel_id=1, replica_groups=mesh['span'=16,'plane'=16] {'span'}, dimensions={0} | all-to-all | bytes 917504 | tf_op jit(solution)/shard_map/all_to_all | solution.py:722
  19.2 1.0 %shard_map.38 = (f32[200,768]{1,0:T(8,128)S(1)}, f32[16,768]{1,0:T(8,128)S(1)}, f32[80,768]{1,0:T(8,128)S(1)}, f32[2,40,256]{2,1,0:T(8,128)S(1)}, f32[2,40,256]{...) custom-call(f32[16,56,128]{2,1,0:T(8,128)S(1)} %all_to_all.15.modal_ref, ...), custom_call_target="tpu_custom_call" | custom-call | tf_op jit(solution)/shard_map/pallas_call | solution.py:693
  20.3 3.7 %collective-permute-start.2 = (f32[40,768]{1,0:T(8,128)S(1)}, f32[40,768]{1,0:T(8,128)S(1)}, u32[]{:S(2)}, u32[]{:S(2)}) collective-permute-start(f32[40,768]{1,0:T(8,128)S(1)} %get-tuple-element.33), channel_id=1, source_target_pairs={{0,15},{1,2},{2,1},{3,4},{4,3},{5,6},{6,5},{7,8},{8,7},{9,10},{10,... | collective-permute-start | bytes 368648 | tf_op jit(solution)/shard_map/ppermute | solution.py:707
  24.0 2.3 %collective-permute-start.3 = (f32[40,768]{1,0:T(8,128)S(1)}, f32[40,768]{1,0:T(8,128)S(1)}, u32[]{:S(2)}, u32[]{:S(2)}) collective-permute-start(f32[40,768]{1,0:T(8,128)S(1)} %get-tuple-element.34), channel_id=1, source_target_pairs={{0,1},{1,0},{2,3},{3,2},{4,5},{5,4},{6,7},{7,6},{8,9},{9,8},{10,11... | collective-permute-start | bytes 368648 | tf_op jit(solution)/shard_map/ppermute | solution.py:706
  26.3 2.2 %collective-permute-start.1 = (f32[2,40,256]{2,1,0:T(8,128)S(1)}, f32[2,40,256]{2,1,0:T(8,128)S(1)}, u32[]{:S(2)}, u32[]{:S(2)}) collective-permute-start(f32[2,40,256]{2,1,0:T(8,128)S(1)} %get-tuple-element.29), channel_id=1, source_target_pairs={{0,1},{1,0},{2,3},{3,2},{4,5},{5,4},{6,7},{7,6},{8,9},{9,8},{10,11... | collective-permute-start | bytes 245768 | tf_op jit(solution)/shard_map/ppermute | solution.py:706
  28.5 1.7 %shard_map.39.inside_ref = f32[2,256,256]{2,1,0:T(8,128)S(1)} custom-call(f32[16,56,128]{2,1,0:T(8,128)S(1)} %all_to_all.15.modal_ref, f32[200,768]{1,0:T(8,128)S(1)} %get-tuple-element.25.field_ref, f32[16,768]{1,0:T(8,128)S(1)} %get-tuple-element.26.side_ref, f32[80,768]{1,0:T(8,128)S(1)} %get-tuple-element.27.edge_ref, bf16[2,2,256,384]{3,2,1,0:T(8,128)(2,1)S(1)} %copy-done), custom_call_target="tpu_custom_call" | custom-call | tf_op jit(solution)/shard_map/pallas_call | solution.py:693
  30.5 1.0 %shard_map.40 = (f32[80,768]{1,0:T(8,128)S(1)}, f32[80,768]{1,0:T(8,128)S(1)}, f32[2,256,128]{2,1,0:T(8,128)S(1)}) custom-call(s32[128]{0:T(128)S(1)} %copy-done.1, f32[200,768]{1,0:T(8,128)S(1)} %get-tuple-element.25.field_ref, f32[2,40,256]{2,1,0:T(8,128)S(1)} %collective-permute-done.cross_ref, f32[2,40,256]{2,1,0:T(8,128)S(1)} %collective-permute-done.1.chip_ref, ...), custom_call_target="tpu_custom_call" | custom-call | tf_op jit(solution)/shard_map/pallas_call | solution.py:693
  31.5 0.8 %shard_map.41 = f32[16,56,128]{2,1,0:T(8,128)S(1)} custom-call(f32[2,256,256]{2,1,0:T(8,128)S(1)} %shard_map.39.inside_ref, f32[80,768]{1,0:T(8,128)S(1)} %get-tuple-element.30.lift_ref, f32[80,768]{1,0:T(8,128)S(1)} %get-tuple-element.31.flux_ref, f32[2,256,128]{2,1,0:T(8,128)S(1)} %get-tuple-element.32.facing_ref, ...), custom_call_target="tpu_custom_call" | custom-call | tf_op jit(solution)/shard_map/pallas_call | solution.py:693
  32.3 11.9 %all_to_all.16.modal_ref = f32[16,56,128]{2,1,0:T(8,128)S(1)} all-to-all(f32[16,56,128]{2,1,0:T(8,128)S(1)} %shard_map.41), channel_id=1, replica_groups=mesh['span'=16,'plane'=16] {'span'}, dimensions={0} | all-to-all | bytes 917504 | tf_op jit(solution)/shard_map/all_to_all | solution.py:740
  44.3 0.8 %shard_map.42 = (f32[25,32,128]{2,1,0:T(8,128)S(1)}, f32[10,32,128]{2,1,0:T(8,128)S(1)}, f32[4,32,128]{2,1,0:T(8,128)S(1)}, f32[4,32,128]{2,1,0:T(8,128)S(1)}) custom-call(f32[16,56,128]{2,1,0:T(8,128)S(1)} %all_to_all.16.modal_ref), custom_call_target="tpu_custom_call" | custom-call | tf_op jit(solution)/shard_map/pallas_call | solution.py:693
  45.1 2.6 %collective-permute-start.4 = (f32[4,32,128]{2,1,0:T(8,128)S(1)}, f32[4,32,128]{2,1,0:T(8,128)S(1)}, u32[]{:S(2)}, u32[]{:S(2)}) collective-permute-start(f32[4,32,128]{2,1,0:T(8,128)S(1)} %get-tuple-element.37), channel_id=1, source_target_pairs={{0,15},{1,2},{2,1},{3,4},{4,3},{5,6},{6,5},{7,8},{8,7},{9,10},{10,... | collective-permute-start | bytes 196616 | tf_op jit(solution)/shard_map/ppermute | solution.py:707
  47.7 1.3 %collective-permute-start.5 = (f32[4,32,128]{2,1,0:T(8,128)S(1)}, f32[4,32,128]{2,1,0:T(8,128)S(1)}, u32[]{:S(2)}, u32[]{:S(2)}) collective-permute-start(f32[4,32,128]{2,1,0:T(8,128)S(1)} %get-tuple-element.38), channel_id=1, source_target_pairs={{0,1},{1,0},{2,3},{3,2},{4,5},{5,4},{6,7},{7,6},{8,9},{9,8},{10,11... | collective-permute-start | bytes 196616 | tf_op jit(solution)/shard_map/ppermute | solution.py:706
  49.3 0.3 collective-permute-done.4.cross_in_ref
  50.2 1.5 %collective-permute-start.6 = (f32[4,32,128]{2,1,0:T(8,128)S(1)}, f32[4,32,128]{2,1,0:T(8,128)S(1)}, u32[]{:S(2)}, u32[]{:S(2)}) collective-permute-start(f32[4,32,128]{2,1,0:T(8,128)S(1)} %get-tuple-element.41), channel_id=1, source_target_pairs={{0,15},{1,2},{2,1},{3,4},{4,3},{5,6},{6,5},{7,8},{8,7},{9,10},{10,... | collective-permute-start | bytes 196616 | tf_op jit(solution)/shard_map/ppermute | solution.py:707
  51.7 2.5 %collective-permute-start.7 = (f32[4,32,128]{2,1,0:T(8,128)S(1)}, f32[4,32,128]{2,1,0:T(8,128)S(1)}, u32[]{:S(2)}, u32[]{:S(2)}) collective-permute-start(f32[4,32,128]{2,1,0:T(8,128)S(1)} %get-tuple-element.42), channel_id=1, source_target_pairs={{0,1},{1,0},{2,3},{3,2},{4,5},{5,4},{6,7},{7,6},{8,9},{9,8},{10,11... | collective-permute-start | bytes 196616 | tf_op jit(solution)/shard_map/ppermute | solution.py:706
  54.9 0.3 collective-permute-done.7.chip_in_ref
  55.2 1.1 %shard_map.47 = (f32[2,32,640]{2,1,0:T(8,128)S(1)}, f32[16,8,128]{2,1,0:T(8,128)}) custom-call(f32[10,32,128]{2,1,0:T(8,128)S(1)} %get-tuple-element.39.edge_ref.edge_in_ref, f32[15,32,128]{2,1,0:T(8,128)S(1)} %shard_map.45.inner_ref, f32[4,32,128]{2,1,0:T(8,128)S(1)} %collective-permute-done.6.cross_in_ref, ...), custom_call_target="tpu_custom_call" | custom-call | tf_op jit(solution)/shard_map/pallas_call | solution.py:693
  56.3 8.4 %all-to-all-start.2 = ((f32[16,8,128]{2,1,0:T(8,128)}), f32[16,8,128]{2,1,0:T(8,128)S(1)}, u32[]{:S(2)}, u32[]{:S(2)}) async-start(f32[16,8,128]{2,1,0:T(8,128)} %get-tuple-element.43), calls=%async_computation.2 | async-start | bytes 131072 | tf_op jit(solution)/shard_map/all_to_all | solution.py:771
  64.7 0.7 shard_map.48.first_ref
  65.4 0.5 shard_map.50.inner_ref
  65.9 0.7 shard_map.49.second_ref
  66.6 5.9 %all-to-all-done.2.sums_ref = f32[16,8,128]{2,1,0:T(8,128)S(1)} async-done(((f32[16,8,128]{2,1,0:T(8,128)}), f32[16,8,128]{2,1,0:T(8,128)S(1)}, u32[]{:S(2)}, u32[]{:S(2)}) %all-to-all-start.2) | async-done | bytes 65568 | tf_op jit(solution)/shard_map/all_to_all | solution.py:771
  72.5 1.1 %shard_map.51 = f32[5,32,640]{2,1,0:T(8,128)} custom-call(f32[16,8,128]{2,1,0:T(8,128)S(1)} %all-to-all-done.2.sums_ref, f32[5,32,640]{2,1,0:T(8,128)S(1)} %shard_map.48.first_ref, f32[5,32,640]{2,1,0:T(8,128)S(1)} %shard_map.49.second_ref, f32[3,32,640]{2,1,0:T(8,128)S(1)} %shard_map.50.inner_ref, f32[2,32,640]{2,1,0:T(8,128)S(1)} %get-tuple-element.44.edge_ref), custom_call_target="tpu_custom_call" | custom-call | tf_op jit(solution)/shard_map/pallas_call | solution.py:693
  (15 shorter events, 1.7 us)
Async XLA Ops:
  0.0 19.2 %copy-start = (bf16[2,2,256,384]{3,2,1,0:T(8,128)(2,1)S(1)}, bf16[2,2,256,384]{3,2,1,0:T(8,128)(2,1)}, u32[]{:S(2)}) copy-start(bf16[2,2,256,384]{3,2,1,0:T(8,128)(2,1)} %constant.2.clone.table_ref) | copy-start | bytes 2359300
  20.3 11.2 %collective-permute-start.2 = (f32[40,768]{1,0:T(8,128)S(1)}, f32[40,768]{1,0:T(8,128)S(1)}, u32[]{:S(2)}, u32[]{:S(2)}) collective-permute-start(f32[40,768]{1,0:T(8,128)S(1)} %get-tuple-element.33), channel_id=1, source_target_pairs={{0,15},{1,2},{2,1},{3,4},{4,3},{5,6},{6,5},{7,8},{8,7},{9,10},{10,... | collective-permute-start | bytes 368648 | tf_op jit(solution)/shard_map/ppermute | solution.py:707
  24.0 7.5 %collective-permute-start.3 = (f32[40,768]{1,0:T(8,128)S(1)}, f32[40,768]{1,0:T(8,128)S(1)}, u32[]{:S(2)}, u32[]{:S(2)}) collective-permute-start(f32[40,768]{1,0:T(8,128)S(1)} %get-tuple-element.34), channel_id=1, source_target_pairs={{0,1},{1,0},{2,3},{3,2},{4,5},{5,4},{6,7},{7,6},{8,9},{9,8},{10,11... | collective-permute-start | bytes 368648 | tf_op jit(solution)/shard_map/ppermute | solution.py:706
  26.3 4.2 %collective-permute-start = (f32[2,40,256]{2,1,0:T(8,128)S(1)}, f32[2,40,256]{2,1,0:T(8,128)S(1)}, u32[]{:S(2)}, u32[]{:S(2)}) collective-permute-start(f32[2,40,256]{2,1,0:T(8,128)S(1)} %get-tuple-element.28), channel_id=1, source_target_pairs={{0,15},{1,2},{2,1},{3,4},{4,3},{5,6},{6,5},{7,8},{8,7},{9,10},{10,... | collective-permute-start | bytes 245768 | tf_op jit(solution)/shard_map/ppermute | solution.py:707
  26.3 4.2 %collective-permute-start.1 = (f32[2,40,256]{2,1,0:T(8,128)S(1)}, f32[2,40,256]{2,1,0:T(8,128)S(1)}, u32[]{:S(2)}, u32[]{:S(2)}) collective-permute-start(f32[2,40,256]{2,1,0:T(8,128)S(1)} %get-tuple-element.29), channel_id=1, source_target_pairs={{0,1},{1,0},{2,3},{3,2},{4,5},{5,4},{6,7},{7,6},{8,9},{9,8},{10,11... | collective-permute-start | bytes 245768 | tf_op jit(solution)/shard_map/ppermute | solution.py:706
  28.5 2.0 %copy-start.1 = (s32[128]{0:T(128)S(1)}, s32[128]{0:T(128)}, u32[]{:S(2)}) copy-start(s32[128]{0:T(128)} %tag_ref.1) | copy-start | bytes 1540
  45.1 4.5 %collective-permute-start.4 = (f32[4,32,128]{2,1,0:T(8,128)S(1)}, f32[4,32,128]{2,1,0:T(8,128)S(1)}, u32[]{:S(2)}, u32[]{:S(2)}) collective-permute-start(f32[4,32,128]{2,1,0:T(8,128)S(1)} %get-tuple-element.37), channel_id=1, source_target_pairs={{0,15},{1,2},{2,1},{3,4},{4,3},{5,6},{6,5},{7,8},{8,7},{9,10},{10,... | collective-permute-start | bytes 196616 | tf_op jit(solution)/shard_map/ppermute | solution.py:707
  47.7 2.2 %collective-permute-start.5 = (f32[4,32,128]{2,1,0:T(8,128)S(1)}, f32[4,32,128]{2,1,0:T(8,128)S(1)}, u32[]{:S(2)}, u32[]{:S(2)}) collective-permute-start(f32[4,32,128]{2,1,0:T(8,128)S(1)} %get-tuple-element.38), channel_id=1, source_target_pairs={{0,1},{1,0},{2,3},{3,2},{4,5},{5,4},{6,7},{7,6},{8,9},{9,8},{10,11... | collective-permute-start | bytes 196616 | tf_op jit(solution)/shard_map/ppermute | solution.py:706
  50.2 4.7 %collective-permute-start.6 = (f32[4,32,128]{2,1,0:T(8,128)S(1)}, f32[4,32,128]{2,1,0:T(8,128)S(1)}, u32[]{:S(2)}, u32[]{:S(2)}) collective-permute-start(f32[4,32,128]{2,1,0:T(8,128)S(1)} %get-tuple-element.41), channel_id=1, source_target_pairs={{0,15},{1,2},{2,1},{3,4},{4,3},{5,6},{6,5},{7,8},{8,7},{9,10},{10,... | collective-permute-start | bytes 196616 | tf_op jit(solution)/shard_map/ppermute | solution.py:707
  51.7 3.4 %collective-permute-start.7 = (f32[4,32,128]{2,1,0:T(8,128)S(1)}, f32[4,32,128]{2,1,0:T(8,128)S(1)}, u32[]{:S(2)}, u32[]{:S(2)}) collective-permute-start(f32[4,32,128]{2,1,0:T(8,128)S(1)} %get-tuple-element.42), channel_id=1, source_target_pairs={{0,1},{1,0},{2,3},{3,2},{4,5},{5,4},{6,7},{7,6},{8,9},{9,8},{10,11... | collective-permute-start | bytes 196616 | tf_op jit(solution)/shard_map/ppermute | solution.py:706
  56.3 16.2 %all-to-all-start.2 = ((f32[16,8,128]{2,1,0:T(8,128)}), f32[16,8,128]{2,1,0:T(8,128)S(1)}, u32[]{:S(2)}, u32[]{:S(2)}) async-start(f32[16,8,128]{2,1,0:T(8,128)} %get-tuple-element.43), calls=%async_computation.2 | async-start | bytes 131072 | tf_op jit(solution)/shard_map/all_to_all | solution.py:771

commit v14 on v12

--- a/solution.py
+++ b/solution.py
@@ -152,8 +152,8 @@
     stacked = jnp.concatenate([state_ref[j] for j in range(5)], axis=0)
     order = order_ref[...]
     contract = ((1,), (0,))
-    high, low = halves(stacked)
-    nodes = dot(low, order, contract) + dot(high, order, contract)
+    both = dot(jnp.concatenate(halves(stacked), axis=0), order, contract)
+    nodes = both[160:] + both[:160]
     for i in range(5):
         chunk_ref[160 * i : 160 * i + 160, :] = nodes[:, 128 * i : 128 * i + 128]
     chunk = [
@@ -282,7 +282,9 @@
 
 def project(planar, parity, table_ref):
     folded = planar[:, :HALF] + planar[:, HALF:] if parity == 0 else planar[:, :HALF] - planar[:, HALF:]
-    return dot_split((table_ref[0, parity], table_ref[1, parity]), halves(folded), ((1,), (1,)))
+    high, low = halves(folded)
+    both = dot(table_ref[:, parity].reshape(512, HALF), high, ((1,), (1,)))
+    return dot(table_ref[0, parity], low, ((1,), (1,))) + both[256:] + both[:256]
 
 
 def tendency(parity, from_rhs, from_flux):
@@ -696,7 +698,7 @@
 
 
 def swap_traces(cross, chip):
-    partner = [(p, (p + 1) % GRID if p % 2 else (p - 1) % GRID) for p in range(GRID)]
+    partner = [(p, min(p + 1, GRID - 1) if p % 2 else max(p - 1, 0)) for p in range(GRID)]
     chip = lax.ppermute(chip, "plane", [(p, p ^ 1) for p in range(GRID)])
     cross = lax.ppermute(cross, "plane", partner)
     return cross, chip

time: 73.7 us -> 81.2 us (1.10)
  starting transfers between devices: 24.6 us -> 29.2 us
  waiting for transfers between devices: 7.02 us -> 8.96 us
  blocking collectives: 28.9 us -> 29.9 us
    ppermute x4, starting transfers between devices: 7.86 us -> 19 us  [swap_traces(): cross = lax.ppermute(cross, 'plane', partner)]
    ppermute x4, starting transfers between devices: 8.36 us -> 0.37 us  [swap_traces(): chip = lax.ppermute(chip, 'plane', [(p, p ^ 1) for p in range(GRID)])]
    ppermute x4, waiting for transfers between devices: 0.58 us -> 3.09 us  [swap_traces(): cross = lax.ppermute(cross, 'plane', partner)]
    all_to_all x1, starting transfers between devices: 8.43 us -> 9.83 us  [on_device(): sums = lax.all_to_all(sums, 'plane', 0, 0, tiled=True)]
    all_to_all x1, blocking collectives: 11.9 us -> 12.9 us  [on_device(): load = lax.all_to_all(sent, 'span', 0, 0, tiled=True)]
  transfers between devices with their start and end apart: 9 -> 9, of which waited for: 5 -> 4; matrix products, arithmetic and copies ran while one was open for 0% -> 0% of each run, Pallas kernels for 7% -> 7%
where the time goes in v14:
time: 81.2 us; the launch traced here: 80.9 us
  blocking collectives  29.9 us (37%)
  starting transfers between devices  29.2 us (36%)
  Pallas kernels  12.8 us (16%)
  waiting for transfers between devices  8.96 us (11%)
    ppermute x4, starting transfers between devices, swap_traces(): cross = lax.ppermute(cross, 'plane', partner)  19 us
    all_to_all x1, blocking collectives, on_device(): modal = lax.all_to_all(packed, 'span', 0, 0, tiled=True)  17 us
    all_to_all x1, blocking collectives, on_device(): load = lax.all_to_all(sent, 'span', 0, 0, tiled=True)  12.9 us
    pallas_call x15, Pallas kernels, call(): pl.pallas_call(kernel, out_shape=[jax.ShapeDtypeStruct(s, jnp.float32) fo...  12.8 us
    all_to_all x1, starting transfers between devices, on_device(): sums = lax.all_to_all(sums, 'plane', 0, 0, tiled=True)  9.83 us
    all_to_all x1, waiting for transfers between devices, on_device(): sums = lax.all_to_all(sums, 'plane', 0, 0, tiled=True)  5.86 us
    ppermute x4, waiting for transfers between devices, swap_traces(): cross = lax.ppermute(cross, 'plane', partner)  3.09 us
  transfers between devices with their start and end apart: 9, of which 4 were waited for; matrix products, arithmetic and copies ran while one was open for 0% of the time, Pallas kernels for 7%

profile of v14, /device:TPU:1, one launch (start us, length us, event | category | flops | bytes accessed | tf_op | source)
XLA Modules:
  0.0 80.9 jit_solution(8988058186631346273)
XLA Ops:
  0.0 2.2 %shard_map.37 = f32[16,56,128]{2,1,0:T(8,128)S(1)} custom-call(f32[5,32,640]{2,1,0:T(8,128)} %bitcast.2), custom_call_target="tpu_custom_call" | custom-call | tf_op jit(solution)/shard_map/pallas_call | solution.py:689
  2.2 17.0 %all_to_all.15.modal_ref = f32[16,56,128]{2,1,0:T(8,128)S(1)} all-to-all(f32[16,56,128]{2,1,0:T(8,128)S(1)} %shard_map.37), channel_id=1, replica_groups=mesh['span'=16,'plane'=16] {'span'}, dimensions={0} | all-to-all | bytes 917504 | tf_op jit(solution)/shard_map/all_to_all | solution.py:718
  19.2 1.0 %shard_map.38 = (f32[200,768]{1,0:T(8,128)S(1)}, f32[16,768]{1,0:T(8,128)S(1)}, f32[80,768]{1,0:T(8,128)S(1)}, f32[2,40,256]{2,1,0:T(8,128)S(1)}, f32[2,40,256]{...) custom-call(f32[16,56,128]{2,1,0:T(8,128)S(1)} %all_to_all.15.modal_ref, ...), custom_call_target="tpu_custom_call" | custom-call | tf_op jit(solution)/shard_map/pallas_call | solution.py:689
  20.2 5.5 %collective-permute-start.2 = (f32[40,768]{1,0:T(8,128)S(1)}, f32[40,768]{1,0:T(8,128)S(1)}, u32[]{:S(2)}, u32[]{:S(2)}) collective-permute-start(f32[40,768]{1,0:T(8,128)S(1)} %get-tuple-element.33), channel_id=1, source_target_pairs={{0,0},{1,2},{2,1},{3,4},{4,3},{5,6},{6,5},{7,8},{8,7},{9,10},{10,9... | collective-permute-start | bytes 368648 | tf_op jit(solution)/shard_map/ppermute | solution.py:703
  25.8 3.9 %collective-permute-start = (f32[2,40,256]{2,1,0:T(8,128)S(1)}, f32[2,40,256]{2,1,0:T(8,128)S(1)}, u32[]{:S(2)}, u32[]{:S(2)}) collective-permute-start(f32[2,40,256]{2,1,0:T(8,128)S(1)} %get-tuple-element.28), channel_id=1, source_target_pairs={{0,0},{1,2},{2,1},{3,4},{4,3},{5,6},{6,5},{7,8},{8,7},{9,10},{10,9... | collective-permute-start | bytes 245768 | tf_op jit(solution)/shard_map/ppermute | solution.py:703
  29.9 1.7 %shard_map.39.inside_ref = f32[2,256,256]{2,1,0:T(8,128)S(1)} custom-call(f32[16,56,128]{2,1,0:T(8,128)S(1)} %all_to_all.15.modal_ref, f32[200,768]{1,0:T(8,128)S(1)} %get-tuple-element.25.field_ref, f32[16,768]{1,0:T(8,128)S(1)} %get-tuple-element.26.side_ref, f32[80,768]{1,0:T(8,128)S(1)} %get-tuple-element.27.edge_ref, bf16[2,2,256,384]{3,2,1,0:T(8,128)(2,1)S(1)} %copy-done), custom_call_target="tpu_custom_call" | custom-call | tf_op jit(solution)/shard_map/pallas_call | solution.py:689
  31.9 1.0 %shard_map.40 = (f32[80,768]{1,0:T(8,128)S(1)}, f32[80,768]{1,0:T(8,128)S(1)}, f32[2,256,128]{2,1,0:T(8,128)S(1)}) custom-call(s32[128]{0:T(128)S(1)} %copy-done.1, f32[200,768]{1,0:T(8,128)S(1)} %get-tuple-element.25.field_ref, f32[2,40,256]{2,1,0:T(8,128)S(1)} %collective-permute-done.cross_ref, f32[2,40,256]{2,1,0:T(8,128)S(1)} %collective-permute-done.1.chip_ref, ...), custom_call_target="tpu_custom_call" | custom-call | tf_op jit(solution)/shard_map/pallas_call | solution.py:689
  32.9 0.8 %shard_map.41 = f32[16,56,128]{2,1,0:T(8,128)S(1)} custom-call(f32[2,256,256]{2,1,0:T(8,128)S(1)} %shard_map.39.inside_ref, f32[80,768]{1,0:T(8,128)S(1)} %get-tuple-element.30.lift_ref, f32[80,768]{1,0:T(8,128)S(1)} %get-tuple-element.31.flux_ref, f32[2,256,128]{2,1,0:T(8,128)S(1)} %get-tuple-element.32.facing_ref, ...), custom_call_target="tpu_custom_call" | custom-call | tf_op jit(solution)/shard_map/pallas_call | solution.py:689
  33.7 12.9 %all_to_all.16.modal_ref = f32[16,56,128]{2,1,0:T(8,128)S(1)} all-to-all(f32[16,56,128]{2,1,0:T(8,128)S(1)} %shard_map.41), channel_id=1, replica_groups=mesh['span'=16,'plane'=16] {'span'}, dimensions={0} | all-to-all | bytes 917504 | tf_op jit(solution)/shard_map/all_to_all | solution.py:736
  46.6 0.8 %shard_map.42 = (f32[25,32,128]{2,1,0:T(8,128)S(1)}, f32[10,32,128]{2,1,0:T(8,128)S(1)}, f32[4,32,128]{2,1,0:T(8,128)S(1)}, f32[4,32,128]{2,1,0:T(8,128)S(1)}) custom-call(f32[16,56,128]{2,1,0:T(8,128)S(1)} %all_to_all.16.modal_ref), custom_call_target="tpu_custom_call" | custom-call | tf_op jit(solution)/shard_map/pallas_call | solution.py:689
  47.4 5.3 %collective-permute-start.4 = (f32[4,32,128]{2,1,0:T(8,128)S(1)}, f32[4,32,128]{2,1,0:T(8,128)S(1)}, u32[]{:S(2)}, u32[]{:S(2)}) collective-permute-start(f32[4,32,128]{2,1,0:T(8,128)S(1)} %get-tuple-element.37), channel_id=1, source_target_pairs={{0,0},{1,2},{2,1},{3,4},{4,3},{5,6},{6,5},{7,8},{8,7},{9,10},{10,9... | collective-permute-start | bytes 196616 | tf_op jit(solution)/shard_map/ppermute | solution.py:703
  52.9 0.3 shard_map.43.inner_ref
  53.1 1.6 %collective-permute-done.4.cross_in_ref = f32[4,32,128]{2,1,0:T(8,128)S(1)} collective-permute-done((f32[4,32,128]{2,1,0:T(8,128)S(1)}, f32[4,32,128]{2,1,0:T(8,128)S(1)}, u32[]{:S(2)}, u32[]{:S(2)}) %collective-permute-start.4) | collective-permute-done | bytes 65568 | tf_op jit(solution)/shard_map/ppermute | solution.py:703
  54.7 0.3 shard_map.44
  55.0 4.2 %collective-permute-start.6 = (f32[4,32,128]{2,1,0:T(8,128)S(1)}, f32[4,32,128]{2,1,0:T(8,128)S(1)}, u32[]{:S(2)}, u32[]{:S(2)}) collective-permute-start(f32[4,32,128]{2,1,0:T(8,128)S(1)} %get-tuple-element.41), channel_id=1, source_target_pairs={{0,0},{1,2},{2,1},{3,4},{4,3},{5,6},{6,5},{7,8},{8,7},{9,10},{10,9... | collective-permute-start | bytes 196616 | tf_op jit(solution)/shard_map/ppermute | solution.py:703
  59.6 0.3 shard_map.46.packed_ref
  59.9 1.3 %collective-permute-done.6.cross_in_ref = f32[4,32,128]{2,1,0:T(8,128)S(1)} collective-permute-done((f32[4,32,128]{2,1,0:T(8,128)S(1)}, f32[4,32,128]{2,1,0:T(8,128)S(1)}, u32[]{:S(2)}, u32[]{:S(2)}) %collective-permute-start.6) | collective-permute-done | bytes 65568 | tf_op jit(solution)/shard_map/ppermute | solution.py:703
  61.2 1.1 %shard_map.47 = (f32[2,32,640]{2,1,0:T(8,128)S(1)}, f32[16,8,128]{2,1,0:T(8,128)}) custom-call(f32[10,32,128]{2,1,0:T(8,128)S(1)} %get-tuple-element.39.edge_ref.edge_in_ref, f32[15,32,128]{2,1,0:T(8,128)S(1)} %shard_map.45.inner_ref, f32[4,32,128]{2,1,0:T(8,128)S(1)} %collective-permute-done.6.cross_in_ref, ...), custom_call_target="tpu_custom_call" | custom-call | tf_op jit(solution)/shard_map/pallas_call | solution.py:689
  62.2 9.8 %all-to-all-start.2 = ((f32[16,8,128]{2,1,0:T(8,128)}), f32[16,8,128]{2,1,0:T(8,128)S(1)}, u32[]{:S(2)}, u32[]{:S(2)}) async-start(f32[16,8,128]{2,1,0:T(8,128)} %get-tuple-element.43), calls=%async_computation.2 | async-start | bytes 131072 | tf_op jit(solution)/shard_map/all_to_all | solution.py:767
  72.1 0.7 shard_map.48.first_ref
  72.8 0.5 shard_map.50.inner_ref
  73.3 0.7 shard_map.49.second_ref
  74.0 5.9 %all-to-all-done.2.sums_ref = f32[16,8,128]{2,1,0:T(8,128)S(1)} async-done(((f32[16,8,128]{2,1,0:T(8,128)}), f32[16,8,128]{2,1,0:T(8,128)S(1)}, u32[]{:S(2)}, u32[]{:S(2)}) %all-to-all-start.2) | async-done | bytes 65568 | tf_op jit(solution)/shard_map/all_to_all | solution.py:767
  79.8 1.1 %shard_map.51 = f32[5,32,640]{2,1,0:T(8,128)} custom-call(f32[16,8,128]{2,1,0:T(8,128)S(1)} %all-to-all-done.2.sums_ref, f32[5,32,640]{2,1,0:T(8,128)S(1)} %shard_map.48.first_ref, f32[5,32,640]{2,1,0:T(8,128)S(1)} %shard_map.49.second_ref, f32[3,32,640]{2,1,0:T(8,128)S(1)} %shard_map.50.inner_ref, f32[2,32,640]{2,1,0:T(8,128)S(1)} %get-tuple-element.44.edge_ref), custom_call_target="tpu_custom_call" | custom-call | tf_op jit(solution)/shard_map/pallas_call | solution.py:689
  (15 shorter events, 0.9 us)
Async XLA Ops:
  0.0 19.2 %copy-start = (bf16[2,2,256,384]{3,2,1,0:T(8,128)(2,1)S(1)}, bf16[2,2,256,384]{3,2,1,0:T(8,128)(2,1)}, u32[]{:S(2)}) copy-start(bf16[2,2,256,384]{3,2,1,0:T(8,128)(2,1)} %constant.2.clone.table_ref) | copy-start | bytes 2359300
  20.2 12.7 %collective-permute-start.2 = (f32[40,768]{1,0:T(8,128)S(1)}, f32[40,768]{1,0:T(8,128)S(1)}, u32[]{:S(2)}, u32[]{:S(2)}) collective-permute-start(f32[40,768]{1,0:T(8,128)S(1)} %get-tuple-element.33), channel_id=1, source_target_pairs={{0,0},{1,2},{2,1},{3,4},{4,3},{5,6},{6,5},{7,8},{8,7},{9,10},{10,9... | collective-permute-start | bytes 368648 | tf_op jit(solution)/shard_map/ppermute | solution.py:703
  25.7 7.2 %collective-permute-start.3 = (f32[40,768]{1,0:T(8,128)S(1)}, f32[40,768]{1,0:T(8,128)S(1)}, u32[]{:S(2)}, u32[]{:S(2)}) collective-permute-start(f32[40,768]{1,0:T(8,128)S(1)} %get-tuple-element.34), channel_id=1, source_target_pairs={{0,1},{1,0},{2,3},{3,2},{4,5},{5,4},{6,7},{7,6},{8,9},{9,8},{10,11... | collective-permute-start | bytes 368648 | tf_op jit(solution)/shard_map/ppermute | solution.py:702
  25.8 6.0 %collective-permute-start = (f32[2,40,256]{2,1,0:T(8,128)S(1)}, f32[2,40,256]{2,1,0:T(8,128)S(1)}, u32[]{:S(2)}, u32[]{:S(2)}) collective-permute-start(f32[2,40,256]{2,1,0:T(8,128)S(1)} %get-tuple-element.28), channel_id=1, source_target_pairs={{0,0},{1,2},{2,1},{3,4},{4,3},{5,6},{6,5},{7,8},{8,7},{9,10},{10,9... | collective-permute-start | bytes 245768 | tf_op jit(solution)/shard_map/ppermute | solution.py:703
  29.8 2.1 %collective-permute-start.1 = (f32[2,40,256]{2,1,0:T(8,128)S(1)}, f32[2,40,256]{2,1,0:T(8,128)S(1)}, u32[]{:S(2)}, u32[]{:S(2)}) collective-permute-start(f32[2,40,256]{2,1,0:T(8,128)S(1)} %get-tuple-element.29), channel_id=1, source_target_pairs={{0,1},{1,0},{2,3},{3,2},{4,5},{5,4},{6,7},{7,6},{8,9},{9,8},{10,11... | collective-permute-start | bytes 245768 | tf_op jit(solution)/shard_map/ppermute | solution.py:702
  29.9 2.0 %copy-start.1 = (s32[128]{0:T(128)S(1)}, s32[128]{0:T(128)}, u32[]{:S(2)}) copy-start(s32[128]{0:T(128)} %tag_ref.1) | copy-start | bytes 1540
  47.4 7.3 %collective-permute-start.4 = (f32[4,32,128]{2,1,0:T(8,128)S(1)}, f32[4,32,128]{2,1,0:T(8,128)S(1)}, u32[]{:S(2)}, u32[]{:S(2)}) collective-permute-start(f32[4,32,128]{2,1,0:T(8,128)S(1)} %get-tuple-element.37), channel_id=1, source_target_pairs={{0,0},{1,2},{2,1},{3,4},{4,3},{5,6},{6,5},{7,8},{8,7},{9,10},{10,9... | collective-permute-start | bytes 196616 | tf_op jit(solution)/shard_map/ppermute | solution.py:703
  52.8 1.9 %collective-permute-start.5 = (f32[4,32,128]{2,1,0:T(8,128)S(1)}, f32[4,32,128]{2,1,0:T(8,128)S(1)}, u32[]{:S(2)}, u32[]{:S(2)}) collective-permute-start(f32[4,32,128]{2,1,0:T(8,128)S(1)} %get-tuple-element.38), channel_id=1, source_target_pairs={{0,1},{1,0},{2,3},{3,2},{4,5},{5,4},{6,7},{7,6},{8,9},{9,8},{10,11... | collective-permute-start | bytes 196616 | tf_op jit(solution)/shard_map/ppermute | solution.py:702
  55.0 6.1 %collective-permute-start.6 = (f32[4,32,128]{2,1,0:T(8,128)S(1)}, f32[4,32,128]{2,1,0:T(8,128)S(1)}, u32[]{:S(2)}, u32[]{:S(2)}) collective-permute-start(f32[4,32,128]{2,1,0:T(8,128)S(1)} %get-tuple-element.41), channel_id=1, source_target_pairs={{0,0},{1,2},{2,1},{3,4},{4,3},{5,6},{6,5},{7,8},{8,7},{9,10},{10,9... | collective-permute-start | bytes 196616 | tf_op jit(solution)/shard_map/ppermute | solution.py:703
  59.2 1.9 %collective-permute-start.7 = (f32[4,32,128]{2,1,0:T(8,128)S(1)}, f32[4,32,128]{2,1,0:T(8,128)S(1)}, u32[]{:S(2)}, u32[]{:S(2)}) collective-permute-start(f32[4,32,128]{2,1,0:T(8,128)S(1)} %get-tuple-element.42), channel_id=1, source_target_pairs={{0,1},{1,0},{2,3},{3,2},{4,5},{5,4},{6,7},{7,6},{8,9},{9,8},{10,11... | collective-permute-start | bytes 196616 | tf_op jit(solution)/shard_map/ppermute | solution.py:702
  62.2 17.6 %all-to-all-start.2 = ((f32[16,8,128]{2,1,0:T(8,128)}), f32[16,8,128]{2,1,0:T(8,128)S(1)}, u32[]{:S(2)}, u32[]{:S(2)}) async-start(f32[16,8,128]{2,1,0:T(8,128)} %get-tuple-element.43), calls=%async_computation.2 | async-start | bytes 131072 | tf_op jit(solution)/shard_map/all_to_all | solution.py:767
